TPU v7x, 512 devices: a whole 4x8x8 slice. The times are simulated.
512 devices in a mesh: blk: 8 (over y_lo, core), team: 64 (over y_hi, x, z).
Axes of the slice: x: 4, y: 8 (y_hi: 2, y_lo: 4; y = y_hi * 4 + y_lo), z: 8, core: 2. Of those that a mesh axis runs over, the one named last changes fastest.
Arguments:
- features: bfloat16 [65536, 256], P(('blk', 'team')), may hold values from -6 to 6
- weight: bfloat16 [256, 256], replicated, may hold values from -0.375 to 0.375
- bias: float32 [256], replicated, may hold values from -3 to 3
- cotangent: bfloat16 [65536, 256], P(('blk', 'team')), may hold values from -6 to 6
- adj_cols: int32 [64, 8, 8, 12], P('team', None, 'blk'), may hold values from 0 to 63, as said below
- adj_vals: bfloat16 [64, 8, 8, 12, 128, 128], P('team', None, 'blk'), as said below
Outputs:
- hidden: bfloat16 [65536, 256], P(('blk', 'team'))
- grad_input: bfloat16 [65536, 256], P(('blk', 'team'))
- grad_weight: float32 [256, 256], replicated
- grad_bias: float32 [256], replicated
Inputs may be any that keep to these rules, and one draw needn't show every extreme that they name: `adj_cols`: for every node panel and column group the 12 entries are distinct. Block (i, j) of A is listed exactly when block (j, i) is, every column panel is listed by exactly 12 row panels of each column group, and A is symmetric. `adj_vals`: the block listed for panels (i, j) is the transpose of the block listed for (j, i), so A is symmetric.
All inputs are finite; a program needn't handle non-finite values.
Results may differ from a plain program's by a relative error of at most 0.0075.
Values may be sent and summed in bfloat16 or wider, within the bound.
No kernel may reach another device: no remote copies, remote signals or barrier semaphores. Data moves between devices by JAX's collectives and lax.ppermute only.
A program may use at most 64 MiB of HBM per device.

v0:
```python
import jax
import jax.numpy as jnp
from jax import lax
from jax.sharding import PartitionSpec as P


def collect(panels, adj_cols, adj_vals):
    block = adj_vals.shape[-1]
    width = panels.shape[1]
    stacked = panels.reshape(panels.shape[0] // block, block, width)
    picked = jnp.take(stacked, adj_cols[0, :, 0, :], axis=0)
    summed = jnp.einsum(
        "rkij,rkjf->rif", adj_vals[0, :, 0], picked, preferred_element_type=jnp.float32
    )
    return summed.reshape(-1, width)


def activation(value):
    return jax.nn.gelu(value, approximate=True)


def local(features, weight, bias, cotangent, adj_cols, adj_vals):
    gathered = jnp.dot(
        lax.all_gather(features, "team", axis=0, tiled=True),
        weight,
        preferred_element_type=jnp.float32,
    ).astype(jnp.bfloat16)
    partial_rows = collect(gathered, adj_cols, adj_vals)
    summed = lax.psum_scatter(partial_rows, "blk", scatter_dimension=0, tiled=True)
    pre = summed + bias[None, :]
    activated, pullback = jax.vjp(activation, pre)
    hidden = activated.astype(jnp.bfloat16)
    pulled = pullback(cotangent.astype(jnp.float32))[0].astype(jnp.bfloat16)
    pulled_group = lax.all_gather(pulled, "team", axis=0, tiled=True)
    partial_back = collect(pulled_group, adj_cols, adj_vals)
    spread = lax.psum_scatter(partial_back, "blk", scatter_dimension=0, tiled=True).astype(
        jnp.bfloat16
    )
    grad_input = jnp.dot(spread, weight.T, preferred_element_type=jnp.float32).astype(jnp.bfloat16)
    local_weight = lax.dot_general(
        features, spread, (((0,), (0,)), ((), ())), preferred_element_type=jnp.float32
    )
    local_bias = jnp.sum(pulled.astype(jnp.float32), axis=0)
    grad_weight, grad_bias = lax.psum((local_weight, local_bias), ("blk", "team"))
    return (hidden, grad_input, grad_weight, grad_bias)


def solution(mesh):
    return jax.shard_map(
        local,
        mesh=mesh,
        in_specs=(
            P(("blk", "team"), None),
            P(),
            P(),
            P(("blk", "team"), None),
            P("team", None, "blk", None),
            P("team", None, "blk", None, None, None),
        ),
        out_specs=(P(("blk", "team"), None), P(("blk", "team"), None), P(), P()),
        check_vma=False,
    )
```

profile of v0, /device:TPU:1, one launch (start us, length us, event | category | flops | bytes accessed | tf_op | source)
XLA Modules:
  0.0 763.9 jit_solution(11650061176644442097)
XLA Ops:
  7.2 0.0 all-gather.3.cloned.1.call-start
  7.2 0.7 all-gather.3.cloned.1.call-update
  7.9 0.0 reduce-scatter.3.cloned.1.call-start
  8.0 0.8 compare_select_fusion
  8.8 0.1 reshape.50
  8.9 0.7 compare_and_fusion
  9.6 153.0 %all-gather.3.cloned.1.call-done = bf16[8192,256]{1,0:T(8,128)(2,1)} async-done(((bf16[128,256]{1,0:T(8,128)(2,1)}), bf16[8192,256]{1,0:T(8,128)(2,1)}) %all-gather.3.cloned.1.call-update) | async-done | bytes 4194320 | tf_op jit(solution)/shard_map/all_gather | solution.py:24
  162.6 5.5 convolution_convert_fusion
  168.1 8.2 %gather_fusion = bf16[96,128,256]{2,1,0:T(8,128)(2,1)} fusion(bf16[64,128,256]{2,1,0:T(8,128)(2,1)} %bitcast.28, s32[1024]{0:T(1024)S(1)} %pad_clamp_fusion), kind=kCustom, calls=%fused_computation.clone | custom fusion | bytes 12583296 | tf_op jit(solution)/shard_map/jit(_take)/gather | solution.py:11
  176.3 5.2 fusion.2
  181.5 0.0 all-gather.5.cloned.1.call-start
  181.6 41.9 %reduce-scatter.3.cloned.1.call-done = f32[128,256]{1,0:T(8,128)} async-done(((f32[1024,256]{1,0:T(8,128)}), f32[128,256]{1,0:T(8,128)}) %reduce-scatter.3.cloned.1.call-update) | async-done | bytes 131088 | tf_op jit(solution)/shard_map/reduce_scatter | solution.py:29
  223.5 1.7 convert_reduce_fusion
  225.1 0.0 all-gather.5.cloned.1.call-update
  225.2 0.0 reduce-scatter.5.cloned.1.call-start
  225.2 148.5 %all-gather.5.cloned.1.call-done = bf16[8192,256]{1,0:T(8,128)(2,1)} async-done(((bf16[128,256]{1,0:T(8,128)(2,1)}), bf16[8192,256]{1,0:T(8,128)(2,1)}) %all-gather.5.cloned.1.call-update) | async-done | bytes 4194320 | tf_op jit(solution)/shard_map/all_gather | solution.py:34
  373.8 8.2 %gather_fusion.1 = bf16[96,128,256]{2,1,0:T(8,128)(2,1)} fusion(bf16[64,128,256]{2,1,0:T(8,128)(2,1)} %bitcast.29, s32[1024]{0:T(1024)S(1)} %pad_clamp_fusion), kind=kCustom, calls=%fused_computation.1.clone | custom fusion | bytes 12583296 | tf_op jit(solution)/shard_map/jit(_take)/gather | solution.py:11
  382.0 5.2 fusion
  387.2 0.0 all-reduce.2.cloned.1.call-start
  387.2 105.9 %psum.15 = f32[256]{0:T(256)} all-reduce(f32[256]{0:T(256)S(1)} %get-tuple-element.9), channel_id=1, replica_groups=mesh['blk'=8,'team'=64] {'blk','team'}, use_global_device_ids=true, to_apply=%region_4.6 | all-reduce | flops 256 | bytes 2048 | tf_op jit(solution)/shard_map/psum | solution.py:44
  493.2 1.8 convolution_bitcast_fusion
  495.0 1.7 convolution_convert_fusion.1
  496.8 258.8 %all-reduce.2.cloned.1.call-done = f32[256,256]{0,1:T(8,128)} async-done(((f32[256,256]{0,1:T(8,128)}), f32[256,256]{0,1:T(8,128)}) %all-reduce.2.cloned.1.call-update) | async-done | bytes 262160 | tf_op jit(solution)/shard_map/psum | solution.py:44
  755.6 1.8 copy.10
  (15 shorter events, 0.1 us)
Async XLA Ops:
  7.2 169.1 %copy-start = (bf16[1,8,1,12,128,128]{5,4,3,2,1,0:T(8,128)(2,1)S(1)}, bf16[1,8,1,12,128,128]{5,4,3,2,1,0:T(8,128)(2,1)}, u32[]{:S(2)}) copy-start(bf16[1,8,1,12,128,128]{5,4,3,2,1,0:T(8,128)(2,1)} %param.13) | copy-start | bytes 9437188
  7.2 155.4 %all-gather.3.cloned.1.call-start = ((), (), s32[]{:S(2)}) async-start(), calls=%async_computation.2 | async-start | bytes 4259840 | tf_op jit(solution)/shard_map/all_gather | solution.py:24
  7.9 215.5 %reduce-scatter.3.cloned.1.call-start = ((), (), s32[]{:S(2)}) async-start(), calls=%async_computation.3 | async-start | bytes 1179648 | tf_op jit(solution)/shard_map/reduce_scatter | solution.py:29
  176.3 47.2 %copy-start.3 = (bf16[128,256]{1,0:T(8,128)(2,1)S(1)}, bf16[128,256]{1,0:T(8,128)(2,1)}, u32[]{:S(2)}) copy-start(bf16[128,256]{1,0:T(8,128)(2,1)} %param.11) | copy-start | bytes 196612
  176.3 47.2 %copy-start.4 = (f32[256]{0:T(256)S(1)}, f32[256]{0:T(256)}, u32[]{:S(2)}) copy-start(f32[256]{0:T(256)} %param.10) | copy-start | bytes 3076
  181.5 192.2 %all-gather.5.cloned.1.call-start = ((), (), s32[]{:S(2)}) async-start(), calls=%async_computation.4 | async-start | bytes 4259840 | tf_op jit(solution)/shard_map/all_gather | solution.py:34
  225.2 268.0 %reduce-scatter.5.cloned.1.call-start = ((), (), s32[]{:S(2)}) async-start(), calls=%async_computation.5 | async-start | bytes 1179648 | tf_op jit(solution)/shard_map/reduce_scatter | solution.py:36
  382.0 111.2 %copy-start.2 = (bf16[128,256]{1,0:T(8,128)(2,1)S(1)}, bf16[128,256]{1,0:T(8,128)(2,1)}, u32[]{:S(2)}) copy-start(bf16[128,256]{1,0:T(8,128)(2,1)} %param.8) | copy-start | bytes 196612
  382.0 113.1 %copy-start.1 = (bf16[256,256]{1,0:T(8,128)(2,1)S(1)}, bf16[256,256]{1,0:T(8,128)(2,1)}, u32[]{:S(2)}) copy-start(bf16[256,256]{1,0:T(8,128)(2,1)} %param.9) | copy-start | bytes 393220
  387.2 368.4 %all-reduce.2.cloned.1.call-start = ((), (), s32[]{:S(2)}) async-start(), calls=%async_computation.6 | async-start | bytes 524288 | tf_op jit(solution)/shard_map/psum | solution.py:44
Sparse Core Ops, SparseCore 0:
  12.5 150.0 all-gather.2
  181.6 41.7 reduce-scatter.2
  228.5 145.1 all-gather.4
  387.3 41.5 reduce-scatter.4
  495.1 260.4 all-reduce.1
where the time goes:
time: 764 us
  waiting for transfers between devices  603 us (79%)
  blocking collectives  106 us (14%)
  matrix products  19.4 us (3%)
  local copies, waits for them, and re-layouts  18.3 us (2%)
  between operations  13.8 us (2%)
    psum x1, waiting for transfers between devices, local(): lax.psum((local_weight, local_bias), ('blk', 'team'))  259 us
    all_gather x1, waiting for transfers between devices, local(): lax.all_gather(features, 'team', axis=0, tiled=True)  153 us
    all_gather x1, waiting for transfers between devices, local(): pulled_group = lax.all_gather(pulled, 'team', axis=0, tiled=True)  149 us
    psum x1, blocking collectives, local(): lax.psum((local_weight, local_bias), ('blk', 'team'))  106 us
    reduce_scatter x1, waiting for transfers between devices, local(): lax.psum_scatter(partial_rows, 'blk', scatter_dimension=0, tiled=True)  41.9 us
    gather x2, local copies, waits for them, and re-layouts, collect(): picked = jnp.take(stacked, adj_cols[0, :, 0, :], axis=0)  16.4 us
  transfers between devices with their start and end apart: 5, of which 4 were waited for; matrix products, arithmetic and copies ran while one was open for 0% of the time, Pallas kernels for 0%

commit v1 on v0

v1 whole, which is shorter than its diff:
```python
import jax
import jax.numpy as jnp
from jax import lax
from jax.sharding import Mesh
from jax.sharding import PartitionSpec as P

BLK_AXES = ("y_lo", "core")
TEAM_AXES = ("y_hi", "x", "z")
PLANE = ("x", "z")
ALL_AXES = BLK_AXES + TEAM_AXES


def fine_mesh(mesh):
    blk = mesh.shape["blk"]
    team = mesh.shape["team"]
    sizes = (blk // 2, 2, 2, 4, team // 8)
    return Mesh(mesh.devices.reshape(sizes), ALL_AXES)


def gather_team(rows):
    other = lax.ppermute(rows, "y_hi", perm=[(0, 1), (1, 0)])
    pair = jnp.stack([rows, other], axis=0)
    full = lax.all_gather(pair, PLANE, axis=0, tiled=True)
    return full.reshape(-1, rows.shape[1])


def member_slots(members, plane_size):
    my_hi = lax.axis_index("y_hi")
    return (members % plane_size) * 2 + (members // plane_size != my_hi).astype(jnp.int32)


def collect(panels, slots, adj_vals):
    block = adj_vals.shape[-1]
    width = panels.shape[1]
    stacked = panels.reshape(panels.shape[0] // block, block, width)
    picked = jnp.take(stacked, slots, axis=0)
    summed = jnp.einsum(
        "rkij,rkjf->rif", adj_vals[0, :, 0], picked, preferred_element_type=jnp.float32
    )
    return summed.reshape(-1, width)


def activation(value):
    return jax.nn.gelu(value, approximate=True)


def local(features, weight, bias, cotangent, adj_cols, adj_vals):
    plane_size = lax.psum(1, PLANE)
    slots = member_slots(adj_cols[0, :, 0, :], plane_size)
    product = jnp.dot(features, weight, preferred_element_type=jnp.float32).astype(jnp.bfloat16)
    gathered = gather_team(product)
    partial_rows = collect(gathered, slots, adj_vals)
    summed = lax.psum_scatter(partial_rows, BLK_AXES, scatter_dimension=0, tiled=True)
    pre = summed + bias[None, :]
    activated, pullback = jax.vjp(activation, pre)
    hidden = activated.astype(jnp.bfloat16)
    pulled = pullback(cotangent.astype(jnp.float32))[0].astype(jnp.bfloat16)
    pulled_group = gather_team(pulled)
    partial_back = collect(pulled_group, slots, adj_vals)
    spread = lax.psum_scatter(partial_back, BLK_AXES, scatter_dimension=0, tiled=True).astype(
        jnp.bfloat16
    )
    grad_input = jnp.dot(spread, weight.T, preferred_element_type=jnp.float32).astype(jnp.bfloat16)
    local_weight = lax.dot_general(
        features, spread, (((0,), (0,)), ((), ())), preferred_element_type=jnp.float32
    )
    local_bias = jnp.sum(pulled.astype(jnp.float32), axis=0)
    both = jnp.concatenate([local_weight, local_bias[None, :]], axis=0)
    both = lax.psum(both, PLANE)
    both = lax.psum(both, ("y_lo", "y_hi", "core"))
    grad_weight = both[:-1]
    grad_bias = both[-1]
    return (hidden, grad_input, grad_weight, grad_bias)


def solution(mesh):
    fine = fine_mesh(mesh)
    rows = P(ALL_AXES, None)
    return jax.shard_map(
        local,
        mesh=fine,
        in_specs=(
            rows,
            P(),
            P(),
            rows,
            P(TEAM_AXES, None, BLK_AXES, None),
            P(TEAM_AXES, None, BLK_AXES, None, None, None),
        ),
        out_specs=(rows, rows, P(), P()),
        check_vma=False,
    )
```

time: 764 us -> 591 us (0.77)
  blocking collectives: 106 us -> 0 us
  waiting for transfers between devices: 603 us -> 524 us
  starting transfers between devices: 0.2 us -> 14 us
    all_gather x2, waiting for transfers between devices: 302 us -> 178 us  [gather_team(): full = lax.all_gather(pair, PLANE, axis=0, tiled=True)]
    psum x1 -> x0, blocking collectives: 106 us -> none  [local(): lax.psum((local_weight, local_bias), ('blk', 'team'))]
    reduce_scatter x2, waiting for transfers between devices: 41.9 us -> 75.9 us  [the longest x1 37.9 us: local(): lax.psum_scatter(partial_rows, BLK_AXES, scatter_dimension=0, tiled=True)]
    ppermute x0 -> x2, starting transfers between devices: none -> 13.8 us  [gather_team(): other = lax.ppermute(rows, 'y_hi', perm=[(0, 1), (1, 0)])]
    psum x1 -> x2, waiting for transfers between devices: 259 us -> 265 us  [the longest x1 153 us: local(): both = lax.psum(both, PLANE)]
  transfers between devices with their start and end apart: 5 -> 8, of which waited for: 4 -> 8; matrix products, arithmetic and copies ran while one was open for 0% -> 0% of each run, Pallas kernels for 0% -> 0%
where the time goes in v1:
time: 591 us; the launch traced here: 590 us
  waiting for transfers between devices  524 us (89%)
  local copies, waits for them, and re-layouts  19.4 us (3%)
  matrix products  14.5 us (2%)
  between operations  14.2 us (2%)
  starting transfers between devices  14 us (2%)
    all_gather x2, waiting for transfers between devices, gather_team(): full = lax.all_gather(pair, PLANE, axis=0, tiled=True)  178 us
    psum x1, waiting for transfers between devices, local(): both = lax.psum(both, PLANE)  153 us
    psum x1, waiting for transfers between devices, local(): both = lax.psum(both, ('y_lo', 'y_hi', 'core'))  112 us
    reduce_scatter x1, waiting for transfers between devices, local(): lax.psum_scatter(partial_rows, BLK_AXES, scatter_dimension=0, tiled=True)  37.9 us
    reduce_scatter x1, waiting for transfers between devices, local(): lax.psum_scatter(partial_back, BLK_AXES, scatter_dimension=0, tiled=True)  37.9 us
    gather x2, local copies, waits for them, and re-layouts, collect(): picked = jnp.take(stacked, slots, axis=0)  16.4 us
    ppermute x2, starting transfers between devices, gather_team(): other = lax.ppermute(rows, 'y_hi', perm=[(0, 1), (1, 0)])  13.8 us
  transfers between devices with their start and end apart: 8, of which 8 were waited for; matrix products, arithmetic and copies ran while one was open for 0% of the time, Pallas kernels for 0%

profile of v1, /device:TPU:1, one launch (start us, length us, event | category | flops | bytes accessed | tf_op | source)
XLA Modules:
  0.0 590.3 jit_solution(9726838023997011577)
XLA Ops:
  7.2 1.2 convolution_convert_fusion.1
  8.5 8.3 %collective-permute-start = (bf16[128,256]{1,0:T(8,128)(2,1)S(1)}, bf16[128,256]{1,0:T(8,128)(2,1)S(1)}, u32[]{:S(2)}, u32[]{:S(2)}) collective-permute-start(bf16[128,256]{1,0:T(8,128)(2,1)S(1)} %convolution_convert_fusion.1), channel_id=1, source_target_pairs={{0,32},{32,0},{1,33},{33,1},{2,34},{34,2},{3,35},{35,3},{4,36},{36... | collective-permute-start | bytes 196616 | tf_op jit(solution)/shard_map/ppermute | solution.py:21
  16.8 1.7 collective-permute-done
  18.5 0.7 pad_maximum_fusion.1
  19.2 0.7 compare_and_fusion
  20.0 91.1 %all-gather.3.cloned.1.call-done = bf16[64,128,256]{2,1,0:T(8,128)(2,1)} async-done(((bf16[2,128,256]{2,1,0:T(8,128)(2,1)}), bf16[64,128,256]{2,1,0:T(8,128)(2,1)}) %all-gather.3.cloned.1.call-update) | async-done | bytes 4194320 | tf_op jit(solution)/shard_map/all_gather | solution.py:23
  111.1 8.2 %gather_fusion = bf16[96,128,256]{2,1,0:T(8,128)(2,1)} fusion(bf16[64,128,256]{2,1,0:T(8,128)(2,1)} %all-gather.3.cloned.1.call-done, s32[1024]{0:T(1024)S(1)} %pad_clamp_fusion), kind=kCustom, calls=%fused_computation.clone | custom fusion | bytes 12583296 | tf_op jit(solution)/shard_map/jit(_take)/gather | solution.py:36
  119.3 5.2 fusion.2
  124.6 37.9 %reduce-scatter.3.cloned.1.call-done = f32[128,256]{1,0:T(8,128)} async-done(((f32[1024,256]{1,0:T(8,128)}), f32[128,256]{1,0:T(8,128)}) %reduce-scatter.3.cloned.1.call-update) | async-done | bytes 131088 | tf_op jit(solution)/shard_map/reduce_scatter | solution.py:53
  162.5 1.6 convert_reduce_fusion
  164.2 5.5 collective-permute-start.1
  169.7 3.7 collective-permute-done.1
  173.3 0.7 pad_maximum_fusion.2
  174.1 86.7 %all-gather.5.cloned.1.call-done = bf16[64,128,256]{2,1,0:T(8,128)(2,1)} async-done(((bf16[2,128,256]{2,1,0:T(8,128)(2,1)}), bf16[64,128,256]{2,1,0:T(8,128)(2,1)}) %all-gather.5.cloned.1.call-update) | async-done | bytes 4194320 | tf_op jit(solution)/shard_map/all_gather | solution.py:23
  260.8 8.2 %gather_fusion.1 = bf16[96,128,256]{2,1,0:T(8,128)(2,1)} fusion(bf16[64,128,256]{2,1,0:T(8,128)(2,1)} %all-gather.5.cloned.1.call-done, s32[1024]{0:T(1024)S(1)} %pad_clamp_fusion), kind=kCustom, calls=%fused_computation.1.clone | custom fusion | bytes 12583296 | tf_op jit(solution)/shard_map/jit(_take)/gather | solution.py:36
  269.0 5.2 fusion
  274.2 37.9 %reduce-scatter.5.cloned.1.call-done = f32[128,256]{1,0:T(8,128)} async-done(((f32[1024,256]{1,0:T(8,128)}), f32[128,256]{1,0:T(8,128)}) %reduce-scatter.5.cloned.1.call-update) | async-done | bytes 131088 | tf_op jit(solution)/shard_map/reduce_scatter | solution.py:60
  312.2 1.1 convolution_bitcast_fusion
  313.3 0.7 pad_maximum_fusion
  314.1 153.0 %all-reduce.3.cloned.1.call-done = f32[257,256]{1,0:T(8,128)} async-done(((f32[257,256]{1,0:T(8,128)}), f32[257,256]{1,0:T(8,128)}) %all-reduce.3.cloned.1.call-update) | async-done | bytes 263184 | tf_op jit(solution)/shard_map/psum | solution.py:69
  467.2 1.7 convolution_convert_fusion
  468.9 111.6 %all-reduce.5.cloned.1.call-done = f32[257,256]{1,0:T(8,128)} async-done(((f32[257,256]{1,0:T(8,128)}), f32[257,256]{1,0:T(8,128)}) %all-reduce.5.cloned.1.call-update) | async-done | bytes 263184 | tf_op jit(solution)/shard_map/psum | solution.py:70
  580.5 1.3 slice.13
  581.8 1.7 slice.12
  (24 shorter events, 0.5 us)
Async XLA Ops:
  7.2 112.2 %copy-start = (bf16[1,8,1,12,128,128]{5,4,3,2,1,0:T(8,128)(2,1)S(1)}, bf16[1,8,1,12,128,128]{5,4,3,2,1,0:T(8,128)(2,1)}, u32[]{:S(2)}) copy-start(bf16[1,8,1,12,128,128]{5,4,3,2,1,0:T(8,128)(2,1)} %param.13) | copy-start | bytes 9437188
  7.2 103.9 %all-gather.3.cloned.1.call-start = ((), (), s32[]{:S(2)}) async-start(), calls=%async_computation.2 | async-start | bytes 4325376 | tf_op jit(solution)/shard_map/all_gather | solution.py:23
  8.5 10.0 %collective-permute-start = (bf16[128,256]{1,0:T(8,128)(2,1)S(1)}, bf16[128,256]{1,0:T(8,128)(2,1)S(1)}, u32[]{:S(2)}, u32[]{:S(2)}) collective-permute-start(bf16[128,256]{1,0:T(8,128)(2,1)S(1)} %convolution_convert_fusion.1), channel_id=1, source_target_pairs={{0,32},{32,0},{1,33},{33,1},{2,34},{34,2},{3,35},{35,3},{4,36},{36... | collective-permute-start | bytes 196616 | tf_op jit(solution)/shard_map/ppermute | solution.py:21
  19.2 143.3 %reduce-scatter.3.cloned.1.call-start = ((), (), s32[]{:S(2)}) async-start(), calls=%async_computation.3 | async-start | bytes 1179648 | tf_op jit(solution)/shard_map/reduce_scatter | solution.py:53
  119.3 43.2 %copy-start.3 = (bf16[128,256]{1,0:T(8,128)(2,1)S(1)}, bf16[128,256]{1,0:T(8,128)(2,1)}, u32[]{:S(2)}) copy-start(bf16[128,256]{1,0:T(8,128)(2,1)} %param.11) | copy-start | bytes 196612
  119.3 43.2 %copy-start.4 = (f32[256]{0:T(256)S(1)}, f32[256]{0:T(256)}, u32[]{:S(2)}) copy-start(f32[256]{0:T(256)} %param.10) | copy-start | bytes 3076
  124.5 136.2 %all-gather.5.cloned.1.call-start = ((), (), s32[]{:S(2)}) async-start(), calls=%async_computation.4 | async-start | bytes 4325376 | tf_op jit(solution)/shard_map/all_gather | solution.py:23
  164.2 9.1 %collective-permute-start.1 = (bf16[128,256]{1,0:T(8,128)(2,1)S(1)}, bf16[128,256]{1,0:T(8,128)(2,1)S(1)}, u32[]{:S(2)}, u32[]{:S(2)}) collective-permute-start(bf16[128,256]{1,0:T(8,128)(2,1)S(1)} %get-tuple-element.6), channel_id=1, source_target_pairs={{0,32},{32,0},{1,33},{33,1},{2,34},{34,2},{3,35},{35,3},{4,36},{36... | collective-permute-start | bytes 196616 | tf_op jit(solution)/shard_map/ppermute | solution.py:21
  174.0 138.2 %reduce-scatter.5.cloned.1.call-start = ((), (), s32[]{:S(2)}) async-start(), calls=%async_computation.5 | async-start | bytes 1179648 | tf_op jit(solution)/shard_map/reduce_scatter | solution.py:60
  268.9 43.2 %copy-start.2 = (bf16[128,256]{1,0:T(8,128)(2,1)S(1)}, bf16[128,256]{1,0:T(8,128)(2,1)}, u32[]{:S(2)}) copy-start(bf16[128,256]{1,0:T(8,128)(2,1)} %param.8) | copy-start | bytes 196612
  268.9 198.2 %copy-start.1 = (bf16[256,256]{1,0:T(8,128)(2,1)S(1)}, bf16[256,256]{1,0:T(8,128)(2,1)}, u32[]{:S(2)}) copy-start(bf16[256,256]{1,0:T(8,128)(2,1)} %param.9) | copy-start | bytes 393220
  274.2 193.0 %all-reduce.3.cloned.1.call-start = ((), (), s32[]{:S(2)}) async-start(), calls=%async_computation.6 | async-start | bytes 540672 | tf_op jit(solution)/shard_map/psum | solution.py:69
  314.0 266.5 %all-reduce.5.cloned.1.call-start = ((), (), s32[]{:S(2)}) async-start(), calls=%async_computation.7 | async-start | bytes 540672 | tf_op jit(solution)/shard_map/psum | solution.py:70
Sparse Core Ops, SparseCore 0:
  19.3 91.7 all-gather.2
  124.7 37.8 reduce-scatter.2
  174.1 86.5 all-gather.4
  274.3 37.8 reduce-scatter.4
  315.4 151.6 all-reduce.2
  469.3 111.1 all-reduce.4

commit v2 on v1

--- a/solution.py
+++ b/solution.py
@@ -6,27 +6,86 @@
 
 BLK_AXES = ("y_lo", "core")
 TEAM_AXES = ("y_hi", "x", "z")
-PLANE = ("x", "z")
 ALL_AXES = BLK_AXES + TEAM_AXES
+SIZES = {}
 
 
 def fine_mesh(mesh):
     blk = mesh.shape["blk"]
     team = mesh.shape["team"]
     sizes = (blk // 2, 2, 2, 4, team // 8)
+    SIZES.update(zip(ALL_AXES, sizes))
     return Mesh(mesh.devices.reshape(sizes), ALL_AXES)
+
+
+def ring_offsets(n):
+    offsets = [0]
+    for step in range(1, n // 2 + 1):
+        offsets.append(-step)
+        if step < n - step:
+            offsets.append(step)
+    return offsets
+
+
+def ring_gather(blocks, axis):
+    n = SIZES[axis]
+    ahead = blocks
+    behind = blocks
+    parts = [blocks]
+    for step in range(1, n // 2 + 1):
+        ahead = lax.ppermute(ahead, axis, [(i, (i + 1) % n) for i in range(n)])
+        parts.append(ahead)
+        if step < n - step:
+            behind = lax.ppermute(behind, axis, [(i, (i - 1) % n) for i in range(n)])
+            parts.append(behind)
+    return jnp.concatenate(parts, axis=0)
 
 
 def gather_team(rows):
     other = lax.ppermute(rows, "y_hi", perm=[(0, 1), (1, 0)])
     pair = jnp.stack([rows, other], axis=0)
-    full = lax.all_gather(pair, PLANE, axis=0, tiled=True)
+    full = ring_gather(ring_gather(pair, "x"), "z")
     return full.reshape(-1, rows.shape[1])
 
 
-def member_slots(members, plane_size):
-    my_hi = lax.axis_index("y_hi")
-    return (members % plane_size) * 2 + (members // plane_size != my_hi).astype(jnp.int32)
+def ring_slot(delta, axis):
+    n = SIZES[axis]
+    order = [o % n for o in ring_offsets(n)]
+    table = [order.index(d) for d in range(n)]
+    return jnp.asarray(table, jnp.int32)[(delta + n) % n]
+
+
+def member_slots(members):
+    nx, nz = SIZES["x"], SIZES["z"]
+    m_hi = members // (nx * nz)
+    m_x = (members // nz) % nx
+    m_z = members % nz
+    y_slot = (m_hi != lax.axis_index("y_hi")).astype(jnp.int32)
+    x_slot = ring_slot(m_x - lax.axis_index("x"), "x")
+    z_slot = ring_slot(m_z - lax.axis_index("z"), "z")
+    return (z_slot * nx + x_slot) * 2 + y_slot
+
+
+def swap(value, axis, bit):
+    n = SIZES[axis]
+    return lax.ppermute(value, axis, [(i, i ^ bit) for i in range(n)])
+
+
+BUTTERFLY = (("y_lo", 1), ("x", 1), ("z", 1), ("y_lo", 2), ("x", 2), ("z", 2), ("z", 4), ("y_hi", 1))
+
+
+def all_sum(value):
+    half = value.shape[0] // 2
+    upper = lax.axis_index("core") == 1
+    low, high = value[:half], value[half:]
+    keep = jnp.where(upper, high, low)
+    send = jnp.where(upper, low, high)
+    part = keep + swap(send, "core", 1)
+    for axis, bit in BUTTERFLY:
+        if bit < SIZES[axis]:
+            part = part + swap(part, axis, bit)
+    other = swap(part, "core", 1)
+    return jnp.where(upper, jnp.concatenate([other, part]), jnp.concatenate([part, other]))
 
 
 def collect(panels, slots, adj_vals):
@@ -45,8 +104,7 @@
 
 
 def local(features, weight, bias, cotangent, adj_cols, adj_vals):
-    plane_size = lax.psum(1, PLANE)
-    slots = member_slots(adj_cols[0, :, 0, :], plane_size)
+    slots = member_slots(adj_cols[0, :, 0, :])
     product = jnp.dot(features, weight, preferred_element_type=jnp.float32).astype(jnp.bfloat16)
     gathered = gather_team(product)
     partial_rows = collect(gathered, slots, adj_vals)
@@ -65,12 +123,10 @@
         features, spread, (((0,), (0,)), ((), ())), preferred_element_type=jnp.float32
     )
     local_bias = jnp.sum(pulled.astype(jnp.float32), axis=0)
-    both = jnp.concatenate([local_weight, local_bias[None, :]], axis=0)
-    both = lax.psum(both, PLANE)
-    both = lax.psum(both, ("y_lo", "y_hi", "core"))
-    grad_weight = both[:-1]
-    grad_bias = both[-1]
-    return (hidden, grad_input, grad_weight, grad_bias)
+    width = local_weight.shape[0]
+    filler = jnp.zeros((7, local_bias.shape[0]), jnp.float32)
+    both = all_sum(jnp.concatenate([local_weight, local_bias[None, :], filler], axis=0))
+    return (hidden, grad_input, both[:width], both[width])
 
 
 def solution(mesh):

time: 591 us -> 379 us (0.64)
  waiting for transfers between devices: 524 us -> 172 us
  starting transfers between devices: 14 us -> 130 us
  local copies, waits for them, and re-layouts: 19.4 us -> 43.9 us
    psum x2 -> x0, waiting for transfers between devices: 265 us -> none  [the longest x1 153 us: local(): both = lax.psum(both, PLANE)]
    all_gather x2 -> x0, waiting for transfers between devices: 178 us -> none  [gather_team(): full = lax.all_gather(pair, PLANE, axis=0, tiled=True)]
    ppermute x0 -> x30, starting transfers between devices: none -> 116 us  [the longest x10 50.9 us: swap(): return lax.ppermute(value, axis, [(i, i ^ bit) for i in range(n)])]
    ppermute x0 -> x30, waiting for transfers between devices: none -> 77.9 us  [the longest x12 45 us: ring_gather(): ahead = lax.ppermute(ahead, axis, [(i, (i + 1) % n) for i in range(n)])]
    unnamed x10 -> x37, local copies, waits for them, and re-layouts: 0.02 us -> 20.3 us
    reduce_scatter x1, waiting for transfers between devices: 37.9 us -> 47 us  [local(): lax.psum_scatter(partial_back, BLK_AXES, scatter_dimension=0, tiled=True)]
  transfers between devices with their start and end apart: 8 -> 34, of which waited for: 8 -> 25; matrix products, arithmetic and copies ran while one was open for 0% -> 7% of each run, Pallas kernels for 0% -> 0%
where the time goes in v2:
time: 379 us; the launch traced here: 378 us
  waiting for transfers between devices  172 us (45%)
  starting transfers between devices  130 us (34%)
  local copies, waits for them, and re-layouts  43.9 us (12%)
  between operations  14.5 us (4%)
  matrix products  14.3 us (4%)
    ppermute x10, starting transfers between devices, swap(): return lax.ppermute(value, axis, [(i, i ^ bit) for i in range(n)])  50.9 us
    reduce_scatter x1, waiting for transfers between devices, local(): lax.psum_scatter(partial_back, BLK_AXES, scatter_dimension=0, tiled=True)  47 us
    ppermute x12, waiting for transfers between devices, ring_gather(): ahead = lax.ppermute(ahead, axis, [(i, (i + 1) % n) for i in range(n)])  45 us
    reduce_scatter x1, waiting for transfers between devices, local(): lax.psum_scatter(partial_rows, BLK_AXES, scatter_dimension=0, tiled=True)  42.7 us
    ppermute x8, starting transfers between devices, ring_gather(): behind = lax.ppermute(behind, axis, [(i, (i - 1) % n) for i in range(n)])  40.1 us
    ppermute x10, waiting for transfers between devices, swap(): return lax.ppermute(value, axis, [(i, i ^ bit) for i in range(n)])  30.5 us
    ppermute x12, starting transfers between devices, ring_gather(): ahead = lax.ppermute(ahead, axis, [(i, (i + 1) % n) for i in range(n)])  24.7 us
    unnamed x37, local copies, waits for them, and re-layouts  20.3 us
  transfers between devices with their start and end apart: 34, of which 25 were waited for; matrix products, arithmetic and copies ran while one was open for 7% of the time, Pallas kernels for 0%

profile of v2, /device:TPU:1, one launch (start us, length us, event | category | flops | bytes accessed | tf_op | source)
XLA Modules:
  0.0 377.6 jit_solution(9419664052484120552)
XLA Ops:
  9.2 8.3 %collective-permute-start = (bf16[128,256]{1,0:T(8,128)(2,1)S(1)}, bf16[128,256]{1,0:T(8,128)(2,1)S(1)}, u32[]{:S(2)}, u32[]{:S(2)}) collective-permute-start(bf16[128,256]{1,0:T(8,128)(2,1)S(1)} %get-tuple-element.32), channel_id=1, source_target_pairs={{0,32},{32,0},{1,33},{33,1},{2,34},{34,2},{3,35},{35,3},{4,36},{36... | collective-permute-start | bytes 196616 | tf_op jit(solution)/shard_map/ppermute | solution.py:45
  29.8 5.0 %collective-permute-done.3 = bf16[2,128,256]{2,1,0:T(8,128)(2,1)S(1)} collective-permute-done((bf16[2,128,256]{2,1,0:T(8,128)(2,1)S(1)}, bf16[2,128,256]{2,1,0:T(8,128)(2,1)S(1)}, u32[]{:S(2)}, u32[]{:S(2)}) %collective-permute-start.3) | collective-permute-done | bytes 131104 | tf_op jit(solution)/shard_map/ppermute | solution.py:36
  38.0 8.6 %collective-permute-start.5 = (bf16[8,128,256]{2,1,0:T(8,128)(2,1)}, bf16[8,128,256]{2,1,0:T(8,128)(2,1)}, u32[]{:S(2)}, u32[]{:S(2)}) collective-permute-start(bf16[8,128,256]{2,1,0:T(8,128)(2,1)} %get-tuple-element.16), channel_id=1, source_target_pairs={{0,7},{1,0},{2,1},{3,2},{4,3},{5,4},{6,5},{7,6},{8,15},{9,8},{10,9... | collective-permute-start | bytes 1572872 | tf_op jit(solution)/shard_map/ppermute | solution.py:39
  46.6 6.3 %collective-permute-done.4 = bf16[8,128,256]{2,1,0:T(8,128)(2,1)} collective-permute-done((bf16[8,128,256]{2,1,0:T(8,128)(2,1)}, bf16[8,128,256]{2,1,0:T(8,128)(2,1)}, u32[]{:S(2)}, u32[]{:S(2)}) %collective-permute-start.4) | collective-permute-done | bytes 524320 | tf_op jit(solution)/shard_map/ppermute | solution.py:36
  69.2 5.0 %collective-permute-start.9 = (bf16[8,128,256]{2,1,0:T(8,128)(2,1)}, bf16[8,128,256]{2,1,0:T(8,128)(2,1)S(1)}, u32[]{:S(2)}, u32[]{:S(2)}) collective-permute-start(bf16[8,128,256]{2,1,0:T(8,128)(2,1)} %collective-permute-done.7), channel_id=1, source_target_pairs={{0,7},{1,0},{2,1},{3,2},{4,3},{5,4},{6,5},{7,6},{8,15},{9,8},{10,9... | collective-permute-start | bytes 1572872 | tf_op jit(solution)/shard_map/ppermute | solution.py:39
  88.9 8.2 %gather_fusion.2 = bf16[96,128,256]{2,1,0:T(8,128)(2,1)} fusion(bf16[64,128,256]{2,1,0:T(8,128)(2,1)} %constant_dynamic-update-slice_fusion.5, s32[1024]{0:T(1024)S(1)} %pad_clamp_fusion), kind=kCustom, calls=%fused_computation.clone | custom fusion | bytes 12583296 | tf_op jit(solution)/shard_map/jit(_take)/gather | solution.py:95
  97.1 5.2 %fusion.2 = f32[8,256,128,1]{1,2,3,0:T(8,128)} fusion(bf16[8,12,128,256]{3,2,1,0:T(8,128)(2,1)} %bitcast.46, pred[8,12]{1,0:T(8,128)(4,1)S(1)} %get-tuple-element.7, bf16[1,8,1,12,128,128]{5,4,3,2,1,0:T(8,128)(2,1)S(1)} %copy-done), kind=kOutput, calls=%fused_computation.6 | convolution fusion | flops 808452096 | bytes 10485856 | tf_op jit(solution)/shard_map/rkij,rkjf->rif/dot_general | solution.py:96
  102.3 42.7 %reduce-scatter.3.cloned.1.call-done = f32[128,256]{1,0:T(8,128)} async-done(((f32[1024,256]{1,0:T(8,128)}), f32[128,256]{1,0:T(8,128)}) %reduce-scatter.3.cloned.1.call-update) | async-done | bytes 131088 | tf_op jit(solution)/shard_map/reduce_scatter | solution.py:111
  146.8 5.7 %collective-permute-start.11 = (bf16[128,256]{1,0:T(8,128)(2,1)S(1)}, bf16[128,256]{1,0:T(8,128)(2,1)S(1)}, u32[]{:S(2)}, u32[]{:S(2)}) collective-permute-start(bf16[128,256]{1,0:T(8,128)(2,1)S(1)} %get-tuple-element.6), channel_id=1, source_target_pairs={{0,32},{32,0},{1,33},{33,1},{2,34},{34,2},{3,35},{35,3},{4,36},{36... | collective-permute-start | bytes 196616 | tf_op jit(solution)/shard_map/ppermute | solution.py:45
  177.2 4.6 %collective-permute-done.15 = bf16[8,128,256]{2,1,0:T(8,128)(2,1)S(1)} collective-permute-done((bf16[8,128,256]{2,1,0:T(8,128)(2,1)S(1)}, bf16[8,128,256]{2,1,0:T(8,128)(2,1)S(1)}, u32[]{:S(2)}, u32[]{:S(2)}) %collective-permute-start.15) | collective-permute-done | bytes 524320 | tf_op jit(solution)/shard_map/ppermute | solution.py:36
  188.4 6.0 %collective-permute-done.17 = bf16[8,128,256]{2,1,0:T(8,128)(2,1)S(1)} collective-permute-done((bf16[8,128,256]{2,1,0:T(8,128)(2,1)S(1)}, bf16[8,128,256]{2,1,0:T(8,128)(2,1)S(1)}, u32[]{:S(2)}, u32[]{:S(2)}) %collective-permute-start.17) | collective-permute-done | bytes 524320 | tf_op jit(solution)/shard_map/ppermute | solution.py:36
  196.3 4.8 %collective-permute-start.20 = (bf16[8,128,256]{2,1,0:T(8,128)(2,1)S(1)}, bf16[8,128,256]{2,1,0:T(8,128)(2,1)S(1)}, u32[]{:S(2)}, u32[]{:S(2)}) collective-permute-start(bf16[8,128,256]{2,1,0:T(8,128)(2,1)S(1)} %collective-permute-done.18), channel_id=1, source_target_pairs={{0,7},{1,0},{2,1},{3,2},{4,3},{5,4},{6,5},{7,6},{8,15},{9,8},{10,9... | collective-permute-start | bytes 1572872 | tf_op jit(solution)/shard_map/ppermute | solution.py:39
  202.0 6.7 %collective-permute-done.19 = bf16[8,128,256]{2,1,0:T(8,128)(2,1)S(1)} collective-permute-done((bf16[8,128,256]{2,1,0:T(8,128)(2,1)S(1)}, bf16[8,128,256]{2,1,0:T(8,128)(2,1)S(1)}, u32[]{:S(2)}, u32[]{:S(2)}) %collective-permute-start.19) | collective-permute-done | bytes 524320 | tf_op jit(solution)/shard_map/ppermute | solution.py:36
  215.0 9.2 %collective-permute-done.21 = bf16[8,128,256]{2,1,0:T(8,128)(2,1)S(1)} collective-permute-done((bf16[8,128,256]{2,1,0:T(8,128)(2,1)S(1)}, bf16[8,128,256]{2,1,0:T(8,128)(2,1)S(1)}, u32[]{:S(2)}, u32[]{:S(2)}) %collective-permute-start.21) | collective-permute-done | bytes 524320 | tf_op jit(solution)/shard_map/ppermute | solution.py:36
  225.0 8.2 %gather_fusion.3 = bf16[96,128,256]{2,1,0:T(8,128)(2,1)} fusion(bf16[64,128,256]{2,1,0:T(8,128)(2,1)} %constant_dynamic-update-slice_fusion.22, s32[1024]{0:T(1024)S(1)} %pad_clamp_fusion), kind=kCustom, calls=%fused_computation.1.clone | custom fusion | bytes 12583296 | tf_op jit(solution)/shard_map/jit(_take)/gather | solution.py:95
  233.2 5.2 %fusion = f32[8,256,128,1]{1,2,3,0:T(8,128)} fusion(bf16[8,12,128,256]{3,2,1,0:T(8,128)(2,1)} %bitcast.45, pred[8,12]{1,0:T(8,128)(4,1)S(1)} %get-tuple-element.7, bf16[1,8,1,12,128,128]{5,4,3,2,1,0:T(8,128)(2,1)S(1)} %copy-done), kind=kOutput, calls=%fused_computation.4 | convolution fusion | flops 808452096 | bytes 10485856 | tf_op jit(solution)/shard_map/rkij,rkjf->rif/dot_general | solution.py:96
  238.5 47.0 %reduce-scatter.5.cloned.1.call-done = f32[128,256]{1,0:T(8,128)} async-done(((f32[1024,256]{1,0:T(8,128)}), f32[128,256]{1,0:T(8,128)}) %reduce-scatter.5.cloned.1.call-update) | async-done | bytes 131088 | tf_op jit(solution)/shard_map/reduce_scatter | solution.py:118
  286.8 4.7 %collective-permute-start.22 = (f32[132,256]{1,0:T(8,128)S(1)}, f32[132,256]{1,0:T(8,128)S(1)}, u32[]{:S(2)}, u32[]{:S(2)}) collective-permute-start(f32[132,256]{1,0:T(8,128)S(1)} %slice_select_fusion), channel_id=1, source_target_pairs={{0,64},{64,0},{1,65},{65,1},{2,66},{66,2},{3,67},{67,3},{4,68},{68... | collective-permute-start | bytes 405512 | tf_op jit(solution)/shard_map/ppermute | solution.py:71
  294.5 4.9 %collective-permute-done.23 = f32[132,256]{1,0:T(8,128)S(1)} collective-permute-done((f32[132,256]{1,0:T(8,128)S(1)}, f32[132,256]{1,0:T(8,128)S(1)}, u32[]{:S(2)}, u32[]{:S(2)}) %collective-permute-start.23) | collective-permute-done | bytes 135200 | tf_op jit(solution)/shard_map/ppermute | solution.py:71
  314.4 4.9 %collective-permute-done.26 = f32[132,256]{1,0:T(8,128)S(1)} collective-permute-done((f32[132,256]{1,0:T(8,128)S(1)}, f32[132,256]{1,0:T(8,128)S(1)}, u32[]{:S(2)}, u32[]{:S(2)}) %collective-permute-start.26) | collective-permute-done | bytes 135200 | tf_op jit(solution)/shard_map/ppermute | solution.py:71
  334.8 7.7 %collective-permute-start.29 = (f32[132,256]{1,0:T(8,128)S(1)}, f32[132,256]{1,0:T(8,128)S(1)}, u32[]{:S(2)}, u32[]{:S(2)}) collective-permute-start(f32[132,256]{1,0:T(8,128)S(1)} %add.173), channel_id=1, source_target_pairs={{0,4},{1,5},{2,6},{3,7},{4,0},{5,1},{6,2},{7,3},{8,12},{9,13},{10,... | collective-permute-start | bytes 405512 | tf_op jit(solution)/shard_map/ppermute | solution.py:71
  345.0 4.7 %collective-permute-start.30 = (f32[132,256]{1,0:T(8,128)S(1)}, f32[132,256]{1,0:T(8,128)S(1)}, u32[]{:S(2)}, u32[]{:S(2)}) collective-permute-start(f32[132,256]{1,0:T(8,128)S(1)} %add.174), channel_id=1, source_target_pairs={{0,32},{32,0},{1,33},{33,1},{2,34},{34,2},{3,35},{35,3},{4,36},{36... | collective-permute-start | bytes 405512 | tf_op jit(solution)/shard_map/ppermute | solution.py:71
  349.7 5.3 %collective-permute-done.30 = f32[132,256]{1,0:T(8,128)S(1)} collective-permute-done((f32[132,256]{1,0:T(8,128)S(1)}, f32[132,256]{1,0:T(8,128)S(1)}, u32[]{:S(2)}, u32[]{:S(2)}) %collective-permute-start.30) | collective-permute-done | bytes 135200 | tf_op jit(solution)/shard_map/ppermute | solution.py:71
  355.0 13.4 %collective-permute-start.31 = (f32[132,256]{1,0:T(8,128)S(1)}, f32[132,256]{1,0:T(8,128)S(1)}, u32[]{:S(2)}, u32[]{:S(2)}) collective-permute-start(f32[132,256]{1,0:T(8,128)S(1)} %add.175), channel_id=1, source_target_pairs={{0,64},{64,0},{1,65},{65,1},{2,66},{66,2},{3,67},{67,3},{4,68},{68... | collective-permute-start | bytes 405512 | tf_op jit(solution)/shard_map/ppermute | solution.py:71
  (123 shorter events, 130.7 us)
Async XLA Ops:
  7.2 137.9 %reduce-scatter.3.cloned.1.call-start = ((), (), s32[]{:S(2)}) async-start(), calls=%async_computation.2 | async-start | bytes 1179648 | tf_op jit(solution)/shard_map/reduce_scatter | solution.py:111
  9.2 10.0 %collective-permute-start = (bf16[128,256]{1,0:T(8,128)(2,1)S(1)}, bf16[128,256]{1,0:T(8,128)(2,1)S(1)}, u32[]{:S(2)}, u32[]{:S(2)}) collective-permute-start(bf16[128,256]{1,0:T(8,128)(2,1)S(1)} %get-tuple-element.32), channel_id=1, source_target_pairs={{0,32},{32,0},{1,33},{33,1},{2,34},{34,2},{3,35},{35,3},{4,36},{36... | collective-permute-start | bytes 196616 | tf_op jit(solution)/shard_map/ppermute | solution.py:45
  26.4 8.4 %collective-permute-start.3 = (bf16[2,128,256]{2,1,0:T(8,128)(2,1)S(1)}, bf16[2,128,256]{2,1,0:T(8,128)(2,1)S(1)}, u32[]{:S(2)}, u32[]{:S(2)}) collective-permute-start(bf16[2,128,256]{2,1,0:T(8,128)(2,1)S(1)} %collective-permute-done.1), channel_id=1, source_target_pairs={{0,8},{8,16},{16,24},{24,0},{1,9},{9,17},{17,25},{25,1},{2,10},{10... | collective-permute-start | bytes 393224 | tf_op jit(solution)/shard_map/ppermute | solution.py:36
  35.5 17.4 %collective-permute-start.4 = (bf16[8,128,256]{2,1,0:T(8,128)(2,1)}, bf16[8,128,256]{2,1,0:T(8,128)(2,1)}, u32[]{:S(2)}, u32[]{:S(2)}) collective-permute-start(bf16[8,128,256]{2,1,0:T(8,128)(2,1)} %get-tuple-element.16), channel_id=1, source_target_pairs={{0,1},{1,2},{2,3},{3,4},{4,5},{5,6},{6,7},{7,0},{8,9},{9,10},{10,1... | collective-permute-start | bytes 1572872 | tf_op jit(solution)/shard_map/ppermute | solution.py:36
  38.0 20.2 %collective-permute-start.5 = (bf16[8,128,256]{2,1,0:T(8,128)(2,1)}, bf16[8,128,256]{2,1,0:T(8,128)(2,1)}, u32[]{:S(2)}, u32[]{:S(2)}) collective-permute-start(bf16[8,128,256]{2,1,0:T(8,128)(2,1)} %get-tuple-element.16), channel_id=1, source_target_pairs={{0,7},{1,0},{2,1},{3,2},{4,3},{5,4},{6,5},{7,6},{8,15},{9,8},{10,9... | collective-permute-start | bytes 1572872 | tf_op jit(solution)/shard_map/ppermute | solution.py:39
  52.9 11.9 %collective-permute-start.6 = (bf16[8,128,256]{2,1,0:T(8,128)(2,1)}, bf16[8,128,256]{2,1,0:T(8,128)(2,1)}, u32[]{:S(2)}, u32[]{:S(2)}) collective-permute-start(bf16[8,128,256]{2,1,0:T(8,128)(2,1)} %collective-permute-done.4), channel_id=1, source_target_pairs={{0,1},{1,2},{2,3},{3,4},{4,5},{5,6},{6,7},{7,0},{8,9},{9,10},{10,1... | collective-permute-start | bytes 1572872 | tf_op jit(solution)/shard_map/ppermute | solution.py:36
  58.2 11.0 %collective-permute-start.7 = (bf16[8,128,256]{2,1,0:T(8,128)(2,1)}, bf16[8,128,256]{2,1,0:T(8,128)(2,1)}, u32[]{:S(2)}, u32[]{:S(2)}) collective-permute-start(bf16[8,128,256]{2,1,0:T(8,128)(2,1)} %collective-permute-done.5), channel_id=1, source_target_pairs={{0,7},{1,0},{2,1},{3,2},{4,3},{5,4},{6,5},{7,6},{8,15},{9,8},{10,9... | collective-permute-start | bytes 1572872 | tf_op jit(solution)/shard_map/ppermute | solution.py:39
  64.7 11.4 %collective-permute-start.8 = (bf16[8,128,256]{2,1,0:T(8,128)(2,1)}, bf16[8,128,256]{2,1,0:T(8,128)(2,1)}, u32[]{:S(2)}, u32[]{:S(2)}) collective-permute-start(bf16[8,128,256]{2,1,0:T(8,128)(2,1)} %collective-permute-done.6), channel_id=1, source_target_pairs={{0,1},{1,2},{2,3},{3,4},{4,5},{5,6},{6,7},{7,0},{8,9},{9,10},{10,1... | collective-permute-start | bytes 1572872 | tf_op jit(solution)/shard_map/ppermute | solution.py:36
  69.2 16.5 %collective-permute-start.9 = (bf16[8,128,256]{2,1,0:T(8,128)(2,1)}, bf16[8,128,256]{2,1,0:T(8,128)(2,1)S(1)}, u32[]{:S(2)}, u32[]{:S(2)}) collective-permute-start(bf16[8,128,256]{2,1,0:T(8,128)(2,1)} %collective-permute-done.7), channel_id=1, source_target_pairs={{0,7},{1,0},{2,1},{3,2},{4,3},{5,4},{6,5},{7,6},{8,15},{9,8},{10,9... | collective-permute-start | bytes 1572872 | tf_op jit(solution)/shard_map/ppermute | solution.py:39
  76.2 11.9 %collective-permute-start.10 = (bf16[8,128,256]{2,1,0:T(8,128)(2,1)}, bf16[8,128,256]{2,1,0:T(8,128)(2,1)S(1)}, u32[]{:S(2)}, u32[]{:S(2)}) collective-permute-start(bf16[8,128,256]{2,1,0:T(8,128)(2,1)} %collective-permute-done.8), channel_id=1, source_target_pairs={{0,1},{1,2},{2,3},{3,4},{4,5},{5,6},{6,7},{7,0},{8,9},{9,10},{10,1... | collective-permute-start | bytes 1572872 | tf_op jit(solution)/shard_map/ppermute | solution.py:36
  102.3 183.2 %reduce-scatter.5.cloned.1.call-start = ((), (), s32[]{:S(2)}) async-start(), calls=%async_computation.3 | async-start | bytes 1179648 | tf_op jit(solution)/shard_map/reduce_scatter | solution.py:118
  146.8 9.2 %collective-permute-start.11 = (bf16[128,256]{1,0:T(8,128)(2,1)S(1)}, bf16[128,256]{1,0:T(8,128)(2,1)S(1)}, u32[]{:S(2)}, u32[]{:S(2)}) collective-permute-start(bf16[128,256]{1,0:T(8,128)(2,1)S(1)} %get-tuple-element.6), channel_id=1, source_target_pairs={{0,32},{32,0},{1,33},{33,1},{2,34},{34,2},{3,35},{35,3},{4,36},{36... | collective-permute-start | bytes 196616 | tf_op jit(solution)/shard_map/ppermute | solution.py:45
  170.7 11.1 %collective-permute-start.15 = (bf16[8,128,256]{2,1,0:T(8,128)(2,1)S(1)}, bf16[8,128,256]{2,1,0:T(8,128)(2,1)S(1)}, u32[]{:S(2)}, u32[]{:S(2)}) collective-permute-start(bf16[8,128,256]{2,1,0:T(8,128)(2,1)S(1)} %get-tuple-element.10), channel_id=1, source_target_pairs={{0,1},{1,2},{2,3},{3,4},{4,5},{5,6},{6,7},{7,0},{8,9},{9,10},{10,1... | collective-permute-start | bytes 1572872 | tf_op jit(solution)/shard_map/ppermute | solution.py:36
  172.7 11.1 %collective-permute-start.16 = (bf16[8,128,256]{2,1,0:T(8,128)(2,1)S(1)}, bf16[8,128,256]{2,1,0:T(8,128)(2,1)S(1)}, u32[]{:S(2)}, u32[]{:S(2)}) collective-permute-start(bf16[8,128,256]{2,1,0:T(8,128)(2,1)S(1)} %get-tuple-element.10), channel_id=1, source_target_pairs={{0,7},{1,0},{2,1},{3,2},{4,3},{5,4},{6,5},{7,6},{8,15},{9,8},{10,9... | collective-permute-start | bytes 1572872 | tf_op jit(solution)/shard_map/ppermute | solution.py:39
  181.9 12.5 %collective-permute-start.17 = (bf16[8,128,256]{2,1,0:T(8,128)(2,1)S(1)}, bf16[8,128,256]{2,1,0:T(8,128)(2,1)S(1)}, u32[]{:S(2)}, u32[]{:S(2)}) collective-permute-start(bf16[8,128,256]{2,1,0:T(8,128)(2,1)S(1)} %collective-permute-done.15), channel_id=1, source_target_pairs={{0,1},{1,2},{2,3},{3,4},{4,5},{5,6},{6,7},{7,0},{8,9},{9,10},{10,1... | collective-permute-start | bytes 1572872 | tf_op jit(solution)/shard_map/ppermute | solution.py:36
  183.8 12.5 %collective-permute-start.18 = (bf16[8,128,256]{2,1,0:T(8,128)(2,1)S(1)}, bf16[8,128,256]{2,1,0:T(8,128)(2,1)S(1)}, u32[]{:S(2)}, u32[]{:S(2)}) collective-permute-start(bf16[8,128,256]{2,1,0:T(8,128)(2,1)S(1)} %collective-permute-done.16), channel_id=1, source_target_pairs={{0,7},{1,0},{2,1},{3,2},{4,3},{5,4},{6,5},{7,6},{8,15},{9,8},{10,9... | collective-permute-start | bytes 1572872 | tf_op jit(solution)/shard_map/ppermute | solution.py:39
  194.4 14.3 %collective-permute-start.19 = (bf16[8,128,256]{2,1,0:T(8,128)(2,1)S(1)}, bf16[8,128,256]{2,1,0:T(8,128)(2,1)S(1)}, u32[]{:S(2)}, u32[]{:S(2)}) collective-permute-start(bf16[8,128,256]{2,1,0:T(8,128)(2,1)S(1)} %collective-permute-done.17), channel_id=1, source_target_pairs={{0,1},{1,2},{2,3},{3,4},{4,5},{5,6},{6,7},{7,0},{8,9},{9,10},{10,1... | collective-permute-start | bytes 1572872 | tf_op jit(solution)/shard_map/ppermute | solution.py:36
  196.3 17.8 %collective-permute-start.20 = (bf16[8,128,256]{2,1,0:T(8,128)(2,1)S(1)}, bf16[8,128,256]{2,1,0:T(8,128)(2,1)S(1)}, u32[]{:S(2)}, u32[]{:S(2)}) collective-permute-start(bf16[8,128,256]{2,1,0:T(8,128)(2,1)S(1)} %collective-permute-done.18), channel_id=1, source_target_pairs={{0,7},{1,0},{2,1},{3,2},{4,3},{5,4},{6,5},{7,6},{8,15},{9,8},{10,9... | collective-permute-start | bytes 1572872 | tf_op jit(solution)/shard_map/ppermute | solution.py:39
  208.7 15.4 %collective-permute-start.21 = (bf16[8,128,256]{2,1,0:T(8,128)(2,1)S(1)}, bf16[8,128,256]{2,1,0:T(8,128)(2,1)S(1)}, u32[]{:S(2)}, u32[]{:S(2)}) collective-permute-start(bf16[8,128,256]{2,1,0:T(8,128)(2,1)S(1)} %collective-permute-done.19), channel_id=1, source_target_pairs={{0,1},{1,2},{2,3},{3,4},{4,5},{5,6},{6,7},{7,0},{8,9},{9,10},{10,1... | collective-permute-start | bytes 1572872 | tf_op jit(solution)/shard_map/ppermute | solution.py:36
  311.1 8.2 %collective-permute-start.26 = (f32[132,256]{1,0:T(8,128)S(1)}, f32[132,256]{1,0:T(8,128)S(1)}, u32[]{:S(2)}, u32[]{:S(2)}) collective-permute-start(f32[132,256]{1,0:T(8,128)S(1)} %add.170), channel_id=1, source_target_pairs={{0,256},{128,384},{256,0},{384,128},{1,257},{129,385},{257,1},{385... | collective-permute-start | bytes 405512 | tf_op jit(solution)/shard_map/ppermute | solution.py:71
  326.6 8.2 %collective-permute-start.28 = (f32[132,256]{1,0:T(8,128)S(1)}, f32[132,256]{1,0:T(8,128)S(1)}, u32[]{:S(2)}, u32[]{:S(2)}) collective-permute-start(f32[132,256]{1,0:T(8,128)S(1)} %add.172), channel_id=1, source_target_pairs={{0,2},{1,3},{2,0},{3,1},{4,6},{5,7},{6,4},{7,5},{8,10},{9,11},{10,... | collective-permute-start | bytes 405512 | tf_op jit(solution)/shard_map/ppermute | solution.py:71
  334.8 10.2 %collective-permute-start.29 = (f32[132,256]{1,0:T(8,128)S(1)}, f32[132,256]{1,0:T(8,128)S(1)}, u32[]{:S(2)}, u32[]{:S(2)}) collective-permute-start(f32[132,256]{1,0:T(8,128)S(1)} %add.173), channel_id=1, source_target_pairs={{0,4},{1,5},{2,6},{3,7},{4,0},{5,1},{6,2},{7,3},{8,12},{9,13},{10,... | collective-permute-start | bytes 405512 | tf_op jit(solution)/shard_map/ppermute | solution.py:71
  345.0 10.0 %collective-permute-start.30 = (f32[132,256]{1,0:T(8,128)S(1)}, f32[132,256]{1,0:T(8,128)S(1)}, u32[]{:S(2)}, u32[]{:S(2)}) collective-permute-start(f32[132,256]{1,0:T(8,128)S(1)} %add.174), channel_id=1, source_target_pairs={{0,32},{32,0},{1,33},{33,1},{2,34},{34,2},{3,35},{35,3},{4,36},{36... | collective-permute-start | bytes 405512 | tf_op jit(solution)/shard_map/ppermute | solution.py:71
  355.0 14.4 %collective-permute-start.31 = (f32[132,256]{1,0:T(8,128)S(1)}, f32[132,256]{1,0:T(8,128)S(1)}, u32[]{:S(2)}, u32[]{:S(2)}) collective-permute-start(f32[132,256]{1,0:T(8,128)S(1)} %add.175), channel_id=1, source_target_pairs={{0,64},{64,0},{1,65},{65,1},{2,66},{66,2},{3,67},{67,3},{4,68},{68... | collective-permute-start | bytes 405512 | tf_op jit(solution)/shard_map/ppermute | solution.py:71
  (19 other events, 627.8 us)
Sparse Core Ops, SparseCore 0:
  102.4 42.6 reduce-scatter.2
  238.6 46.8 reduce-scatter.4

commit v3 on v2

--- a/solution.py
+++ b/solution.py
@@ -88,6 +88,25 @@
     return jnp.where(upper, jnp.concatenate([other, part]), jnp.concatenate([part, other]))
 
 
+def blk_reduce_scatter(partial):
+    width = partial.shape[-1]
+    block = partial.shape[0] // (SIZES["y_lo"] * SIZES["core"])
+    cur = partial.reshape(-1, 2, block, width)
+    upper = lax.axis_index("core") == 1
+    keep = jnp.where(upper, cur[:, 1], cur[:, 0])
+    send = jnp.where(upper, cur[:, 0], cur[:, 1])
+    cur = keep + swap(send, "core", 1)
+    bit = 1
+    while bit < SIZES["y_lo"]:
+        cur = cur.reshape(-1, 2, block, width)
+        upper = (lax.axis_index("y_lo") & bit) != 0
+        keep = jnp.where(upper, cur[:, 1], cur[:, 0])
+        send = jnp.where(upper, cur[:, 0], cur[:, 1])
+        cur = keep + swap(send, "y_lo", bit)
+        bit *= 2
+    return cur.reshape(block, width)
+
+
 def collect(panels, slots, adj_vals):
     block = adj_vals.shape[-1]
     width = panels.shape[1]
@@ -108,16 +127,14 @@
     product = jnp.dot(features, weight, preferred_element_type=jnp.float32).astype(jnp.bfloat16)
     gathered = gather_team(product)
     partial_rows = collect(gathered, slots, adj_vals)
-    summed = lax.psum_scatter(partial_rows, BLK_AXES, scatter_dimension=0, tiled=True)
+    summed = blk_reduce_scatter(partial_rows)
     pre = summed + bias[None, :]
     activated, pullback = jax.vjp(activation, pre)
     hidden = activated.astype(jnp.bfloat16)
     pulled = pullback(cotangent.astype(jnp.float32))[0].astype(jnp.bfloat16)
     pulled_group = gather_team(pulled)
     partial_back = collect(pulled_group, slots, adj_vals)
-    spread = lax.psum_scatter(partial_back, BLK_AXES, scatter_dimension=0, tiled=True).astype(
-        jnp.bfloat16
-    )
+    spread = blk_reduce_scatter(partial_back).astype(jnp.bfloat16)
     grad_input = jnp.dot(spread, weight.T, preferred_element_type=jnp.float32).astype(jnp.bfloat16)
     local_weight = lax.dot_general(
         features, spread, (((0,), (0,)), ((), ())), preferred_element_type=jnp.float32

time: 379 us -> 354 us (0.934)
  waiting for transfers between devices: 172 us -> 116 us
  starting transfers between devices: 130 us -> 152 us
  local copies, waits for them, and re-layouts: 43.9 us -> 59.6 us
  between operations: 14.5 us -> 1.25 us
  other arithmetic: 2.81 us -> 8.54 us
    reduce_scatter x2 -> x0, waiting for transfers between devices: 89.7 us -> none  [the longest x1 47 us: local(): lax.psum_scatter(partial_back, BLK_AXES, scatter_dimension=0, tiled=True)]
    ppermute x10 -> x16, waiting for transfers between devices: 30.5 us -> 68.7 us  [swap(): return lax.ppermute(value, axis, [(i, i ^ bit) for i in range(n)])]
    ppermute x10 -> x16, starting transfers between devices: 50.9 us -> 75.9 us  [swap(): return lax.ppermute(value, axis, [(i, i ^ bit) for i in range(n)])]
    gather x2 -> x3, local copies, waits for them, and re-layouts: 16.4 us -> 25.1 us  [collect(): picked = jnp.take(stacked, slots, axis=0)]
    ppermute x12, waiting for transfers between devices: 45 us -> 38.8 us  [ring_gather(): ahead = lax.ppermute(ahead, axis, [(i, (i + 1) % n) for i in range(n)])]
    unnamed x37 -> x41, local copies, waits for them, and re-layouts: 20.3 us -> 26.2 us
  transfers between devices with their start and end apart: 34 -> 38, of which waited for: 25 -> 28; matrix products, arithmetic and copies ran while one was open for 7% -> 7% of each run, Pallas kernels for 0% -> 0%
where the time goes in v3:
time: 354 us; the launch traced here: 350 us
  starting transfers between devices  152 us (43%)
  waiting for transfers between devices  116 us (33%)
  local copies, waits for them, and re-layouts  59.6 us (17%)
  matrix products  11.7 us (3%)
  other arithmetic  8.54 us (2%)
    ppermute x16, starting transfers between devices, swap(): return lax.ppermute(value, axis, [(i, i ^ bit) for i in range(n)])  75.9 us
    ppermute x16, waiting for transfers between devices, swap(): return lax.ppermute(value, axis, [(i, i ^ bit) for i in range(n)])  68.7 us
    ppermute x8, starting transfers between devices, ring_gather(): behind = lax.ppermute(behind, axis, [(i, (i - 1) % n) for i in range(n)])  39.8 us
    ppermute x12, waiting for transfers between devices, ring_gather(): ahead = lax.ppermute(ahead, axis, [(i, (i + 1) % n) for i in range(n)])  38.8 us
    unnamed x41, local copies, waits for them, and re-layouts  26.2 us
    gather x3, local copies, waits for them, and re-layouts, collect(): picked = jnp.take(stacked, slots, axis=0)  25.1 us
    ppermute x12, starting transfers between devices, ring_gather(): ahead = lax.ppermute(ahead, axis, [(i, (i + 1) % n) for i in range(n)])  24.7 us
    ppermute x2, starting transfers between devices, gather_team(): other = lax.ppermute(rows, 'y_hi', perm=[(0, 1), (1, 0)])  11.9 us
  transfers between devices with their start and end apart: 38, of which 28 were waited for; matrix products, arithmetic and copies ran while one was open for 7% of the time, Pallas kernels for 0%

profile of v3, /device:TPU:1, one launch (start us, length us, event | category | flops | bytes accessed | tf_op | source)
XLA Modules:
  0.0 349.8 jit_solution(12811602895523154810)
XLA Ops:
  2.6 8.3 %collective-permute-start = (bf16[128,256]{1,0:T(8,128)(2,1)S(1)}, bf16[128,256]{1,0:T(8,128)(2,1)S(1)}, u32[]{:S(2)}, u32[]{:S(2)}) collective-permute-start(bf16[128,256]{1,0:T(8,128)(2,1)S(1)} %get-tuple-element.34), channel_id=1, source_target_pairs={{0,32},{32,0},{1,33},{33,1},{2,34},{34,2},{3,35},{35,3},{4,36},{36... | collective-permute-start | bytes 196616 | tf_op jit(solution)/shard_map/ppermute | solution.py:45
  23.2 5.0 %collective-permute-done.3 = bf16[2,128,256]{2,1,0:T(8,128)(2,1)S(1)} collective-permute-done((bf16[2,128,256]{2,1,0:T(8,128)(2,1)S(1)}, bf16[2,128,256]{2,1,0:T(8,128)(2,1)S(1)}, u32[]{:S(2)}, u32[]{:S(2)}) %collective-permute-start.3) | collective-permute-done | bytes 131104 | tf_op jit(solution)/shard_map/ppermute | solution.py:36
  31.4 8.6 %collective-permute-start.5 = (bf16[8,128,256]{2,1,0:T(8,128)(2,1)}, bf16[8,128,256]{2,1,0:T(8,128)(2,1)}, u32[]{:S(2)}, u32[]{:S(2)}) collective-permute-start(bf16[8,128,256]{2,1,0:T(8,128)(2,1)} %get-tuple-element.18), channel_id=1, source_target_pairs={{0,7},{1,0},{2,1},{3,2},{4,3},{5,4},{6,5},{7,6},{8,15},{9,8},{10,9... | collective-permute-start | bytes 1572872 | tf_op jit(solution)/shard_map/ppermute | solution.py:39
  40.0 6.3 %collective-permute-done.4 = bf16[8,128,256]{2,1,0:T(8,128)(2,1)} collective-permute-done((bf16[8,128,256]{2,1,0:T(8,128)(2,1)}, bf16[8,128,256]{2,1,0:T(8,128)(2,1)}, u32[]{:S(2)}, u32[]{:S(2)}) %collective-permute-start.4) | collective-permute-done | bytes 524320 | tf_op jit(solution)/shard_map/ppermute | solution.py:36
  62.6 5.0 %collective-permute-start.9 = (bf16[8,128,256]{2,1,0:T(8,128)(2,1)}, bf16[8,128,256]{2,1,0:T(8,128)(2,1)S(1)}, u32[]{:S(2)}, u32[]{:S(2)}) collective-permute-start(bf16[8,128,256]{2,1,0:T(8,128)(2,1)} %collective-permute-done.7), channel_id=1, source_target_pairs={{0,7},{1,0},{2,1},{3,2},{4,3},{5,4},{6,5},{7,6},{8,15},{9,8},{10,9... | collective-permute-start | bytes 1572872 | tf_op jit(solution)/shard_map/ppermute | solution.py:39
  82.3 8.2 %gather_fusion.2 = bf16[96,128,256]{2,1,0:T(8,128)(2,1)} fusion(bf16[64,128,256]{2,1,0:T(8,128)(2,1)} %constant_dynamic-update-slice_fusion.5, s32[1024]{0:T(1024)S(1)} %pad_clamp_fusion), kind=kCustom, calls=%fused_computation.clone | custom fusion | bytes 12583296 | tf_op jit(solution)/shard_map/jit(_take)/gather | solution.py:114
  96.6 10.0 %collective-permute-start.11 = (f32[4,128,256]{2,1,0:T(8,128)}, f32[4,128,256]{2,1,0:T(8,128)}, u32[]{:S(2)}, u32[]{:S(2)}) collective-permute-start(f32[4,128,256]{2,1,0:T(8,128)} %select_bitcast_fusion.1), channel_id=1, source_target_pairs={{0,64},{64,0},{1,65},{65,1},{2,66},{66,2},{3,67},{67,3},{4,68},{68... | collective-permute-start | bytes 1572872 | tf_op jit(solution)/shard_map/ppermute | solution.py:71
  114.6 6.4 %collective-permute-done.12 = f32[2,128,256]{2,1,0:T(8,128)S(1)} collective-permute-done((f32[2,128,256]{2,1,0:T(8,128)}, f32[2,128,256]{2,1,0:T(8,128)S(1)}, u32[]{:S(2)}, u32[]{:S(2)}) %collective-permute-start.12) | collective-permute-done | bytes 262176 | tf_op jit(solution)/shard_map/ppermute | solution.py:71
  122.2 8.2 %collective-permute-start.13 = (f32[1,128,256]{2,1,0:T(8,128)S(1)}, f32[1,128,256]{2,1,0:T(8,128)S(1)}, u32[]{:S(2)}, u32[]{:S(2)}) collective-permute-start(f32[1,128,256]{2,1,0:T(8,128)S(1)} %select_bitcast_fusion.5), channel_id=1, source_target_pairs={{0,256},{128,384},{256,0},{384,128},{1,257},{129,385},{257,1},{385... | collective-permute-start | bytes 393224 | tf_op jit(solution)/shard_map/ppermute | solution.py:71
  130.4 6.7 %collective-permute-done.13 = f32[1,128,256]{2,1,0:T(8,128)S(1)} collective-permute-done((f32[1,128,256]{2,1,0:T(8,128)S(1)}, f32[1,128,256]{2,1,0:T(8,128)S(1)}, u32[]{:S(2)}, u32[]{:S(2)}) %collective-permute-start.13) | collective-permute-done | bytes 131104 | tf_op jit(solution)/shard_map/ppermute | solution.py:71
  167.4 5.7 %collective-permute-done.18 = bf16[8,128,256]{2,1,0:T(8,128)(2,1)S(1)} collective-permute-done((bf16[8,128,256]{2,1,0:T(8,128)(2,1)S(1)}, bf16[8,128,256]{2,1,0:T(8,128)(2,1)S(1)}, u32[]{:S(2)}, u32[]{:S(2)}) %collective-permute-start.18) | collective-permute-done | bytes 524320 | tf_op jit(solution)/shard_map/ppermute | solution.py:36
  201.7 6.1 %collective-permute-done.24 = bf16[8,128,256]{2,1,0:T(8,128)(2,1)S(1)} collective-permute-done((bf16[8,128,256]{2,1,0:T(8,128)(2,1)S(1)}, bf16[8,128,256]{2,1,0:T(8,128)(2,1)S(1)}, u32[]{:S(2)}, u32[]{:S(2)}) %collective-permute-start.24) | collective-permute-done | bytes 524320 | tf_op jit(solution)/shard_map/ppermute | solution.py:36
  208.7 8.2 %gather_fusion.3 = bf16[96,128,256]{2,1,0:T(8,128)(2,1)} fusion(bf16[64,128,256]{2,1,0:T(8,128)(2,1)} %constant_dynamic-update-slice_fusion.22, s32[1024]{0:T(1024)S(1)} %pad_clamp_fusion), kind=kCustom, calls=%fused_computation.1.clone | custom fusion | bytes 12583296 | tf_op jit(solution)/shard_map/jit(_take)/gather | solution.py:114
  216.9 8.7 %copy.25 = bf16[8,12,128,256]{2,3,1,0:T(8,128)(2,1)} copy(bf16[8,12,128,256]{3,2,1,0:T(8,128)(2,1)} %bitcast.133) | data formatting | bytes 12582912 | tf_op jit(solution)/shard_map/jit(_take)/gather | solution.py:114
  236.5 10.4 %collective-permute-start.25 = (f32[4,128,256]{2,1,0:T(8,128)S(1)}, f32[4,128,256]{2,1,0:T(8,128)S(1)}, u32[]{:S(2)}, u32[]{:S(2)}) collective-permute-start(f32[4,128,256]{2,1,0:T(8,128)S(1)} %select_bitcast_fusion), channel_id=1, source_target_pairs={{0,64},{64,0},{1,65},{65,1},{2,66},{66,2},{3,67},{67,3},{4,68},{68... | collective-permute-start | bytes 1572872 | tf_op jit(solution)/shard_map/ppermute | solution.py:71
  251.6 7.5 %collective-permute-done.26 = f32[2,128,256]{2,1,0:T(8,128)S(1)} collective-permute-done((f32[2,128,256]{2,1,0:T(8,128)S(1)}, f32[2,128,256]{2,1,0:T(8,128)S(1)}, u32[]{:S(2)}, u32[]{:S(2)}) %collective-permute-start.26) | collective-permute-done | bytes 262176 | tf_op jit(solution)/shard_map/ppermute | solution.py:71
  259.2 5.3 %collective-permute-start.27 = (f32[1,128,256]{2,1,0:T(8,128)S(1)}, f32[1,128,256]{2,1,0:T(8,128)S(1)}, u32[]{:S(2)}, u32[]{:S(2)}) collective-permute-start(f32[1,128,256]{2,1,0:T(8,128)S(1)} %select_bitcast_fusion.4), channel_id=1, source_target_pairs={{0,256},{128,384},{256,0},{384,128},{1,257},{129,385},{257,1},{385... | collective-permute-start | bytes 393224 | tf_op jit(solution)/shard_map/ppermute | solution.py:71
  264.6 5.8 %collective-permute-done.27 = f32[1,128,256]{2,1,0:T(8,128)S(1)} collective-permute-done((f32[1,128,256]{2,1,0:T(8,128)S(1)}, f32[1,128,256]{2,1,0:T(8,128)S(1)}, u32[]{:S(2)}, u32[]{:S(2)}) %collective-permute-start.27) | collective-permute-done | bytes 131104 | tf_op jit(solution)/shard_map/ppermute | solution.py:71
  304.1 5.4 %collective-permute-done.33 = f32[132,256]{1,0:T(8,128)S(1)} collective-permute-done((f32[132,256]{1,0:T(8,128)S(1)}, f32[132,256]{1,0:T(8,128)S(1)}, u32[]{:S(2)}, u32[]{:S(2)}) %collective-permute-start.33) | collective-permute-done | bytes 135200 | tf_op jit(solution)/shard_map/ppermute | solution.py:71
  311.4 6.0 %collective-permute-done.34 = f32[132,256]{1,0:T(8,128)S(1)} collective-permute-done((f32[132,256]{1,0:T(8,128)S(1)}, f32[132,256]{1,0:T(8,128)S(1)}, u32[]{:S(2)}, u32[]{:S(2)}) %collective-permute-start.34) | collective-permute-done | bytes 135200 | tf_op jit(solution)/shard_map/ppermute | solution.py:71
  317.4 5.1 %collective-permute-start.35 = (f32[132,256]{1,0:T(8,128)S(1)}, f32[132,256]{1,0:T(8,128)S(1)}, u32[]{:S(2)}, u32[]{:S(2)}) collective-permute-start(f32[132,256]{1,0:T(8,128)S(1)} %add.193), channel_id=1, source_target_pairs={{0,4},{1,5},{2,6},{3,7},{4,0},{5,1},{6,2},{7,3},{8,12},{9,13},{10,... | collective-permute-start | bytes 405512 | tf_op jit(solution)/shard_map/ppermute | solution.py:71
  322.6 6.1 %collective-permute-done.35 = f32[132,256]{1,0:T(8,128)S(1)} collective-permute-done((f32[132,256]{1,0:T(8,128)S(1)}, f32[132,256]{1,0:T(8,128)S(1)}, u32[]{:S(2)}, u32[]{:S(2)}) %collective-permute-start.35) | collective-permute-done | bytes 135200 | tf_op jit(solution)/shard_map/ppermute | solution.py:71
  328.7 4.7 %collective-permute-start.36 = (f32[132,256]{1,0:T(8,128)S(1)}, f32[132,256]{1,0:T(8,128)S(1)}, u32[]{:S(2)}, u32[]{:S(2)}) collective-permute-start(f32[132,256]{1,0:T(8,128)S(1)} %add.194), channel_id=1, source_target_pairs={{0,32},{32,0},{1,33},{33,1},{2,34},{34,2},{3,35},{35,3},{4,36},{36... | collective-permute-start | bytes 405512 | tf_op jit(solution)/shard_map/ppermute | solution.py:71
  338.4 9.1 %collective-permute-start.37 = (f32[132,256]{1,0:T(8,128)S(1)}, f32[132,256]{1,0:T(8,128)S(1)}, u32[]{:S(2)}, u32[]{:S(2)}) collective-permute-start(f32[132,256]{1,0:T(8,128)S(1)} %add.195), channel_id=1, source_target_pairs={{0,64},{64,0},{1,65},{65,1},{2,66},{66,2},{3,67},{67,3},{4,68},{68... | collective-permute-start | bytes 405512 | tf_op jit(solution)/shard_map/ppermute | solution.py:71
  (147 shorter events, 181.7 us)
Async XLA Ops:
  2.6 10.0 %collective-permute-start = (bf16[128,256]{1,0:T(8,128)(2,1)S(1)}, bf16[128,256]{1,0:T(8,128)(2,1)S(1)}, u32[]{:S(2)}, u32[]{:S(2)}) collective-permute-start(bf16[128,256]{1,0:T(8,128)(2,1)S(1)} %get-tuple-element.34), channel_id=1, source_target_pairs={{0,32},{32,0},{1,33},{33,1},{2,34},{34,2},{3,35},{35,3},{4,36},{36... | collective-permute-start | bytes 196616 | tf_op jit(solution)/shard_map/ppermute | solution.py:45
  28.9 17.4 %collective-permute-start.4 = (bf16[8,128,256]{2,1,0:T(8,128)(2,1)}, bf16[8,128,256]{2,1,0:T(8,128)(2,1)}, u32[]{:S(2)}, u32[]{:S(2)}) collective-permute-start(bf16[8,128,256]{2,1,0:T(8,128)(2,1)} %get-tuple-element.18), channel_id=1, source_target_pairs={{0,1},{1,2},{2,3},{3,4},{4,5},{5,6},{6,7},{7,0},{8,9},{9,10},{10,1... | collective-permute-start | bytes 1572872 | tf_op jit(solution)/shard_map/ppermute | solution.py:36
  31.4 20.2 %collective-permute-start.5 = (bf16[8,128,256]{2,1,0:T(8,128)(2,1)}, bf16[8,128,256]{2,1,0:T(8,128)(2,1)}, u32[]{:S(2)}, u32[]{:S(2)}) collective-permute-start(bf16[8,128,256]{2,1,0:T(8,128)(2,1)} %get-tuple-element.18), channel_id=1, source_target_pairs={{0,7},{1,0},{2,1},{3,2},{4,3},{5,4},{6,5},{7,6},{8,15},{9,8},{10,9... | collective-permute-start | bytes 1572872 | tf_op jit(solution)/shard_map/ppermute | solution.py:39
  46.3 11.8 %collective-permute-start.6 = (bf16[8,128,256]{2,1,0:T(8,128)(2,1)}, bf16[8,128,256]{2,1,0:T(8,128)(2,1)}, u32[]{:S(2)}, u32[]{:S(2)}) collective-permute-start(bf16[8,128,256]{2,1,0:T(8,128)(2,1)} %collective-permute-done.4), channel_id=1, source_target_pairs={{0,1},{1,2},{2,3},{3,4},{4,5},{5,6},{6,7},{7,0},{8,9},{9,10},{10,1... | collective-permute-start | bytes 1572872 | tf_op jit(solution)/shard_map/ppermute | solution.py:36
  51.6 11.0 %collective-permute-start.7 = (bf16[8,128,256]{2,1,0:T(8,128)(2,1)}, bf16[8,128,256]{2,1,0:T(8,128)(2,1)}, u32[]{:S(2)}, u32[]{:S(2)}) collective-permute-start(bf16[8,128,256]{2,1,0:T(8,128)(2,1)} %collective-permute-done.5), channel_id=1, source_target_pairs={{0,7},{1,0},{2,1},{3,2},{4,3},{5,4},{6,5},{7,6},{8,15},{9,8},{10,9... | collective-permute-start | bytes 1572872 | tf_op jit(solution)/shard_map/ppermute | solution.py:39
  58.1 11.4 %collective-permute-start.8 = (bf16[8,128,256]{2,1,0:T(8,128)(2,1)}, bf16[8,128,256]{2,1,0:T(8,128)(2,1)}, u32[]{:S(2)}, u32[]{:S(2)}) collective-permute-start(bf16[8,128,256]{2,1,0:T(8,128)(2,1)} %collective-permute-done.6), channel_id=1, source_target_pairs={{0,1},{1,2},{2,3},{3,4},{4,5},{5,6},{6,7},{7,0},{8,9},{9,10},{10,1... | collective-permute-start | bytes 1572872 | tf_op jit(solution)/shard_map/ppermute | solution.py:36
  62.6 16.5 %collective-permute-start.9 = (bf16[8,128,256]{2,1,0:T(8,128)(2,1)}, bf16[8,128,256]{2,1,0:T(8,128)(2,1)S(1)}, u32[]{:S(2)}, u32[]{:S(2)}) collective-permute-start(bf16[8,128,256]{2,1,0:T(8,128)(2,1)} %collective-permute-done.7), channel_id=1, source_target_pairs={{0,7},{1,0},{2,1},{3,2},{4,3},{5,4},{6,5},{7,6},{8,15},{9,8},{10,9... | collective-permute-start | bytes 1572872 | tf_op jit(solution)/shard_map/ppermute | solution.py:39
  69.6 11.9 %collective-permute-start.10 = (bf16[8,128,256]{2,1,0:T(8,128)(2,1)}, bf16[8,128,256]{2,1,0:T(8,128)(2,1)S(1)}, u32[]{:S(2)}, u32[]{:S(2)}) collective-permute-start(bf16[8,128,256]{2,1,0:T(8,128)(2,1)} %collective-permute-done.8), channel_id=1, source_target_pairs={{0,1},{1,2},{2,3},{3,4},{4,5},{5,6},{6,7},{7,0},{8,9},{9,10},{10,1... | collective-permute-start | bytes 1572872 | tf_op jit(solution)/shard_map/ppermute | solution.py:36
  96.6 11.9 %collective-permute-start.11 = (f32[4,128,256]{2,1,0:T(8,128)}, f32[4,128,256]{2,1,0:T(8,128)}, u32[]{:S(2)}, u32[]{:S(2)}) collective-permute-start(f32[4,128,256]{2,1,0:T(8,128)} %select_bitcast_fusion.1), channel_id=1, source_target_pairs={{0,64},{64,0},{1,65},{65,1},{2,66},{66,2},{3,67},{67,3},{4,68},{68... | collective-permute-start | bytes 1572872 | tf_op jit(solution)/shard_map/ppermute | solution.py:71
  111.5 9.6 %collective-permute-start.12 = (f32[2,128,256]{2,1,0:T(8,128)}, f32[2,128,256]{2,1,0:T(8,128)S(1)}, u32[]{:S(2)}, u32[]{:S(2)}) collective-permute-start(f32[2,128,256]{2,1,0:T(8,128)} %select_bitcast_fusion.3), channel_id=1, source_target_pairs={{0,128},{128,0},{256,384},{384,256},{1,129},{129,1},{257,385},{385... | collective-permute-start | bytes 786440 | tf_op jit(solution)/shard_map/ppermute | solution.py:71
  122.2 14.9 %collective-permute-start.13 = (f32[1,128,256]{2,1,0:T(8,128)S(1)}, f32[1,128,256]{2,1,0:T(8,128)S(1)}, u32[]{:S(2)}, u32[]{:S(2)}) collective-permute-start(f32[1,128,256]{2,1,0:T(8,128)S(1)} %select_bitcast_fusion.5), channel_id=1, source_target_pairs={{0,256},{128,384},{256,0},{384,128},{1,257},{129,385},{257,1},{385... | collective-permute-start | bytes 393224 | tf_op jit(solution)/shard_map/ppermute | solution.py:71
  160.9 12.2 %collective-permute-start.18 = (bf16[8,128,256]{2,1,0:T(8,128)(2,1)S(1)}, bf16[8,128,256]{2,1,0:T(8,128)(2,1)S(1)}, u32[]{:S(2)}, u32[]{:S(2)}) collective-permute-start(bf16[8,128,256]{2,1,0:T(8,128)(2,1)S(1)} %get-tuple-element.12), channel_id=1, source_target_pairs={{0,1},{1,2},{2,3},{3,4},{4,5},{5,6},{6,7},{7,0},{8,9},{9,10},{10,1... | collective-permute-start | bytes 1572872 | tf_op jit(solution)/shard_map/ppermute | solution.py:36
  162.8 12.2 %collective-permute-start.19 = (bf16[8,128,256]{2,1,0:T(8,128)(2,1)S(1)}, bf16[8,128,256]{2,1,0:T(8,128)(2,1)S(1)}, u32[]{:S(2)}, u32[]{:S(2)}) collective-permute-start(bf16[8,128,256]{2,1,0:T(8,128)(2,1)S(1)} %get-tuple-element.12), channel_id=1, source_target_pairs={{0,7},{1,0},{2,1},{3,2},{4,3},{5,4},{6,5},{7,6},{8,15},{9,8},{10,9... | collective-permute-start | bytes 1572872 | tf_op jit(solution)/shard_map/ppermute | solution.py:39
  173.1 11.1 %collective-permute-start.20 = (bf16[8,128,256]{2,1,0:T(8,128)(2,1)S(1)}, bf16[8,128,256]{2,1,0:T(8,128)(2,1)S(1)}, u32[]{:S(2)}, u32[]{:S(2)}) collective-permute-start(bf16[8,128,256]{2,1,0:T(8,128)(2,1)S(1)} %collective-permute-done.18), channel_id=1, source_target_pairs={{0,1},{1,2},{2,3},{3,4},{4,5},{5,6},{6,7},{7,0},{8,9},{9,10},{10,1... | collective-permute-start | bytes 1572872 | tf_op jit(solution)/shard_map/ppermute | solution.py:36
  175.0 11.1 %collective-permute-start.21 = (bf16[8,128,256]{2,1,0:T(8,128)(2,1)S(1)}, bf16[8,128,256]{2,1,0:T(8,128)(2,1)S(1)}, u32[]{:S(2)}, u32[]{:S(2)}) collective-permute-start(bf16[8,128,256]{2,1,0:T(8,128)(2,1)S(1)} %collective-permute-done.19), channel_id=1, source_target_pairs={{0,7},{1,0},{2,1},{3,2},{4,3},{5,4},{6,5},{7,6},{8,15},{9,8},{10,9... | collective-permute-start | bytes 1572872 | tf_op jit(solution)/shard_map/ppermute | solution.py:39
  184.2 11.3 %collective-permute-start.22 = (bf16[8,128,256]{2,1,0:T(8,128)(2,1)S(1)}, bf16[8,128,256]{2,1,0:T(8,128)(2,1)S(1)}, u32[]{:S(2)}, u32[]{:S(2)}) collective-permute-start(bf16[8,128,256]{2,1,0:T(8,128)(2,1)S(1)} %collective-permute-done.20), channel_id=1, source_target_pairs={{0,1},{1,2},{2,3},{3,4},{4,5},{5,6},{6,7},{7,0},{8,9},{9,10},{10,1... | collective-permute-start | bytes 1572872 | tf_op jit(solution)/shard_map/ppermute | solution.py:36
  186.1 14.7 %collective-permute-start.23 = (bf16[8,128,256]{2,1,0:T(8,128)(2,1)S(1)}, bf16[8,128,256]{2,1,0:T(8,128)(2,1)S(1)}, u32[]{:S(2)}, u32[]{:S(2)}) collective-permute-start(bf16[8,128,256]{2,1,0:T(8,128)(2,1)S(1)} %collective-permute-done.21), channel_id=1, source_target_pairs={{0,7},{1,0},{2,1},{3,2},{4,3},{5,4},{6,5},{7,6},{8,15},{9,8},{10,9... | collective-permute-start | bytes 1572872 | tf_op jit(solution)/shard_map/ppermute | solution.py:39
  195.5 12.4 %collective-permute-start.24 = (bf16[8,128,256]{2,1,0:T(8,128)(2,1)S(1)}, bf16[8,128,256]{2,1,0:T(8,128)(2,1)S(1)}, u32[]{:S(2)}, u32[]{:S(2)}) collective-permute-start(bf16[8,128,256]{2,1,0:T(8,128)(2,1)S(1)} %collective-permute-done.22), channel_id=1, source_target_pairs={{0,1},{1,2},{2,3},{3,4},{4,5},{5,6},{6,7},{7,0},{8,9},{9,10},{10,1... | collective-permute-start | bytes 1572872 | tf_op jit(solution)/shard_map/ppermute | solution.py:36
  236.5 11.9 %collective-permute-start.25 = (f32[4,128,256]{2,1,0:T(8,128)S(1)}, f32[4,128,256]{2,1,0:T(8,128)S(1)}, u32[]{:S(2)}, u32[]{:S(2)}) collective-permute-start(f32[4,128,256]{2,1,0:T(8,128)S(1)} %select_bitcast_fusion), channel_id=1, source_target_pairs={{0,64},{64,0},{1,65},{65,1},{2,66},{66,2},{3,67},{67,3},{4,68},{68... | collective-permute-start | bytes 1572872 | tf_op jit(solution)/shard_map/ppermute | solution.py:71
  249.7 9.4 %collective-permute-start.26 = (f32[2,128,256]{2,1,0:T(8,128)S(1)}, f32[2,128,256]{2,1,0:T(8,128)S(1)}, u32[]{:S(2)}, u32[]{:S(2)}) collective-permute-start(f32[2,128,256]{2,1,0:T(8,128)S(1)} %select_bitcast_fusion.2), channel_id=1, source_target_pairs={{0,128},{128,0},{256,384},{384,256},{1,129},{129,1},{257,385},{385... | collective-permute-start | bytes 786440 | tf_op jit(solution)/shard_map/ppermute | solution.py:71
  259.2 11.2 %collective-permute-start.27 = (f32[1,128,256]{2,1,0:T(8,128)S(1)}, f32[1,128,256]{2,1,0:T(8,128)S(1)}, u32[]{:S(2)}, u32[]{:S(2)}) collective-permute-start(f32[1,128,256]{2,1,0:T(8,128)S(1)} %select_bitcast_fusion.4), channel_id=1, source_target_pairs={{0,256},{128,384},{256,0},{384,128},{1,257},{129,385},{257,1},{385... | collective-permute-start | bytes 393224 | tf_op jit(solution)/shard_map/ppermute | solution.py:71
  317.4 11.2 %collective-permute-start.35 = (f32[132,256]{1,0:T(8,128)S(1)}, f32[132,256]{1,0:T(8,128)S(1)}, u32[]{:S(2)}, u32[]{:S(2)}) collective-permute-start(f32[132,256]{1,0:T(8,128)S(1)} %add.193), channel_id=1, source_target_pairs={{0,4},{1,5},{2,6},{3,7},{4,0},{5,1},{6,2},{7,3},{8,12},{9,13},{10,... | collective-permute-start | bytes 405512 | tf_op jit(solution)/shard_map/ppermute | solution.py:71
  328.7 9.7 %collective-permute-start.36 = (f32[132,256]{1,0:T(8,128)S(1)}, f32[132,256]{1,0:T(8,128)S(1)}, u32[]{:S(2)}, u32[]{:S(2)}) collective-permute-start(f32[132,256]{1,0:T(8,128)S(1)} %add.194), channel_id=1, source_target_pairs={{0,32},{32,0},{1,33},{33,1},{2,34},{34,2},{3,35},{35,3},{4,36},{36... | collective-permute-start | bytes 405512 | tf_op jit(solution)/shard_map/ppermute | solution.py:71
  338.4 10.1 %collective-permute-start.37 = (f32[132,256]{1,0:T(8,128)S(1)}, f32[132,256]{1,0:T(8,128)S(1)}, u32[]{:S(2)}, u32[]{:S(2)}) collective-permute-start(f32[132,256]{1,0:T(8,128)S(1)} %add.195), channel_id=1, source_target_pairs={{0,64},{64,0},{1,65},{65,1},{2,66},{66,2},{3,67},{67,3},{4,68},{68... | collective-permute-start | bytes 405512 | tf_op jit(solution)/shard_map/ppermute | solution.py:71
  (24 other events, 522.2 us)

commit v4 on v3

--- a/solution.py
+++ b/solution.py
@@ -124,25 +124,32 @@
 
 def local(features, weight, bias, cotangent, adj_cols, adj_vals):
     slots = member_slots(adj_cols[0, :, 0, :])
-    product = jnp.dot(features, weight, preferred_element_type=jnp.float32).astype(jnp.bfloat16)
-    gathered = gather_team(product)
-    partial_rows = collect(gathered, slots, adj_vals)
+    width = features.shape[1]
+    block = adj_vals.shape[-1]
+    gathered = gather_team(features)
+    products = jnp.dot(gathered, weight, preferred_element_type=jnp.float32).astype(jnp.bfloat16)
+    partial_rows = collect(products, slots, adj_vals)
+    partial_ax = collect(gathered, slots, adj_vals)
     summed = blk_reduce_scatter(partial_rows)
     pre = summed + bias[None, :]
     activated, pullback = jax.vjp(activation, pre)
     hidden = activated.astype(jnp.bfloat16)
     pulled = pullback(cotangent.astype(jnp.float32))[0].astype(jnp.bfloat16)
+    pulled_rows = lax.all_gather(pulled, BLK_AXES, axis=0, tiled=False)
+    local_weight = jnp.einsum(
+        "rnf,rng->fg",
+        partial_ax.reshape(-1, block, width),
+        pulled_rows.astype(jnp.float32),
+        precision=lax.Precision.HIGHEST,
+        preferred_element_type=jnp.float32,
+    )
+    local_bias = jnp.sum(pulled.astype(jnp.float32), axis=0)
+    filler = jnp.zeros((7, local_bias.shape[0]), jnp.float32)
+    both = all_sum(jnp.concatenate([local_weight, local_bias[None, :], filler], axis=0))
     pulled_group = gather_team(pulled)
     partial_back = collect(pulled_group, slots, adj_vals)
     spread = blk_reduce_scatter(partial_back).astype(jnp.bfloat16)
     grad_input = jnp.dot(spread, weight.T, preferred_element_type=jnp.float32).astype(jnp.bfloat16)
-    local_weight = lax.dot_general(
-        features, spread, (((0,), (0,)), ((), ())), preferred_element_type=jnp.float32
-    )
-    local_bias = jnp.sum(pulled.astype(jnp.float32), axis=0)
-    width = local_weight.shape[0]
-    filler = jnp.zeros((7, local_bias.shape[0]), jnp.float32)
-    both = all_sum(jnp.concatenate([local_weight, local_bias[None, :], filler], axis=0))
     return (hidden, grad_input, both[:width], both[width])
 
 

time: 354 us -> 358 us (1.011)
  blocking collectives: 0 us -> 19 us
  waiting for transfers between devices: 116 us -> 98.2 us
  starting transfers between devices: 152 us -> 136 us
  local copies, waits for them, and re-layouts: 59.6 us -> 69.3 us
  matrix products: 11.7 us -> 20.7 us
    all_gather x0 -> x1, blocking collectives: none -> 19 us  [local(): pulled_rows = lax.all_gather(pulled, BLK_AXES, axis=0, tiled=False)]
    ppermute x16, starting transfers between devices: 75.9 us -> 57.3 us  [swap(): return lax.ppermute(value, axis, [(i, i ^ bit) for i in range(n)])]
    ppermute x12, waiting for transfers between devices: 38.8 us -> 20.8 us  [ring_gather(): ahead = lax.ppermute(ahead, axis, [(i, (i + 1) % n) for i in range(n)])]
    ppermute x8, waiting for transfers between devices: 2.38 us -> 12.2 us  [ring_gather(): behind = lax.ppermute(behind, axis, [(i, (i - 1) % n) for i in range(n)])]
    ppermute x16, waiting for transfers between devices: 68.7 us -> 60.2 us  [swap(): return lax.ppermute(value, axis, [(i, i ^ bit) for i in range(n)])]
    gather x3 -> x4, local copies, waits for them, and re-layouts: 25.1 us -> 33.3 us  [collect(): picked = jnp.take(stacked, slots, axis=0)]
    dot_general x2 -> x3, matrix products: 8.77 us -> 13.7 us  [collect(): jnp.einsum('rkij,rkjf->rif', adj_vals[0, :, 0], picked, preferred_element...]
    dot_general x2, matrix products: 2.14 us -> 6.13 us  [the longest x1 5.48 us: local(): jnp.dot(gathered, weight, preferred_element_type=jnp.float32)]
  transfers between devices with their start and end apart: 38 -> 38, of which waited for: 28 -> 21; matrix products, arithmetic and copies ran while one was open for 7% -> 20% of each run, Pallas kernels for 0% -> 0%
where the time goes in v4:
time: 358 us; the launch traced here: 356 us
  starting transfers between devices  136 us (38%)
  waiting for transfers between devices  98.2 us (27%)
  local copies, waits for them, and re-layouts  69.3 us (19%)
  matrix products  20.7 us (6%)
  blocking collectives  19 us (5%)
  other arithmetic  11.9 us (3%)
    ppermute x16, waiting for transfers between devices, swap(): return lax.ppermute(value, axis, [(i, i ^ bit) for i in range(n)])  60.2 us
    ppermute x16, starting transfers between devices, swap(): return lax.ppermute(value, axis, [(i, i ^ bit) for i in range(n)])  57.3 us
    ppermute x8, starting transfers between devices, ring_gather(): behind = lax.ppermute(behind, axis, [(i, (i - 1) % n) for i in range(n)])  40.9 us
    gather x4, local copies, waits for them, and re-layouts, collect(): picked = jnp.take(stacked, slots, axis=0)  33.3 us
    unnamed x40, local copies, waits for them, and re-layouts  27.6 us
    ppermute x12, starting transfers between devices, ring_gather(): ahead = lax.ppermute(ahead, axis, [(i, (i + 1) % n) for i in range(n)])  24.8 us
    ppermute x12, waiting for transfers between devices, ring_gather(): ahead = lax.ppermute(ahead, axis, [(i, (i + 1) % n) for i in range(n)])  20.8 us
    all_gather x1, blocking collectives, local(): pulled_rows = lax.all_gather(pulled, BLK_AXES, axis=0, tiled=False)  19 us
  transfers between devices with their start and end apart: 38, of which 21 were waited for; matrix products, arithmetic and copies ran while one was open for 20% of the time, Pallas kernels for 0%

profile of v4, /device:TPU:1, one launch (start us, length us, event | category | flops | bytes accessed | tf_op | source)
XLA Modules:
  0.0 356.2 jit_solution(18099412193265278464)
XLA Ops:
  0.7 8.5 %collective-permute-start = (bf16[128,256]{1,0:T(8,128)(2,1)}, bf16[128,256]{1,0:T(8,128)(2,1)S(1)}, u32[]{:S(2)}, u32[]{:S(2)}) collective-permute-start(bf16[128,256]{1,0:T(8,128)(2,1)} %param.10), channel_id=1, source_target_pairs={{0,32},{32,0},{1,33},{33,1},{2,34},{34,2},{3,35},{35,3},{4,36},{36... | collective-permute-start | bytes 196616 | tf_op jit(solution)/shard_map/ppermute | solution.py:45
  22.5 5.0 %collective-permute-done.3 = bf16[2,128,256]{2,1,0:T(8,128)(2,1)S(1)} collective-permute-done((bf16[2,128,256]{2,1,0:T(8,128)(2,1)S(1)}, bf16[2,128,256]{2,1,0:T(8,128)(2,1)S(1)}, u32[]{:S(2)}, u32[]{:S(2)}) %collective-permute-start.3) | collective-permute-done | bytes 131104 | tf_op jit(solution)/shard_map/ppermute | solution.py:36
  30.8 8.6 %collective-permute-start.5 = (bf16[8,128,256]{2,1,0:T(8,128)(2,1)}, bf16[8,128,256]{2,1,0:T(8,128)(2,1)}, u32[]{:S(2)}, u32[]{:S(2)}) collective-permute-start(bf16[8,128,256]{2,1,0:T(8,128)(2,1)} %get-tuple-element.18), channel_id=1, source_target_pairs={{0,7},{1,0},{2,1},{3,2},{4,3},{5,4},{6,5},{7,6},{8,15},{9,8},{10,9... | collective-permute-start | bytes 1572872 | tf_op jit(solution)/shard_map/ppermute | solution.py:39
  39.4 6.3 %collective-permute-done.4 = bf16[8,128,256]{2,1,0:T(8,128)(2,1)} collective-permute-done((bf16[8,128,256]{2,1,0:T(8,128)(2,1)}, bf16[8,128,256]{2,1,0:T(8,128)(2,1)}, u32[]{:S(2)}, u32[]{:S(2)}) %collective-permute-start.4) | collective-permute-done | bytes 524320 | tf_op jit(solution)/shard_map/ppermute | solution.py:36
  62.2 5.0 %collective-permute-start.9 = (bf16[8,128,256]{2,1,0:T(8,128)(2,1)}, bf16[8,128,256]{2,1,0:T(8,128)(2,1)S(1)}, u32[]{:S(2)}, u32[]{:S(2)}) collective-permute-start(bf16[8,128,256]{2,1,0:T(8,128)(2,1)} %collective-permute-done.7), channel_id=1, source_target_pairs={{0,7},{1,0},{2,1},{3,2},{4,3},{5,4},{6,5},{7,6},{8,15},{9,8},{10,9... | collective-permute-start | bytes 1572872 | tf_op jit(solution)/shard_map/ppermute | solution.py:39
  81.7 5.5 %convolution_convert_fusion = bf16[8192,256]{1,0:T(8,128)(2,1)} fusion(bf16[8192,256]{1,0:T(8,128)(2,1)} %bitcast.4, bf16[256,256]{1,0:T(8,128)(2,1)S(1)} %copy-done.5), kind=kOutput, calls=%fused_computation.5 | convolution fusion | flops 1075838976 | bytes 8519680 | tf_op jit(solution)/shard_map/dot_general | solution.py:130
  87.2 8.2 %gather_fusion.2 = bf16[96,128,256]{2,1,0:T(8,128)(2,1)} fusion(bf16[64,128,256]{2,1,0:T(8,128)(2,1)} %bitcast.147, s32[1024]{0:T(1024)S(1)} %pad_clamp_fusion), kind=kCustom, calls=%fused_computation.clone | custom fusion | bytes 12583296 | tf_op jit(solution)/shard_map/jit(_take)/gather | solution.py:114
  101.5 10.0 %collective-permute-start.11 = (f32[4,128,256]{2,1,0:T(8,128)}, f32[4,128,256]{2,1,0:T(8,128)}, u32[]{:S(2)}, u32[]{:S(2)}) collective-permute-start(f32[4,128,256]{2,1,0:T(8,128)} %select_bitcast_fusion.1), channel_id=1, source_target_pairs={{0,64},{64,0},{1,65},{65,1},{2,66},{66,2},{3,67},{67,3},{4,68},{68... | collective-permute-start | bytes 1572872 | tf_op jit(solution)/shard_map/ppermute | solution.py:71
  118.8 6.3 %collective-permute-done.12 = f32[2,128,256]{2,1,0:T(8,128)} collective-permute-done((f32[2,128,256]{2,1,0:T(8,128)S(1)}, f32[2,128,256]{2,1,0:T(8,128)}, u32[]{:S(2)}, u32[]{:S(2)}) %collective-permute-start.12) | collective-permute-done | bytes 262176 | tf_op jit(solution)/shard_map/ppermute | solution.py:71
  127.0 8.2 %collective-permute-start.13 = (f32[1,128,256]{2,1,0:T(8,128)}, f32[1,128,256]{2,1,0:T(8,128)}, u32[]{:S(2)}, u32[]{:S(2)}) collective-permute-start(f32[1,128,256]{2,1,0:T(8,128)} %select_bitcast_fusion.5), channel_id=1, source_target_pairs={{0,256},{128,384},{256,0},{384,128},{1,257},{129,385},{257,1},{385... | collective-permute-start | bytes 393224 | tf_op jit(solution)/shard_map/ppermute | solution.py:71
  135.3 8.2 %gather_fusion.4 = bf16[96,128,256]{2,1,0:T(8,128)(2,1)} fusion(bf16[64,128,256]{2,1,0:T(8,128)(2,1)} %constant_dynamic-update-slice_fusion.5, s32[1024]{0:T(1024)S(1)} %pad_clamp_fusion), kind=kCustom, calls=%fused_computation.2.clone | custom fusion | bytes 12583296 | tf_op jit(solution)/shard_map/jit(_take)/gather | solution.py:114
  176.4 19.0 %all-gather = bf16[1024,256]{1,0:T(8,128)(2,1)S(1)} all-gather(bf16[128,256]{1,0:T(8,128)(2,1)S(1)} %get-tuple-element.6), channel_id=2, replica_groups=mesh['y_lo'=4,'core'=2,'y_hi'=2,'x'=4,'z'=8] {'y_lo','core'}, dimensions={0}, use_global_device_ids=true | all-gather | bytes 589824 | tf_op jit(solution)/shard_map/all_gather | solution.py:138
  195.4 5.0 %collective-permute-start.19 = (bf16[8,128,256]{2,1,0:T(8,128)(2,1)S(1)}, bf16[8,128,256]{2,1,0:T(8,128)(2,1)S(1)}, u32[]{:S(2)}, u32[]{:S(2)}) collective-permute-start(bf16[8,128,256]{2,1,0:T(8,128)(2,1)S(1)} %get-tuple-element.12), channel_id=1, source_target_pairs={{0,7},{1,0},{2,1},{3,2},{4,3},{5,4},{6,5},{7,6},{8,15},{9,8},{10,9... | collective-permute-start | bytes 1572872 | tf_op jit(solution)/shard_map/ppermute | solution.py:39
  205.5 5.9 %collective-permute-done.19 = bf16[8,128,256]{2,1,0:T(8,128)(2,1)S(1)} collective-permute-done((bf16[8,128,256]{2,1,0:T(8,128)(2,1)S(1)}, bf16[8,128,256]{2,1,0:T(8,128)(2,1)S(1)}, u32[]{:S(2)}, u32[]{:S(2)}) %collective-permute-start.19) | collective-permute-done | bytes 524320 | tf_op jit(solution)/shard_map/ppermute | solution.py:39
  211.4 5.3 %collective-permute-start.21 = (bf16[8,128,256]{2,1,0:T(8,128)(2,1)S(1)}, bf16[8,128,256]{2,1,0:T(8,128)(2,1)S(1)}, u32[]{:S(2)}, u32[]{:S(2)}) collective-permute-start(bf16[8,128,256]{2,1,0:T(8,128)(2,1)S(1)} %collective-permute-done.19), channel_id=1, source_target_pairs={{0,7},{1,0},{2,1},{3,2},{4,3},{5,4},{6,5},{7,6},{8,15},{9,8},{10,9... | collective-permute-start | bytes 1572872 | tf_op jit(solution)/shard_map/ppermute | solution.py:39
  251.6 8.2 %gather_fusion.3 = bf16[96,128,256]{2,1,0:T(8,128)(2,1)} fusion(bf16[64,128,256]{2,1,0:T(8,128)(2,1)} %constant_dynamic-update-slice_fusion.22, s32[1024]{0:T(1024)S(1)} %pad_clamp_fusion), kind=kCustom, calls=%fused_computation.1.clone | custom fusion | bytes 12583296 | tf_op jit(solution)/shard_map/jit(_take)/gather | solution.py:114
  259.8 8.7 %copy.25 = bf16[8,12,128,256]{2,3,1,0:T(8,128)(2,1)} copy(bf16[8,12,128,256]{3,2,1,0:T(8,128)(2,1)} %bitcast.148) | data formatting | bytes 12582912 | tf_op jit(solution)/shard_map/jit(_take)/gather | solution.py:114
  279.4 6.6 %collective-permute-start.25 = (f32[4,128,256]{2,1,0:T(8,128)S(1)}, f32[4,128,256]{2,1,0:T(8,128)S(1)}, u32[]{:S(2)}, u32[]{:S(2)}) collective-permute-start(f32[4,128,256]{2,1,0:T(8,128)S(1)} %select_bitcast_fusion), channel_id=1, source_target_pairs={{0,64},{64,0},{1,65},{65,1},{2,66},{66,2},{3,67},{67,3},{4,68},{68... | collective-permute-start | bytes 1572872 | tf_op jit(solution)/shard_map/ppermute | solution.py:71
  289.3 8.9 %collective-permute-done.32 = f32[132,256]{1,0:T(8,128)S(1)} collective-permute-done((f32[132,256]{1,0:T(8,128)S(1)}, f32[132,256]{1,0:T(8,128)S(1)}, u32[]{:S(2)}, u32[]{:S(2)}) %collective-permute-start.32) | collective-permute-done | bytes 135200 | tf_op jit(solution)/shard_map/ppermute | solution.py:71
  300.1 6.3 %collective-permute-done.33 = f32[132,256]{1,0:T(8,128)S(1)} collective-permute-done((f32[132,256]{1,0:T(8,128)S(1)}, f32[132,256]{1,0:T(8,128)S(1)}, u32[]{:S(2)}, u32[]{:S(2)}) %collective-permute-start.33) | collective-permute-done | bytes 135200 | tf_op jit(solution)/shard_map/ppermute | solution.py:71
  308.3 7.8 %collective-permute-done.34 = f32[132,256]{1,0:T(8,128)S(1)} collective-permute-done((f32[132,256]{1,0:T(8,128)S(1)}, f32[132,256]{1,0:T(8,128)S(1)}, u32[]{:S(2)}, u32[]{:S(2)}) %collective-permute-start.34) | collective-permute-done | bytes 135200 | tf_op jit(solution)/shard_map/ppermute | solution.py:71
  323.8 6.2 %collective-permute-done.35 = f32[132,256]{1,0:T(8,128)S(1)} collective-permute-done((f32[132,256]{1,0:T(8,128)S(1)}, f32[132,256]{1,0:T(8,128)S(1)}, u32[]{:S(2)}, u32[]{:S(2)}) %collective-permute-start.35) | collective-permute-done | bytes 135200 | tf_op jit(solution)/shard_map/ppermute | solution.py:71
  334.3 9.3 %collective-permute-done.36 = f32[132,256]{1,0:T(8,128)S(1)} collective-permute-done((f32[132,256]{1,0:T(8,128)S(1)}, f32[132,256]{1,0:T(8,128)S(1)}, u32[]{:S(2)}, u32[]{:S(2)}) %collective-permute-start.36) | collective-permute-done | bytes 135200 | tf_op jit(solution)/shard_map/ppermute | solution.py:71
  350.1 5.2 %collective-permute-done.27 = f32[1,128,256]{2,1,0:T(8,128)S(1)} collective-permute-done((f32[1,128,256]{2,1,0:T(8,128)S(1)}, f32[1,128,256]{2,1,0:T(8,128)S(1)}, u32[]{:S(2)}, u32[]{:S(2)}) %collective-permute-start.27) | collective-permute-done | bytes 131104 | tf_op jit(solution)/shard_map/ppermute | solution.py:71
  (148 shorter events, 172.6 us)
Async XLA Ops:
  0.7 10.5 %collective-permute-start = (bf16[128,256]{1,0:T(8,128)(2,1)}, bf16[128,256]{1,0:T(8,128)(2,1)S(1)}, u32[]{:S(2)}, u32[]{:S(2)}) collective-permute-start(bf16[128,256]{1,0:T(8,128)(2,1)} %param.10), channel_id=1, source_target_pairs={{0,32},{32,0},{1,33},{33,1},{2,34},{34,2},{3,35},{35,3},{4,36},{36... | collective-permute-start | bytes 196616 | tf_op jit(solution)/shard_map/ppermute | solution.py:45
  28.3 17.4 %collective-permute-start.4 = (bf16[8,128,256]{2,1,0:T(8,128)(2,1)}, bf16[8,128,256]{2,1,0:T(8,128)(2,1)}, u32[]{:S(2)}, u32[]{:S(2)}) collective-permute-start(bf16[8,128,256]{2,1,0:T(8,128)(2,1)} %get-tuple-element.18), channel_id=1, source_target_pairs={{0,1},{1,2},{2,3},{3,4},{4,5},{5,6},{6,7},{7,0},{8,9},{9,10},{10,1... | collective-permute-start | bytes 1572872 | tf_op jit(solution)/shard_map/ppermute | solution.py:36
  30.8 20.2 %collective-permute-start.5 = (bf16[8,128,256]{2,1,0:T(8,128)(2,1)}, bf16[8,128,256]{2,1,0:T(8,128)(2,1)}, u32[]{:S(2)}, u32[]{:S(2)}) collective-permute-start(bf16[8,128,256]{2,1,0:T(8,128)(2,1)} %get-tuple-element.18), channel_id=1, source_target_pairs={{0,7},{1,0},{2,1},{3,2},{4,3},{5,4},{6,5},{7,6},{8,15},{9,8},{10,9... | collective-permute-start | bytes 1572872 | tf_op jit(solution)/shard_map/ppermute | solution.py:39
  45.7 11.8 %collective-permute-start.6 = (bf16[8,128,256]{2,1,0:T(8,128)(2,1)}, bf16[8,128,256]{2,1,0:T(8,128)(2,1)}, u32[]{:S(2)}, u32[]{:S(2)}) collective-permute-start(bf16[8,128,256]{2,1,0:T(8,128)(2,1)} %collective-permute-done.4), channel_id=1, source_target_pairs={{0,1},{1,2},{2,3},{3,4},{4,5},{5,6},{6,7},{7,0},{8,9},{9,10},{10,1... | collective-permute-start | bytes 1572872 | tf_op jit(solution)/shard_map/ppermute | solution.py:36
  51.0 11.1 %collective-permute-start.7 = (bf16[8,128,256]{2,1,0:T(8,128)(2,1)}, bf16[8,128,256]{2,1,0:T(8,128)(2,1)}, u32[]{:S(2)}, u32[]{:S(2)}) collective-permute-start(bf16[8,128,256]{2,1,0:T(8,128)(2,1)} %collective-permute-done.5), channel_id=1, source_target_pairs={{0,7},{1,0},{2,1},{3,2},{4,3},{5,4},{6,5},{7,6},{8,15},{9,8},{10,9... | collective-permute-start | bytes 1572872 | tf_op jit(solution)/shard_map/ppermute | solution.py:39
  57.5 11.5 %collective-permute-start.8 = (bf16[8,128,256]{2,1,0:T(8,128)(2,1)}, bf16[8,128,256]{2,1,0:T(8,128)(2,1)}, u32[]{:S(2)}, u32[]{:S(2)}) collective-permute-start(bf16[8,128,256]{2,1,0:T(8,128)(2,1)} %collective-permute-done.6), channel_id=1, source_target_pairs={{0,1},{1,2},{2,3},{3,4},{4,5},{5,6},{6,7},{7,0},{8,9},{9,10},{10,1... | collective-permute-start | bytes 1572872 | tf_op jit(solution)/shard_map/ppermute | solution.py:36
  62.2 16.4 %collective-permute-start.9 = (bf16[8,128,256]{2,1,0:T(8,128)(2,1)}, bf16[8,128,256]{2,1,0:T(8,128)(2,1)S(1)}, u32[]{:S(2)}, u32[]{:S(2)}) collective-permute-start(bf16[8,128,256]{2,1,0:T(8,128)(2,1)} %collective-permute-done.7), channel_id=1, source_target_pairs={{0,7},{1,0},{2,1},{3,2},{4,3},{5,4},{6,5},{7,6},{8,15},{9,8},{10,9... | collective-permute-start | bytes 1572872 | tf_op jit(solution)/shard_map/ppermute | solution.py:39
  69.1 11.8 %collective-permute-start.10 = (bf16[8,128,256]{2,1,0:T(8,128)(2,1)}, bf16[8,128,256]{2,1,0:T(8,128)(2,1)S(1)}, u32[]{:S(2)}, u32[]{:S(2)}) collective-permute-start(bf16[8,128,256]{2,1,0:T(8,128)(2,1)} %collective-permute-done.8), channel_id=1, source_target_pairs={{0,1},{1,2},{2,3},{3,4},{4,5},{5,6},{6,7},{7,0},{8,9},{9,10},{10,1... | collective-permute-start | bytes 1572872 | tf_op jit(solution)/shard_map/ppermute | solution.py:36
  101.5 11.8 %collective-permute-start.11 = (f32[4,128,256]{2,1,0:T(8,128)}, f32[4,128,256]{2,1,0:T(8,128)}, u32[]{:S(2)}, u32[]{:S(2)}) collective-permute-start(f32[4,128,256]{2,1,0:T(8,128)} %select_bitcast_fusion.1), channel_id=1, source_target_pairs={{0,64},{64,0},{1,65},{65,1},{2,66},{66,2},{3,67},{67,3},{4,68},{68... | collective-permute-start | bytes 1572872 | tf_op jit(solution)/shard_map/ppermute | solution.py:71
  127.0 16.5 %collective-permute-start.13 = (f32[1,128,256]{2,1,0:T(8,128)}, f32[1,128,256]{2,1,0:T(8,128)}, u32[]{:S(2)}, u32[]{:S(2)}) collective-permute-start(f32[1,128,256]{2,1,0:T(8,128)} %select_bitcast_fusion.5), channel_id=1, source_target_pairs={{0,256},{128,384},{256,0},{384,128},{1,257},{129,385},{257,1},{385... | collective-permute-start | bytes 393224 | tf_op jit(solution)/shard_map/ppermute | solution.py:71
  169.6 30.9 %collective-permute-start.18 = (bf16[8,128,256]{2,1,0:T(8,128)(2,1)S(1)}, bf16[8,128,256]{2,1,0:T(8,128)(2,1)S(1)}, u32[]{:S(2)}, u32[]{:S(2)}) collective-permute-start(bf16[8,128,256]{2,1,0:T(8,128)(2,1)S(1)} %get-tuple-element.12), channel_id=1, source_target_pairs={{0,1},{1,2},{2,3},{3,4},{4,5},{5,6},{6,7},{7,0},{8,9},{9,10},{10,1... | collective-permute-start | bytes 1572872 | tf_op jit(solution)/shard_map/ppermute | solution.py:36
  195.4 16.0 %collective-permute-start.19 = (bf16[8,128,256]{2,1,0:T(8,128)(2,1)S(1)}, bf16[8,128,256]{2,1,0:T(8,128)(2,1)S(1)}, u32[]{:S(2)}, u32[]{:S(2)}) collective-permute-start(bf16[8,128,256]{2,1,0:T(8,128)(2,1)S(1)} %get-tuple-element.12), channel_id=1, source_target_pairs={{0,7},{1,0},{2,1},{3,2},{4,3},{5,4},{6,5},{7,6},{8,15},{9,8},{10,9... | collective-permute-start | bytes 1572872 | tf_op jit(solution)/shard_map/ppermute | solution.py:39
  200.4 16.3 %collective-permute-start.20 = (bf16[8,128,256]{2,1,0:T(8,128)(2,1)S(1)}, bf16[8,128,256]{2,1,0:T(8,128)(2,1)S(1)}, u32[]{:S(2)}, u32[]{:S(2)}) collective-permute-start(bf16[8,128,256]{2,1,0:T(8,128)(2,1)S(1)} %collective-permute-done.18), channel_id=1, source_target_pairs={{0,1},{1,2},{2,3},{3,4},{4,5},{5,6},{6,7},{7,0},{8,9},{9,10},{10,1... | collective-permute-start | bytes 1572872 | tf_op jit(solution)/shard_map/ppermute | solution.py:36
  203.1 15.5 %collective-permute-start.28 = (f32[132,256]{1,0:T(8,128)S(1)}, f32[132,256]{1,0:T(8,128)S(1)}, u32[]{:S(2)}, u32[]{:S(2)}) collective-permute-start(f32[132,256]{1,0:T(8,128)S(1)} %slice_select_fusion), channel_id=1, source_target_pairs={{0,64},{64,0},{1,65},{65,1},{2,66},{66,2},{3,67},{67,3},{4,68},{68... | collective-permute-start | bytes 405512 | tf_op jit(solution)/shard_map/ppermute | solution.py:71
  211.4 21.5 %collective-permute-start.21 = (bf16[8,128,256]{2,1,0:T(8,128)(2,1)S(1)}, bf16[8,128,256]{2,1,0:T(8,128)(2,1)S(1)}, u32[]{:S(2)}, u32[]{:S(2)}) collective-permute-start(bf16[8,128,256]{2,1,0:T(8,128)(2,1)S(1)} %collective-permute-done.19), channel_id=1, source_target_pairs={{0,7},{1,0},{2,1},{3,2},{4,3},{5,4},{6,5},{7,6},{8,15},{9,8},{10,9... | collective-permute-start | bytes 1572872 | tf_op jit(solution)/shard_map/ppermute | solution.py:39
  216.7 21.3 %collective-permute-start.22 = (bf16[8,128,256]{2,1,0:T(8,128)(2,1)S(1)}, bf16[8,128,256]{2,1,0:T(8,128)(2,1)S(1)}, u32[]{:S(2)}, u32[]{:S(2)}) collective-permute-start(bf16[8,128,256]{2,1,0:T(8,128)(2,1)S(1)} %collective-permute-done.20), channel_id=1, source_target_pairs={{0,1},{1,2},{2,3},{3,4},{4,5},{5,6},{6,7},{7,0},{8,9},{9,10},{10,1... | collective-permute-start | bytes 1572872 | tf_op jit(solution)/shard_map/ppermute | solution.py:36
  231.0 55.1 %collective-permute-start.31 = (f32[132,256]{1,0:T(8,128)S(1)}, f32[132,256]{1,0:T(8,128)}, u32[]{:S(2)}, u32[]{:S(2)}) collective-permute-start(f32[132,256]{1,0:T(8,128)S(1)} %add.189), channel_id=1, source_target_pairs={{0,1},{1,0},{2,3},{3,2},{4,5},{5,4},{6,7},{7,6},{8,9},{9,8},{10,11... | collective-permute-start | bytes 405512 | tf_op jit(solution)/shard_map/ppermute | solution.py:71
  232.9 14.3 %collective-permute-start.23 = (bf16[8,128,256]{2,1,0:T(8,128)(2,1)S(1)}, bf16[8,128,256]{2,1,0:T(8,128)(2,1)S(1)}, u32[]{:S(2)}, u32[]{:S(2)}) collective-permute-start(bf16[8,128,256]{2,1,0:T(8,128)(2,1)S(1)} %collective-permute-done.21), channel_id=1, source_target_pairs={{0,7},{1,0},{2,1},{3,2},{4,3},{5,4},{6,5},{7,6},{8,15},{9,8},{10,9... | collective-permute-start | bytes 1572872 | tf_op jit(solution)/shard_map/ppermute | solution.py:39
  238.1 12.7 %collective-permute-start.24 = (bf16[8,128,256]{2,1,0:T(8,128)(2,1)S(1)}, bf16[8,128,256]{2,1,0:T(8,128)(2,1)S(1)}, u32[]{:S(2)}, u32[]{:S(2)}) collective-permute-start(bf16[8,128,256]{2,1,0:T(8,128)(2,1)S(1)} %collective-permute-done.22), channel_id=1, source_target_pairs={{0,1},{1,2},{2,3},{3,4},{4,5},{5,6},{6,7},{7,0},{8,9},{9,10},{10,1... | collective-permute-start | bytes 1572872 | tf_op jit(solution)/shard_map/ppermute | solution.py:36
  279.4 41.2 %collective-permute-start.25 = (f32[4,128,256]{2,1,0:T(8,128)S(1)}, f32[4,128,256]{2,1,0:T(8,128)S(1)}, u32[]{:S(2)}, u32[]{:S(2)}) collective-permute-start(f32[4,128,256]{2,1,0:T(8,128)S(1)} %select_bitcast_fusion), channel_id=1, source_target_pairs={{0,64},{64,0},{1,65},{65,1},{2,66},{66,2},{3,67},{67,3},{4,68},{68... | collective-permute-start | bytes 1572872 | tf_op jit(solution)/shard_map/ppermute | solution.py:71
  287.0 11.1 %collective-permute-start.32 = (f32[132,256]{1,0:T(8,128)S(1)}, f32[132,256]{1,0:T(8,128)S(1)}, u32[]{:S(2)}, u32[]{:S(2)}) collective-permute-start(f32[132,256]{1,0:T(8,128)S(1)} %add.190), channel_id=1, source_target_pairs={{0,256},{128,384},{256,0},{384,128},{1,257},{129,385},{257,1},{385... | collective-permute-start | bytes 405512 | tf_op jit(solution)/shard_map/ppermute | solution.py:71
  316.2 13.8 %collective-permute-start.35 = (f32[132,256]{1,0:T(8,128)S(1)}, f32[132,256]{1,0:T(8,128)S(1)}, u32[]{:S(2)}, u32[]{:S(2)}) collective-permute-start(f32[132,256]{1,0:T(8,128)S(1)} %add.193), channel_id=1, source_target_pairs={{0,4},{1,5},{2,6},{3,7},{4,0},{5,1},{6,2},{7,3},{8,12},{9,13},{10,... | collective-permute-start | bytes 405512 | tf_op jit(solution)/shard_map/ppermute | solution.py:71
  321.8 24.3 %collective-permute-start.26 = (f32[2,128,256]{2,1,0:T(8,128)S(1)}, f32[2,128,256]{2,1,0:T(8,128)S(1)}, u32[]{:S(2)}, u32[]{:S(2)}) collective-permute-start(f32[2,128,256]{2,1,0:T(8,128)S(1)} %select_bitcast_fusion.2), channel_id=1, source_target_pairs={{0,128},{128,0},{256,384},{384,256},{1,129},{129,1},{257,385},{385... | collective-permute-start | bytes 786440 | tf_op jit(solution)/shard_map/ppermute | solution.py:71
  330.0 13.7 %collective-permute-start.36 = (f32[132,256]{1,0:T(8,128)S(1)}, f32[132,256]{1,0:T(8,128)S(1)}, u32[]{:S(2)}, u32[]{:S(2)}) collective-permute-start(f32[132,256]{1,0:T(8,128)S(1)} %add.194), channel_id=1, source_target_pairs={{0,32},{32,0},{1,33},{33,1},{2,34},{34,2},{3,35},{35,3},{4,36},{36... | collective-permute-start | bytes 405512 | tf_op jit(solution)/shard_map/ppermute | solution.py:71
  (23 other events, 421.0 us)

commit v5 on v3

--- a/solution.py
+++ b/solution.py
@@ -1,6 +1,8 @@
 import jax
 import jax.numpy as jnp
 from jax import lax
+from jax.experimental import pallas as pl
+from jax.experimental.pallas import tpu as pltpu
 from jax.sharding import Mesh
 from jax.sharding import PartitionSpec as P
 
@@ -107,15 +109,40 @@
     return cur.reshape(block, width)
 
 
+def collect_kernel(slots_ref, vals_ref, panels_ref, out_ref):
+    row = pl.program_id(0)
+    nnz = vals_ref.shape[0]
+    total = jnp.zeros(out_ref.shape, jnp.float32)
+    for k in range(nnz):
+        slot = slots_ref[row * nnz + k]
+        total = total + jnp.dot(vals_ref[k], panels_ref[slot], preferred_element_type=jnp.float32)
+    out_ref[...] = total
+
+
 def collect(panels, slots, adj_vals):
     block = adj_vals.shape[-1]
     width = panels.shape[1]
+    rows, nnz = slots.shape
     stacked = panels.reshape(panels.shape[0] // block, block, width)
-    picked = jnp.take(stacked, slots, axis=0)
-    summed = jnp.einsum(
-        "rkij,rkjf->rif", adj_vals[0, :, 0], picked, preferred_element_type=jnp.float32
+    grid_spec = pltpu.PrefetchScalarGridSpec(
+        num_scalar_prefetch=1,
+        grid=(rows,),
+        in_specs=[
+            pl.BlockSpec((None, None, None, nnz, block, block), lambda r, s: (0, r, 0, 0, 0, 0)),
+            pl.BlockSpec(stacked.shape, lambda r, s: (0, 0, 0)),
+        ],
+        out_specs=pl.BlockSpec((block, width), lambda r, s: (r, 0)),
     )
-    return summed.reshape(-1, width)
+    return pl.pallas_call(
+        collect_kernel,
+        grid_spec=grid_spec,
+        out_shape=jax.ShapeDtypeStruct((rows * block, width), jnp.float32),
+        cost_estimate=pl.CostEstimate(
+            flops=2 * rows * nnz * block * block * width,
+            transcendentals=0,
+            bytes_accessed=stacked.size * 2 + rows * nnz * block * block * 2 + rows * block * width * 4,
+        ),
+    )(slots.reshape(-1), adj_vals, stacked)
 
 
 def activation(value):

time: 354 us -> 330 us (0.932)
  local copies, waits for them, and re-layouts: 59.6 us -> 23.1 us
  Pallas kernels: 0 us -> 17.8 us
  matrix products: 11.7 us -> 2.68 us
  waiting for transfers between devices: 116 us -> 120 us
    gather x3 -> x0, local copies, waits for them, and re-layouts: 25.1 us -> none  [collect(): picked = jnp.take(stacked, slots, axis=0)]
    pallas_call x0 -> x2, Pallas kernels: none -> 17.8 us  [collect(): pl.pallas_call(collect_kernel, grid_spec=grid_spec, out_shape=jax.ShapeDt...]
    unnamed x41 -> x32, local copies, waits for them, and re-layouts: 26.2 us -> 16.1 us
    dot_general x2 -> x0, matrix products: 8.77 us -> none  [collect(): jnp.einsum('rkij,rkjf->rif', adj_vals[0, :, 0], picked, preferred_element...]
    ppermute x12, waiting for transfers between devices: 38.8 us -> 45.2 us  [ring_gather(): ahead = lax.ppermute(ahead, axis, [(i, (i + 1) % n) for i in range(n)])]
  transfers between devices with their start and end apart: 38 -> 38, of which waited for: 28 -> 27; matrix products, arithmetic and copies ran while one was open for 7% -> 7% of each run, Pallas kernels for 0% -> 0%
where the time goes in v5:
time: 330 us; the launch traced here: 328 us
  starting transfers between devices  154 us (47%)
  waiting for transfers between devices  120 us (36%)
  local copies, waits for them, and re-layouts  23.1 us (7%)
  Pallas kernels  17.8 us (5%)
  other arithmetic  9.26 us (3%)
    ppermute x16, starting transfers between devices, swap(): return lax.ppermute(value, axis, [(i, i ^ bit) for i in range(n)])  77.9 us
    ppermute x16, waiting for transfers between devices, swap(): return lax.ppermute(value, axis, [(i, i ^ bit) for i in range(n)])  68.7 us
    ppermute x12, waiting for transfers between devices, ring_gather(): ahead = lax.ppermute(ahead, axis, [(i, (i + 1) % n) for i in range(n)])  45.2 us
    ppermute x8, starting transfers between devices, ring_gather(): behind = lax.ppermute(behind, axis, [(i, (i - 1) % n) for i in range(n)])  39.4 us
    ppermute x12, starting transfers between devices, ring_gather(): ahead = lax.ppermute(ahead, axis, [(i, (i + 1) % n) for i in range(n)])  24.8 us
    pallas_call x2, Pallas kernels, collect(): pl.pallas_call(collect_kernel, grid_spec=grid_spec, out_shape=jax.ShapeDt...  17.8 us
    unnamed x32, local copies, waits for them, and re-layouts  16.1 us
    ppermute x2, starting transfers between devices, gather_team(): other = lax.ppermute(rows, 'y_hi', perm=[(0, 1), (1, 0)])  11.8 us
  transfers between devices with their start and end apart: 38, of which 27 were waited for; matrix products, arithmetic and copies ran while one was open for 7% of the time, Pallas kernels for 0%

profile of v5, /device:TPU:1, one launch (start us, length us, event | category | flops | bytes accessed | tf_op | source)
XLA Modules:
  0.0 328.3 jit_solution(16869326058895143962)
XLA Ops:
  3.2 8.3 %collective-permute-start = (bf16[128,256]{1,0:T(8,128)(2,1)S(1)}, bf16[128,256]{1,0:T(8,128)(2,1)S(1)}, u32[]{:S(2)}, u32[]{:S(2)}) collective-permute-start(bf16[128,256]{1,0:T(8,128)(2,1)S(1)} %get-tuple-element.29), channel_id=1, source_target_pairs={{0,32},{32,0},{1,33},{33,1},{2,34},{34,2},{3,35},{35,3},{4,36},{36... | collective-permute-start | bytes 196616 | tf_op jit(solution)/shard_map/ppermute | solution.py:47
  23.6 5.1 %collective-permute-done.3 = bf16[2,128,256]{2,1,0:T(8,128)(2,1)S(1)} collective-permute-done((bf16[2,128,256]{2,1,0:T(8,128)(2,1)S(1)}, bf16[2,128,256]{2,1,0:T(8,128)(2,1)S(1)}, u32[]{:S(2)}, u32[]{:S(2)}) %collective-permute-start.3) | collective-permute-done | bytes 131104 | tf_op jit(solution)/shard_map/ppermute | solution.py:38
  31.9 8.6 %collective-permute-start.5 = (bf16[8,128,256]{2,1,0:T(8,128)(2,1)S(1)}, bf16[8,128,256]{2,1,0:T(8,128)(2,1)S(1)}, u32[]{:S(2)}, u32[]{:S(2)}) collective-permute-start(bf16[8,128,256]{2,1,0:T(8,128)(2,1)S(1)} %get-tuple-element.13), channel_id=1, source_target_pairs={{0,7},{1,0},{2,1},{3,2},{4,3},{5,4},{6,5},{7,6},{8,15},{9,8},{10,9... | collective-permute-start | bytes 1572872 | tf_op jit(solution)/shard_map/ppermute | solution.py:41
  40.5 5.9 %collective-permute-done.4 = bf16[8,128,256]{2,1,0:T(8,128)(2,1)S(1)} collective-permute-done((bf16[8,128,256]{2,1,0:T(8,128)(2,1)S(1)}, bf16[8,128,256]{2,1,0:T(8,128)(2,1)S(1)}, u32[]{:S(2)}, u32[]{:S(2)}) %collective-permute-start.4) | collective-permute-done | bytes 524320 | tf_op jit(solution)/shard_map/ppermute | solution.py:38
  52.9 5.0 %collective-permute-done.6 = bf16[8,128,256]{2,1,0:T(8,128)(2,1)S(1)} collective-permute-done((bf16[8,128,256]{2,1,0:T(8,128)(2,1)S(1)}, bf16[8,128,256]{2,1,0:T(8,128)(2,1)S(1)}, u32[]{:S(2)}, u32[]{:S(2)}) %collective-permute-start.6) | collective-permute-done | bytes 524320 | tf_op jit(solution)/shard_map/ppermute | solution.py:38
  77.3 5.0 %collective-permute-done.10 = bf16[8,128,256]{2,1,0:T(8,128)(2,1)S(1)} collective-permute-done((bf16[8,128,256]{2,1,0:T(8,128)(2,1)S(1)}, bf16[8,128,256]{2,1,0:T(8,128)(2,1)S(1)}, u32[]{:S(2)}, u32[]{:S(2)}) %collective-permute-start.10) | collective-permute-done | bytes 524320 | tf_op jit(solution)/shard_map/ppermute | solution.py:38
  83.1 8.9 %shard_map.111 = f32[1024,256]{1,0:T(8,128)} custom-call(s32[96]{0:T(128)} %fusion.24.slots_ref, bf16[1,8,1,12,128,128]{5,4,3,2,1,0:T(8,128)(2,1)} %vals_ref.3, bf16[64,128,256]{2,1,0:T(8,128)(2,1)} %constant_dynamic-update-slice_fusion.5.panels_ref), custom_call_target="tpu_custom_call" | custom-call | flops 805306368 | bytes 8388608 | tf_op jit(solution)/shard_map/pallas_call | solution.py:136
  93.3 9.5 %collective-permute-start.11 = (f32[4,128,256]{2,1,0:T(8,128)S(1)}, f32[4,128,256]{2,1,0:T(8,128)S(1)}, u32[]{:S(2)}, u32[]{:S(2)}) collective-permute-start(f32[4,128,256]{2,1,0:T(8,128)S(1)} %select_bitcast_fusion.1), channel_id=1, source_target_pairs={{0,64},{64,0},{1,65},{65,1},{2,66},{66,2},{3,67},{67,3},{4,68},{68... | collective-permute-start | bytes 1572872 | tf_op jit(solution)/shard_map/ppermute | solution.py:73
  109.3 6.3 %collective-permute-done.12 = f32[2,128,256]{2,1,0:T(8,128)S(1)} collective-permute-done((f32[2,128,256]{2,1,0:T(8,128)S(1)}, f32[2,128,256]{2,1,0:T(8,128)S(1)}, u32[]{:S(2)}, u32[]{:S(2)}) %collective-permute-start.12) | collective-permute-done | bytes 262176 | tf_op jit(solution)/shard_map/ppermute | solution.py:73
  115.7 7.6 %collective-permute-start.13 = (f32[1,128,256]{2,1,0:T(8,128)S(1)}, f32[1,128,256]{2,1,0:T(8,128)S(1)}, u32[]{:S(2)}, u32[]{:S(2)}) collective-permute-start(f32[1,128,256]{2,1,0:T(8,128)S(1)} %select_bitcast_fusion.5), channel_id=1, source_target_pairs={{0,256},{128,384},{256,0},{384,128},{1,257},{129,385},{257,1},{385... | collective-permute-start | bytes 393224 | tf_op jit(solution)/shard_map/ppermute | solution.py:73
  123.3 6.7 %collective-permute-done.13 = f32[1,128,256]{2,1,0:T(8,128)S(1)} collective-permute-done((f32[1,128,256]{2,1,0:T(8,128)S(1)}, f32[1,128,256]{2,1,0:T(8,128)S(1)}, u32[]{:S(2)}, u32[]{:S(2)}) %collective-permute-start.13) | collective-permute-done | bytes 131104 | tf_op jit(solution)/shard_map/ppermute | solution.py:73
  134.4 4.7 %collective-permute-done.14 = bf16[128,256]{1,0:T(8,128)(2,1)S(1)} collective-permute-done((bf16[128,256]{1,0:T(8,128)(2,1)S(1)}, bf16[128,256]{1,0:T(8,128)(2,1)S(1)}, u32[]{:S(2)}, u32[]{:S(2)}) %collective-permute-start.14) | collective-permute-done | bytes 65568 | tf_op jit(solution)/shard_map/ppermute | solution.py:47
  160.3 5.8 %collective-permute-done.18 = bf16[8,128,256]{2,1,0:T(8,128)(2,1)S(1)} collective-permute-done((bf16[8,128,256]{2,1,0:T(8,128)(2,1)S(1)}, bf16[8,128,256]{2,1,0:T(8,128)(2,1)S(1)}, u32[]{:S(2)}, u32[]{:S(2)}) %collective-permute-start.18) | collective-permute-done | bytes 524320 | tf_op jit(solution)/shard_map/ppermute | solution.py:38
  194.6 6.2 %collective-permute-done.24 = bf16[8,128,256]{2,1,0:T(8,128)(2,1)S(1)} collective-permute-done((bf16[8,128,256]{2,1,0:T(8,128)(2,1)S(1)}, bf16[8,128,256]{2,1,0:T(8,128)(2,1)S(1)}, u32[]{:S(2)}, u32[]{:S(2)}) %collective-permute-start.24) | collective-permute-done | bytes 524320 | tf_op jit(solution)/shard_map/ppermute | solution.py:38
  201.6 8.9 %shard_map.112 = f32[1024,256]{1,0:T(8,128)} custom-call(s32[96]{0:T(128)} %fusion.24.slots_ref, bf16[1,8,1,12,128,128]{5,4,3,2,1,0:T(8,128)(2,1)} %vals_ref.3, bf16[64,128,256]{2,1,0:T(8,128)(2,1)} %constant_dynamic-update-slice_fusion.22.panels_ref), custom_call_target="tpu_custom_call" | custom-call | flops 805306368 | bytes 8388608 | tf_op jit(solution)/shard_map/pallas_call | solution.py:136
  211.9 10.4 %collective-permute-start.25 = (f32[4,128,256]{2,1,0:T(8,128)S(1)}, f32[4,128,256]{2,1,0:T(8,128)S(1)}, u32[]{:S(2)}, u32[]{:S(2)}) collective-permute-start(f32[4,128,256]{2,1,0:T(8,128)S(1)} %select_bitcast_fusion), channel_id=1, source_target_pairs={{0,64},{64,0},{1,65},{65,1},{2,66},{66,2},{3,67},{67,3},{4,68},{68... | collective-permute-start | bytes 1572872 | tf_op jit(solution)/shard_map/ppermute | solution.py:73
  227.0 7.5 %collective-permute-done.26 = f32[2,128,256]{2,1,0:T(8,128)S(1)} collective-permute-done((f32[2,128,256]{2,1,0:T(8,128)S(1)}, f32[2,128,256]{2,1,0:T(8,128)S(1)}, u32[]{:S(2)}, u32[]{:S(2)}) %collective-permute-start.26) | collective-permute-done | bytes 262176 | tf_op jit(solution)/shard_map/ppermute | solution.py:73
  234.6 5.5 %collective-permute-start.27 = (f32[1,128,256]{2,1,0:T(8,128)S(1)}, f32[1,128,256]{2,1,0:T(8,128)S(1)}, u32[]{:S(2)}, u32[]{:S(2)}) collective-permute-start(f32[1,128,256]{2,1,0:T(8,128)S(1)} %select_bitcast_fusion.4), channel_id=1, source_target_pairs={{0,256},{128,384},{256,0},{384,128},{1,257},{129,385},{257,1},{385... | collective-permute-start | bytes 393224 | tf_op jit(solution)/shard_map/ppermute | solution.py:73
  240.1 5.8 %collective-permute-done.27 = f32[1,128,256]{2,1,0:T(8,128)S(1)} collective-permute-done((f32[1,128,256]{2,1,0:T(8,128)S(1)}, f32[1,128,256]{2,1,0:T(8,128)S(1)}, u32[]{:S(2)}, u32[]{:S(2)}) %collective-permute-start.27) | collective-permute-done | bytes 131104 | tf_op jit(solution)/shard_map/ppermute | solution.py:73
  279.7 5.4 %collective-permute-done.33 = f32[132,256]{1,0:T(8,128)S(1)} collective-permute-done((f32[132,256]{1,0:T(8,128)S(1)}, f32[132,256]{1,0:T(8,128)S(1)}, u32[]{:S(2)}, u32[]{:S(2)}) %collective-permute-start.33) | collective-permute-done | bytes 135200 | tf_op jit(solution)/shard_map/ppermute | solution.py:73
  287.0 6.0 %collective-permute-done.34 = f32[132,256]{1,0:T(8,128)S(1)} collective-permute-done((f32[132,256]{1,0:T(8,128)S(1)}, f32[132,256]{1,0:T(8,128)S(1)}, u32[]{:S(2)}, u32[]{:S(2)}) %collective-permute-start.34) | collective-permute-done | bytes 135200 | tf_op jit(solution)/shard_map/ppermute | solution.py:73
  297.2 6.5 %collective-permute-done.35 = f32[132,256]{1,0:T(8,128)S(1)} collective-permute-done((f32[132,256]{1,0:T(8,128)S(1)}, f32[132,256]{1,0:T(8,128)S(1)}, u32[]{:S(2)}, u32[]{:S(2)}) %collective-permute-start.35) | collective-permute-done | bytes 135200 | tf_op jit(solution)/shard_map/ppermute | solution.py:73
  303.7 4.8 %collective-permute-start.36 = (f32[132,256]{1,0:T(8,128)S(1)}, f32[132,256]{1,0:T(8,128)S(1)}, u32[]{:S(2)}, u32[]{:S(2)}) collective-permute-start(f32[132,256]{1,0:T(8,128)S(1)} %add.192), channel_id=1, source_target_pairs={{0,32},{32,0},{1,33},{33,1},{2,34},{34,2},{3,35},{35,3},{4,36},{36... | collective-permute-start | bytes 405512 | tf_op jit(solution)/shard_map/ppermute | solution.py:73
  313.5 12.5 %collective-permute-start.37 = (f32[132,256]{1,0:T(8,128)S(1)}, f32[132,256]{1,0:T(8,128)S(1)}, u32[]{:S(2)}, u32[]{:S(2)}) collective-permute-start(f32[132,256]{1,0:T(8,128)S(1)} %add.193), channel_id=1, source_target_pairs={{0,64},{64,0},{1,65},{65,1},{2,66},{66,2},{3,67},{67,3},{4,68},{68... | collective-permute-start | bytes 405512 | tf_op jit(solution)/shard_map/ppermute | solution.py:73
  (132 shorter events, 160.2 us)
Async XLA Ops:
  3.2 10.0 %collective-permute-start = (bf16[128,256]{1,0:T(8,128)(2,1)S(1)}, bf16[128,256]{1,0:T(8,128)(2,1)S(1)}, u32[]{:S(2)}, u32[]{:S(2)}) collective-permute-start(bf16[128,256]{1,0:T(8,128)(2,1)S(1)} %get-tuple-element.29), channel_id=1, source_target_pairs={{0,32},{32,0},{1,33},{33,1},{2,34},{34,2},{3,35},{35,3},{4,36},{36... | collective-permute-start | bytes 196616 | tf_op jit(solution)/shard_map/ppermute | solution.py:47
  29.3 17.1 %collective-permute-start.4 = (bf16[8,128,256]{2,1,0:T(8,128)(2,1)S(1)}, bf16[8,128,256]{2,1,0:T(8,128)(2,1)S(1)}, u32[]{:S(2)}, u32[]{:S(2)}) collective-permute-start(bf16[8,128,256]{2,1,0:T(8,128)(2,1)S(1)} %get-tuple-element.13), channel_id=1, source_target_pairs={{0,1},{1,2},{2,3},{3,4},{4,5},{5,6},{6,7},{7,0},{8,9},{9,10},{10,1... | collective-permute-start | bytes 1572872 | tf_op jit(solution)/shard_map/ppermute | solution.py:38
  31.9 16.5 %collective-permute-start.5 = (bf16[8,128,256]{2,1,0:T(8,128)(2,1)S(1)}, bf16[8,128,256]{2,1,0:T(8,128)(2,1)S(1)}, u32[]{:S(2)}, u32[]{:S(2)}) collective-permute-start(bf16[8,128,256]{2,1,0:T(8,128)(2,1)S(1)} %get-tuple-element.13), channel_id=1, source_target_pairs={{0,7},{1,0},{2,1},{3,2},{4,3},{5,4},{6,5},{7,6},{8,15},{9,8},{10,9... | collective-permute-start | bytes 1572872 | tf_op jit(solution)/shard_map/ppermute | solution.py:41
  46.4 11.5 %collective-permute-start.6 = (bf16[8,128,256]{2,1,0:T(8,128)(2,1)S(1)}, bf16[8,128,256]{2,1,0:T(8,128)(2,1)S(1)}, u32[]{:S(2)}, u32[]{:S(2)}) collective-permute-start(bf16[8,128,256]{2,1,0:T(8,128)(2,1)S(1)} %collective-permute-done.4), channel_id=1, source_target_pairs={{0,1},{1,2},{2,3},{3,4},{4,5},{5,6},{6,7},{7,0},{8,9},{9,10},{10,1... | collective-permute-start | bytes 1572872 | tf_op jit(solution)/shard_map/ppermute | solution.py:38
  48.4 17.4 %collective-permute-start.7 = (bf16[8,128,256]{2,1,0:T(8,128)(2,1)S(1)}, bf16[8,128,256]{2,1,0:T(8,128)(2,1)S(1)}, u32[]{:S(2)}, u32[]{:S(2)}) collective-permute-start(bf16[8,128,256]{2,1,0:T(8,128)(2,1)S(1)} %collective-permute-done.5), channel_id=1, source_target_pairs={{0,7},{1,0},{2,1},{3,2},{4,3},{5,4},{6,5},{7,6},{8,15},{9,8},{10,9... | collective-permute-start | bytes 1572872 | tf_op jit(solution)/shard_map/ppermute | solution.py:41
  57.9 13.2 %collective-permute-start.8 = (bf16[8,128,256]{2,1,0:T(8,128)(2,1)S(1)}, bf16[8,128,256]{2,1,0:T(8,128)(2,1)S(1)}, u32[]{:S(2)}, u32[]{:S(2)}) collective-permute-start(bf16[8,128,256]{2,1,0:T(8,128)(2,1)S(1)} %collective-permute-done.6), channel_id=1, source_target_pairs={{0,1},{1,2},{2,3},{3,4},{4,5},{5,6},{6,7},{7,0},{8,9},{9,10},{10,1... | collective-permute-start | bytes 1572872 | tf_op jit(solution)/shard_map/ppermute | solution.py:38
  65.7 10.7 %collective-permute-start.9 = (bf16[8,128,256]{2,1,0:T(8,128)(2,1)S(1)}, bf16[8,128,256]{2,1,0:T(8,128)(2,1)S(1)}, u32[]{:S(2)}, u32[]{:S(2)}) collective-permute-start(bf16[8,128,256]{2,1,0:T(8,128)(2,1)S(1)} %collective-permute-done.7), channel_id=1, source_target_pairs={{0,7},{1,0},{2,1},{3,2},{4,3},{5,4},{6,5},{7,6},{8,15},{9,8},{10,9... | collective-permute-start | bytes 1572872 | tf_op jit(solution)/shard_map/ppermute | solution.py:41
  71.1 11.1 %collective-permute-start.10 = (bf16[8,128,256]{2,1,0:T(8,128)(2,1)S(1)}, bf16[8,128,256]{2,1,0:T(8,128)(2,1)S(1)}, u32[]{:S(2)}, u32[]{:S(2)}) collective-permute-start(bf16[8,128,256]{2,1,0:T(8,128)(2,1)S(1)} %collective-permute-done.8), channel_id=1, source_target_pairs={{0,1},{1,2},{2,3},{3,4},{4,5},{5,6},{6,7},{7,0},{8,9},{9,10},{10,1... | collective-permute-start | bytes 1572872 | tf_op jit(solution)/shard_map/ppermute | solution.py:38
  93.3 11.0 %collective-permute-start.11 = (f32[4,128,256]{2,1,0:T(8,128)S(1)}, f32[4,128,256]{2,1,0:T(8,128)S(1)}, u32[]{:S(2)}, u32[]{:S(2)}) collective-permute-start(f32[4,128,256]{2,1,0:T(8,128)S(1)} %select_bitcast_fusion.1), channel_id=1, source_target_pairs={{0,64},{64,0},{1,65},{65,1},{2,66},{66,2},{3,67},{67,3},{4,68},{68... | collective-permute-start | bytes 1572872 | tf_op jit(solution)/shard_map/ppermute | solution.py:73
  105.7 9.9 %collective-permute-start.12 = (f32[2,128,256]{2,1,0:T(8,128)S(1)}, f32[2,128,256]{2,1,0:T(8,128)S(1)}, u32[]{:S(2)}, u32[]{:S(2)}) collective-permute-start(f32[2,128,256]{2,1,0:T(8,128)S(1)} %select_bitcast_fusion.3), channel_id=1, source_target_pairs={{0,128},{128,0},{256,384},{384,256},{1,129},{129,1},{257,385},{385... | collective-permute-start | bytes 786440 | tf_op jit(solution)/shard_map/ppermute | solution.py:73
  115.7 14.3 %collective-permute-start.13 = (f32[1,128,256]{2,1,0:T(8,128)S(1)}, f32[1,128,256]{2,1,0:T(8,128)S(1)}, u32[]{:S(2)}, u32[]{:S(2)}) collective-permute-start(f32[1,128,256]{2,1,0:T(8,128)S(1)} %select_bitcast_fusion.5), channel_id=1, source_target_pairs={{0,256},{128,384},{256,0},{384,128},{1,257},{129,385},{257,1},{385... | collective-permute-start | bytes 393224 | tf_op jit(solution)/shard_map/ppermute | solution.py:73
  153.8 12.3 %collective-permute-start.18 = (bf16[8,128,256]{2,1,0:T(8,128)(2,1)S(1)}, bf16[8,128,256]{2,1,0:T(8,128)(2,1)S(1)}, u32[]{:S(2)}, u32[]{:S(2)}) collective-permute-start(bf16[8,128,256]{2,1,0:T(8,128)(2,1)S(1)} %get-tuple-element.7), channel_id=1, source_target_pairs={{0,1},{1,2},{2,3},{3,4},{4,5},{5,6},{6,7},{7,0},{8,9},{9,10},{10,1... | collective-permute-start | bytes 1572872 | tf_op jit(solution)/shard_map/ppermute | solution.py:38
  155.7 12.3 %collective-permute-start.19 = (bf16[8,128,256]{2,1,0:T(8,128)(2,1)S(1)}, bf16[8,128,256]{2,1,0:T(8,128)(2,1)S(1)}, u32[]{:S(2)}, u32[]{:S(2)}) collective-permute-start(bf16[8,128,256]{2,1,0:T(8,128)(2,1)S(1)} %get-tuple-element.7), channel_id=1, source_target_pairs={{0,7},{1,0},{2,1},{3,2},{4,3},{5,4},{6,5},{7,6},{8,15},{9,8},{10,9... | collective-permute-start | bytes 1572872 | tf_op jit(solution)/shard_map/ppermute | solution.py:41
  166.1 11.1 %collective-permute-start.20 = (bf16[8,128,256]{2,1,0:T(8,128)(2,1)S(1)}, bf16[8,128,256]{2,1,0:T(8,128)(2,1)S(1)}, u32[]{:S(2)}, u32[]{:S(2)}) collective-permute-start(bf16[8,128,256]{2,1,0:T(8,128)(2,1)S(1)} %collective-permute-done.18), channel_id=1, source_target_pairs={{0,1},{1,2},{2,3},{3,4},{4,5},{5,6},{6,7},{7,0},{8,9},{9,10},{10,1... | collective-permute-start | bytes 1572872 | tf_op jit(solution)/shard_map/ppermute | solution.py:38
  168.0 11.1 %collective-permute-start.21 = (bf16[8,128,256]{2,1,0:T(8,128)(2,1)S(1)}, bf16[8,128,256]{2,1,0:T(8,128)(2,1)S(1)}, u32[]{:S(2)}, u32[]{:S(2)}) collective-permute-start(bf16[8,128,256]{2,1,0:T(8,128)(2,1)S(1)} %collective-permute-done.19), channel_id=1, source_target_pairs={{0,7},{1,0},{2,1},{3,2},{4,3},{5,4},{6,5},{7,6},{8,15},{9,8},{10,9... | collective-permute-start | bytes 1572872 | tf_op jit(solution)/shard_map/ppermute | solution.py:41
  177.2 11.2 %collective-permute-start.22 = (bf16[8,128,256]{2,1,0:T(8,128)(2,1)S(1)}, bf16[8,128,256]{2,1,0:T(8,128)(2,1)S(1)}, u32[]{:S(2)}, u32[]{:S(2)}) collective-permute-start(bf16[8,128,256]{2,1,0:T(8,128)(2,1)S(1)} %collective-permute-done.20), channel_id=1, source_target_pairs={{0,1},{1,2},{2,3},{3,4},{4,5},{5,6},{6,7},{7,0},{8,9},{9,10},{10,1... | collective-permute-start | bytes 1572872 | tf_op jit(solution)/shard_map/ppermute | solution.py:38
  179.2 14.6 %collective-permute-start.23 = (bf16[8,128,256]{2,1,0:T(8,128)(2,1)S(1)}, bf16[8,128,256]{2,1,0:T(8,128)(2,1)S(1)}, u32[]{:S(2)}, u32[]{:S(2)}) collective-permute-start(bf16[8,128,256]{2,1,0:T(8,128)(2,1)S(1)} %collective-permute-done.21), channel_id=1, source_target_pairs={{0,7},{1,0},{2,1},{3,2},{4,3},{5,4},{6,5},{7,6},{8,15},{9,8},{10,9... | collective-permute-start | bytes 1572872 | tf_op jit(solution)/shard_map/ppermute | solution.py:41
  188.5 12.3 %collective-permute-start.24 = (bf16[8,128,256]{2,1,0:T(8,128)(2,1)S(1)}, bf16[8,128,256]{2,1,0:T(8,128)(2,1)S(1)}, u32[]{:S(2)}, u32[]{:S(2)}) collective-permute-start(bf16[8,128,256]{2,1,0:T(8,128)(2,1)S(1)} %collective-permute-done.22), channel_id=1, source_target_pairs={{0,1},{1,2},{2,3},{3,4},{4,5},{5,6},{6,7},{7,0},{8,9},{9,10},{10,1... | collective-permute-start | bytes 1572872 | tf_op jit(solution)/shard_map/ppermute | solution.py:38
  211.9 11.9 %collective-permute-start.25 = (f32[4,128,256]{2,1,0:T(8,128)S(1)}, f32[4,128,256]{2,1,0:T(8,128)S(1)}, u32[]{:S(2)}, u32[]{:S(2)}) collective-permute-start(f32[4,128,256]{2,1,0:T(8,128)S(1)} %select_bitcast_fusion), channel_id=1, source_target_pairs={{0,64},{64,0},{1,65},{65,1},{2,66},{66,2},{3,67},{67,3},{4,68},{68... | collective-permute-start | bytes 1572872 | tf_op jit(solution)/shard_map/ppermute | solution.py:73
  225.1 9.4 %collective-permute-start.26 = (f32[2,128,256]{2,1,0:T(8,128)S(1)}, f32[2,128,256]{2,1,0:T(8,128)S(1)}, u32[]{:S(2)}, u32[]{:S(2)}) collective-permute-start(f32[2,128,256]{2,1,0:T(8,128)S(1)} %select_bitcast_fusion.2), channel_id=1, source_target_pairs={{0,128},{128,0},{256,384},{384,256},{1,129},{129,1},{257,385},{385... | collective-permute-start | bytes 786440 | tf_op jit(solution)/shard_map/ppermute | solution.py:73
  234.6 11.3 %collective-permute-start.27 = (f32[1,128,256]{2,1,0:T(8,128)S(1)}, f32[1,128,256]{2,1,0:T(8,128)S(1)}, u32[]{:S(2)}, u32[]{:S(2)}) collective-permute-start(f32[1,128,256]{2,1,0:T(8,128)S(1)} %select_bitcast_fusion.4), channel_id=1, source_target_pairs={{0,256},{128,384},{256,0},{384,128},{1,257},{129,385},{257,1},{385... | collective-permute-start | bytes 393224 | tf_op jit(solution)/shard_map/ppermute | solution.py:73
  293.0 10.7 %collective-permute-start.35 = (f32[132,256]{1,0:T(8,128)S(1)}, f32[132,256]{1,0:T(8,128)S(1)}, u32[]{:S(2)}, u32[]{:S(2)}) collective-permute-start(f32[132,256]{1,0:T(8,128)S(1)} %add.191), channel_id=1, source_target_pairs={{0,4},{1,5},{2,6},{3,7},{4,0},{5,1},{6,2},{7,3},{8,12},{9,13},{10,... | collective-permute-start | bytes 405512 | tf_op jit(solution)/shard_map/ppermute | solution.py:73
  303.7 9.8 %collective-permute-start.36 = (f32[132,256]{1,0:T(8,128)S(1)}, f32[132,256]{1,0:T(8,128)S(1)}, u32[]{:S(2)}, u32[]{:S(2)}) collective-permute-start(f32[132,256]{1,0:T(8,128)S(1)} %add.192), channel_id=1, source_target_pairs={{0,32},{32,0},{1,33},{33,1},{2,34},{34,2},{3,35},{35,3},{4,36},{36... | collective-permute-start | bytes 405512 | tf_op jit(solution)/shard_map/ppermute | solution.py:73
  313.5 13.5 %collective-permute-start.37 = (f32[132,256]{1,0:T(8,128)S(1)}, f32[132,256]{1,0:T(8,128)S(1)}, u32[]{:S(2)}, u32[]{:S(2)}) collective-permute-start(f32[132,256]{1,0:T(8,128)S(1)} %add.193), channel_id=1, source_target_pairs={{0,64},{64,0},{1,65},{65,1},{2,66},{66,2},{3,67},{67,3},{4,68},{68... | collective-permute-start | bytes 405512 | tf_op jit(solution)/shard_map/ppermute | solution.py:73
  (20 other events, 337.1 us)

commit v6 on v5

--- a/solution.py
+++ b/solution.py
@@ -107,6 +107,20 @@
         cur = keep + swap(send, "y_lo", bit)
         bit *= 2
     return cur.reshape(block, width)
+
+
+def blk_all_gather(rows):
+    cur = rows[None]
+    bit = 1
+    while bit < SIZES["y_lo"]:
+        upper = (lax.axis_index("y_lo") & bit) != 0
+        got = swap(cur, "y_lo", bit)
+        cur = jnp.where(upper, jnp.concatenate([got, cur]), jnp.concatenate([cur, got]))
+        bit *= 2
+    upper = lax.axis_index("core") == 1
+    got = swap(cur, "core", 1)
+    cur = jnp.where(upper, jnp.stack([got, cur], axis=1), jnp.stack([cur, got], axis=1))
+    return cur.reshape((-1,) + rows.shape)
 
 
 def collect_kernel(slots_ref, vals_ref, panels_ref, out_ref):
@@ -151,25 +165,31 @@
 
 def local(features, weight, bias, cotangent, adj_cols, adj_vals):
     slots = member_slots(adj_cols[0, :, 0, :])
-    product = jnp.dot(features, weight, preferred_element_type=jnp.float32).astype(jnp.bfloat16)
-    gathered = gather_team(product)
-    partial_rows = collect(gathered, slots, adj_vals)
+    width = features.shape[1]
+    gathered = gather_team(features)
+    products = jnp.dot(gathered, weight, preferred_element_type=jnp.float32).astype(jnp.bfloat16)
+    partial_rows = collect(products, slots, adj_vals)
+    partial_ax = collect(gathered, slots, adj_vals)
     summed = blk_reduce_scatter(partial_rows)
     pre = summed + bias[None, :]
     activated, pullback = jax.vjp(activation, pre)
     hidden = activated.astype(jnp.bfloat16)
     pulled = pullback(cotangent.astype(jnp.float32))[0].astype(jnp.bfloat16)
+    pulled_rows = blk_all_gather(pulled)
+    local_weight = jnp.einsum(
+        "rnf,rng->fg",
+        partial_ax.reshape(pulled_rows.shape),
+        pulled_rows.astype(jnp.float32),
+        precision=lax.Precision.HIGHEST,
+        preferred_element_type=jnp.float32,
+    )
+    local_bias = jnp.sum(pulled.astype(jnp.float32), axis=0)
+    filler = jnp.zeros((7, local_bias.shape[0]), jnp.float32)
+    both = all_sum(jnp.concatenate([local_weight, local_bias[None, :], filler], axis=0))
     pulled_group = gather_team(pulled)
     partial_back = collect(pulled_group, slots, adj_vals)
     spread = blk_reduce_scatter(partial_back).astype(jnp.bfloat16)
     grad_input = jnp.dot(spread, weight.T, preferred_element_type=jnp.float32).astype(jnp.bfloat16)
-    local_weight = lax.dot_general(
-        features, spread, (((0,), (0,)), ((), ())), preferred_element_type=jnp.float32
-    )
-    local_bias = jnp.sum(pulled.astype(jnp.float32), axis=0)
-    width = local_weight.shape[0]
-    filler = jnp.zeros((7, local_bias.shape[0]), jnp.float32)
-    both = all_sum(jnp.concatenate([local_weight, local_bias[None, :], filler], axis=0))
     return (hidden, grad_input, both[:width], both[width])
 
 

time: 330 us -> 318 us (0.964)
  waiting for transfers between devices: 120 us -> 98.8 us
  Pallas kernels: 17.8 us -> 26.8 us
  starting transfers between devices: 154 us -> 147 us
  matrix products: 2.68 us -> 8.52 us
    ppermute x12, waiting for transfers between devices: 45.2 us -> 34.4 us  [ring_gather(): ahead = lax.ppermute(ahead, axis, [(i, (i + 1) % n) for i in range(n)])]
    pallas_call x2 -> x3, Pallas kernels: 17.8 us -> 26.8 us  [collect(): pl.pallas_call(collect_kernel, grid_spec=grid_spec, out_shape=jax.ShapeDt...]
    ppermute x16 -> x19, starting transfers between devices: 77.9 us -> 70.5 us  [swap(): return lax.ppermute(value, axis, [(i, i ^ bit) for i in range(n)])]
    ppermute x16 -> x19, waiting for transfers between devices: 68.7 us -> 61.3 us  [swap(): return lax.ppermute(value, axis, [(i, i ^ bit) for i in range(n)])]
    dot_general x2, matrix products: 1.85 us -> 7.69 us  [the longest x1 5.45 us: local(): jnp.dot(gathered, weight, preferred_element_type=jnp.float32)]
    ppermute x2, waiting for transfers between devices: 6.43 us -> 1.95 us  [gather_team(): other = lax.ppermute(rows, 'y_hi', perm=[(0, 1), (1, 0)])]
    unnamed x32 -> x31, local copies, waits for them, and re-layouts: 16.1 us -> 16.7 us
  transfers between devices with their start and end apart: 38 -> 41, of which waited for: 27 -> 20; matrix products, arithmetic and copies ran while one was open for 7% -> 10% of each run, Pallas kernels for 0% -> 6%
where the time goes in v6:
time: 318 us; the launch traced here: 316 us
  starting transfers between devices  147 us (46%)
  waiting for transfers between devices  98.8 us (31%)
  Pallas kernels  26.8 us (8%)
  local copies, waits for them, and re-layouts  23.9 us (8%)
  other arithmetic  10.2 us (3%)
  matrix products  8.52 us (3%)
    ppermute x19, starting transfers between devices, swap(): return lax.ppermute(value, axis, [(i, i ^ bit) for i in range(n)])  70.5 us
    ppermute x19, waiting for transfers between devices, swap(): return lax.ppermute(value, axis, [(i, i ^ bit) for i in range(n)])  61.3 us
    ppermute x8, starting transfers between devices, ring_gather(): behind = lax.ppermute(behind, axis, [(i, (i - 1) % n) for i in range(n)])  39.5 us
    ppermute x12, waiting for transfers between devices, ring_gather(): ahead = lax.ppermute(ahead, axis, [(i, (i + 1) % n) for i in range(n)])  34.4 us
    pallas_call x3, Pallas kernels, collect(): pl.pallas_call(collect_kernel, grid_spec=grid_spec, out_shape=jax.ShapeDt...  26.8 us
    ppermute x12, starting transfers between devices, ring_gather(): ahead = lax.ppermute(ahead, axis, [(i, (i + 1) % n) for i in range(n)])  24.8 us
    unnamed x31, local copies, waits for them, and re-layouts  16.7 us
    ppermute x2, starting transfers between devices, gather_team(): other = lax.ppermute(rows, 'y_hi', perm=[(0, 1), (1, 0)])  12.1 us
  transfers between devices with their start and end apart: 41, of which 20 were waited for; matrix products, arithmetic and copies ran while one was open for 10% of the time, Pallas kernels for 6%

profile of v6, /device:TPU:1, one launch (start us, length us, event | category | flops | bytes accessed | tf_op | source)
XLA Modules:
  0.0 316.3 jit_solution(4964391715653036277)
XLA Ops:
  0.7 8.4 %collective-permute-start = (bf16[128,256]{1,0:T(8,128)(2,1)}, bf16[128,256]{1,0:T(8,128)(2,1)S(1)}, u32[]{:S(2)}, u32[]{:S(2)}) collective-permute-start(bf16[128,256]{1,0:T(8,128)(2,1)} %param.8), channel_id=1, source_target_pairs={{0,32},{32,0},{1,33},{33,1},{2,34},{34,2},{3,35},{35,3},{4,36},{36... | collective-permute-start | bytes 196616 | tf_op jit(solution)/shard_map/ppermute | solution.py:47
  22.3 5.1 %collective-permute-done.3 = bf16[2,128,256]{2,1,0:T(8,128)(2,1)S(1)} collective-permute-done((bf16[2,128,256]{2,1,0:T(8,128)(2,1)S(1)}, bf16[2,128,256]{2,1,0:T(8,128)(2,1)S(1)}, u32[]{:S(2)}, u32[]{:S(2)}) %collective-permute-start.3) | collective-permute-done | bytes 131104 | tf_op jit(solution)/shard_map/ppermute | solution.py:38
  30.6 8.6 %collective-permute-start.5 = (bf16[8,128,256]{2,1,0:T(8,128)(2,1)S(1)}, bf16[8,128,256]{2,1,0:T(8,128)(2,1)S(1)}, u32[]{:S(2)}, u32[]{:S(2)}) collective-permute-start(bf16[8,128,256]{2,1,0:T(8,128)(2,1)S(1)} %get-tuple-element.13), channel_id=1, source_target_pairs={{0,7},{1,0},{2,1},{3,2},{4,3},{5,4},{6,5},{7,6},{8,15},{9,8},{10,9... | collective-permute-start | bytes 1572872 | tf_op jit(solution)/shard_map/ppermute | solution.py:41
  39.2 5.9 %collective-permute-done.4 = bf16[8,128,256]{2,1,0:T(8,128)(2,1)S(1)} collective-permute-done((bf16[8,128,256]{2,1,0:T(8,128)(2,1)S(1)}, bf16[8,128,256]{2,1,0:T(8,128)(2,1)S(1)}, u32[]{:S(2)}, u32[]{:S(2)}) %collective-permute-start.4) | collective-permute-done | bytes 524320 | tf_op jit(solution)/shard_map/ppermute | solution.py:38
  51.6 5.0 %collective-permute-done.6 = bf16[8,128,256]{2,1,0:T(8,128)(2,1)S(1)} collective-permute-done((bf16[8,128,256]{2,1,0:T(8,128)(2,1)S(1)}, bf16[8,128,256]{2,1,0:T(8,128)(2,1)S(1)}, u32[]{:S(2)}, u32[]{:S(2)}) %collective-permute-start.6) | collective-permute-done | bytes 524320 | tf_op jit(solution)/shard_map/ppermute | solution.py:38
  75.9 5.0 %collective-permute-done.10 = bf16[8,128,256]{2,1,0:T(8,128)(2,1)S(1)} collective-permute-done((bf16[8,128,256]{2,1,0:T(8,128)(2,1)S(1)}, bf16[8,128,256]{2,1,0:T(8,128)(2,1)S(1)}, u32[]{:S(2)}, u32[]{:S(2)}) %collective-permute-start.10) | collective-permute-done | bytes 524320 | tf_op jit(solution)/shard_map/ppermute | solution.py:38
  81.8 5.5 %convolution_convert_fusion = bf16[8192,256]{1,0:T(8,128)(2,1)} fusion(bf16[8192,256]{1,0:T(8,128)(2,1)} %bitcast.3, bf16[256,256]{1,0:T(8,128)(2,1)S(1)} %copy-done), kind=kOutput, calls=%fused_computation.2 | convolution fusion | flops 1075838976 | bytes 8519680 | tf_op jit(solution)/shard_map/dot_general | solution.py:170
  87.2 8.9 %shard_map.111 = f32[1024,256]{1,0:T(8,128)} custom-call(s32[96]{0:T(128)} %fusion.27.slots_ref, bf16[1,8,1,12,128,128]{5,4,3,2,1,0:T(8,128)(2,1)} %vals_ref.5, bf16[64,128,256]{2,1,0:T(8,128)(2,1)} %bitcast.131), custom_call_target="tpu_custom_call" | custom-call | flops 805306368 | bytes 8388608 | tf_op jit(solution)/shard_map/pallas_call | solution.py:150
  97.5 9.6 %collective-permute-start.11 = (f32[4,128,256]{2,1,0:T(8,128)S(1)}, f32[4,128,256]{2,1,0:T(8,128)S(1)}, u32[]{:S(2)}, u32[]{:S(2)}) collective-permute-start(f32[4,128,256]{2,1,0:T(8,128)S(1)} %select_bitcast_fusion.1), channel_id=1, source_target_pairs={{0,64},{64,0},{1,65},{65,1},{2,66},{66,2},{3,67},{67,3},{4,68},{68... | collective-permute-start | bytes 1572872 | tf_op jit(solution)/shard_map/ppermute | solution.py:73
  113.5 6.3 %collective-permute-done.12 = f32[2,128,256]{2,1,0:T(8,128)S(1)} collective-permute-done((f32[2,128,256]{2,1,0:T(8,128)S(1)}, f32[2,128,256]{2,1,0:T(8,128)S(1)}, u32[]{:S(2)}, u32[]{:S(2)}) %collective-permute-start.12) | collective-permute-done | bytes 262176 | tf_op jit(solution)/shard_map/ppermute | solution.py:73
  119.9 7.6 %collective-permute-start.13 = (f32[1,128,256]{2,1,0:T(8,128)S(1)}, f32[1,128,256]{2,1,0:T(8,128)S(1)}, u32[]{:S(2)}, u32[]{:S(2)}) collective-permute-start(f32[1,128,256]{2,1,0:T(8,128)S(1)} %select_bitcast_fusion.5), channel_id=1, source_target_pairs={{0,256},{128,384},{256,0},{384,128},{1,257},{129,385},{257,1},{385... | collective-permute-start | bytes 393224 | tf_op jit(solution)/shard_map/ppermute | solution.py:73
  127.5 6.7 %collective-permute-done.13 = f32[1,128,256]{2,1,0:T(8,128)S(1)} collective-permute-done((f32[1,128,256]{2,1,0:T(8,128)S(1)}, f32[1,128,256]{2,1,0:T(8,128)S(1)}, u32[]{:S(2)}, u32[]{:S(2)}) %collective-permute-start.13) | collective-permute-done | bytes 131104 | tf_op jit(solution)/shard_map/ppermute | solution.py:73
  164.7 5.4 %collective-permute-start.30 = (bf16[4,128,256]{2,1,0:T(8,128)(2,1)S(1)}, bf16[4,128,256]{2,1,0:T(8,128)(2,1)S(1)}, u32[]{:S(2)}, u32[]{:S(2)}) collective-permute-start(bf16[4,128,256]{2,1,0:T(8,128)(2,1)S(1)} %maximum_select_fusion.2), channel_id=1, source_target_pairs={{0,64},{64,0},{1,65},{65,1},{2,66},{66,2},{3,67},{67,3},{4,68},{68... | collective-permute-start | bytes 786440 | tf_op jit(solution)/shard_map/ppermute | solution.py:73
  170.1 4.9 %collective-permute-start.19 = (bf16[8,128,256]{2,1,0:T(8,128)(2,1)S(1)}, bf16[8,128,256]{2,1,0:T(8,128)(2,1)S(1)}, u32[]{:S(2)}, u32[]{:S(2)}) collective-permute-start(bf16[8,128,256]{2,1,0:T(8,128)(2,1)S(1)} %get-tuple-element.7), channel_id=1, source_target_pairs={{0,7},{1,0},{2,1},{3,2},{4,3},{5,4},{6,5},{7,6},{8,15},{9,8},{10,9... | collective-permute-start | bytes 1572872 | tf_op jit(solution)/shard_map/ppermute | solution.py:41
  175.1 8.9 %shard_map.113 = f32[1024,256]{1,0:T(8,128)} custom-call(s32[96]{0:T(128)} %fusion.27.slots_ref, bf16[1,8,1,12,128,128]{5,4,3,2,1,0:T(8,128)(2,1)} %vals_ref.5, bf16[64,128,256]{2,1,0:T(8,128)(2,1)} %constant_dynamic-update-slice_fusion.5.panels_ref), custom_call_target="tpu_custom_call" | custom-call | flops 805306368 | bytes 8388608 | tf_op jit(solution)/shard_map/pallas_call | solution.py:150
  225.4 5.0 %collective-permute-done.24 = bf16[8,128,256]{2,1,0:T(8,128)(2,1)S(1)} collective-permute-done((bf16[8,128,256]{2,1,0:T(8,128)(2,1)S(1)}, bf16[8,128,256]{2,1,0:T(8,128)(2,1)S(1)}, u32[]{:S(2)}, u32[]{:S(2)}) %collective-permute-start.24) | collective-permute-done | bytes 524320 | tf_op jit(solution)/shard_map/ppermute | solution.py:38
  231.3 8.9 %shard_map.112 = f32[1024,256]{1,0:T(8,128)} custom-call(s32[96]{0:T(128)} %fusion.27.slots_ref, bf16[1,8,1,12,128,128]{5,4,3,2,1,0:T(8,128)(2,1)} %vals_ref.5, bf16[64,128,256]{2,1,0:T(8,128)(2,1)} %constant_dynamic-update-slice_fusion.22.panels_ref), custom_call_target="tpu_custom_call" | custom-call | flops 805306368 | bytes 8388608 | tf_op jit(solution)/shard_map/pallas_call | solution.py:150
  241.5 5.1 %collective-permute-start.25 = (f32[4,128,256]{2,1,0:T(8,128)S(1)}, f32[4,128,256]{2,1,0:T(8,128)S(1)}, u32[]{:S(2)}, u32[]{:S(2)}) collective-permute-start(f32[4,128,256]{2,1,0:T(8,128)S(1)} %select_bitcast_fusion), channel_id=1, source_target_pairs={{0,64},{64,0},{1,65},{65,1},{2,66},{66,2},{3,67},{67,3},{4,68},{68... | collective-permute-start | bytes 1572872 | tf_op jit(solution)/shard_map/ppermute | solution.py:73
  249.4 8.3 %collective-permute-done.35 = f32[132,256]{1,0:T(8,128)S(1)} collective-permute-done((f32[132,256]{1,0:T(8,128)S(1)}, f32[132,256]{1,0:T(8,128)S(1)}, u32[]{:S(2)}, u32[]{:S(2)}) %collective-permute-start.35) | collective-permute-done | bytes 135200 | tf_op jit(solution)/shard_map/ppermute | solution.py:73
  260.1 5.4 %collective-permute-done.36 = f32[132,256]{1,0:T(8,128)S(1)} collective-permute-done((f32[132,256]{1,0:T(8,128)S(1)}, f32[132,256]{1,0:T(8,128)S(1)}, u32[]{:S(2)}, u32[]{:S(2)}) %collective-permute-start.36) | collective-permute-done | bytes 135200 | tf_op jit(solution)/shard_map/ppermute | solution.py:73
  267.4 8.8 %collective-permute-done.37 = f32[132,256]{1,0:T(8,128)S(1)} collective-permute-done((f32[132,256]{1,0:T(8,128)S(1)}, f32[132,256]{1,0:T(8,128)S(1)}, u32[]{:S(2)}, u32[]{:S(2)}) %collective-permute-start.37) | collective-permute-done | bytes 135200 | tf_op jit(solution)/shard_map/ppermute | solution.py:73
  283.7 6.0 %collective-permute-done.38 = f32[132,256]{1,0:T(8,128)S(1)} collective-permute-done((f32[132,256]{1,0:T(8,128)S(1)}, f32[132,256]{1,0:T(8,128)S(1)}, u32[]{:S(2)}, u32[]{:S(2)}) %collective-permute-start.38) | collective-permute-done | bytes 135200 | tf_op jit(solution)/shard_map/ppermute | solution.py:73
  293.7 9.4 %collective-permute-done.39 = f32[132,256]{1,0:T(8,128)S(1)} collective-permute-done((f32[132,256]{1,0:T(8,128)S(1)}, f32[132,256]{1,0:T(8,128)S(1)}, u32[]{:S(2)}, u32[]{:S(2)}) %collective-permute-start.39) | collective-permute-done | bytes 135200 | tf_op jit(solution)/shard_map/ppermute | solution.py:73
  309.5 5.9 %collective-permute-done.27 = f32[1,128,256]{2,1,0:T(8,128)S(1)} collective-permute-done((f32[1,128,256]{2,1,0:T(8,128)S(1)}, f32[1,128,256]{2,1,0:T(8,128)S(1)}, u32[]{:S(2)}, u32[]{:S(2)}) %collective-permute-start.27) | collective-permute-done | bytes 131104 | tf_op jit(solution)/shard_map/ppermute | solution.py:73
  (141 shorter events, 150.5 us)
Async XLA Ops:
  28.0 17.1 %collective-permute-start.4 = (bf16[8,128,256]{2,1,0:T(8,128)(2,1)S(1)}, bf16[8,128,256]{2,1,0:T(8,128)(2,1)S(1)}, u32[]{:S(2)}, u32[]{:S(2)}) collective-permute-start(bf16[8,128,256]{2,1,0:T(8,128)(2,1)S(1)} %get-tuple-element.13), channel_id=1, source_target_pairs={{0,1},{1,2},{2,3},{3,4},{4,5},{5,6},{6,7},{7,0},{8,9},{9,10},{10,1... | collective-permute-start | bytes 1572872 | tf_op jit(solution)/shard_map/ppermute | solution.py:38
  30.6 16.5 %collective-permute-start.5 = (bf16[8,128,256]{2,1,0:T(8,128)(2,1)S(1)}, bf16[8,128,256]{2,1,0:T(8,128)(2,1)S(1)}, u32[]{:S(2)}, u32[]{:S(2)}) collective-permute-start(bf16[8,128,256]{2,1,0:T(8,128)(2,1)S(1)} %get-tuple-element.13), channel_id=1, source_target_pairs={{0,7},{1,0},{2,1},{3,2},{4,3},{5,4},{6,5},{7,6},{8,15},{9,8},{10,9... | collective-permute-start | bytes 1572872 | tf_op jit(solution)/shard_map/ppermute | solution.py:41
  45.1 11.5 %collective-permute-start.6 = (bf16[8,128,256]{2,1,0:T(8,128)(2,1)S(1)}, bf16[8,128,256]{2,1,0:T(8,128)(2,1)S(1)}, u32[]{:S(2)}, u32[]{:S(2)}) collective-permute-start(bf16[8,128,256]{2,1,0:T(8,128)(2,1)S(1)} %collective-permute-done.4), channel_id=1, source_target_pairs={{0,1},{1,2},{2,3},{3,4},{4,5},{5,6},{6,7},{7,0},{8,9},{9,10},{10,1... | collective-permute-start | bytes 1572872 | tf_op jit(solution)/shard_map/ppermute | solution.py:38
  47.1 17.3 %collective-permute-start.7 = (bf16[8,128,256]{2,1,0:T(8,128)(2,1)S(1)}, bf16[8,128,256]{2,1,0:T(8,128)(2,1)S(1)}, u32[]{:S(2)}, u32[]{:S(2)}) collective-permute-start(bf16[8,128,256]{2,1,0:T(8,128)(2,1)S(1)} %collective-permute-done.5), channel_id=1, source_target_pairs={{0,7},{1,0},{2,1},{3,2},{4,3},{5,4},{6,5},{7,6},{8,15},{9,8},{10,9... | collective-permute-start | bytes 1572872 | tf_op jit(solution)/shard_map/ppermute | solution.py:41
  56.6 13.2 %collective-permute-start.8 = (bf16[8,128,256]{2,1,0:T(8,128)(2,1)S(1)}, bf16[8,128,256]{2,1,0:T(8,128)(2,1)S(1)}, u32[]{:S(2)}, u32[]{:S(2)}) collective-permute-start(bf16[8,128,256]{2,1,0:T(8,128)(2,1)S(1)} %collective-permute-done.6), channel_id=1, source_target_pairs={{0,1},{1,2},{2,3},{3,4},{4,5},{5,6},{6,7},{7,0},{8,9},{9,10},{10,1... | collective-permute-start | bytes 1572872 | tf_op jit(solution)/shard_map/ppermute | solution.py:38
  69.8 11.1 %collective-permute-start.10 = (bf16[8,128,256]{2,1,0:T(8,128)(2,1)S(1)}, bf16[8,128,256]{2,1,0:T(8,128)(2,1)S(1)}, u32[]{:S(2)}, u32[]{:S(2)}) collective-permute-start(bf16[8,128,256]{2,1,0:T(8,128)(2,1)S(1)} %collective-permute-done.8), channel_id=1, source_target_pairs={{0,1},{1,2},{2,3},{3,4},{4,5},{5,6},{6,7},{7,0},{8,9},{9,10},{10,1... | collective-permute-start | bytes 1572872 | tf_op jit(solution)/shard_map/ppermute | solution.py:38
  97.5 11.1 %collective-permute-start.11 = (f32[4,128,256]{2,1,0:T(8,128)S(1)}, f32[4,128,256]{2,1,0:T(8,128)S(1)}, u32[]{:S(2)}, u32[]{:S(2)}) collective-permute-start(f32[4,128,256]{2,1,0:T(8,128)S(1)} %select_bitcast_fusion.1), channel_id=1, source_target_pairs={{0,64},{64,0},{1,65},{65,1},{2,66},{66,2},{3,67},{67,3},{4,68},{68... | collective-permute-start | bytes 1572872 | tf_op jit(solution)/shard_map/ppermute | solution.py:73
  119.9 14.3 %collective-permute-start.13 = (f32[1,128,256]{2,1,0:T(8,128)S(1)}, f32[1,128,256]{2,1,0:T(8,128)S(1)}, u32[]{:S(2)}, u32[]{:S(2)}) collective-permute-start(f32[1,128,256]{2,1,0:T(8,128)S(1)} %select_bitcast_fusion.5), channel_id=1, source_target_pairs={{0,256},{128,384},{256,0},{384,128},{1,257},{129,385},{257,1},{385... | collective-permute-start | bytes 393224 | tf_op jit(solution)/shard_map/ppermute | solution.py:73
  143.3 11.8 %collective-permute-start.15 = (bf16[2,128,256]{2,1,0:T(8,128)(2,1)S(1)}, bf16[2,128,256]{2,1,0:T(8,128)(2,1)S(1)}, u32[]{:S(2)}, u32[]{:S(2)}) collective-permute-start(bf16[2,128,256]{2,1,0:T(8,128)(2,1)S(1)} %get-tuple-element.20), channel_id=1, source_target_pairs={{0,8},{8,16},{16,24},{24,0},{1,9},{9,17},{17,25},{25,1},{2,10},{10... | collective-permute-start | bytes 393224 | tf_op jit(solution)/shard_map/ppermute | solution.py:38
  145.2 12.4 %collective-permute-start.16 = (bf16[2,128,256]{2,1,0:T(8,128)(2,1)S(1)}, bf16[2,128,256]{2,1,0:T(8,128)(2,1)S(1)}, u32[]{:S(2)}, u32[]{:S(2)}) collective-permute-start(bf16[2,128,256]{2,1,0:T(8,128)(2,1)S(1)} %get-tuple-element.20), channel_id=1, source_target_pairs={{0,24},{8,0},{16,8},{24,16},{1,25},{9,1},{17,9},{25,17},{2,26},{10... | collective-permute-start | bytes 393224 | tf_op jit(solution)/shard_map/ppermute | solution.py:41
  149.8 14.9 %collective-permute-start.29 = (bf16[2,128,256]{2,1,0:T(8,128)(2,1)S(1)}, bf16[2,128,256]{2,1,0:T(8,128)(2,1)S(1)}, u32[]{:S(2)}, u32[]{:S(2)}) collective-permute-start(bf16[2,128,256]{2,1,0:T(8,128)(2,1)S(1)} %get-tuple-element.19), channel_id=1, source_target_pairs={{0,256},{128,384},{256,0},{384,128},{1,257},{129,385},{257,1},{385... | collective-permute-start | bytes 393224 | tf_op jit(solution)/shard_map/ppermute | solution.py:73
  162.8 21.2 %collective-permute-start.18 = (bf16[8,128,256]{2,1,0:T(8,128)(2,1)S(1)}, bf16[8,128,256]{2,1,0:T(8,128)(2,1)S(1)}, u32[]{:S(2)}, u32[]{:S(2)}) collective-permute-start(bf16[8,128,256]{2,1,0:T(8,128)(2,1)S(1)} %get-tuple-element.7), channel_id=1, source_target_pairs={{0,1},{1,2},{2,3},{3,4},{4,5},{5,6},{6,7},{7,0},{8,9},{9,10},{10,1... | collective-permute-start | bytes 1572872 | tf_op jit(solution)/shard_map/ppermute | solution.py:38
  164.7 21.2 %collective-permute-start.30 = (bf16[4,128,256]{2,1,0:T(8,128)(2,1)S(1)}, bf16[4,128,256]{2,1,0:T(8,128)(2,1)S(1)}, u32[]{:S(2)}, u32[]{:S(2)}) collective-permute-start(bf16[4,128,256]{2,1,0:T(8,128)(2,1)S(1)} %maximum_select_fusion.2), channel_id=1, source_target_pairs={{0,64},{64,0},{1,65},{65,1},{2,66},{66,2},{3,67},{67,3},{4,68},{68... | collective-permute-start | bytes 786440 | tf_op jit(solution)/shard_map/ppermute | solution.py:73
  170.1 18.2 %collective-permute-start.19 = (bf16[8,128,256]{2,1,0:T(8,128)(2,1)S(1)}, bf16[8,128,256]{2,1,0:T(8,128)(2,1)S(1)}, u32[]{:S(2)}, u32[]{:S(2)}) collective-permute-start(bf16[8,128,256]{2,1,0:T(8,128)(2,1)S(1)} %get-tuple-element.7), channel_id=1, source_target_pairs={{0,7},{1,0},{2,1},{3,2},{4,3},{5,4},{6,5},{7,6},{8,15},{9,8},{10,9... | collective-permute-start | bytes 1572872 | tf_op jit(solution)/shard_map/ppermute | solution.py:41
  184.0 16.3 %collective-permute-start.20 = (bf16[8,128,256]{2,1,0:T(8,128)(2,1)S(1)}, bf16[8,128,256]{2,1,0:T(8,128)(2,1)S(1)}, u32[]{:S(2)}, u32[]{:S(2)}) collective-permute-start(bf16[8,128,256]{2,1,0:T(8,128)(2,1)S(1)} %collective-permute-done.18), channel_id=1, source_target_pairs={{0,1},{1,2},{2,3},{3,4},{4,5},{5,6},{6,7},{7,0},{8,9},{9,10},{10,1... | collective-permute-start | bytes 1572872 | tf_op jit(solution)/shard_map/ppermute | solution.py:38
  188.3 22.5 %collective-permute-start.21 = (bf16[8,128,256]{2,1,0:T(8,128)(2,1)S(1)}, bf16[8,128,256]{2,1,0:T(8,128)(2,1)S(1)}, u32[]{:S(2)}, u32[]{:S(2)}) collective-permute-start(bf16[8,128,256]{2,1,0:T(8,128)(2,1)S(1)} %collective-permute-done.19), channel_id=1, source_target_pairs={{0,7},{1,0},{2,1},{3,2},{4,3},{5,4},{6,5},{7,6},{8,15},{9,8},{10,9... | collective-permute-start | bytes 1572872 | tf_op jit(solution)/shard_map/ppermute | solution.py:41
  200.3 15.8 %collective-permute-start.22 = (bf16[8,128,256]{2,1,0:T(8,128)(2,1)S(1)}, bf16[8,128,256]{2,1,0:T(8,128)(2,1)S(1)}, u32[]{:S(2)}, u32[]{:S(2)}) collective-permute-start(bf16[8,128,256]{2,1,0:T(8,128)(2,1)S(1)} %collective-permute-done.20), channel_id=1, source_target_pairs={{0,1},{1,2},{2,3},{3,4},{4,5},{5,6},{6,7},{7,0},{8,9},{9,10},{10,1... | collective-permute-start | bytes 1572872 | tf_op jit(solution)/shard_map/ppermute | solution.py:38
  210.9 13.6 %collective-permute-start.23 = (bf16[8,128,256]{2,1,0:T(8,128)(2,1)S(1)}, bf16[8,128,256]{2,1,0:T(8,128)(2,1)S(1)}, u32[]{:S(2)}, u32[]{:S(2)}) collective-permute-start(bf16[8,128,256]{2,1,0:T(8,128)(2,1)S(1)} %collective-permute-done.21), channel_id=1, source_target_pairs={{0,7},{1,0},{2,1},{3,2},{4,3},{5,4},{6,5},{7,6},{8,15},{9,8},{10,9... | collective-permute-start | bytes 1572872 | tf_op jit(solution)/shard_map/ppermute | solution.py:41
  216.1 14.3 %collective-permute-start.24 = (bf16[8,128,256]{2,1,0:T(8,128)(2,1)S(1)}, bf16[8,128,256]{2,1,0:T(8,128)(2,1)S(1)}, u32[]{:S(2)}, u32[]{:S(2)}) collective-permute-start(bf16[8,128,256]{2,1,0:T(8,128)(2,1)S(1)} %collective-permute-done.22), channel_id=1, source_target_pairs={{0,1},{1,2},{2,3},{3,4},{4,5},{5,6},{6,7},{7,0},{8,9},{9,10},{10,1... | collective-permute-start | bytes 1572872 | tf_op jit(solution)/shard_map/ppermute | solution.py:38
  218.9 27.7 %collective-permute-start.34 = (f32[132,256]{1,0:T(8,128)S(1)}, f32[132,256]{1,0:T(8,128)S(1)}, u32[]{:S(2)}, u32[]{:S(2)}) collective-permute-start(f32[132,256]{1,0:T(8,128)S(1)} %add.187), channel_id=1, source_target_pairs={{0,1},{1,0},{2,3},{3,2},{4,5},{5,4},{6,7},{7,6},{8,9},{9,8},{10,11... | collective-permute-start | bytes 405512 | tf_op jit(solution)/shard_map/ppermute | solution.py:73
  241.5 38.9 %collective-permute-start.25 = (f32[4,128,256]{2,1,0:T(8,128)S(1)}, f32[4,128,256]{2,1,0:T(8,128)S(1)}, u32[]{:S(2)}, u32[]{:S(2)}) collective-permute-start(f32[4,128,256]{2,1,0:T(8,128)S(1)} %select_bitcast_fusion), channel_id=1, source_target_pairs={{0,64},{64,0},{1,65},{65,1},{2,66},{66,2},{3,67},{67,3},{4,68},{68... | collective-permute-start | bytes 1572872 | tf_op jit(solution)/shard_map/ppermute | solution.py:73
  276.3 13.5 %collective-permute-start.38 = (f32[132,256]{1,0:T(8,128)S(1)}, f32[132,256]{1,0:T(8,128)S(1)}, u32[]{:S(2)}, u32[]{:S(2)}) collective-permute-start(f32[132,256]{1,0:T(8,128)S(1)} %add.191), channel_id=1, source_target_pairs={{0,4},{1,5},{2,6},{3,7},{4,0},{5,1},{6,2},{7,3},{8,12},{9,13},{10,... | collective-permute-start | bytes 405512 | tf_op jit(solution)/shard_map/ppermute | solution.py:73
  281.8 23.7 %collective-permute-start.26 = (f32[2,128,256]{2,1,0:T(8,128)S(1)}, f32[2,128,256]{2,1,0:T(8,128)S(1)}, u32[]{:S(2)}, u32[]{:S(2)}) collective-permute-start(f32[2,128,256]{2,1,0:T(8,128)S(1)} %select_bitcast_fusion.2), channel_id=1, source_target_pairs={{0,128},{128,0},{256,384},{384,256},{1,129},{129,1},{257,385},{385... | collective-permute-start | bytes 786440 | tf_op jit(solution)/shard_map/ppermute | solution.py:73
  289.8 13.3 %collective-permute-start.39 = (f32[132,256]{1,0:T(8,128)S(1)}, f32[132,256]{1,0:T(8,128)S(1)}, u32[]{:S(2)}, u32[]{:S(2)}) collective-permute-start(f32[132,256]{1,0:T(8,128)S(1)} %add.192), channel_id=1, source_target_pairs={{0,32},{32,0},{1,33},{33,1},{2,34},{34,2},{3,35},{35,3},{4,36},{36... | collective-permute-start | bytes 405512 | tf_op jit(solution)/shard_map/ppermute | solution.py:73
  (22 other events, 424.6 us)

commit v7 on v6

--- a/solution.py
+++ b/solution.py
@@ -167,9 +167,13 @@
     slots = member_slots(adj_cols[0, :, 0, :])
     width = features.shape[1]
     gathered = gather_team(features)
-    products = jnp.dot(gathered, weight, preferred_element_type=jnp.float32).astype(jnp.bfloat16)
-    partial_rows = collect(products, slots, adj_vals)
     partial_ax = collect(gathered, slots, adj_vals)
+    partial_rows = jnp.dot(
+        partial_ax,
+        weight.astype(jnp.float32),
+        precision=lax.Precision.HIGHEST,
+        preferred_element_type=jnp.float32,
+    )
     summed = blk_reduce_scatter(partial_rows)
     pre = summed + bias[None, :]
     activated, pullback = jax.vjp(activation, pre)

time: 318 us -> 315 us (level)
  waiting for transfers between devices: 98.8 us -> 110 us
  Pallas kernels: 26.8 us -> 17.9 us
  matrix products: 8.52 us -> 3.71 us
    pallas_call x3 -> x2, Pallas kernels: 26.8 us -> 17.9 us  [collect(): pl.pallas_call(collect_kernel, grid_spec=grid_spec, out_shape=jax.ShapeDt...]
    ppermute x8, waiting for transfers between devices: 1.2 us -> 10 us  [ring_gather(): behind = lax.ppermute(behind, axis, [(i, (i - 1) % n) for i in range(n)])]
    ppermute x19, waiting for transfers between devices: 61.3 us -> 67.8 us  [swap(): return lax.ppermute(value, axis, [(i, i ^ bit) for i in range(n)])]
    ppermute x12, waiting for transfers between devices: 34.4 us -> 30.7 us  [ring_gather(): ahead = lax.ppermute(ahead, axis, [(i, (i + 1) % n) for i in range(n)])]
    dot_general x1, matrix products: 5.45 us -> 1.86 us  [local(): jnp.dot(partial_ax, weight.astype(jnp.float32), precision=lax.Precision.H...]
    unnamed x31 -> x33, local copies, waits for them, and re-layouts: 16.7 us -> 16.6 us
  transfers between devices with their start and end apart: 41 -> 41, of which waited for: 20 -> 22; matrix products, arithmetic and copies ran while one was open for 10% -> 9% of each run, Pallas kernels for 6% -> 3%
where the time goes in v7:
time: 315 us; the launch traced here: 313 us
  starting transfers between devices  149 us (47%)
  waiting for transfers between devices  110 us (35%)
  local copies, waits for them, and re-layouts  23.7 us (8%)
  Pallas kernels  17.9 us (6%)
  other arithmetic  7.78 us (2%)
  matrix products  3.71 us (1%)
    ppermute x19, starting transfers between devices, swap(): return lax.ppermute(value, axis, [(i, i ^ bit) for i in range(n)])  71.7 us
    ppermute x19, waiting for transfers between devices, swap(): return lax.ppermute(value, axis, [(i, i ^ bit) for i in range(n)])  67.8 us
    ppermute x8, starting transfers between devices, ring_gather(): behind = lax.ppermute(behind, axis, [(i, (i - 1) % n) for i in range(n)])  40.1 us
    ppermute x12, waiting for transfers between devices, ring_gather(): ahead = lax.ppermute(ahead, axis, [(i, (i + 1) % n) for i in range(n)])  30.7 us
    ppermute x12, starting transfers between devices, ring_gather(): ahead = lax.ppermute(ahead, axis, [(i, (i + 1) % n) for i in range(n)])  24.8 us
    pallas_call x2, Pallas kernels, collect(): pl.pallas_call(collect_kernel, grid_spec=grid_spec, out_shape=jax.ShapeDt...  17.9 us
    unnamed x33, local copies, waits for them, and re-layouts  16.6 us
    ppermute x2, starting transfers between devices, gather_team(): other = lax.ppermute(rows, 'y_hi', perm=[(0, 1), (1, 0)])  12.1 us
  transfers between devices with their start and end apart: 41, of which 22 were waited for; matrix products, arithmetic and copies ran while one was open for 9% of the time, Pallas kernels for 3%

profile of v7, /device:TPU:1, one launch (start us, length us, event | category | flops | bytes accessed | tf_op | source)
XLA Modules:
  0.0 313.4 jit_solution(12270361698647160455)
XLA Ops:
  0.7 8.4 %collective-permute-start = (bf16[128,256]{1,0:T(8,128)(2,1)}, bf16[128,256]{1,0:T(8,128)(2,1)S(1)}, u32[]{:S(2)}, u32[]{:S(2)}) collective-permute-start(bf16[128,256]{1,0:T(8,128)(2,1)} %param.8), channel_id=1, source_target_pairs={{0,32},{32,0},{1,33},{33,1},{2,34},{34,2},{3,35},{35,3},{4,36},{36... | collective-permute-start | bytes 196616 | tf_op jit(solution)/shard_map/ppermute | solution.py:47
  22.3 5.1 %collective-permute-done.3 = bf16[2,128,256]{2,1,0:T(8,128)(2,1)S(1)} collective-permute-done((bf16[2,128,256]{2,1,0:T(8,128)(2,1)S(1)}, bf16[2,128,256]{2,1,0:T(8,128)(2,1)S(1)}, u32[]{:S(2)}, u32[]{:S(2)}) %collective-permute-start.3) | collective-permute-done | bytes 131104 | tf_op jit(solution)/shard_map/ppermute | solution.py:38
  30.6 8.6 %collective-permute-start.5 = (bf16[8,128,256]{2,1,0:T(8,128)(2,1)S(1)}, bf16[8,128,256]{2,1,0:T(8,128)(2,1)S(1)}, u32[]{:S(2)}, u32[]{:S(2)}) collective-permute-start(bf16[8,128,256]{2,1,0:T(8,128)(2,1)S(1)} %get-tuple-element.13), channel_id=1, source_target_pairs={{0,7},{1,0},{2,1},{3,2},{4,3},{5,4},{6,5},{7,6},{8,15},{9,8},{10,9... | collective-permute-start | bytes 1572872 | tf_op jit(solution)/shard_map/ppermute | solution.py:41
  39.2 5.9 %collective-permute-done.4 = bf16[8,128,256]{2,1,0:T(8,128)(2,1)S(1)} collective-permute-done((bf16[8,128,256]{2,1,0:T(8,128)(2,1)S(1)}, bf16[8,128,256]{2,1,0:T(8,128)(2,1)S(1)}, u32[]{:S(2)}, u32[]{:S(2)}) %collective-permute-start.4) | collective-permute-done | bytes 524320 | tf_op jit(solution)/shard_map/ppermute | solution.py:38
  51.6 5.0 %collective-permute-done.6 = bf16[8,128,256]{2,1,0:T(8,128)(2,1)S(1)} collective-permute-done((bf16[8,128,256]{2,1,0:T(8,128)(2,1)S(1)}, bf16[8,128,256]{2,1,0:T(8,128)(2,1)S(1)}, u32[]{:S(2)}, u32[]{:S(2)}) %collective-permute-start.6) | collective-permute-done | bytes 524320 | tf_op jit(solution)/shard_map/ppermute | solution.py:38
  75.9 5.0 %collective-permute-done.10 = bf16[8,128,256]{2,1,0:T(8,128)(2,1)S(1)} collective-permute-done((bf16[8,128,256]{2,1,0:T(8,128)(2,1)S(1)}, bf16[8,128,256]{2,1,0:T(8,128)(2,1)S(1)}, u32[]{:S(2)}, u32[]{:S(2)}) %collective-permute-start.10) | collective-permute-done | bytes 524320 | tf_op jit(solution)/shard_map/ppermute | solution.py:38
  81.8 8.9 %shard_map.111 = f32[1024,256]{1,0:T(8,128)} custom-call(s32[96]{0:T(128)} %fusion.27.slots_ref, bf16[1,8,1,12,128,128]{5,4,3,2,1,0:T(8,128)(2,1)} %vals_ref.3, bf16[64,128,256]{2,1,0:T(8,128)(2,1)} %constant_dynamic-update-slice_fusion.5.panels_ref), custom_call_target="tpu_custom_call" | custom-call | flops 805306368 | bytes 8388608 | tf_op jit(solution)/shard_map/pallas_call | solution.py:150
  92.7 9.5 %collective-permute-start.11 = (f32[4,128,256]{2,1,0:T(8,128)S(1)}, f32[4,128,256]{2,1,0:T(8,128)S(1)}, u32[]{:S(2)}, u32[]{:S(2)}) collective-permute-start(f32[4,128,256]{2,1,0:T(8,128)S(1)} %select_bitcast_fusion.1), channel_id=1, source_target_pairs={{0,64},{64,0},{1,65},{65,1},{2,66},{66,2},{3,67},{67,3},{4,68},{68... | collective-permute-start | bytes 1572872 | tf_op jit(solution)/shard_map/ppermute | solution.py:73
  107.7 6.3 %collective-permute-done.12 = f32[2,128,256]{2,1,0:T(8,128)S(1)} collective-permute-done((f32[2,128,256]{2,1,0:T(8,128)S(1)}, f32[2,128,256]{2,1,0:T(8,128)S(1)}, u32[]{:S(2)}, u32[]{:S(2)}) %collective-permute-start.12) | collective-permute-done | bytes 262176 | tf_op jit(solution)/shard_map/ppermute | solution.py:73
  114.1 7.6 %collective-permute-start.13 = (f32[1,128,256]{2,1,0:T(8,128)S(1)}, f32[1,128,256]{2,1,0:T(8,128)S(1)}, u32[]{:S(2)}, u32[]{:S(2)}) collective-permute-start(f32[1,128,256]{2,1,0:T(8,128)S(1)} %select_bitcast_fusion.5), channel_id=1, source_target_pairs={{0,256},{128,384},{256,0},{384,128},{1,257},{129,385},{257,1},{385... | collective-permute-start | bytes 393224 | tf_op jit(solution)/shard_map/ppermute | solution.py:73
  121.6 6.7 %collective-permute-done.13 = f32[1,128,256]{2,1,0:T(8,128)S(1)} collective-permute-done((f32[1,128,256]{2,1,0:T(8,128)S(1)}, f32[1,128,256]{2,1,0:T(8,128)S(1)}, u32[]{:S(2)}, u32[]{:S(2)}) %collective-permute-start.13) | collective-permute-done | bytes 131104 | tf_op jit(solution)/shard_map/ppermute | solution.py:73
  161.0 9.3 %collective-permute-start.30 = (bf16[4,128,256]{2,1,0:T(8,128)(2,1)S(1)}, bf16[4,128,256]{2,1,0:T(8,128)(2,1)S(1)}, u32[]{:S(2)}, u32[]{:S(2)}) collective-permute-start(bf16[4,128,256]{2,1,0:T(8,128)(2,1)S(1)} %maximum_select_fusion.2), channel_id=1, source_target_pairs={{0,64},{64,0},{1,65},{65,1},{2,66},{66,2},{3,67},{67,3},{4,68},{68... | collective-permute-start | bytes 786440 | tf_op jit(solution)/shard_map/ppermute | solution.py:73
  170.3 4.9 %collective-permute-start.19 = (bf16[8,128,256]{2,1,0:T(8,128)(2,1)S(1)}, bf16[8,128,256]{2,1,0:T(8,128)(2,1)S(1)}, u32[]{:S(2)}, u32[]{:S(2)}) collective-permute-start(bf16[8,128,256]{2,1,0:T(8,128)(2,1)S(1)} %get-tuple-element.7), channel_id=1, source_target_pairs={{0,7},{1,0},{2,1},{3,2},{4,3},{5,4},{6,5},{7,6},{8,15},{9,8},{10,9... | collective-permute-start | bytes 1572872 | tf_op jit(solution)/shard_map/ppermute | solution.py:41
  178.4 8.1 %collective-permute-done.19 = bf16[8,128,256]{2,1,0:T(8,128)(2,1)S(1)} collective-permute-done((bf16[8,128,256]{2,1,0:T(8,128)(2,1)S(1)}, bf16[8,128,256]{2,1,0:T(8,128)(2,1)S(1)}, u32[]{:S(2)}, u32[]{:S(2)}) %collective-permute-start.19) | collective-permute-done | bytes 524320 | tf_op jit(solution)/shard_map/ppermute | solution.py:41
  186.5 5.3 %collective-permute-start.21 = (bf16[8,128,256]{2,1,0:T(8,128)(2,1)S(1)}, bf16[8,128,256]{2,1,0:T(8,128)(2,1)S(1)}, u32[]{:S(2)}, u32[]{:S(2)}) collective-permute-start(bf16[8,128,256]{2,1,0:T(8,128)(2,1)S(1)} %collective-permute-done.19), channel_id=1, source_target_pairs={{0,7},{1,0},{2,1},{3,2},{4,3},{5,4},{6,5},{7,6},{8,15},{9,8},{10,9... | collective-permute-start | bytes 1572872 | tf_op jit(solution)/shard_map/ppermute | solution.py:41
  198.9 5.3 %collective-permute-done.32 = f32[132,256]{1,0:T(8,128)S(1)} collective-permute-done((f32[132,256]{1,0:T(8,128)S(1)}, f32[132,256]{1,0:T(8,128)S(1)}, u32[]{:S(2)}, u32[]{:S(2)}) %collective-permute-start.32) | collective-permute-done | bytes 135200 | tf_op jit(solution)/shard_map/ppermute | solution.py:73
  221.5 5.6 %collective-permute-done.24 = bf16[8,128,256]{2,1,0:T(8,128)(2,1)S(1)} collective-permute-done((bf16[8,128,256]{2,1,0:T(8,128)(2,1)S(1)}, bf16[8,128,256]{2,1,0:T(8,128)(2,1)S(1)}, u32[]{:S(2)}, u32[]{:S(2)}) %collective-permute-start.24) | collective-permute-done | bytes 524320 | tf_op jit(solution)/shard_map/ppermute | solution.py:38
  227.9 8.9 %shard_map.112 = f32[1024,256]{1,0:T(8,128)} custom-call(s32[96]{0:T(128)} %fusion.27.slots_ref, bf16[1,8,1,12,128,128]{5,4,3,2,1,0:T(8,128)(2,1)} %vals_ref.3, bf16[64,128,256]{2,1,0:T(8,128)(2,1)} %constant_dynamic-update-slice_fusion.22.panels_ref), custom_call_target="tpu_custom_call" | custom-call | flops 805306368 | bytes 8388608 | tf_op jit(solution)/shard_map/pallas_call | solution.py:150
  244.8 8.4 %collective-permute-done.35 = f32[132,256]{1,0:T(8,128)S(1)} collective-permute-done((f32[132,256]{1,0:T(8,128)S(1)}, f32[132,256]{1,0:T(8,128)S(1)}, u32[]{:S(2)}, u32[]{:S(2)}) %collective-permute-start.35) | collective-permute-done | bytes 135200 | tf_op jit(solution)/shard_map/ppermute | solution.py:73
  255.4 6.0 %collective-permute-done.36 = f32[132,256]{1,0:T(8,128)S(1)} collective-permute-done((f32[132,256]{1,0:T(8,128)S(1)}, f32[132,256]{1,0:T(8,128)S(1)}, u32[]{:S(2)}, u32[]{:S(2)}) %collective-permute-start.36) | collective-permute-done | bytes 135200 | tf_op jit(solution)/shard_map/ppermute | solution.py:73
  263.3 9.0 %collective-permute-done.37 = f32[132,256]{1,0:T(8,128)S(1)} collective-permute-done((f32[132,256]{1,0:T(8,128)S(1)}, f32[132,256]{1,0:T(8,128)S(1)}, u32[]{:S(2)}, u32[]{:S(2)}) %collective-permute-start.37) | collective-permute-done | bytes 135200 | tf_op jit(solution)/shard_map/ppermute | solution.py:73
  279.8 6.0 %collective-permute-done.38 = f32[132,256]{1,0:T(8,128)S(1)} collective-permute-done((f32[132,256]{1,0:T(8,128)S(1)}, f32[132,256]{1,0:T(8,128)S(1)}, u32[]{:S(2)}, u32[]{:S(2)}) %collective-permute-start.38) | collective-permute-done | bytes 135200 | tf_op jit(solution)/shard_map/ppermute | solution.py:73
  290.0 9.3 %collective-permute-done.39 = f32[132,256]{1,0:T(8,128)S(1)} collective-permute-done((f32[132,256]{1,0:T(8,128)S(1)}, f32[132,256]{1,0:T(8,128)S(1)}, u32[]{:S(2)}, u32[]{:S(2)}) %collective-permute-start.39) | collective-permute-done | bytes 135200 | tf_op jit(solution)/shard_map/ppermute | solution.py:73
  305.7 6.9 %collective-permute-done.27 = f32[1,128,256]{2,1,0:T(8,128)S(1)} collective-permute-done((f32[1,128,256]{2,1,0:T(8,128)S(1)}, f32[1,128,256]{2,1,0:T(8,128)S(1)}, u32[]{:S(2)}, u32[]{:S(2)}) %collective-permute-start.27) | collective-permute-done | bytes 131104 | tf_op jit(solution)/shard_map/ppermute | solution.py:73
  (142 shorter events, 142.1 us)
Async XLA Ops:
  28.0 17.1 %collective-permute-start.4 = (bf16[8,128,256]{2,1,0:T(8,128)(2,1)S(1)}, bf16[8,128,256]{2,1,0:T(8,128)(2,1)S(1)}, u32[]{:S(2)}, u32[]{:S(2)}) collective-permute-start(bf16[8,128,256]{2,1,0:T(8,128)(2,1)S(1)} %get-tuple-element.13), channel_id=1, source_target_pairs={{0,1},{1,2},{2,3},{3,4},{4,5},{5,6},{6,7},{7,0},{8,9},{9,10},{10,1... | collective-permute-start | bytes 1572872 | tf_op jit(solution)/shard_map/ppermute | solution.py:38
  30.6 16.5 %collective-permute-start.5 = (bf16[8,128,256]{2,1,0:T(8,128)(2,1)S(1)}, bf16[8,128,256]{2,1,0:T(8,128)(2,1)S(1)}, u32[]{:S(2)}, u32[]{:S(2)}) collective-permute-start(bf16[8,128,256]{2,1,0:T(8,128)(2,1)S(1)} %get-tuple-element.13), channel_id=1, source_target_pairs={{0,7},{1,0},{2,1},{3,2},{4,3},{5,4},{6,5},{7,6},{8,15},{9,8},{10,9... | collective-permute-start | bytes 1572872 | tf_op jit(solution)/shard_map/ppermute | solution.py:41
  45.1 11.5 %collective-permute-start.6 = (bf16[8,128,256]{2,1,0:T(8,128)(2,1)S(1)}, bf16[8,128,256]{2,1,0:T(8,128)(2,1)S(1)}, u32[]{:S(2)}, u32[]{:S(2)}) collective-permute-start(bf16[8,128,256]{2,1,0:T(8,128)(2,1)S(1)} %collective-permute-done.4), channel_id=1, source_target_pairs={{0,1},{1,2},{2,3},{3,4},{4,5},{5,6},{6,7},{7,0},{8,9},{9,10},{10,1... | collective-permute-start | bytes 1572872 | tf_op jit(solution)/shard_map/ppermute | solution.py:38
  47.1 17.3 %collective-permute-start.7 = (bf16[8,128,256]{2,1,0:T(8,128)(2,1)S(1)}, bf16[8,128,256]{2,1,0:T(8,128)(2,1)S(1)}, u32[]{:S(2)}, u32[]{:S(2)}) collective-permute-start(bf16[8,128,256]{2,1,0:T(8,128)(2,1)S(1)} %collective-permute-done.5), channel_id=1, source_target_pairs={{0,7},{1,0},{2,1},{3,2},{4,3},{5,4},{6,5},{7,6},{8,15},{9,8},{10,9... | collective-permute-start | bytes 1572872 | tf_op jit(solution)/shard_map/ppermute | solution.py:41
  56.6 13.2 %collective-permute-start.8 = (bf16[8,128,256]{2,1,0:T(8,128)(2,1)S(1)}, bf16[8,128,256]{2,1,0:T(8,128)(2,1)S(1)}, u32[]{:S(2)}, u32[]{:S(2)}) collective-permute-start(bf16[8,128,256]{2,1,0:T(8,128)(2,1)S(1)} %collective-permute-done.6), channel_id=1, source_target_pairs={{0,1},{1,2},{2,3},{3,4},{4,5},{5,6},{6,7},{7,0},{8,9},{9,10},{10,1... | collective-permute-start | bytes 1572872 | tf_op jit(solution)/shard_map/ppermute | solution.py:38
  69.8 11.1 %collective-permute-start.10 = (bf16[8,128,256]{2,1,0:T(8,128)(2,1)S(1)}, bf16[8,128,256]{2,1,0:T(8,128)(2,1)S(1)}, u32[]{:S(2)}, u32[]{:S(2)}) collective-permute-start(bf16[8,128,256]{2,1,0:T(8,128)(2,1)S(1)} %collective-permute-done.8), channel_id=1, source_target_pairs={{0,1},{1,2},{2,3},{3,4},{4,5},{5,6},{6,7},{7,0},{8,9},{9,10},{10,1... | collective-permute-start | bytes 1572872 | tf_op jit(solution)/shard_map/ppermute | solution.py:38
  92.7 11.1 %collective-permute-start.11 = (f32[4,128,256]{2,1,0:T(8,128)S(1)}, f32[4,128,256]{2,1,0:T(8,128)S(1)}, u32[]{:S(2)}, u32[]{:S(2)}) collective-permute-start(f32[4,128,256]{2,1,0:T(8,128)S(1)} %select_bitcast_fusion.1), channel_id=1, source_target_pairs={{0,64},{64,0},{1,65},{65,1},{2,66},{66,2},{3,67},{67,3},{4,68},{68... | collective-permute-start | bytes 1572872 | tf_op jit(solution)/shard_map/ppermute | solution.py:73
  114.1 14.3 %collective-permute-start.13 = (f32[1,128,256]{2,1,0:T(8,128)S(1)}, f32[1,128,256]{2,1,0:T(8,128)S(1)}, u32[]{:S(2)}, u32[]{:S(2)}) collective-permute-start(f32[1,128,256]{2,1,0:T(8,128)S(1)} %select_bitcast_fusion.5), channel_id=1, source_target_pairs={{0,256},{128,384},{256,0},{384,128},{1,257},{129,385},{257,1},{385... | collective-permute-start | bytes 393224 | tf_op jit(solution)/shard_map/ppermute | solution.py:73
  152.1 23.2 %collective-permute-start.18 = (bf16[8,128,256]{2,1,0:T(8,128)(2,1)S(1)}, bf16[8,128,256]{2,1,0:T(8,128)(2,1)S(1)}, u32[]{:S(2)}, u32[]{:S(2)}) collective-permute-start(bf16[8,128,256]{2,1,0:T(8,128)(2,1)S(1)} %get-tuple-element.7), channel_id=1, source_target_pairs={{0,1},{1,2},{2,3},{3,4},{4,5},{5,6},{6,7},{7,0},{8,9},{9,10},{10,1... | collective-permute-start | bytes 1572872 | tf_op jit(solution)/shard_map/ppermute | solution.py:38
  161.0 16.2 %collective-permute-start.30 = (bf16[4,128,256]{2,1,0:T(8,128)(2,1)S(1)}, bf16[4,128,256]{2,1,0:T(8,128)(2,1)S(1)}, u32[]{:S(2)}, u32[]{:S(2)}) collective-permute-start(bf16[4,128,256]{2,1,0:T(8,128)(2,1)S(1)} %maximum_select_fusion.2), channel_id=1, source_target_pairs={{0,64},{64,0},{1,65},{65,1},{2,66},{66,2},{3,67},{67,3},{4,68},{68... | collective-permute-start | bytes 786440 | tf_op jit(solution)/shard_map/ppermute | solution.py:73
  170.3 16.2 %collective-permute-start.19 = (bf16[8,128,256]{2,1,0:T(8,128)(2,1)S(1)}, bf16[8,128,256]{2,1,0:T(8,128)(2,1)S(1)}, u32[]{:S(2)}, u32[]{:S(2)}) collective-permute-start(bf16[8,128,256]{2,1,0:T(8,128)(2,1)S(1)} %get-tuple-element.7), channel_id=1, source_target_pairs={{0,7},{1,0},{2,1},{3,2},{4,3},{5,4},{6,5},{7,6},{8,15},{9,8},{10,9... | collective-permute-start | bytes 1572872 | tf_op jit(solution)/shard_map/ppermute | solution.py:41
  175.3 19.6 %collective-permute-start.20 = (bf16[8,128,256]{2,1,0:T(8,128)(2,1)S(1)}, bf16[8,128,256]{2,1,0:T(8,128)(2,1)S(1)}, u32[]{:S(2)}, u32[]{:S(2)}) collective-permute-start(bf16[8,128,256]{2,1,0:T(8,128)(2,1)S(1)} %collective-permute-done.18), channel_id=1, source_target_pairs={{0,1},{1,2},{2,3},{3,4},{4,5},{5,6},{6,7},{7,0},{8,9},{9,10},{10,1... | collective-permute-start | bytes 1572872 | tf_op jit(solution)/shard_map/ppermute | solution.py:38
  186.5 19.6 %collective-permute-start.21 = (bf16[8,128,256]{2,1,0:T(8,128)(2,1)S(1)}, bf16[8,128,256]{2,1,0:T(8,128)(2,1)S(1)}, u32[]{:S(2)}, u32[]{:S(2)}) collective-permute-start(bf16[8,128,256]{2,1,0:T(8,128)(2,1)S(1)} %collective-permute-done.19), channel_id=1, source_target_pairs={{0,7},{1,0},{2,1},{3,2},{4,3},{5,4},{6,5},{7,6},{8,15},{9,8},{10,9... | collective-permute-start | bytes 1572872 | tf_op jit(solution)/shard_map/ppermute | solution.py:41
  194.9 16.6 %collective-permute-start.22 = (bf16[8,128,256]{2,1,0:T(8,128)(2,1)S(1)}, bf16[8,128,256]{2,1,0:T(8,128)(2,1)S(1)}, u32[]{:S(2)}, u32[]{:S(2)}) collective-permute-start(bf16[8,128,256]{2,1,0:T(8,128)(2,1)S(1)} %collective-permute-done.20), channel_id=1, source_target_pairs={{0,1},{1,2},{2,3},{3,4},{4,5},{5,6},{6,7},{7,0},{8,9},{9,10},{10,1... | collective-permute-start | bytes 1572872 | tf_op jit(solution)/shard_map/ppermute | solution.py:38
  206.1 14.5 %collective-permute-start.23 = (bf16[8,128,256]{2,1,0:T(8,128)(2,1)S(1)}, bf16[8,128,256]{2,1,0:T(8,128)(2,1)S(1)}, u32[]{:S(2)}, u32[]{:S(2)}) collective-permute-start(bf16[8,128,256]{2,1,0:T(8,128)(2,1)S(1)} %collective-permute-done.21), channel_id=1, source_target_pairs={{0,7},{1,0},{2,1},{3,2},{4,3},{5,4},{6,5},{7,6},{8,15},{9,8},{10,9... | collective-permute-start | bytes 1572872 | tf_op jit(solution)/shard_map/ppermute | solution.py:41
  211.6 15.5 %collective-permute-start.24 = (bf16[8,128,256]{2,1,0:T(8,128)(2,1)S(1)}, bf16[8,128,256]{2,1,0:T(8,128)(2,1)S(1)}, u32[]{:S(2)}, u32[]{:S(2)}) collective-permute-start(bf16[8,128,256]{2,1,0:T(8,128)(2,1)S(1)} %collective-permute-done.22), channel_id=1, source_target_pairs={{0,1},{1,2},{2,3},{3,4},{4,5},{5,6},{6,7},{7,0},{8,9},{9,10},{10,1... | collective-permute-start | bytes 1572872 | tf_op jit(solution)/shard_map/ppermute | solution.py:38
  214.4 27.6 %collective-permute-start.34 = (f32[132,256]{1,0:T(8,128)S(1)}, f32[132,256]{1,0:T(8,128)S(1)}, u32[]{:S(2)}, u32[]{:S(2)}) collective-permute-start(f32[132,256]{1,0:T(8,128)S(1)} %add.187), channel_id=1, source_target_pairs={{0,1},{1,0},{2,3},{3,2},{4,5},{5,4},{6,7},{7,6},{8,9},{9,8},{10,11... | collective-permute-start | bytes 405512 | tf_op jit(solution)/shard_map/ppermute | solution.py:73
  238.1 38.4 %collective-permute-start.25 = (f32[4,128,256]{2,1,0:T(8,128)S(1)}, f32[4,128,256]{2,1,0:T(8,128)S(1)}, u32[]{:S(2)}, u32[]{:S(2)}) collective-permute-start(f32[4,128,256]{2,1,0:T(8,128)S(1)} %select_bitcast_fusion), channel_id=1, source_target_pairs={{0,64},{64,0},{1,65},{65,1},{2,66},{66,2},{3,67},{67,3},{4,68},{68... | collective-permute-start | bytes 1572872 | tf_op jit(solution)/shard_map/ppermute | solution.py:73
  242.0 11.2 %collective-permute-start.35 = (f32[132,256]{1,0:T(8,128)S(1)}, f32[132,256]{1,0:T(8,128)S(1)}, u32[]{:S(2)}, u32[]{:S(2)}) collective-permute-start(f32[132,256]{1,0:T(8,128)S(1)} %add.188), channel_id=1, source_target_pairs={{0,256},{128,384},{256,0},{384,128},{1,257},{129,385},{257,1},{385... | collective-permute-start | bytes 405512 | tf_op jit(solution)/shard_map/ppermute | solution.py:73
  261.4 11.0 %collective-permute-start.37 = (f32[132,256]{1,0:T(8,128)S(1)}, f32[132,256]{1,0:T(8,128)S(1)}, u32[]{:S(2)}, u32[]{:S(2)}) collective-permute-start(f32[132,256]{1,0:T(8,128)S(1)} %add.190), channel_id=1, source_target_pairs={{0,2},{1,3},{2,0},{3,1},{4,6},{5,7},{6,4},{7,5},{8,10},{9,11},{10,... | collective-permute-start | bytes 405512 | tf_op jit(solution)/shard_map/ppermute | solution.py:73
  272.4 13.5 %collective-permute-start.38 = (f32[132,256]{1,0:T(8,128)S(1)}, f32[132,256]{1,0:T(8,128)S(1)}, u32[]{:S(2)}, u32[]{:S(2)}) collective-permute-start(f32[132,256]{1,0:T(8,128)S(1)} %add.191), channel_id=1, source_target_pairs={{0,4},{1,5},{2,6},{3,7},{4,0},{5,1},{6,2},{7,3},{8,12},{9,13},{10,... | collective-permute-start | bytes 405512 | tf_op jit(solution)/shard_map/ppermute | solution.py:73
  277.9 23.8 %collective-permute-start.26 = (f32[2,128,256]{2,1,0:T(8,128)S(1)}, f32[2,128,256]{2,1,0:T(8,128)S(1)}, u32[]{:S(2)}, u32[]{:S(2)}) collective-permute-start(f32[2,128,256]{2,1,0:T(8,128)S(1)} %select_bitcast_fusion.2), channel_id=1, source_target_pairs={{0,128},{128,0},{256,384},{384,256},{1,129},{129,1},{257,385},{385... | collective-permute-start | bytes 786440 | tf_op jit(solution)/shard_map/ppermute | solution.py:73
  285.9 13.4 %collective-permute-start.39 = (f32[132,256]{1,0:T(8,128)S(1)}, f32[132,256]{1,0:T(8,128)S(1)}, u32[]{:S(2)}, u32[]{:S(2)}) collective-permute-start(f32[132,256]{1,0:T(8,128)S(1)} %add.192), channel_id=1, source_target_pairs={{0,32},{32,0},{1,33},{33,1},{2,34},{34,2},{3,35},{35,3},{4,36},{36... | collective-permute-start | bytes 405512 | tf_op jit(solution)/shard_map/ppermute | solution.py:73
  301.8 10.8 %collective-permute-start.27 = (f32[1,128,256]{2,1,0:T(8,128)S(1)}, f32[1,128,256]{2,1,0:T(8,128)S(1)}, u32[]{:S(2)}, u32[]{:S(2)}) collective-permute-start(f32[1,128,256]{2,1,0:T(8,128)S(1)} %select_bitcast_fusion.4), channel_id=1, source_target_pairs={{0,256},{128,384},{256,0},{384,128},{1,257},{129,385},{257,1},{385... | collective-permute-start | bytes 393224 | tf_op jit(solution)/shard_map/ppermute | solution.py:73
  (23 other events, 493.5 us)

commit v8 on v7

--- a/solution.py
+++ b/solution.py
@@ -29,24 +29,46 @@
     return offsets
 
 
-def ring_gather(blocks, axis):
+class Chain:
+    def __init__(self, value, steps):
+        self.value = value
+        self.steps = list(steps)
+
+    def tick(self, values):
+        if self.steps:
+            self.value = self.steps.pop(0)(self.value)
+        values, self.value = lax.optimization_barrier((values, self.value))
+        return values
+
+    def finish(self):
+        while self.steps:
+            self.value = self.steps.pop(0)(self.value)
+        return self.value
+
+
+def ring_gather(blocks, axis, chain=None):
     n = SIZES[axis]
     ahead = blocks
     behind = blocks
     parts = [blocks]
     for step in range(1, n // 2 + 1):
         ahead = lax.ppermute(ahead, axis, [(i, (i + 1) % n) for i in range(n)])
+        if step < n - step:
+            behind = lax.ppermute(behind, axis, [(i, (i - 1) % n) for i in range(n)])
+        if chain is not None:
+            ahead, behind = chain.tick((ahead, behind))
         parts.append(ahead)
         if step < n - step:
-            behind = lax.ppermute(behind, axis, [(i, (i - 1) % n) for i in range(n)])
             parts.append(behind)
     return jnp.concatenate(parts, axis=0)
 
 
-def gather_team(rows):
+def gather_team(rows, chain=None):
     other = lax.ppermute(rows, "y_hi", perm=[(0, 1), (1, 0)])
+    if chain is not None:
+        other = chain.tick(other)
     pair = jnp.stack([rows, other], axis=0)
-    full = ring_gather(ring_gather(pair, "x"), "z")
+    full = ring_gather(ring_gather(pair, "x", chain), "z", chain)
     return full.reshape(-1, rows.shape[1])
 
 
@@ -76,18 +98,25 @@
 BUTTERFLY = (("y_lo", 1), ("x", 1), ("z", 1), ("y_lo", 2), ("x", 2), ("z", 2), ("z", 4), ("y_hi", 1))
 
 
-def all_sum(value):
-    half = value.shape[0] // 2
-    upper = lax.axis_index("core") == 1
-    low, high = value[:half], value[half:]
-    keep = jnp.where(upper, high, low)
-    send = jnp.where(upper, low, high)
-    part = keep + swap(send, "core", 1)
+def all_sum_steps():
+    def split(value):
+        half = value.shape[0] // 2
+        upper = lax.axis_index("core") == 1
+        keep = jnp.where(upper, value[half:], value[:half])
+        send = jnp.where(upper, value[:half], value[half:])
+        return keep + swap(send, "core", 1)
+
+    def join(part):
+        upper = lax.axis_index("core") == 1
+        other = swap(part, "core", 1)
+        return jnp.where(upper, jnp.concatenate([other, part]), jnp.concatenate([part, other]))
+
+    steps = [split]
     for axis, bit in BUTTERFLY:
         if bit < SIZES[axis]:
-            part = part + swap(part, axis, bit)
-    other = swap(part, "core", 1)
-    return jnp.where(upper, jnp.concatenate([other, part]), jnp.concatenate([part, other]))
+            steps.append(lambda part, axis=axis, bit=bit: part + swap(part, axis, bit))
+    steps.append(join)
+    return steps
 
 
 def blk_reduce_scatter(partial):
@@ -109,18 +138,25 @@
     return cur.reshape(block, width)
 
 
-def blk_all_gather(rows):
-    cur = rows[None]
+def blk_all_gather_steps():
+    steps = [lambda rows: rows[None]]
     bit = 1
     while bit < SIZES["y_lo"]:
-        upper = (lax.axis_index("y_lo") & bit) != 0
-        got = swap(cur, "y_lo", bit)
-        cur = jnp.where(upper, jnp.concatenate([got, cur]), jnp.concatenate([cur, got]))
+        def double(cur, bit=bit):
+            upper = (lax.axis_index("y_lo") & bit) != 0
+            got = swap(cur, "y_lo", bit)
+            return jnp.where(upper, jnp.concatenate([got, cur]), jnp.concatenate([cur, got]))
+        steps.append(double)
         bit *= 2
-    upper = lax.axis_index("core") == 1
-    got = swap(cur, "core", 1)
-    cur = jnp.where(upper, jnp.stack([got, cur], axis=1), jnp.stack([cur, got], axis=1))
-    return cur.reshape((-1,) + rows.shape)
+
+    def cores(cur):
+        upper = lax.axis_index("core") == 1
+        got = swap(cur, "core", 1)
+        both = jnp.where(upper, jnp.stack([got, cur], axis=1), jnp.stack([cur, got], axis=1))
+        return both.reshape((-1,) + cur.shape[1:])
+
+    steps.append(cores)
+    return steps
 
 
 def collect_kernel(slots_ref, vals_ref, panels_ref, out_ref):
@@ -179,20 +215,27 @@
     activated, pullback = jax.vjp(activation, pre)
     hidden = activated.astype(jnp.bfloat16)
     pulled = pullback(cotangent.astype(jnp.float32))[0].astype(jnp.bfloat16)
-    pulled_rows = blk_all_gather(pulled)
-    local_weight = jnp.einsum(
-        "rnf,rng->fg",
-        partial_ax.reshape(pulled_rows.shape),
-        pulled_rows.astype(jnp.float32),
-        precision=lax.Precision.HIGHEST,
-        preferred_element_type=jnp.float32,
-    )
     local_bias = jnp.sum(pulled.astype(jnp.float32), axis=0)
-    filler = jnp.zeros((7, local_bias.shape[0]), jnp.float32)
-    both = all_sum(jnp.concatenate([local_weight, local_bias[None, :], filler], axis=0))
-    pulled_group = gather_team(pulled)
+
+    def weight_partial(pulled_rows):
+        local_weight = jnp.einsum(
+            "rnf,rng->fg",
+            partial_ax.reshape(pulled_rows.shape),
+            pulled_rows.astype(jnp.float32),
+            precision=lax.Precision.HIGHEST,
+            preferred_element_type=jnp.float32,
+        )
+        filler = jnp.zeros((7, local_bias.shape[0]), jnp.float32)
+        return jnp.concatenate([local_weight, local_bias[None, :], filler], axis=0)
+
+    gather_steps = blk_all_gather_steps()
+    sum_steps = all_sum_steps()
+    steps = gather_steps[1:-1] + [lambda cur: sum_steps[0](weight_partial(gather_steps[-1](cur)))]
+    chain = Chain(gather_steps[0](pulled), steps + sum_steps[1:])
+    pulled_group = gather_team(pulled, chain)
     partial_back = collect(pulled_group, slots, adj_vals)
     spread = blk_reduce_scatter(partial_back).astype(jnp.bfloat16)
+    both = chain.finish()
     grad_input = jnp.dot(spread, weight.T, preferred_element_type=jnp.float32).astype(jnp.bfloat16)
     return (hidden, grad_input, both[:width], both[width])
 

time: 315 us -> 314 us (level)
  waiting for transfers between devices: 110 us -> 90.3 us
  starting transfers between devices: 149 us -> 168 us
    ppermute x19, starting transfers between devices: 71.7 us -> 85.8 us  [swap(): return lax.ppermute(value, axis, [(i, i ^ bit) for i in range(n)])]
    ppermute x19, waiting for transfers between devices: 67.8 us -> 54.1 us  [swap(): return lax.ppermute(value, axis, [(i, i ^ bit) for i in range(n)])]
    ppermute x8, waiting for transfers between devices: 10 us -> 3.31 us  [ring_gather(): behind = lax.ppermute(behind, axis, [(i, (i - 1) % n) for i in range(n)])]
  transfers between devices with their start and end apart: 41 -> 41, of which waited for: 22 -> 25; matrix products, arithmetic and copies ran while one was open for 9% -> 9% of each run, Pallas kernels for 3% -> 0%
where the time goes in v8:
time: 314 us; the launch traced here: 312 us
  starting transfers between devices  168 us (54%)
  waiting for transfers between devices  90.3 us (29%)
  local copies, waits for them, and re-layouts  23.7 us (8%)
  Pallas kernels  17.8 us (6%)
  other arithmetic  7.78 us (2%)
  matrix products  3.71 us (1%)
    ppermute x19, starting transfers between devices, swap(): return lax.ppermute(value, axis, [(i, i ^ bit) for i in range(n)])  85.8 us
    ppermute x19, waiting for transfers between devices, swap(): return lax.ppermute(value, axis, [(i, i ^ bit) for i in range(n)])  54.1 us
    ppermute x8, starting transfers between devices, ring_gather(): behind = lax.ppermute(behind, axis, [(i, (i - 1) % n) for i in range(n)])  38.7 us
    ppermute x12, waiting for transfers between devices, ring_gather(): ahead = lax.ppermute(ahead, axis, [(i, (i + 1) % n) for i in range(n)])  30.1 us
    ppermute x12, starting transfers between devices, ring_gather(): ahead = lax.ppermute(ahead, axis, [(i, (i + 1) % n) for i in range(n)])  27.9 us
    pallas_call x2, Pallas kernels, collect(): pl.pallas_call(collect_kernel, grid_spec=grid_spec, out_shape=jax.ShapeDt...  17.8 us
    unnamed x33, local copies, waits for them, and re-layouts  16.6 us
    ppermute x2, starting transfers between devices, gather_team(): other = lax.ppermute(rows, 'y_hi', perm=[(0, 1), (1, 0)])  15.1 us
  transfers between devices with their start and end apart: 41, of which 25 were waited for; matrix products, arithmetic and copies ran while one was open for 9% of the time, Pallas kernels for 0%

profile of v8, /device:TPU:1, one launch (start us, length us, event | category | flops | bytes accessed | tf_op | source)
XLA Modules:
  0.0 312.1 jit_solution(129570567498199639)
XLA Ops:
  0.7 8.4 %collective-permute-start = (bf16[128,256]{1,0:T(8,128)(2,1)}, bf16[128,256]{1,0:T(8,128)(2,1)S(1)}, u32[]{:S(2)}, u32[]{:S(2)}) collective-permute-start(bf16[128,256]{1,0:T(8,128)(2,1)} %param.8), channel_id=1, source_target_pairs={{0,32},{32,0},{1,33},{33,1},{2,34},{34,2},{3,35},{35,3},{4,36},{36... | collective-permute-start | bytes 196616 | tf_op jit(solution)/shard_map/ppermute | solution.py:67
  34.8 8.6 %collective-permute-start.5 = (bf16[8,128,256]{2,1,0:T(8,128)(2,1)S(1)}, bf16[8,128,256]{2,1,0:T(8,128)(2,1)S(1)}, u32[]{:S(2)}, u32[]{:S(2)}) collective-permute-start(bf16[8,128,256]{2,1,0:T(8,128)(2,1)S(1)} %get-tuple-element.49), channel_id=1, source_target_pairs={{0,7},{1,0},{2,1},{3,2},{4,3},{5,4},{6,5},{7,6},{8,15},{9,8},{10,9... | collective-permute-start | bytes 1572872 | tf_op jit(solution)/shard_map/ppermute | solution.py:57
  43.4 5.4 %collective-permute-done.4 = bf16[8,128,256]{2,1,0:T(8,128)(2,1)S(1)} collective-permute-done((bf16[8,128,256]{2,1,0:T(8,128)(2,1)S(1)}, bf16[8,128,256]{2,1,0:T(8,128)(2,1)S(1)}, u32[]{:S(2)}, u32[]{:S(2)}) %collective-permute-start.4) | collective-permute-done | bytes 524320 | tf_op jit(solution)/shard_map/ppermute | solution.py:55
  55.3 4.6 %collective-permute-done.6 = bf16[8,128,256]{2,1,0:T(8,128)(2,1)S(1)} collective-permute-done((bf16[8,128,256]{2,1,0:T(8,128)(2,1)S(1)}, bf16[8,128,256]{2,1,0:T(8,128)(2,1)S(1)}, u32[]{:S(2)}, u32[]{:S(2)}) %collective-permute-start.6) | collective-permute-done | bytes 524320 | tf_op jit(solution)/shard_map/ppermute | solution.py:55
  79.2 5.0 %collective-permute-done.10 = bf16[8,128,256]{2,1,0:T(8,128)(2,1)S(1)} collective-permute-done((bf16[8,128,256]{2,1,0:T(8,128)(2,1)S(1)}, bf16[8,128,256]{2,1,0:T(8,128)(2,1)S(1)}, u32[]{:S(2)}, u32[]{:S(2)}) %collective-permute-start.10) | collective-permute-done | bytes 524320 | tf_op jit(solution)/shard_map/ppermute | solution.py:55
  85.0 8.9 %shard_map.111 = f32[1024,256]{1,0:T(8,128)} custom-call(s32[96]{0:T(128)} %fusion.27.slots_ref, bf16[1,8,1,12,128,128]{5,4,3,2,1,0:T(8,128)(2,1)} %vals_ref.3, bf16[64,128,256]{2,1,0:T(8,128)(2,1)} %constant_dynamic-update-slice_fusion.5.panels_ref), custom_call_target="tpu_custom_call" | custom-call | flops 805306368 | bytes 8388608 | tf_op jit(solution)/shard_map/pallas_call | solution.py:186
  95.9 10.7 %collective-permute-start.11 = (f32[4,128,256]{2,1,0:T(8,128)S(1)}, f32[4,128,256]{2,1,0:T(8,128)S(1)}, u32[]{:S(2)}, u32[]{:S(2)}) collective-permute-start(f32[4,128,256]{2,1,0:T(8,128)S(1)} %select_bitcast_fusion.1), channel_id=1, source_target_pairs={{0,64},{64,0},{1,65},{65,1},{2,66},{66,2},{3,67},{67,3},{4,68},{68... | collective-permute-start | bytes 1572872 | tf_op jit(solution)/shard_map/ppermute | solution.py:95
  111.1 6.5 %collective-permute-done.12 = f32[2,128,256]{2,1,0:T(8,128)S(1)} collective-permute-done((f32[2,128,256]{2,1,0:T(8,128)S(1)}, f32[2,128,256]{2,1,0:T(8,128)S(1)}, u32[]{:S(2)}, u32[]{:S(2)}) %collective-permute-start.12) | collective-permute-done | bytes 262176 | tf_op jit(solution)/shard_map/ppermute | solution.py:95
  117.8 6.8 %collective-permute-start.13 = (f32[1,128,256]{2,1,0:T(8,128)S(1)}, f32[1,128,256]{2,1,0:T(8,128)S(1)}, u32[]{:S(2)}, u32[]{:S(2)}) collective-permute-start(f32[1,128,256]{2,1,0:T(8,128)S(1)} %select_bitcast_fusion.5), channel_id=1, source_target_pairs={{0,256},{128,384},{256,0},{384,128},{1,257},{129,385},{257,1},{385... | collective-permute-start | bytes 393224 | tf_op jit(solution)/shard_map/ppermute | solution.py:95
  124.6 6.7 %collective-permute-done.13 = f32[1,128,256]{2,1,0:T(8,128)S(1)} collective-permute-done((f32[1,128,256]{2,1,0:T(8,128)S(1)}, f32[1,128,256]{2,1,0:T(8,128)S(1)}, u32[]{:S(2)}, u32[]{:S(2)}) %collective-permute-start.13) | collective-permute-done | bytes 131104 | tf_op jit(solution)/shard_map/ppermute | solution.py:95
  133.5 6.7 %collective-permute-start.14 = (bf16[128,256]{1,0:T(8,128)(2,1)S(1)}, bf16[128,256]{1,0:T(8,128)(2,1)S(1)}, u32[]{:S(2)}, u32[]{:S(2)}) collective-permute-start(bf16[128,256]{1,0:T(8,128)(2,1)S(1)} %get-tuple-element.41), channel_id=1, source_target_pairs={{0,32},{32,0},{1,33},{33,1},{2,34},{34,2},{3,35},{35,3},{4,36},{36... | collective-permute-start | bytes 196616 | tf_op jit(solution)/shard_map/ppermute | solution.py:67
  147.8 5.0 %collective-permute-start.18 = (bf16[2,128,256]{2,1,0:T(8,128)(2,1)S(1)}, bf16[2,128,256]{2,1,0:T(8,128)(2,1)S(1)}, u32[]{:S(2)}, u32[]{:S(2)}) collective-permute-start(bf16[2,128,256]{2,1,0:T(8,128)(2,1)S(1)} %fusion.3), channel_id=1, source_target_pairs={{0,256},{128,384},{256,0},{384,128},{1,257},{129,385},{257,1},{385... | collective-permute-start | bytes 393224 | tf_op jit(solution)/shard_map/ppermute | solution.py:95
  155.2 5.4 %collective-permute-start.20 = (bf16[4,128,256]{2,1,0:T(8,128)(2,1)S(1)}, bf16[4,128,256]{2,1,0:T(8,128)(2,1)S(1)}, u32[]{:S(2)}, u32[]{:S(2)}) collective-permute-start(bf16[4,128,256]{2,1,0:T(8,128)(2,1)S(1)} %maximum_select_fusion.2), channel_id=1, source_target_pairs={{0,64},{64,0},{1,65},{65,1},{2,66},{66,2},{3,67},{67,3},{4,68},{68... | collective-permute-start | bytes 786440 | tf_op jit(solution)/shard_map/ppermute | solution.py:95
  170.2 4.8 %collective-permute-start.23 = (bf16[8,128,256]{2,1,0:T(8,128)(2,1)S(1)}, bf16[8,128,256]{2,1,0:T(8,128)(2,1)S(1)}, u32[]{:S(2)}, u32[]{:S(2)}) collective-permute-start(bf16[8,128,256]{2,1,0:T(8,128)(2,1)S(1)} %get-tuple-element.43), channel_id=1, source_target_pairs={{0,7},{1,0},{2,1},{3,2},{4,3},{5,4},{6,5},{7,6},{8,15},{9,8},{10,9... | collective-permute-start | bytes 1572872 | tf_op jit(solution)/shard_map/ppermute | solution.py:57
  185.5 5.0 %collective-permute-done.22 = bf16[8,128,256]{2,1,0:T(8,128)(2,1)S(1)} collective-permute-done((bf16[8,128,256]{2,1,0:T(8,128)(2,1)S(1)}, bf16[8,128,256]{2,1,0:T(8,128)(2,1)S(1)}, u32[]{:S(2)}, u32[]{:S(2)}) %collective-permute-start.22) | collective-permute-done | bytes 524320 | tf_op jit(solution)/shard_map/ppermute | solution.py:55
  207.8 5.3 %collective-permute-start.29 = (bf16[8,128,256]{2,1,0:T(8,128)(2,1)S(1)}, bf16[8,128,256]{2,1,0:T(8,128)(2,1)S(1)}, u32[]{:S(2)}, u32[]{:S(2)}) collective-permute-start(bf16[8,128,256]{2,1,0:T(8,128)(2,1)S(1)} %collective-permute-done.26), channel_id=1, source_target_pairs={{0,7},{1,0},{2,1},{3,2},{4,3},{5,4},{6,5},{7,6},{8,15},{9,8},{10,9... | collective-permute-start | bytes 1572872 | tf_op jit(solution)/shard_map/ppermute | solution.py:57
  215.9 7.0 %collective-permute-done.30 = f32[132,256]{1,0:T(8,128)S(1)} collective-permute-done((f32[132,256]{1,0:T(8,128)S(1)}, f32[132,256]{1,0:T(8,128)S(1)}, u32[]{:S(2)}, u32[]{:S(2)}) %collective-permute-start.30) | collective-permute-done | bytes 135200 | tf_op jit(solution)/shard_map/ppermute | solution.py:95
  236.2 8.9 %shard_map.112 = f32[1024,256]{1,0:T(8,128)} custom-call(s32[96]{0:T(128)} %fusion.27.slots_ref, bf16[1,8,1,12,128,128]{5,4,3,2,1,0:T(8,128)(2,1)} %vals_ref.3, bf16[64,128,256]{2,1,0:T(8,128)(2,1)} %constant_dynamic-update-slice_fusion.22.panels_ref), custom_call_target="tpu_custom_call" | custom-call | flops 805306368 | bytes 8388608 | tf_op jit(solution)/shard_map/pallas_call | solution.py:186
  246.4 6.9 %collective-permute-start.33 = (f32[4,128,256]{2,1,0:T(8,128)S(1)}, f32[4,128,256]{2,1,0:T(8,128)S(1)}, u32[]{:S(2)}, u32[]{:S(2)}) collective-permute-start(f32[4,128,256]{2,1,0:T(8,128)S(1)} %select_bitcast_fusion), channel_id=1, source_target_pairs={{0,64},{64,0},{1,65},{65,1},{2,66},{66,2},{3,67},{67,3},{4,68},{68... | collective-permute-start | bytes 1572872 | tf_op jit(solution)/shard_map/ppermute | solution.py:95
  253.3 4.6 %collective-permute-start.36 = (f32[132,256]{1,0:T(8,128)S(1)}, f32[132,256]{1,0:T(8,128)S(1)}, u32[]{:S(2)}, u32[]{:S(2)}) collective-permute-start(f32[132,256]{1,0:T(8,128)S(1)} %add.186), channel_id=1, source_target_pairs={{0,16},{8,24},{16,0},{24,8},{1,17},{9,25},{17,1},{25,9},{2,18},{10... | collective-permute-start | bytes 405512 | tf_op jit(solution)/shard_map/ppermute | solution.py:95
  270.0 5.6 %collective-permute-start.38 = (f32[132,256]{1,0:T(8,128)S(1)}, f32[132,256]{1,0:T(8,128)S(1)}, u32[]{:S(2)}, u32[]{:S(2)}) collective-permute-start(f32[132,256]{1,0:T(8,128)S(1)} %add.191), channel_id=1, source_target_pairs={{0,4},{1,5},{2,6},{3,7},{4,0},{5,1},{6,2},{7,3},{8,12},{9,13},{10,... | collective-permute-start | bytes 405512 | tf_op jit(solution)/shard_map/ppermute | solution.py:95
  279.8 6.6 %collective-permute-start.39 = (f32[132,256]{1,0:T(8,128)S(1)}, f32[132,256]{1,0:T(8,128)S(1)}, u32[]{:S(2)}, u32[]{:S(2)}) collective-permute-start(f32[132,256]{1,0:T(8,128)S(1)} %add.192), channel_id=1, source_target_pairs={{0,32},{32,0},{1,33},{33,1},{2,34},{34,2},{3,35},{35,3},{4,36},{36... | collective-permute-start | bytes 405512 | tf_op jit(solution)/shard_map/ppermute | solution.py:95
  290.0 10.8 %collective-permute-start.40 = (f32[132,256]{1,0:T(8,128)S(1)}, f32[132,256]{1,0:T(8,128)S(1)}, u32[]{:S(2)}, u32[]{:S(2)}) collective-permute-start(f32[132,256]{1,0:T(8,128)S(1)} %add.193), channel_id=1, source_target_pairs={{0,64},{64,0},{1,65},{65,1},{2,66},{66,2},{3,67},{67,3},{4,68},{68... | collective-permute-start | bytes 405512 | tf_op jit(solution)/shard_map/ppermute | solution.py:95
  304.8 6.5 %collective-permute-done.35 = f32[1,128,256]{2,1,0:T(8,128)S(1)} collective-permute-done((f32[1,128,256]{2,1,0:T(8,128)S(1)}, f32[1,128,256]{2,1,0:T(8,128)S(1)}, u32[]{:S(2)}, u32[]{:S(2)}) %collective-permute-start.35) | collective-permute-done | bytes 131104 | tf_op jit(solution)/shard_map/ppermute | solution.py:95
  (143 shorter events, 149.8 us)
Async XLA Ops:
  0.7 10.3 %collective-permute-start = (bf16[128,256]{1,0:T(8,128)(2,1)}, bf16[128,256]{1,0:T(8,128)(2,1)S(1)}, u32[]{:S(2)}, u32[]{:S(2)}) collective-permute-start(bf16[128,256]{1,0:T(8,128)(2,1)} %param.8), channel_id=1, source_target_pairs={{0,32},{32,0},{1,33},{33,1},{2,34},{34,2},{3,35},{35,3},{4,36},{36... | collective-permute-start | bytes 196616 | tf_op jit(solution)/shard_map/ppermute | solution.py:67
  11.9 13.9 %collective-permute-start.2 = (bf16[2,128,256]{2,1,0:T(8,128)(2,1)S(1)}, bf16[2,128,256]{2,1,0:T(8,128)(2,1)S(1)}, u32[]{:S(2)}, u32[]{:S(2)}) collective-permute-start(bf16[2,128,256]{2,1,0:T(8,128)(2,1)S(1)} %pad_maximum_fusion.3), channel_id=1, source_target_pairs={{0,24},{8,0},{16,8},{24,16},{1,25},{9,1},{17,9},{25,17},{2,26},{10... | collective-permute-start | bytes 393224 | tf_op jit(solution)/shard_map/ppermute | solution.py:57
  30.8 18.0 %collective-permute-start.4 = (bf16[8,128,256]{2,1,0:T(8,128)(2,1)S(1)}, bf16[8,128,256]{2,1,0:T(8,128)(2,1)S(1)}, u32[]{:S(2)}, u32[]{:S(2)}) collective-permute-start(bf16[8,128,256]{2,1,0:T(8,128)(2,1)S(1)} %get-tuple-element.49), channel_id=1, source_target_pairs={{0,1},{1,2},{2,3},{3,4},{4,5},{5,6},{6,7},{7,0},{8,9},{9,10},{10,1... | collective-permute-start | bytes 1572872 | tf_op jit(solution)/shard_map/ppermute | solution.py:55
  34.8 15.9 %collective-permute-start.5 = (bf16[8,128,256]{2,1,0:T(8,128)(2,1)S(1)}, bf16[8,128,256]{2,1,0:T(8,128)(2,1)S(1)}, u32[]{:S(2)}, u32[]{:S(2)}) collective-permute-start(bf16[8,128,256]{2,1,0:T(8,128)(2,1)S(1)} %get-tuple-element.49), channel_id=1, source_target_pairs={{0,7},{1,0},{2,1},{3,2},{4,3},{5,4},{6,5},{7,6},{8,15},{9,8},{10,9... | collective-permute-start | bytes 1572872 | tf_op jit(solution)/shard_map/ppermute | solution.py:57
  48.8 11.1 %collective-permute-start.6 = (bf16[8,128,256]{2,1,0:T(8,128)(2,1)S(1)}, bf16[8,128,256]{2,1,0:T(8,128)(2,1)S(1)}, u32[]{:S(2)}, u32[]{:S(2)}) collective-permute-start(bf16[8,128,256]{2,1,0:T(8,128)(2,1)S(1)} %collective-permute-done.4), channel_id=1, source_target_pairs={{0,1},{1,2},{2,3},{3,4},{4,5},{5,6},{6,7},{7,0},{8,9},{9,10},{10,1... | collective-permute-start | bytes 1572872 | tf_op jit(solution)/shard_map/ppermute | solution.py:55
  50.7 17.0 %collective-permute-start.7 = (bf16[8,128,256]{2,1,0:T(8,128)(2,1)S(1)}, bf16[8,128,256]{2,1,0:T(8,128)(2,1)S(1)}, u32[]{:S(2)}, u32[]{:S(2)}) collective-permute-start(bf16[8,128,256]{2,1,0:T(8,128)(2,1)S(1)} %collective-permute-done.5), channel_id=1, source_target_pairs={{0,7},{1,0},{2,1},{3,2},{4,3},{5,4},{6,5},{7,6},{8,15},{9,8},{10,9... | collective-permute-start | bytes 1572872 | tf_op jit(solution)/shard_map/ppermute | solution.py:57
  59.9 13.2 %collective-permute-start.8 = (bf16[8,128,256]{2,1,0:T(8,128)(2,1)S(1)}, bf16[8,128,256]{2,1,0:T(8,128)(2,1)S(1)}, u32[]{:S(2)}, u32[]{:S(2)}) collective-permute-start(bf16[8,128,256]{2,1,0:T(8,128)(2,1)S(1)} %collective-permute-done.6), channel_id=1, source_target_pairs={{0,1},{1,2},{2,3},{3,4},{4,5},{5,6},{6,7},{7,0},{8,9},{9,10},{10,1... | collective-permute-start | bytes 1572872 | tf_op jit(solution)/shard_map/ppermute | solution.py:55
  67.7 10.7 %collective-permute-start.9 = (bf16[8,128,256]{2,1,0:T(8,128)(2,1)S(1)}, bf16[8,128,256]{2,1,0:T(8,128)(2,1)S(1)}, u32[]{:S(2)}, u32[]{:S(2)}) collective-permute-start(bf16[8,128,256]{2,1,0:T(8,128)(2,1)S(1)} %collective-permute-done.7), channel_id=1, source_target_pairs={{0,7},{1,0},{2,1},{3,2},{4,3},{5,4},{6,5},{7,6},{8,15},{9,8},{10,9... | collective-permute-start | bytes 1572872 | tf_op jit(solution)/shard_map/ppermute | solution.py:57
  73.1 11.1 %collective-permute-start.10 = (bf16[8,128,256]{2,1,0:T(8,128)(2,1)S(1)}, bf16[8,128,256]{2,1,0:T(8,128)(2,1)S(1)}, u32[]{:S(2)}, u32[]{:S(2)}) collective-permute-start(bf16[8,128,256]{2,1,0:T(8,128)(2,1)S(1)} %collective-permute-done.8), channel_id=1, source_target_pairs={{0,1},{1,2},{2,3},{3,4},{4,5},{5,6},{6,7},{7,0},{8,9},{9,10},{10,1... | collective-permute-start | bytes 1572872 | tf_op jit(solution)/shard_map/ppermute | solution.py:55
  95.9 12.2 %collective-permute-start.11 = (f32[4,128,256]{2,1,0:T(8,128)S(1)}, f32[4,128,256]{2,1,0:T(8,128)S(1)}, u32[]{:S(2)}, u32[]{:S(2)}) collective-permute-start(f32[4,128,256]{2,1,0:T(8,128)S(1)} %select_bitcast_fusion.1), channel_id=1, source_target_pairs={{0,64},{64,0},{1,65},{65,1},{2,66},{66,2},{3,67},{67,3},{4,68},{68... | collective-permute-start | bytes 1572872 | tf_op jit(solution)/shard_map/ppermute | solution.py:95
  117.8 13.6 %collective-permute-start.13 = (f32[1,128,256]{2,1,0:T(8,128)S(1)}, f32[1,128,256]{2,1,0:T(8,128)S(1)}, u32[]{:S(2)}, u32[]{:S(2)}) collective-permute-start(f32[1,128,256]{2,1,0:T(8,128)S(1)} %select_bitcast_fusion.5), channel_id=1, source_target_pairs={{0,256},{128,384},{256,0},{384,128},{1,257},{129,385},{257,1},{385... | collective-permute-start | bytes 393224 | tf_op jit(solution)/shard_map/ppermute | solution.py:95
  142.5 12.7 %collective-permute-start.17 = (bf16[2,128,256]{2,1,0:T(8,128)(2,1)S(1)}, bf16[2,128,256]{2,1,0:T(8,128)(2,1)S(1)}, u32[]{:S(2)}, u32[]{:S(2)}) collective-permute-start(bf16[2,128,256]{2,1,0:T(8,128)(2,1)S(1)} %pad_maximum_fusion), channel_id=1, source_target_pairs={{0,24},{8,0},{16,8},{24,16},{1,25},{9,1},{17,9},{25,17},{2,26},{10... | collective-permute-start | bytes 393224 | tf_op jit(solution)/shard_map/ppermute | solution.py:57
  144.4 10.8 %collective-permute-start.16 = (bf16[2,128,256]{2,1,0:T(8,128)(2,1)S(1)}, bf16[2,128,256]{2,1,0:T(8,128)(2,1)S(1)}, u32[]{:S(2)}, u32[]{:S(2)}) collective-permute-start(bf16[2,128,256]{2,1,0:T(8,128)(2,1)S(1)} %pad_maximum_fusion), channel_id=1, source_target_pairs={{0,8},{8,16},{16,24},{24,0},{1,9},{9,17},{17,25},{25,1},{2,10},{10... | collective-permute-start | bytes 393224 | tf_op jit(solution)/shard_map/ppermute | solution.py:55
  170.2 15.2 %collective-permute-start.23 = (bf16[8,128,256]{2,1,0:T(8,128)(2,1)S(1)}, bf16[8,128,256]{2,1,0:T(8,128)(2,1)S(1)}, u32[]{:S(2)}, u32[]{:S(2)}) collective-permute-start(bf16[8,128,256]{2,1,0:T(8,128)(2,1)S(1)} %get-tuple-element.43), channel_id=1, source_target_pairs={{0,7},{1,0},{2,1},{3,2},{4,3},{5,4},{6,5},{7,6},{8,15},{9,8},{10,9... | collective-permute-start | bytes 1572872 | tf_op jit(solution)/shard_map/ppermute | solution.py:57
  175.0 15.4 %collective-permute-start.22 = (bf16[8,128,256]{2,1,0:T(8,128)(2,1)S(1)}, bf16[8,128,256]{2,1,0:T(8,128)(2,1)S(1)}, u32[]{:S(2)}, u32[]{:S(2)}) collective-permute-start(bf16[8,128,256]{2,1,0:T(8,128)(2,1)S(1)} %get-tuple-element.43), channel_id=1, source_target_pairs={{0,1},{1,2},{2,3},{3,4},{4,5},{5,6},{6,7},{7,0},{8,9},{9,10},{10,1... | collective-permute-start | bytes 1572872 | tf_op jit(solution)/shard_map/ppermute | solution.py:55
  190.5 14.5 %collective-permute-start.25 = (bf16[8,128,256]{2,1,0:T(8,128)(2,1)S(1)}, bf16[8,128,256]{2,1,0:T(8,128)(2,1)S(1)}, u32[]{:S(2)}, u32[]{:S(2)}) collective-permute-start(bf16[8,128,256]{2,1,0:T(8,128)(2,1)S(1)} %collective-permute-done.22), channel_id=1, source_target_pairs={{0,1},{1,2},{2,3},{3,4},{4,5},{5,6},{6,7},{7,0},{8,9},{9,10},{10,1... | collective-permute-start | bytes 1572872 | tf_op jit(solution)/shard_map/ppermute | solution.py:55
  192.4 13.5 %collective-permute-start.26 = (bf16[8,128,256]{2,1,0:T(8,128)(2,1)S(1)}, bf16[8,128,256]{2,1,0:T(8,128)(2,1)S(1)}, u32[]{:S(2)}, u32[]{:S(2)}) collective-permute-start(bf16[8,128,256]{2,1,0:T(8,128)(2,1)S(1)} %collective-permute-done.23), channel_id=1, source_target_pairs={{0,7},{1,0},{2,1},{3,2},{4,3},{5,4},{6,5},{7,6},{8,15},{9,8},{10,9... | collective-permute-start | bytes 1572872 | tf_op jit(solution)/shard_map/ppermute | solution.py:57
  205.9 17.0 %collective-permute-start.28 = (bf16[8,128,256]{2,1,0:T(8,128)(2,1)S(1)}, bf16[8,128,256]{2,1,0:T(8,128)(2,1)S(1)}, u32[]{:S(2)}, u32[]{:S(2)}) collective-permute-start(bf16[8,128,256]{2,1,0:T(8,128)(2,1)S(1)} %collective-permute-done.25), channel_id=1, source_target_pairs={{0,1},{1,2},{2,3},{3,4},{4,5},{5,6},{6,7},{7,0},{8,9},{9,10},{10,1... | collective-permute-start | bytes 1572872 | tf_op jit(solution)/shard_map/ppermute | solution.py:55
  207.8 15.1 %collective-permute-start.29 = (bf16[8,128,256]{2,1,0:T(8,128)(2,1)S(1)}, bf16[8,128,256]{2,1,0:T(8,128)(2,1)S(1)}, u32[]{:S(2)}, u32[]{:S(2)}) collective-permute-start(bf16[8,128,256]{2,1,0:T(8,128)(2,1)S(1)} %collective-permute-done.26), channel_id=1, source_target_pairs={{0,7},{1,0},{2,1},{3,2},{4,3},{5,4},{6,5},{7,6},{8,15},{9,8},{10,9... | collective-permute-start | bytes 1572872 | tf_op jit(solution)/shard_map/ppermute | solution.py:57
  222.9 12.4 %collective-permute-start.31 = (bf16[8,128,256]{2,1,0:T(8,128)(2,1)S(1)}, bf16[8,128,256]{2,1,0:T(8,128)(2,1)S(1)}, u32[]{:S(2)}, u32[]{:S(2)}) collective-permute-start(bf16[8,128,256]{2,1,0:T(8,128)(2,1)S(1)} %collective-permute-done.28), channel_id=1, source_target_pairs={{0,1},{1,2},{2,3},{3,4},{4,5},{5,6},{6,7},{7,0},{8,9},{9,10},{10,1... | collective-permute-start | bytes 1572872 | tf_op jit(solution)/shard_map/ppermute | solution.py:55
  246.4 29.2 %collective-permute-start.33 = (f32[4,128,256]{2,1,0:T(8,128)S(1)}, f32[4,128,256]{2,1,0:T(8,128)S(1)}, u32[]{:S(2)}, u32[]{:S(2)}) collective-permute-start(f32[4,128,256]{2,1,0:T(8,128)S(1)} %select_bitcast_fusion), channel_id=1, source_target_pairs={{0,64},{64,0},{1,65},{65,1},{2,66},{66,2},{3,67},{67,3},{4,68},{68... | collective-permute-start | bytes 1572872 | tf_op jit(solution)/shard_map/ppermute | solution.py:95
  277.0 23.8 %collective-permute-start.34 = (f32[2,128,256]{2,1,0:T(8,128)S(1)}, f32[2,128,256]{2,1,0:T(8,128)S(1)}, u32[]{:S(2)}, u32[]{:S(2)}) collective-permute-start(f32[2,128,256]{2,1,0:T(8,128)S(1)} %select_bitcast_fusion.2), channel_id=1, source_target_pairs={{0,128},{128,0},{256,384},{384,256},{1,129},{129,1},{257,385},{385... | collective-permute-start | bytes 786440 | tf_op jit(solution)/shard_map/ppermute | solution.py:95
  290.0 13.5 %collective-permute-start.40 = (f32[132,256]{1,0:T(8,128)S(1)}, f32[132,256]{1,0:T(8,128)S(1)}, u32[]{:S(2)}, u32[]{:S(2)}) collective-permute-start(f32[132,256]{1,0:T(8,128)S(1)} %add.193), channel_id=1, source_target_pairs={{0,64},{64,0},{1,65},{65,1},{2,66},{66,2},{3,67},{67,3},{4,68},{68... | collective-permute-start | bytes 405512 | tf_op jit(solution)/shard_map/ppermute | solution.py:95
  300.9 10.4 %collective-permute-start.35 = (f32[1,128,256]{2,1,0:T(8,128)S(1)}, f32[1,128,256]{2,1,0:T(8,128)S(1)}, u32[]{:S(2)}, u32[]{:S(2)}) collective-permute-start(f32[1,128,256]{2,1,0:T(8,128)S(1)} %select_bitcast_fusion.4), channel_id=1, source_target_pairs={{0,256},{128,384},{256,0},{384,128},{1,257},{129,385},{257,1},{385... | collective-permute-start | bytes 393224 | tf_op jit(solution)/shard_map/ppermute | solution.py:95
  (23 other events, 491.4 us)

commit v9 on v6

--- a/solution.py
+++ b/solution.py
@@ -123,6 +123,65 @@
     return cur.reshape((-1,) + rows.shape)
 
 
+def fused_collect_kernel(slots_ref, vals_ref, panels_ref, weight_ref, rows_ref, ax_ref, products):
+    row = pl.program_id(0)
+    nnz = vals_ref.shape[0]
+
+    @pl.when(row == 0)
+    def _():
+        def one_panel(p, carry):
+            products[p] = jnp.dot(
+                panels_ref[p], weight_ref[...], preferred_element_type=jnp.float32
+            ).astype(products.dtype)
+            return carry
+
+        lax.fori_loop(0, panels_ref.shape[0], one_panel, 0)
+
+    total_rows = jnp.zeros(rows_ref.shape, jnp.float32)
+    total_ax = jnp.zeros(ax_ref.shape, jnp.float32)
+    for k in range(nnz):
+        slot = slots_ref[row * nnz + k]
+        values = vals_ref[k]
+        total_rows = total_rows + jnp.dot(values, products[slot], preferred_element_type=jnp.float32)
+        total_ax = total_ax + jnp.dot(values, panels_ref[slot], preferred_element_type=jnp.float32)
+    rows_ref[...] = total_rows
+    ax_ref[...] = total_ax
+
+
+def fused_collect(panels, weight, slots, adj_vals):
+    block = adj_vals.shape[-1]
+    width = panels.shape[1]
+    rows, nnz = slots.shape
+    stacked = panels.reshape(panels.shape[0] // block, block, width)
+    count = stacked.shape[0]
+    grid_spec = pltpu.PrefetchScalarGridSpec(
+        num_scalar_prefetch=1,
+        grid=(rows,),
+        in_specs=[
+            pl.BlockSpec((None, None, None, nnz, block, block), lambda r, s: (0, r, 0, 0, 0, 0)),
+            pl.BlockSpec(stacked.shape, lambda r, s: (0, 0, 0)),
+            pl.BlockSpec(weight.shape, lambda r, s: (0, 0)),
+        ],
+        out_specs=[
+            pl.BlockSpec((block, width), lambda r, s: (r, 0)),
+            pl.BlockSpec((block, width), lambda r, s: (r, 0)),
+        ],
+        scratch_shapes=[pltpu.VMEM(stacked.shape, stacked.dtype)],
+    )
+    out = jax.ShapeDtypeStruct((rows * block, width), jnp.float32)
+    return pl.pallas_call(
+        fused_collect_kernel,
+        grid_spec=grid_spec,
+        out_shape=(out, out),
+        compiler_params=pltpu.CompilerParams(dimension_semantics=("arbitrary",)),
+        cost_estimate=pl.CostEstimate(
+            flops=2 * count * block * width * width + 4 * rows * nnz * block * block * width,
+            transcendentals=0,
+            bytes_accessed=stacked.size * 2 + rows * nnz * block * block * 2 + 2 * rows * block * width * 4,
+        ),
+    )(slots.reshape(-1), adj_vals, stacked, weight)
+
+
 def collect_kernel(slots_ref, vals_ref, panels_ref, out_ref):
     row = pl.program_id(0)
     nnz = vals_ref.shape[0]
@@ -167,9 +226,7 @@
     slots = member_slots(adj_cols[0, :, 0, :])
     width = features.shape[1]
     gathered = gather_team(features)
-    products = jnp.dot(gathered, weight, preferred_element_type=jnp.float32).astype(jnp.bfloat16)
-    partial_rows = collect(products, slots, adj_vals)
-    partial_ax = collect(gathered, slots, adj_vals)
+    partial_rows, partial_ax = fused_collect(gathered, weight, slots, adj_vals)
     summed = blk_reduce_scatter(partial_rows)
     pre = summed + bias[None, :]
     activated, pullback = jax.vjp(activation, pre)

time: 318 us -> 328 us (1.031)
  waiting for transfers between devices: 98.8 us -> 110 us
  matrix products: 8.52 us -> 1.85 us
    pallas_call x0 -> x1, Pallas kernels: none -> 20.7 us  [fused_collect(): pl.pallas_call(fused_collect_kernel, grid_spec=grid_spec, out_shape=(out,...]
    pallas_call x3 -> x1, Pallas kernels: 26.8 us -> 8.92 us  [collect(): pl.pallas_call(collect_kernel, grid_spec=grid_spec, out_shape=jax.ShapeDt...]
    ppermute x8, waiting for transfers between devices: 1.2 us -> 9.98 us  [ring_gather(): behind = lax.ppermute(behind, axis, [(i, (i - 1) % n) for i in range(n)])]
    ppermute x19, waiting for transfers between devices: 61.3 us -> 67.9 us  [swap(): return lax.ppermute(value, axis, [(i, i ^ bit) for i in range(n)])]
    dot_general x1 -> x0, matrix products: 5.45 us -> none  [local(): jnp.dot(gathered, weight, preferred_element_type=jnp.float32)]
    ppermute x12, waiting for transfers between devices: 34.4 us -> 30.6 us  [ring_gather(): ahead = lax.ppermute(ahead, axis, [(i, (i + 1) % n) for i in range(n)])]
    unnamed x31 -> x33, local copies, waits for them, and re-layouts: 16.7 us -> 16.7 us
  transfers between devices with their start and end apart: 41 -> 41, of which waited for: 20 -> 22; matrix products, arithmetic and copies ran while one was open for 10% -> 9% of each run, Pallas kernels for 6% -> 3%
where the time goes in v9:
time: 328 us; the launch traced here: 326 us
  starting transfers between devices  149 us (45%)
  waiting for transfers between devices  110 us (34%)
  Pallas kernels  29.6 us (9%)
  local copies, waits for them, and re-layouts  23.8 us (7%)
  other arithmetic  10.2 us (3%)
    ppermute x19, starting transfers between devices, swap(): return lax.ppermute(value, axis, [(i, i ^ bit) for i in range(n)])  71.8 us
    ppermute x19, waiting for transfers between devices, swap(): return lax.ppermute(value, axis, [(i, i ^ bit) for i in range(n)])  67.9 us
    ppermute x8, starting transfers between devices, ring_gather(): behind = lax.ppermute(behind, axis, [(i, (i - 1) % n) for i in range(n)])  40.1 us
    ppermute x12, waiting for transfers between devices, ring_gather(): ahead = lax.ppermute(ahead, axis, [(i, (i + 1) % n) for i in range(n)])  30.6 us
    ppermute x12, starting transfers between devices, ring_gather(): ahead = lax.ppermute(ahead, axis, [(i, (i + 1) % n) for i in range(n)])  24.8 us
    pallas_call x1, Pallas kernels, fused_collect(): pl.pallas_call(fused_collect_kernel, grid_spec=grid_spec, out_shape=(out,...  20.7 us
    unnamed x33, local copies, waits for them, and re-layouts  16.7 us
    ppermute x2, starting transfers between devices, gather_team(): other = lax.ppermute(rows, 'y_hi', perm=[(0, 1), (1, 0)])  11.9 us
  transfers between devices with their start and end apart: 41, of which 22 were waited for; matrix products, arithmetic and copies ran while one was open for 9% of the time, Pallas kernels for 3%

profile of v9, /device:TPU:1, one launch (start us, length us, event | category | flops | bytes accessed | tf_op | source)
XLA Modules:
  0.0 325.8 jit_solution(11663041224656905212)
XLA Ops:
  0.7 8.3 %collective-permute-start = (bf16[128,256]{1,0:T(8,128)(2,1)}, bf16[128,256]{1,0:T(8,128)(2,1)S(1)}, u32[]{:S(2)}, u32[]{:S(2)}) collective-permute-start(bf16[128,256]{1,0:T(8,128)(2,1)} %param.8), channel_id=1, source_target_pairs={{0,32},{32,0},{1,33},{33,1},{2,34},{34,2},{3,35},{35,3},{4,36},{36... | collective-permute-start | bytes 196616 | tf_op jit(solution)/shard_map/ppermute | solution.py:47
  22.2 5.1 %collective-permute-done.3 = bf16[2,128,256]{2,1,0:T(8,128)(2,1)S(1)} collective-permute-done((bf16[2,128,256]{2,1,0:T(8,128)(2,1)S(1)}, bf16[2,128,256]{2,1,0:T(8,128)(2,1)S(1)}, u32[]{:S(2)}, u32[]{:S(2)}) %collective-permute-start.3) | collective-permute-done | bytes 131104 | tf_op jit(solution)/shard_map/ppermute | solution.py:38
  30.5 8.6 %collective-permute-start.5 = (bf16[8,128,256]{2,1,0:T(8,128)(2,1)S(1)}, bf16[8,128,256]{2,1,0:T(8,128)(2,1)S(1)}, u32[]{:S(2)}, u32[]{:S(2)}) collective-permute-start(bf16[8,128,256]{2,1,0:T(8,128)(2,1)S(1)} %get-tuple-element.17), channel_id=1, source_target_pairs={{0,7},{1,0},{2,1},{3,2},{4,3},{5,4},{6,5},{7,6},{8,15},{9,8},{10,9... | collective-permute-start | bytes 1572872 | tf_op jit(solution)/shard_map/ppermute | solution.py:41
  39.1 5.9 %collective-permute-done.4 = bf16[8,128,256]{2,1,0:T(8,128)(2,1)S(1)} collective-permute-done((bf16[8,128,256]{2,1,0:T(8,128)(2,1)S(1)}, bf16[8,128,256]{2,1,0:T(8,128)(2,1)S(1)}, u32[]{:S(2)}, u32[]{:S(2)}) %collective-permute-start.4) | collective-permute-done | bytes 524320 | tf_op jit(solution)/shard_map/ppermute | solution.py:38
  51.5 5.0 %collective-permute-done.6 = bf16[8,128,256]{2,1,0:T(8,128)(2,1)S(1)} collective-permute-done((bf16[8,128,256]{2,1,0:T(8,128)(2,1)S(1)}, bf16[8,128,256]{2,1,0:T(8,128)(2,1)S(1)}, u32[]{:S(2)}, u32[]{:S(2)}) %collective-permute-start.6) | collective-permute-done | bytes 524320 | tf_op jit(solution)/shard_map/ppermute | solution.py:38
  75.8 5.0 %collective-permute-done.10 = bf16[8,128,256]{2,1,0:T(8,128)(2,1)S(1)} collective-permute-done((bf16[8,128,256]{2,1,0:T(8,128)(2,1)S(1)}, bf16[8,128,256]{2,1,0:T(8,128)(2,1)S(1)}, u32[]{:S(2)}, u32[]{:S(2)}) %collective-permute-start.10) | collective-permute-done | bytes 524320 | tf_op jit(solution)/shard_map/ppermute | solution.py:38
  81.6 20.7 %shard_map.111 = (f32[1024,256]{1,0:T(8,128)}, f32[1024,256]{1,0:T(8,128)}) custom-call(s32[96]{0:T(128)} %fusion.27.slots_ref, bf16[1,8,1,12,128,128]{5,4,3,2,1,0:T(8,128)(2,1)} %vals_ref.3, bf16[64,128,256]{2,1,0:T(8,128)(2,1)} %constant_dynamic-update-slice_fusion.5.panels_ref, bf16[256,256]{1,0:T(8,128)(2,1)} %weight_ref.1), custom_call_target="tpu_custom_call" | custom-call | flops 2684354560 | bytes 9437184 | tf_op jit(solution)/shard_map/pallas_call | solution.py:172
  103.7 9.5 %collective-permute-start.11 = (f32[4,128,256]{2,1,0:T(8,128)S(1)}, f32[4,128,256]{2,1,0:T(8,128)S(1)}, u32[]{:S(2)}, u32[]{:S(2)}) collective-permute-start(f32[4,128,256]{2,1,0:T(8,128)S(1)} %select_bitcast_fusion.1), channel_id=1, source_target_pairs={{0,64},{64,0},{1,65},{65,1},{2,66},{66,2},{3,67},{67,3},{4,68},{68... | collective-permute-start | bytes 1572872 | tf_op jit(solution)/shard_map/ppermute | solution.py:73
  119.8 6.3 %collective-permute-done.12 = f32[2,128,256]{2,1,0:T(8,128)S(1)} collective-permute-done((f32[2,128,256]{2,1,0:T(8,128)S(1)}, f32[2,128,256]{2,1,0:T(8,128)S(1)}, u32[]{:S(2)}, u32[]{:S(2)}) %collective-permute-start.12) | collective-permute-done | bytes 262176 | tf_op jit(solution)/shard_map/ppermute | solution.py:73
  126.2 7.6 %collective-permute-start.13 = (f32[1,128,256]{2,1,0:T(8,128)S(1)}, f32[1,128,256]{2,1,0:T(8,128)S(1)}, u32[]{:S(2)}, u32[]{:S(2)}) collective-permute-start(f32[1,128,256]{2,1,0:T(8,128)S(1)} %select_bitcast_fusion.5), channel_id=1, source_target_pairs={{0,256},{128,384},{256,0},{384,128},{1,257},{129,385},{257,1},{385... | collective-permute-start | bytes 393224 | tf_op jit(solution)/shard_map/ppermute | solution.py:73
  133.8 6.7 %collective-permute-done.13 = f32[1,128,256]{2,1,0:T(8,128)S(1)} collective-permute-done((f32[1,128,256]{2,1,0:T(8,128)S(1)}, f32[1,128,256]{2,1,0:T(8,128)S(1)}, u32[]{:S(2)}, u32[]{:S(2)}) %collective-permute-start.13) | collective-permute-done | bytes 131104 | tf_op jit(solution)/shard_map/ppermute | solution.py:73
  173.3 9.3 %collective-permute-start.30 = (bf16[4,128,256]{2,1,0:T(8,128)(2,1)S(1)}, bf16[4,128,256]{2,1,0:T(8,128)(2,1)S(1)}, u32[]{:S(2)}, u32[]{:S(2)}) collective-permute-start(bf16[4,128,256]{2,1,0:T(8,128)(2,1)S(1)} %maximum_select_fusion.2), channel_id=1, source_target_pairs={{0,64},{64,0},{1,65},{65,1},{2,66},{66,2},{3,67},{67,3},{4,68},{68... | collective-permute-start | bytes 786440 | tf_op jit(solution)/shard_map/ppermute | solution.py:73
  182.5 4.9 %collective-permute-start.19 = (bf16[8,128,256]{2,1,0:T(8,128)(2,1)S(1)}, bf16[8,128,256]{2,1,0:T(8,128)(2,1)S(1)}, u32[]{:S(2)}, u32[]{:S(2)}) collective-permute-start(bf16[8,128,256]{2,1,0:T(8,128)(2,1)S(1)} %get-tuple-element.11), channel_id=1, source_target_pairs={{0,7},{1,0},{2,1},{3,2},{4,3},{5,4},{6,5},{7,6},{8,15},{9,8},{10,9... | collective-permute-start | bytes 1572872 | tf_op jit(solution)/shard_map/ppermute | solution.py:41
  190.6 8.1 %collective-permute-done.19 = bf16[8,128,256]{2,1,0:T(8,128)(2,1)S(1)} collective-permute-done((bf16[8,128,256]{2,1,0:T(8,128)(2,1)S(1)}, bf16[8,128,256]{2,1,0:T(8,128)(2,1)S(1)}, u32[]{:S(2)}, u32[]{:S(2)}) %collective-permute-start.19) | collective-permute-done | bytes 524320 | tf_op jit(solution)/shard_map/ppermute | solution.py:41
  198.7 5.3 %collective-permute-start.21 = (bf16[8,128,256]{2,1,0:T(8,128)(2,1)S(1)}, bf16[8,128,256]{2,1,0:T(8,128)(2,1)S(1)}, u32[]{:S(2)}, u32[]{:S(2)}) collective-permute-start(bf16[8,128,256]{2,1,0:T(8,128)(2,1)S(1)} %collective-permute-done.19), channel_id=1, source_target_pairs={{0,7},{1,0},{2,1},{3,2},{4,3},{5,4},{6,5},{7,6},{8,15},{9,8},{10,9... | collective-permute-start | bytes 1572872 | tf_op jit(solution)/shard_map/ppermute | solution.py:41
  211.1 5.3 %collective-permute-done.32 = f32[132,256]{1,0:T(8,128)S(1)} collective-permute-done((f32[132,256]{1,0:T(8,128)S(1)}, f32[132,256]{1,0:T(8,128)S(1)}, u32[]{:S(2)}, u32[]{:S(2)}) %collective-permute-start.32) | collective-permute-done | bytes 135200 | tf_op jit(solution)/shard_map/ppermute | solution.py:73
  233.7 5.6 %collective-permute-done.24 = bf16[8,128,256]{2,1,0:T(8,128)(2,1)S(1)} collective-permute-done((bf16[8,128,256]{2,1,0:T(8,128)(2,1)S(1)}, bf16[8,128,256]{2,1,0:T(8,128)(2,1)S(1)}, u32[]{:S(2)}, u32[]{:S(2)}) %collective-permute-start.24) | collective-permute-done | bytes 524320 | tf_op jit(solution)/shard_map/ppermute | solution.py:38
  240.1 8.9 %shard_map.112 = f32[1024,256]{1,0:T(8,128)} custom-call(s32[96]{0:T(128)} %fusion.27.slots_ref, bf16[1,8,1,12,128,128]{5,4,3,2,1,0:T(8,128)(2,1)} %vals_ref.3, bf16[64,128,256]{2,1,0:T(8,128)(2,1)} %constant_dynamic-update-slice_fusion.22.panels_ref), custom_call_target="tpu_custom_call" | custom-call | flops 805306368 | bytes 8388608 | tf_op jit(solution)/shard_map/pallas_call | solution.py:209
  257.1 8.4 %collective-permute-done.35 = f32[132,256]{1,0:T(8,128)S(1)} collective-permute-done((f32[132,256]{1,0:T(8,128)S(1)}, f32[132,256]{1,0:T(8,128)S(1)}, u32[]{:S(2)}, u32[]{:S(2)}) %collective-permute-start.35) | collective-permute-done | bytes 135200 | tf_op jit(solution)/shard_map/ppermute | solution.py:73
  267.7 6.0 %collective-permute-done.36 = f32[132,256]{1,0:T(8,128)S(1)} collective-permute-done((f32[132,256]{1,0:T(8,128)S(1)}, f32[132,256]{1,0:T(8,128)S(1)}, u32[]{:S(2)}, u32[]{:S(2)}) %collective-permute-start.36) | collective-permute-done | bytes 135200 | tf_op jit(solution)/shard_map/ppermute | solution.py:73
  275.7 9.0 %collective-permute-done.37 = f32[132,256]{1,0:T(8,128)S(1)} collective-permute-done((f32[132,256]{1,0:T(8,128)S(1)}, f32[132,256]{1,0:T(8,128)S(1)}, u32[]{:S(2)}, u32[]{:S(2)}) %collective-permute-start.37) | collective-permute-done | bytes 135200 | tf_op jit(solution)/shard_map/ppermute | solution.py:73
  292.2 6.1 %collective-permute-done.38 = f32[132,256]{1,0:T(8,128)S(1)} collective-permute-done((f32[132,256]{1,0:T(8,128)S(1)}, f32[132,256]{1,0:T(8,128)S(1)}, u32[]{:S(2)}, u32[]{:S(2)}) %collective-permute-start.38) | collective-permute-done | bytes 135200 | tf_op jit(solution)/shard_map/ppermute | solution.py:73
  302.3 9.3 %collective-permute-done.39 = f32[132,256]{1,0:T(8,128)S(1)} collective-permute-done((f32[132,256]{1,0:T(8,128)S(1)}, f32[132,256]{1,0:T(8,128)S(1)}, u32[]{:S(2)}, u32[]{:S(2)}) %collective-permute-start.39) | collective-permute-done | bytes 135200 | tf_op jit(solution)/shard_map/ppermute | solution.py:73
  318.1 6.9 %collective-permute-done.27 = f32[1,128,256]{2,1,0:T(8,128)S(1)} collective-permute-done((f32[1,128,256]{2,1,0:T(8,128)S(1)}, f32[1,128,256]{2,1,0:T(8,128)S(1)}, u32[]{:S(2)}, u32[]{:S(2)}) %collective-permute-start.27) | collective-permute-done | bytes 131104 | tf_op jit(solution)/shard_map/ppermute | solution.py:73
  (141 shorter events, 142.7 us)
Async XLA Ops:
  27.9 17.1 %collective-permute-start.4 = (bf16[8,128,256]{2,1,0:T(8,128)(2,1)S(1)}, bf16[8,128,256]{2,1,0:T(8,128)(2,1)S(1)}, u32[]{:S(2)}, u32[]{:S(2)}) collective-permute-start(bf16[8,128,256]{2,1,0:T(8,128)(2,1)S(1)} %get-tuple-element.17), channel_id=1, source_target_pairs={{0,1},{1,2},{2,3},{3,4},{4,5},{5,6},{6,7},{7,0},{8,9},{9,10},{10,1... | collective-permute-start | bytes 1572872 | tf_op jit(solution)/shard_map/ppermute | solution.py:38
  30.5 16.5 %collective-permute-start.5 = (bf16[8,128,256]{2,1,0:T(8,128)(2,1)S(1)}, bf16[8,128,256]{2,1,0:T(8,128)(2,1)S(1)}, u32[]{:S(2)}, u32[]{:S(2)}) collective-permute-start(bf16[8,128,256]{2,1,0:T(8,128)(2,1)S(1)} %get-tuple-element.17), channel_id=1, source_target_pairs={{0,7},{1,0},{2,1},{3,2},{4,3},{5,4},{6,5},{7,6},{8,15},{9,8},{10,9... | collective-permute-start | bytes 1572872 | tf_op jit(solution)/shard_map/ppermute | solution.py:41
  45.0 11.5 %collective-permute-start.6 = (bf16[8,128,256]{2,1,0:T(8,128)(2,1)S(1)}, bf16[8,128,256]{2,1,0:T(8,128)(2,1)S(1)}, u32[]{:S(2)}, u32[]{:S(2)}) collective-permute-start(bf16[8,128,256]{2,1,0:T(8,128)(2,1)S(1)} %collective-permute-done.4), channel_id=1, source_target_pairs={{0,1},{1,2},{2,3},{3,4},{4,5},{5,6},{6,7},{7,0},{8,9},{9,10},{10,1... | collective-permute-start | bytes 1572872 | tf_op jit(solution)/shard_map/ppermute | solution.py:38
  46.9 17.3 %collective-permute-start.7 = (bf16[8,128,256]{2,1,0:T(8,128)(2,1)S(1)}, bf16[8,128,256]{2,1,0:T(8,128)(2,1)S(1)}, u32[]{:S(2)}, u32[]{:S(2)}) collective-permute-start(bf16[8,128,256]{2,1,0:T(8,128)(2,1)S(1)} %collective-permute-done.5), channel_id=1, source_target_pairs={{0,7},{1,0},{2,1},{3,2},{4,3},{5,4},{6,5},{7,6},{8,15},{9,8},{10,9... | collective-permute-start | bytes 1572872 | tf_op jit(solution)/shard_map/ppermute | solution.py:41
  56.5 13.2 %collective-permute-start.8 = (bf16[8,128,256]{2,1,0:T(8,128)(2,1)S(1)}, bf16[8,128,256]{2,1,0:T(8,128)(2,1)S(1)}, u32[]{:S(2)}, u32[]{:S(2)}) collective-permute-start(bf16[8,128,256]{2,1,0:T(8,128)(2,1)S(1)} %collective-permute-done.6), channel_id=1, source_target_pairs={{0,1},{1,2},{2,3},{3,4},{4,5},{5,6},{6,7},{7,0},{8,9},{9,10},{10,1... | collective-permute-start | bytes 1572872 | tf_op jit(solution)/shard_map/ppermute | solution.py:38
  69.7 11.1 %collective-permute-start.10 = (bf16[8,128,256]{2,1,0:T(8,128)(2,1)S(1)}, bf16[8,128,256]{2,1,0:T(8,128)(2,1)S(1)}, u32[]{:S(2)}, u32[]{:S(2)}) collective-permute-start(bf16[8,128,256]{2,1,0:T(8,128)(2,1)S(1)} %collective-permute-done.8), channel_id=1, source_target_pairs={{0,1},{1,2},{2,3},{3,4},{4,5},{5,6},{6,7},{7,0},{8,9},{9,10},{10,1... | collective-permute-start | bytes 1572872 | tf_op jit(solution)/shard_map/ppermute | solution.py:38
  103.7 11.1 %collective-permute-start.11 = (f32[4,128,256]{2,1,0:T(8,128)S(1)}, f32[4,128,256]{2,1,0:T(8,128)S(1)}, u32[]{:S(2)}, u32[]{:S(2)}) collective-permute-start(f32[4,128,256]{2,1,0:T(8,128)S(1)} %select_bitcast_fusion.1), channel_id=1, source_target_pairs={{0,64},{64,0},{1,65},{65,1},{2,66},{66,2},{3,67},{67,3},{4,68},{68... | collective-permute-start | bytes 1572872 | tf_op jit(solution)/shard_map/ppermute | solution.py:73
  126.2 14.3 %collective-permute-start.13 = (f32[1,128,256]{2,1,0:T(8,128)S(1)}, f32[1,128,256]{2,1,0:T(8,128)S(1)}, u32[]{:S(2)}, u32[]{:S(2)}) collective-permute-start(f32[1,128,256]{2,1,0:T(8,128)S(1)} %select_bitcast_fusion.5), channel_id=1, source_target_pairs={{0,256},{128,384},{256,0},{384,128},{1,257},{129,385},{257,1},{385... | collective-permute-start | bytes 393224 | tf_op jit(solution)/shard_map/ppermute | solution.py:73
  164.4 23.2 %collective-permute-start.18 = (bf16[8,128,256]{2,1,0:T(8,128)(2,1)S(1)}, bf16[8,128,256]{2,1,0:T(8,128)(2,1)S(1)}, u32[]{:S(2)}, u32[]{:S(2)}) collective-permute-start(bf16[8,128,256]{2,1,0:T(8,128)(2,1)S(1)} %get-tuple-element.11), channel_id=1, source_target_pairs={{0,1},{1,2},{2,3},{3,4},{4,5},{5,6},{6,7},{7,0},{8,9},{9,10},{10,1... | collective-permute-start | bytes 1572872 | tf_op jit(solution)/shard_map/ppermute | solution.py:38
  173.3 16.2 %collective-permute-start.30 = (bf16[4,128,256]{2,1,0:T(8,128)(2,1)S(1)}, bf16[4,128,256]{2,1,0:T(8,128)(2,1)S(1)}, u32[]{:S(2)}, u32[]{:S(2)}) collective-permute-start(bf16[4,128,256]{2,1,0:T(8,128)(2,1)S(1)} %maximum_select_fusion.2), channel_id=1, source_target_pairs={{0,64},{64,0},{1,65},{65,1},{2,66},{66,2},{3,67},{67,3},{4,68},{68... | collective-permute-start | bytes 786440 | tf_op jit(solution)/shard_map/ppermute | solution.py:73
  182.5 16.2 %collective-permute-start.19 = (bf16[8,128,256]{2,1,0:T(8,128)(2,1)S(1)}, bf16[8,128,256]{2,1,0:T(8,128)(2,1)S(1)}, u32[]{:S(2)}, u32[]{:S(2)}) collective-permute-start(bf16[8,128,256]{2,1,0:T(8,128)(2,1)S(1)} %get-tuple-element.11), channel_id=1, source_target_pairs={{0,7},{1,0},{2,1},{3,2},{4,3},{5,4},{6,5},{7,6},{8,15},{9,8},{10,9... | collective-permute-start | bytes 1572872 | tf_op jit(solution)/shard_map/ppermute | solution.py:41
  187.5 19.6 %collective-permute-start.20 = (bf16[8,128,256]{2,1,0:T(8,128)(2,1)S(1)}, bf16[8,128,256]{2,1,0:T(8,128)(2,1)S(1)}, u32[]{:S(2)}, u32[]{:S(2)}) collective-permute-start(bf16[8,128,256]{2,1,0:T(8,128)(2,1)S(1)} %collective-permute-done.18), channel_id=1, source_target_pairs={{0,1},{1,2},{2,3},{3,4},{4,5},{5,6},{6,7},{7,0},{8,9},{9,10},{10,1... | collective-permute-start | bytes 1572872 | tf_op jit(solution)/shard_map/ppermute | solution.py:38
  198.7 19.6 %collective-permute-start.21 = (bf16[8,128,256]{2,1,0:T(8,128)(2,1)S(1)}, bf16[8,128,256]{2,1,0:T(8,128)(2,1)S(1)}, u32[]{:S(2)}, u32[]{:S(2)}) collective-permute-start(bf16[8,128,256]{2,1,0:T(8,128)(2,1)S(1)} %collective-permute-done.19), channel_id=1, source_target_pairs={{0,7},{1,0},{2,1},{3,2},{4,3},{5,4},{6,5},{7,6},{8,15},{9,8},{10,9... | collective-permute-start | bytes 1572872 | tf_op jit(solution)/shard_map/ppermute | solution.py:41
  207.1 16.6 %collective-permute-start.22 = (bf16[8,128,256]{2,1,0:T(8,128)(2,1)S(1)}, bf16[8,128,256]{2,1,0:T(8,128)(2,1)S(1)}, u32[]{:S(2)}, u32[]{:S(2)}) collective-permute-start(bf16[8,128,256]{2,1,0:T(8,128)(2,1)S(1)} %collective-permute-done.20), channel_id=1, source_target_pairs={{0,1},{1,2},{2,3},{3,4},{4,5},{5,6},{6,7},{7,0},{8,9},{9,10},{10,1... | collective-permute-start | bytes 1572872 | tf_op jit(solution)/shard_map/ppermute | solution.py:38
  218.3 14.5 %collective-permute-start.23 = (bf16[8,128,256]{2,1,0:T(8,128)(2,1)S(1)}, bf16[8,128,256]{2,1,0:T(8,128)(2,1)S(1)}, u32[]{:S(2)}, u32[]{:S(2)}) collective-permute-start(bf16[8,128,256]{2,1,0:T(8,128)(2,1)S(1)} %collective-permute-done.21), channel_id=1, source_target_pairs={{0,7},{1,0},{2,1},{3,2},{4,3},{5,4},{6,5},{7,6},{8,15},{9,8},{10,9... | collective-permute-start | bytes 1572872 | tf_op jit(solution)/shard_map/ppermute | solution.py:41
  223.8 15.5 %collective-permute-start.24 = (bf16[8,128,256]{2,1,0:T(8,128)(2,1)S(1)}, bf16[8,128,256]{2,1,0:T(8,128)(2,1)S(1)}, u32[]{:S(2)}, u32[]{:S(2)}) collective-permute-start(bf16[8,128,256]{2,1,0:T(8,128)(2,1)S(1)} %collective-permute-done.22), channel_id=1, source_target_pairs={{0,1},{1,2},{2,3},{3,4},{4,5},{5,6},{6,7},{7,0},{8,9},{9,10},{10,1... | collective-permute-start | bytes 1572872 | tf_op jit(solution)/shard_map/ppermute | solution.py:38
  226.6 27.7 %collective-permute-start.34 = (f32[132,256]{1,0:T(8,128)S(1)}, f32[132,256]{1,0:T(8,128)S(1)}, u32[]{:S(2)}, u32[]{:S(2)}) collective-permute-start(f32[132,256]{1,0:T(8,128)S(1)} %add.187), channel_id=1, source_target_pairs={{0,1},{1,0},{2,3},{3,2},{4,5},{5,4},{6,7},{7,6},{8,9},{9,8},{10,11... | collective-permute-start | bytes 405512 | tf_op jit(solution)/shard_map/ppermute | solution.py:73
  250.3 38.5 %collective-permute-start.25 = (f32[4,128,256]{2,1,0:T(8,128)S(1)}, f32[4,128,256]{2,1,0:T(8,128)S(1)}, u32[]{:S(2)}, u32[]{:S(2)}) collective-permute-start(f32[4,128,256]{2,1,0:T(8,128)S(1)} %select_bitcast_fusion), channel_id=1, source_target_pairs={{0,64},{64,0},{1,65},{65,1},{2,66},{66,2},{3,67},{67,3},{4,68},{68... | collective-permute-start | bytes 1572872 | tf_op jit(solution)/shard_map/ppermute | solution.py:73
  254.3 11.2 %collective-permute-start.35 = (f32[132,256]{1,0:T(8,128)S(1)}, f32[132,256]{1,0:T(8,128)S(1)}, u32[]{:S(2)}, u32[]{:S(2)}) collective-permute-start(f32[132,256]{1,0:T(8,128)S(1)} %add.188), channel_id=1, source_target_pairs={{0,256},{128,384},{256,0},{384,128},{1,257},{129,385},{257,1},{385... | collective-permute-start | bytes 405512 | tf_op jit(solution)/shard_map/ppermute | solution.py:73
  273.8 11.0 %collective-permute-start.37 = (f32[132,256]{1,0:T(8,128)S(1)}, f32[132,256]{1,0:T(8,128)S(1)}, u32[]{:S(2)}, u32[]{:S(2)}) collective-permute-start(f32[132,256]{1,0:T(8,128)S(1)} %add.190), channel_id=1, source_target_pairs={{0,2},{1,3},{2,0},{3,1},{4,6},{5,7},{6,4},{7,5},{8,10},{9,11},{10,... | collective-permute-start | bytes 405512 | tf_op jit(solution)/shard_map/ppermute | solution.py:73
  284.7 13.5 %collective-permute-start.38 = (f32[132,256]{1,0:T(8,128)S(1)}, f32[132,256]{1,0:T(8,128)S(1)}, u32[]{:S(2)}, u32[]{:S(2)}) collective-permute-start(f32[132,256]{1,0:T(8,128)S(1)} %add.191), channel_id=1, source_target_pairs={{0,4},{1,5},{2,6},{3,7},{4,0},{5,1},{6,2},{7,3},{8,12},{9,13},{10,... | collective-permute-start | bytes 405512 | tf_op jit(solution)/shard_map/ppermute | solution.py:73
  290.2 23.8 %collective-permute-start.26 = (f32[2,128,256]{2,1,0:T(8,128)S(1)}, f32[2,128,256]{2,1,0:T(8,128)S(1)}, u32[]{:S(2)}, u32[]{:S(2)}) collective-permute-start(f32[2,128,256]{2,1,0:T(8,128)S(1)} %select_bitcast_fusion.2), channel_id=1, source_target_pairs={{0,128},{128,0},{256,384},{384,256},{1,129},{129,1},{257,385},{385... | collective-permute-start | bytes 786440 | tf_op jit(solution)/shard_map/ppermute | solution.py:73
  298.2 13.4 %collective-permute-start.39 = (f32[132,256]{1,0:T(8,128)S(1)}, f32[132,256]{1,0:T(8,128)S(1)}, u32[]{:S(2)}, u32[]{:S(2)}) collective-permute-start(f32[132,256]{1,0:T(8,128)S(1)} %add.192), channel_id=1, source_target_pairs={{0,32},{32,0},{1,33},{33,1},{2,34},{34,2},{3,35},{35,3},{4,36},{36... | collective-permute-start | bytes 405512 | tf_op jit(solution)/shard_map/ppermute | solution.py:73
  314.1 10.8 %collective-permute-start.27 = (f32[1,128,256]{2,1,0:T(8,128)S(1)}, f32[1,128,256]{2,1,0:T(8,128)S(1)}, u32[]{:S(2)}, u32[]{:S(2)}) collective-permute-start(f32[1,128,256]{2,1,0:T(8,128)S(1)} %select_bitcast_fusion.4), channel_id=1, source_target_pairs={{0,256},{128,384},{256,0},{384,128},{1,257},{129,385},{257,1},{385... | collective-permute-start | bytes 393224 | tf_op jit(solution)/shard_map/ppermute | solution.py:73
  (23 other events, 478.8 us)

commit v10 on v6

--- a/solution.py
+++ b/solution.py
@@ -123,13 +123,30 @@
     return cur.reshape((-1,) + rows.shape)
 
 
-def collect_kernel(slots_ref, vals_ref, panels_ref, out_ref):
+def collect_kernel(slots_ref, vals_ref, panels_hbm, out_ref, held, sems):
     row = pl.program_id(0)
+    rows = pl.num_programs(0)
     nnz = vals_ref.shape[0]
+
+    def fetch(target, buffer):
+        for k in range(nnz):
+            pltpu.make_async_copy(
+                panels_hbm.at[slots_ref[target * nnz + k]], held.at[buffer, k], sems.at[buffer, k]
+            ).start()
+
+    @pl.when(row == 0)
+    def _():
+        fetch(0, 0)
+
+    @pl.when(row + 1 < rows)
+    def _():
+        fetch(row + 1, (row + 1) % 2)
+
+    current = row % 2
     total = jnp.zeros(out_ref.shape, jnp.float32)
     for k in range(nnz):
-        slot = slots_ref[row * nnz + k]
-        total = total + jnp.dot(vals_ref[k], panels_ref[slot], preferred_element_type=jnp.float32)
+        pltpu.make_async_copy(panels_hbm.at[0], held.at[current, k], sems.at[current, k]).wait()
+        total = total + jnp.dot(vals_ref[k], held[current, k], preferred_element_type=jnp.float32)
     out_ref[...] = total
 
 
@@ -143,18 +160,23 @@
         grid=(rows,),
         in_specs=[
             pl.BlockSpec((None, None, None, nnz, block, block), lambda r, s: (0, r, 0, 0, 0, 0)),
-            pl.BlockSpec(stacked.shape, lambda r, s: (0, 0, 0)),
+            pl.BlockSpec(memory_space=pl.ANY),
         ],
         out_specs=pl.BlockSpec((block, width), lambda r, s: (r, 0)),
+        scratch_shapes=[
+            pltpu.VMEM((2, nnz, block, width), stacked.dtype),
+            pltpu.SemaphoreType.DMA((2, nnz)),
+        ],
     )
     return pl.pallas_call(
         collect_kernel,
         grid_spec=grid_spec,
         out_shape=jax.ShapeDtypeStruct((rows * block, width), jnp.float32),
+        compiler_params=pltpu.CompilerParams(dimension_semantics=("arbitrary",)),
         cost_estimate=pl.CostEstimate(
             flops=2 * rows * nnz * block * block * width,
             transcendentals=0,
-            bytes_accessed=stacked.size * 2 + rows * nnz * block * block * 2 + rows * block * width * 4,
+            bytes_accessed=rows * nnz * block * (block + width) * 2 + rows * block * width * 4,
         ),
     )(slots.reshape(-1), adj_vals, stacked)
 

time: 318 us -> 325 us (1.022)
  Pallas kernels: 26.8 us -> 32.9 us
    pallas_call x3, Pallas kernels: 26.8 us -> 32.9 us  [collect(): pl.pallas_call(collect_kernel, grid_spec=grid_spec, out_shape=jax.ShapeDt...]
  transfers between devices with their start and end apart: 41 -> 41, of which waited for: 20 -> 20; matrix products, arithmetic and copies ran while one was open for 10% -> 10% of each run, Pallas kernels for 6% -> 7%
where the time goes in v10:
time: 325 us; the launch traced here: 323 us
  starting transfers between devices  147 us (45%)
  waiting for transfers between devices  98.8 us (30%)
  Pallas kernels  32.9 us (10%)
  local copies, waits for them, and re-layouts  23.9 us (7%)
  other arithmetic  10.2 us (3%)
  matrix products  8.52 us (3%)
    ppermute x19, starting transfers between devices, swap(): return lax.ppermute(value, axis, [(i, i ^ bit) for i in range(n)])  70.5 us
    ppermute x19, waiting for transfers between devices, swap(): return lax.ppermute(value, axis, [(i, i ^ bit) for i in range(n)])  61.3 us
    ppermute x8, starting transfers between devices, ring_gather(): behind = lax.ppermute(behind, axis, [(i, (i - 1) % n) for i in range(n)])  39.5 us
    ppermute x12, waiting for transfers between devices, ring_gather(): ahead = lax.ppermute(ahead, axis, [(i, (i + 1) % n) for i in range(n)])  34.4 us
    pallas_call x3, Pallas kernels, collect(): pl.pallas_call(collect_kernel, grid_spec=grid_spec, out_shape=jax.ShapeDt...  32.9 us
    ppermute x12, starting transfers between devices, ring_gather(): ahead = lax.ppermute(ahead, axis, [(i, (i + 1) % n) for i in range(n)])  24.8 us
    unnamed x31, local copies, waits for them, and re-layouts  16.7 us
    ppermute x2, starting transfers between devices, gather_team(): other = lax.ppermute(rows, 'y_hi', perm=[(0, 1), (1, 0)])  12.1 us
  transfers between devices with their start and end apart: 41, of which 20 were waited for; matrix products, arithmetic and copies ran while one was open for 10% of the time, Pallas kernels for 7%

profile of v10, /device:TPU:1, one launch (start us, length us, event | category | flops | bytes accessed | tf_op | source)
XLA Modules:
  0.0 322.5 jit_solution(8358233750709438563)
XLA Ops:
  0.7 8.4 %collective-permute-start = (bf16[128,256]{1,0:T(8,128)(2,1)}, bf16[128,256]{1,0:T(8,128)(2,1)S(1)}, u32[]{:S(2)}, u32[]{:S(2)}) collective-permute-start(bf16[128,256]{1,0:T(8,128)(2,1)} %param.8), channel_id=1, source_target_pairs={{0,32},{32,0},{1,33},{33,1},{2,34},{34,2},{3,35},{35,3},{4,36},{36... | collective-permute-start | bytes 196616 | tf_op jit(solution)/shard_map/ppermute | solution.py:47
  22.3 5.1 %collective-permute-done.3 = bf16[2,128,256]{2,1,0:T(8,128)(2,1)S(1)} collective-permute-done((bf16[2,128,256]{2,1,0:T(8,128)(2,1)S(1)}, bf16[2,128,256]{2,1,0:T(8,128)(2,1)S(1)}, u32[]{:S(2)}, u32[]{:S(2)}) %collective-permute-start.3) | collective-permute-done | bytes 131104 | tf_op jit(solution)/shard_map/ppermute | solution.py:38
  30.6 8.6 %collective-permute-start.5 = (bf16[8,128,256]{2,1,0:T(8,128)(2,1)S(1)}, bf16[8,128,256]{2,1,0:T(8,128)(2,1)S(1)}, u32[]{:S(2)}, u32[]{:S(2)}) collective-permute-start(bf16[8,128,256]{2,1,0:T(8,128)(2,1)S(1)} %get-tuple-element.13), channel_id=1, source_target_pairs={{0,7},{1,0},{2,1},{3,2},{4,3},{5,4},{6,5},{7,6},{8,15},{9,8},{10,9... | collective-permute-start | bytes 1572872 | tf_op jit(solution)/shard_map/ppermute | solution.py:41
  39.2 5.9 %collective-permute-done.4 = bf16[8,128,256]{2,1,0:T(8,128)(2,1)S(1)} collective-permute-done((bf16[8,128,256]{2,1,0:T(8,128)(2,1)S(1)}, bf16[8,128,256]{2,1,0:T(8,128)(2,1)S(1)}, u32[]{:S(2)}, u32[]{:S(2)}) %collective-permute-start.4) | collective-permute-done | bytes 524320 | tf_op jit(solution)/shard_map/ppermute | solution.py:38
  51.6 5.0 %collective-permute-done.6 = bf16[8,128,256]{2,1,0:T(8,128)(2,1)S(1)} collective-permute-done((bf16[8,128,256]{2,1,0:T(8,128)(2,1)S(1)}, bf16[8,128,256]{2,1,0:T(8,128)(2,1)S(1)}, u32[]{:S(2)}, u32[]{:S(2)}) %collective-permute-start.6) | collective-permute-done | bytes 524320 | tf_op jit(solution)/shard_map/ppermute | solution.py:38
  75.9 5.0 %collective-permute-done.10 = bf16[8,128,256]{2,1,0:T(8,128)(2,1)S(1)} collective-permute-done((bf16[8,128,256]{2,1,0:T(8,128)(2,1)S(1)}, bf16[8,128,256]{2,1,0:T(8,128)(2,1)S(1)}, u32[]{:S(2)}, u32[]{:S(2)}) %collective-permute-start.10) | collective-permute-done | bytes 524320 | tf_op jit(solution)/shard_map/ppermute | solution.py:38
  81.8 5.5 %convolution_convert_fusion = bf16[8192,256]{1,0:T(8,128)(2,1)} fusion(bf16[8192,256]{1,0:T(8,128)(2,1)} %bitcast.3, bf16[256,256]{1,0:T(8,128)(2,1)S(1)} %copy-done), kind=kOutput, calls=%fused_computation.2 | convolution fusion | flops 1075838976 | bytes 8519680 | tf_op jit(solution)/shard_map/dot_general | solution.py:192
  87.2 11.0 %shard_map.111 = f32[1024,256]{1,0:T(8,128)} custom-call(s32[96]{0:T(128)} %fusion.27.slots_ref, bf16[1,8,1,12,128,128]{5,4,3,2,1,0:T(8,128)(2,1)} %vals_ref.5, bf16[64,128,256]{2,1,0:T(8,128)(2,1)} %bitcast.131), custom_call_target="tpu_custom_call" | custom-call | flops 805306368 | bytes 10485760 | tf_op jit(solution)/shard_map/pallas_call | solution.py:171
  99.5 9.5 %collective-permute-start.11 = (f32[4,128,256]{2,1,0:T(8,128)S(1)}, f32[4,128,256]{2,1,0:T(8,128)S(1)}, u32[]{:S(2)}, u32[]{:S(2)}) collective-permute-start(f32[4,128,256]{2,1,0:T(8,128)S(1)} %select_bitcast_fusion.1), channel_id=1, source_target_pairs={{0,64},{64,0},{1,65},{65,1},{2,66},{66,2},{3,67},{67,3},{4,68},{68... | collective-permute-start | bytes 1572872 | tf_op jit(solution)/shard_map/ppermute | solution.py:73
  115.6 6.3 %collective-permute-done.12 = f32[2,128,256]{2,1,0:T(8,128)S(1)} collective-permute-done((f32[2,128,256]{2,1,0:T(8,128)S(1)}, f32[2,128,256]{2,1,0:T(8,128)S(1)}, u32[]{:S(2)}, u32[]{:S(2)}) %collective-permute-start.12) | collective-permute-done | bytes 262176 | tf_op jit(solution)/shard_map/ppermute | solution.py:73
  122.0 7.6 %collective-permute-start.13 = (f32[1,128,256]{2,1,0:T(8,128)S(1)}, f32[1,128,256]{2,1,0:T(8,128)S(1)}, u32[]{:S(2)}, u32[]{:S(2)}) collective-permute-start(f32[1,128,256]{2,1,0:T(8,128)S(1)} %select_bitcast_fusion.5), channel_id=1, source_target_pairs={{0,256},{128,384},{256,0},{384,128},{1,257},{129,385},{257,1},{385... | collective-permute-start | bytes 393224 | tf_op jit(solution)/shard_map/ppermute | solution.py:73
  129.6 6.7 %collective-permute-done.13 = f32[1,128,256]{2,1,0:T(8,128)S(1)} collective-permute-done((f32[1,128,256]{2,1,0:T(8,128)S(1)}, f32[1,128,256]{2,1,0:T(8,128)S(1)}, u32[]{:S(2)}, u32[]{:S(2)}) %collective-permute-start.13) | collective-permute-done | bytes 131104 | tf_op jit(solution)/shard_map/ppermute | solution.py:73
  166.8 5.4 %collective-permute-start.30 = (bf16[4,128,256]{2,1,0:T(8,128)(2,1)S(1)}, bf16[4,128,256]{2,1,0:T(8,128)(2,1)S(1)}, u32[]{:S(2)}, u32[]{:S(2)}) collective-permute-start(bf16[4,128,256]{2,1,0:T(8,128)(2,1)S(1)} %maximum_select_fusion.2), channel_id=1, source_target_pairs={{0,64},{64,0},{1,65},{65,1},{2,66},{66,2},{3,67},{67,3},{4,68},{68... | collective-permute-start | bytes 786440 | tf_op jit(solution)/shard_map/ppermute | solution.py:73
  172.2 4.9 %collective-permute-start.19 = (bf16[8,128,256]{2,1,0:T(8,128)(2,1)S(1)}, bf16[8,128,256]{2,1,0:T(8,128)(2,1)S(1)}, u32[]{:S(2)}, u32[]{:S(2)}) collective-permute-start(bf16[8,128,256]{2,1,0:T(8,128)(2,1)S(1)} %get-tuple-element.7), channel_id=1, source_target_pairs={{0,7},{1,0},{2,1},{3,2},{4,3},{5,4},{6,5},{7,6},{8,15},{9,8},{10,9... | collective-permute-start | bytes 1572872 | tf_op jit(solution)/shard_map/ppermute | solution.py:41
  177.1 11.0 %shard_map.113 = f32[1024,256]{1,0:T(8,128)} custom-call(s32[96]{0:T(128)} %fusion.27.slots_ref, bf16[1,8,1,12,128,128]{5,4,3,2,1,0:T(8,128)(2,1)} %vals_ref.5, bf16[64,128,256]{2,1,0:T(8,128)(2,1)} %constant_dynamic-update-slice_fusion.5.panels_hbm), custom_call_target="tpu_custom_call" | custom-call | flops 805306368 | bytes 10485760 | tf_op jit(solution)/shard_map/pallas_call | solution.py:171
  229.5 5.0 %collective-permute-done.24 = bf16[8,128,256]{2,1,0:T(8,128)(2,1)S(1)} collective-permute-done((bf16[8,128,256]{2,1,0:T(8,128)(2,1)S(1)}, bf16[8,128,256]{2,1,0:T(8,128)(2,1)S(1)}, u32[]{:S(2)}, u32[]{:S(2)}) %collective-permute-start.24) | collective-permute-done | bytes 524320 | tf_op jit(solution)/shard_map/ppermute | solution.py:38
  235.4 11.0 %shard_map.112 = f32[1024,256]{1,0:T(8,128)} custom-call(s32[96]{0:T(128)} %fusion.27.slots_ref, bf16[1,8,1,12,128,128]{5,4,3,2,1,0:T(8,128)(2,1)} %vals_ref.5, bf16[64,128,256]{2,1,0:T(8,128)(2,1)} %constant_dynamic-update-slice_fusion.22.panels_hbm), custom_call_target="tpu_custom_call" | custom-call | flops 805306368 | bytes 10485760 | tf_op jit(solution)/shard_map/pallas_call | solution.py:171
  247.7 5.1 %collective-permute-start.25 = (f32[4,128,256]{2,1,0:T(8,128)S(1)}, f32[4,128,256]{2,1,0:T(8,128)S(1)}, u32[]{:S(2)}, u32[]{:S(2)}) collective-permute-start(f32[4,128,256]{2,1,0:T(8,128)S(1)} %select_bitcast_fusion), channel_id=1, source_target_pairs={{0,64},{64,0},{1,65},{65,1},{2,66},{66,2},{3,67},{67,3},{4,68},{68... | collective-permute-start | bytes 1572872 | tf_op jit(solution)/shard_map/ppermute | solution.py:73
  255.6 8.3 %collective-permute-done.35 = f32[132,256]{1,0:T(8,128)S(1)} collective-permute-done((f32[132,256]{1,0:T(8,128)S(1)}, f32[132,256]{1,0:T(8,128)S(1)}, u32[]{:S(2)}, u32[]{:S(2)}) %collective-permute-start.35) | collective-permute-done | bytes 135200 | tf_op jit(solution)/shard_map/ppermute | solution.py:73
  266.3 5.4 %collective-permute-done.36 = f32[132,256]{1,0:T(8,128)S(1)} collective-permute-done((f32[132,256]{1,0:T(8,128)S(1)}, f32[132,256]{1,0:T(8,128)S(1)}, u32[]{:S(2)}, u32[]{:S(2)}) %collective-permute-start.36) | collective-permute-done | bytes 135200 | tf_op jit(solution)/shard_map/ppermute | solution.py:73
  273.7 8.8 %collective-permute-done.37 = f32[132,256]{1,0:T(8,128)S(1)} collective-permute-done((f32[132,256]{1,0:T(8,128)S(1)}, f32[132,256]{1,0:T(8,128)S(1)}, u32[]{:S(2)}, u32[]{:S(2)}) %collective-permute-start.37) | collective-permute-done | bytes 135200 | tf_op jit(solution)/shard_map/ppermute | solution.py:73
  289.9 6.0 %collective-permute-done.38 = f32[132,256]{1,0:T(8,128)S(1)} collective-permute-done((f32[132,256]{1,0:T(8,128)S(1)}, f32[132,256]{1,0:T(8,128)S(1)}, u32[]{:S(2)}, u32[]{:S(2)}) %collective-permute-start.38) | collective-permute-done | bytes 135200 | tf_op jit(solution)/shard_map/ppermute | solution.py:73
  299.9 9.4 %collective-permute-done.39 = f32[132,256]{1,0:T(8,128)S(1)} collective-permute-done((f32[132,256]{1,0:T(8,128)S(1)}, f32[132,256]{1,0:T(8,128)S(1)}, u32[]{:S(2)}, u32[]{:S(2)}) %collective-permute-start.39) | collective-permute-done | bytes 135200 | tf_op jit(solution)/shard_map/ppermute | solution.py:73
  315.7 5.9 %collective-permute-done.27 = f32[1,128,256]{2,1,0:T(8,128)S(1)} collective-permute-done((f32[1,128,256]{2,1,0:T(8,128)S(1)}, f32[1,128,256]{2,1,0:T(8,128)S(1)}, u32[]{:S(2)}, u32[]{:S(2)}) %collective-permute-start.27) | collective-permute-done | bytes 131104 | tf_op jit(solution)/shard_map/ppermute | solution.py:73
  (141 shorter events, 150.5 us)
Async XLA Ops:
  28.0 17.1 %collective-permute-start.4 = (bf16[8,128,256]{2,1,0:T(8,128)(2,1)S(1)}, bf16[8,128,256]{2,1,0:T(8,128)(2,1)S(1)}, u32[]{:S(2)}, u32[]{:S(2)}) collective-permute-start(bf16[8,128,256]{2,1,0:T(8,128)(2,1)S(1)} %get-tuple-element.13), channel_id=1, source_target_pairs={{0,1},{1,2},{2,3},{3,4},{4,5},{5,6},{6,7},{7,0},{8,9},{9,10},{10,1... | collective-permute-start | bytes 1572872 | tf_op jit(solution)/shard_map/ppermute | solution.py:38
  30.6 16.5 %collective-permute-start.5 = (bf16[8,128,256]{2,1,0:T(8,128)(2,1)S(1)}, bf16[8,128,256]{2,1,0:T(8,128)(2,1)S(1)}, u32[]{:S(2)}, u32[]{:S(2)}) collective-permute-start(bf16[8,128,256]{2,1,0:T(8,128)(2,1)S(1)} %get-tuple-element.13), channel_id=1, source_target_pairs={{0,7},{1,0},{2,1},{3,2},{4,3},{5,4},{6,5},{7,6},{8,15},{9,8},{10,9... | collective-permute-start | bytes 1572872 | tf_op jit(solution)/shard_map/ppermute | solution.py:41
  45.1 11.5 %collective-permute-start.6 = (bf16[8,128,256]{2,1,0:T(8,128)(2,1)S(1)}, bf16[8,128,256]{2,1,0:T(8,128)(2,1)S(1)}, u32[]{:S(2)}, u32[]{:S(2)}) collective-permute-start(bf16[8,128,256]{2,1,0:T(8,128)(2,1)S(1)} %collective-permute-done.4), channel_id=1, source_target_pairs={{0,1},{1,2},{2,3},{3,4},{4,5},{5,6},{6,7},{7,0},{8,9},{9,10},{10,1... | collective-permute-start | bytes 1572872 | tf_op jit(solution)/shard_map/ppermute | solution.py:38
  47.1 17.3 %collective-permute-start.7 = (bf16[8,128,256]{2,1,0:T(8,128)(2,1)S(1)}, bf16[8,128,256]{2,1,0:T(8,128)(2,1)S(1)}, u32[]{:S(2)}, u32[]{:S(2)}) collective-permute-start(bf16[8,128,256]{2,1,0:T(8,128)(2,1)S(1)} %collective-permute-done.5), channel_id=1, source_target_pairs={{0,7},{1,0},{2,1},{3,2},{4,3},{5,4},{6,5},{7,6},{8,15},{9,8},{10,9... | collective-permute-start | bytes 1572872 | tf_op jit(solution)/shard_map/ppermute | solution.py:41
  56.6 13.2 %collective-permute-start.8 = (bf16[8,128,256]{2,1,0:T(8,128)(2,1)S(1)}, bf16[8,128,256]{2,1,0:T(8,128)(2,1)S(1)}, u32[]{:S(2)}, u32[]{:S(2)}) collective-permute-start(bf16[8,128,256]{2,1,0:T(8,128)(2,1)S(1)} %collective-permute-done.6), channel_id=1, source_target_pairs={{0,1},{1,2},{2,3},{3,4},{4,5},{5,6},{6,7},{7,0},{8,9},{9,10},{10,1... | collective-permute-start | bytes 1572872 | tf_op jit(solution)/shard_map/ppermute | solution.py:38
  69.8 11.1 %collective-permute-start.10 = (bf16[8,128,256]{2,1,0:T(8,128)(2,1)S(1)}, bf16[8,128,256]{2,1,0:T(8,128)(2,1)S(1)}, u32[]{:S(2)}, u32[]{:S(2)}) collective-permute-start(bf16[8,128,256]{2,1,0:T(8,128)(2,1)S(1)} %collective-permute-done.8), channel_id=1, source_target_pairs={{0,1},{1,2},{2,3},{3,4},{4,5},{5,6},{6,7},{7,0},{8,9},{9,10},{10,1... | collective-permute-start | bytes 1572872 | tf_op jit(solution)/shard_map/ppermute | solution.py:38
  99.5 11.1 %collective-permute-start.11 = (f32[4,128,256]{2,1,0:T(8,128)S(1)}, f32[4,128,256]{2,1,0:T(8,128)S(1)}, u32[]{:S(2)}, u32[]{:S(2)}) collective-permute-start(f32[4,128,256]{2,1,0:T(8,128)S(1)} %select_bitcast_fusion.1), channel_id=1, source_target_pairs={{0,64},{64,0},{1,65},{65,1},{2,66},{66,2},{3,67},{67,3},{4,68},{68... | collective-permute-start | bytes 1572872 | tf_op jit(solution)/shard_map/ppermute | solution.py:73
  122.0 14.3 %collective-permute-start.13 = (f32[1,128,256]{2,1,0:T(8,128)S(1)}, f32[1,128,256]{2,1,0:T(8,128)S(1)}, u32[]{:S(2)}, u32[]{:S(2)}) collective-permute-start(f32[1,128,256]{2,1,0:T(8,128)S(1)} %select_bitcast_fusion.5), channel_id=1, source_target_pairs={{0,256},{128,384},{256,0},{384,128},{1,257},{129,385},{257,1},{385... | collective-permute-start | bytes 393224 | tf_op jit(solution)/shard_map/ppermute | solution.py:73
  145.4 11.8 %collective-permute-start.15 = (bf16[2,128,256]{2,1,0:T(8,128)(2,1)S(1)}, bf16[2,128,256]{2,1,0:T(8,128)(2,1)S(1)}, u32[]{:S(2)}, u32[]{:S(2)}) collective-permute-start(bf16[2,128,256]{2,1,0:T(8,128)(2,1)S(1)} %get-tuple-element.20), channel_id=1, source_target_pairs={{0,8},{8,16},{16,24},{24,0},{1,9},{9,17},{17,25},{25,1},{2,10},{10... | collective-permute-start | bytes 393224 | tf_op jit(solution)/shard_map/ppermute | solution.py:38
  147.3 12.4 %collective-permute-start.16 = (bf16[2,128,256]{2,1,0:T(8,128)(2,1)S(1)}, bf16[2,128,256]{2,1,0:T(8,128)(2,1)S(1)}, u32[]{:S(2)}, u32[]{:S(2)}) collective-permute-start(bf16[2,128,256]{2,1,0:T(8,128)(2,1)S(1)} %get-tuple-element.20), channel_id=1, source_target_pairs={{0,24},{8,0},{16,8},{24,16},{1,25},{9,1},{17,9},{25,17},{2,26},{10... | collective-permute-start | bytes 393224 | tf_op jit(solution)/shard_map/ppermute | solution.py:41
  151.9 14.9 %collective-permute-start.29 = (bf16[2,128,256]{2,1,0:T(8,128)(2,1)S(1)}, bf16[2,128,256]{2,1,0:T(8,128)(2,1)S(1)}, u32[]{:S(2)}, u32[]{:S(2)}) collective-permute-start(bf16[2,128,256]{2,1,0:T(8,128)(2,1)S(1)} %get-tuple-element.19), channel_id=1, source_target_pairs={{0,256},{128,384},{256,0},{384,128},{1,257},{129,385},{257,1},{385... | collective-permute-start | bytes 393224 | tf_op jit(solution)/shard_map/ppermute | solution.py:73
  164.9 23.3 %collective-permute-start.18 = (bf16[8,128,256]{2,1,0:T(8,128)(2,1)S(1)}, bf16[8,128,256]{2,1,0:T(8,128)(2,1)S(1)}, u32[]{:S(2)}, u32[]{:S(2)}) collective-permute-start(bf16[8,128,256]{2,1,0:T(8,128)(2,1)S(1)} %get-tuple-element.7), channel_id=1, source_target_pairs={{0,1},{1,2},{2,3},{3,4},{4,5},{5,6},{6,7},{7,0},{8,9},{9,10},{10,1... | collective-permute-start | bytes 1572872 | tf_op jit(solution)/shard_map/ppermute | solution.py:38
  166.8 23.3 %collective-permute-start.30 = (bf16[4,128,256]{2,1,0:T(8,128)(2,1)S(1)}, bf16[4,128,256]{2,1,0:T(8,128)(2,1)S(1)}, u32[]{:S(2)}, u32[]{:S(2)}) collective-permute-start(bf16[4,128,256]{2,1,0:T(8,128)(2,1)S(1)} %maximum_select_fusion.2), channel_id=1, source_target_pairs={{0,64},{64,0},{1,65},{65,1},{2,66},{66,2},{3,67},{67,3},{4,68},{68... | collective-permute-start | bytes 786440 | tf_op jit(solution)/shard_map/ppermute | solution.py:73
  172.2 20.3 %collective-permute-start.19 = (bf16[8,128,256]{2,1,0:T(8,128)(2,1)S(1)}, bf16[8,128,256]{2,1,0:T(8,128)(2,1)S(1)}, u32[]{:S(2)}, u32[]{:S(2)}) collective-permute-start(bf16[8,128,256]{2,1,0:T(8,128)(2,1)S(1)} %get-tuple-element.7), channel_id=1, source_target_pairs={{0,7},{1,0},{2,1},{3,2},{4,3},{5,4},{6,5},{7,6},{8,15},{9,8},{10,9... | collective-permute-start | bytes 1572872 | tf_op jit(solution)/shard_map/ppermute | solution.py:41
  188.2 16.3 %collective-permute-start.20 = (bf16[8,128,256]{2,1,0:T(8,128)(2,1)S(1)}, bf16[8,128,256]{2,1,0:T(8,128)(2,1)S(1)}, u32[]{:S(2)}, u32[]{:S(2)}) collective-permute-start(bf16[8,128,256]{2,1,0:T(8,128)(2,1)S(1)} %collective-permute-done.18), channel_id=1, source_target_pairs={{0,1},{1,2},{2,3},{3,4},{4,5},{5,6},{6,7},{7,0},{8,9},{9,10},{10,1... | collective-permute-start | bytes 1572872 | tf_op jit(solution)/shard_map/ppermute | solution.py:38
  192.5 22.5 %collective-permute-start.21 = (bf16[8,128,256]{2,1,0:T(8,128)(2,1)S(1)}, bf16[8,128,256]{2,1,0:T(8,128)(2,1)S(1)}, u32[]{:S(2)}, u32[]{:S(2)}) collective-permute-start(bf16[8,128,256]{2,1,0:T(8,128)(2,1)S(1)} %collective-permute-done.19), channel_id=1, source_target_pairs={{0,7},{1,0},{2,1},{3,2},{4,3},{5,4},{6,5},{7,6},{8,15},{9,8},{10,9... | collective-permute-start | bytes 1572872 | tf_op jit(solution)/shard_map/ppermute | solution.py:41
  204.5 15.8 %collective-permute-start.22 = (bf16[8,128,256]{2,1,0:T(8,128)(2,1)S(1)}, bf16[8,128,256]{2,1,0:T(8,128)(2,1)S(1)}, u32[]{:S(2)}, u32[]{:S(2)}) collective-permute-start(bf16[8,128,256]{2,1,0:T(8,128)(2,1)S(1)} %collective-permute-done.20), channel_id=1, source_target_pairs={{0,1},{1,2},{2,3},{3,4},{4,5},{5,6},{6,7},{7,0},{8,9},{9,10},{10,1... | collective-permute-start | bytes 1572872 | tf_op jit(solution)/shard_map/ppermute | solution.py:38
  215.0 13.6 %collective-permute-start.23 = (bf16[8,128,256]{2,1,0:T(8,128)(2,1)S(1)}, bf16[8,128,256]{2,1,0:T(8,128)(2,1)S(1)}, u32[]{:S(2)}, u32[]{:S(2)}) collective-permute-start(bf16[8,128,256]{2,1,0:T(8,128)(2,1)S(1)} %collective-permute-done.21), channel_id=1, source_target_pairs={{0,7},{1,0},{2,1},{3,2},{4,3},{5,4},{6,5},{7,6},{8,15},{9,8},{10,9... | collective-permute-start | bytes 1572872 | tf_op jit(solution)/shard_map/ppermute | solution.py:41
  220.3 14.3 %collective-permute-start.24 = (bf16[8,128,256]{2,1,0:T(8,128)(2,1)S(1)}, bf16[8,128,256]{2,1,0:T(8,128)(2,1)S(1)}, u32[]{:S(2)}, u32[]{:S(2)}) collective-permute-start(bf16[8,128,256]{2,1,0:T(8,128)(2,1)S(1)} %collective-permute-done.22), channel_id=1, source_target_pairs={{0,1},{1,2},{2,3},{3,4},{4,5},{5,6},{6,7},{7,0},{8,9},{9,10},{10,1... | collective-permute-start | bytes 1572872 | tf_op jit(solution)/shard_map/ppermute | solution.py:38
  223.1 29.7 %collective-permute-start.34 = (f32[132,256]{1,0:T(8,128)S(1)}, f32[132,256]{1,0:T(8,128)S(1)}, u32[]{:S(2)}, u32[]{:S(2)}) collective-permute-start(f32[132,256]{1,0:T(8,128)S(1)} %add.187), channel_id=1, source_target_pairs={{0,1},{1,0},{2,3},{3,2},{4,5},{5,4},{6,7},{7,6},{8,9},{9,8},{10,11... | collective-permute-start | bytes 405512 | tf_op jit(solution)/shard_map/ppermute | solution.py:73
  247.7 38.9 %collective-permute-start.25 = (f32[4,128,256]{2,1,0:T(8,128)S(1)}, f32[4,128,256]{2,1,0:T(8,128)S(1)}, u32[]{:S(2)}, u32[]{:S(2)}) collective-permute-start(f32[4,128,256]{2,1,0:T(8,128)S(1)} %select_bitcast_fusion), channel_id=1, source_target_pairs={{0,64},{64,0},{1,65},{65,1},{2,66},{66,2},{3,67},{67,3},{4,68},{68... | collective-permute-start | bytes 1572872 | tf_op jit(solution)/shard_map/ppermute | solution.py:73
  282.5 13.5 %collective-permute-start.38 = (f32[132,256]{1,0:T(8,128)S(1)}, f32[132,256]{1,0:T(8,128)S(1)}, u32[]{:S(2)}, u32[]{:S(2)}) collective-permute-start(f32[132,256]{1,0:T(8,128)S(1)} %add.191), channel_id=1, source_target_pairs={{0,4},{1,5},{2,6},{3,7},{4,0},{5,1},{6,2},{7,3},{8,12},{9,13},{10,... | collective-permute-start | bytes 405512 | tf_op jit(solution)/shard_map/ppermute | solution.py:73
  288.0 23.7 %collective-permute-start.26 = (f32[2,128,256]{2,1,0:T(8,128)S(1)}, f32[2,128,256]{2,1,0:T(8,128)S(1)}, u32[]{:S(2)}, u32[]{:S(2)}) collective-permute-start(f32[2,128,256]{2,1,0:T(8,128)S(1)} %select_bitcast_fusion.2), channel_id=1, source_target_pairs={{0,128},{128,0},{256,384},{384,256},{1,129},{129,1},{257,385},{385... | collective-permute-start | bytes 786440 | tf_op jit(solution)/shard_map/ppermute | solution.py:73
  296.0 13.3 %collective-permute-start.39 = (f32[132,256]{1,0:T(8,128)S(1)}, f32[132,256]{1,0:T(8,128)S(1)}, u32[]{:S(2)}, u32[]{:S(2)}) collective-permute-start(f32[132,256]{1,0:T(8,128)S(1)} %add.192), channel_id=1, source_target_pairs={{0,32},{32,0},{1,33},{33,1},{2,34},{34,2},{3,35},{35,3},{4,36},{36... | collective-permute-start | bytes 405512 | tf_op jit(solution)/shard_map/ppermute | solution.py:73
  (22 other events, 424.7 us)

commit v11 on v8

--- a/solution.py
+++ b/solution.py
@@ -34,9 +34,10 @@
         self.value = value
         self.steps = list(steps)
 
-    def tick(self, values):
-        if self.steps:
-            self.value = self.steps.pop(0)(self.value)
+    def tick(self, values, count=1):
+        for _ in range(count):
+            if self.steps:
+                self.value = self.steps.pop(0)(self.value)
         values, self.value = lax.optimization_barrier((values, self.value))
         return values
 
@@ -46,7 +47,7 @@
         return self.value
 
 
-def ring_gather(blocks, axis, chain=None):
+def ring_gather(blocks, axis, chain=None, per_round=1):
     n = SIZES[axis]
     ahead = blocks
     behind = blocks
@@ -56,7 +57,7 @@
         if step < n - step:
             behind = lax.ppermute(behind, axis, [(i, (i - 1) % n) for i in range(n)])
         if chain is not None:
-            ahead, behind = chain.tick((ahead, behind))
+            ahead, behind = chain.tick((ahead, behind), per_round)
         parts.append(ahead)
         if step < n - step:
             parts.append(behind)
@@ -68,7 +69,7 @@
     if chain is not None:
         other = chain.tick(other)
     pair = jnp.stack([rows, other], axis=0)
-    full = ring_gather(ring_gather(pair, "x", chain), "z", chain)
+    full = ring_gather(ring_gather(pair, "x", chain), "z", chain, 2)
     return full.reshape(-1, rows.shape[1])
 
 

time: 314 us -> 312 us (level)
  starting transfers between devices: 168 us -> 160 us
  waiting for transfers between devices: 90.3 us -> 95.9 us
    ppermute x19, waiting for transfers between devices: 54.1 us -> 68.8 us  [swap(): return lax.ppermute(value, axis, [(i, i ^ bit) for i in range(n)])]
    ppermute x19, starting transfers between devices: 85.8 us -> 78.6 us  [swap(): return lax.ppermute(value, axis, [(i, i ^ bit) for i in range(n)])]
    ppermute x12, waiting for transfers between devices: 30.1 us -> 24.4 us  [ring_gather(): ahead = lax.ppermute(ahead, axis, [(i, (i + 1) % n) for i in range(n)])]
    ppermute x8, waiting for transfers between devices: 3.31 us -> 0.02 us  [ring_gather(): behind = lax.ppermute(behind, axis, [(i, (i - 1) % n) for i in range(n)])]
  transfers between devices with their start and end apart: 41 -> 41, of which waited for: 25 -> 23; matrix products, arithmetic and copies ran while one was open for 9% -> 8% of each run, Pallas kernels for 0% -> 0%
where the time goes in v11:
time: 312 us; the launch traced here: 310 us
  starting transfers between devices  160 us (51%)
  waiting for transfers between devices  95.9 us (31%)
  local copies, waits for them, and re-layouts  23.7 us (8%)
  Pallas kernels  17.8 us (6%)
  other arithmetic  7.74 us (2%)
  matrix products  3.71 us (1%)
    ppermute x19, starting transfers between devices, swap(): return lax.ppermute(value, axis, [(i, i ^ bit) for i in range(n)])  78.6 us
    ppermute x19, waiting for transfers between devices, swap(): return lax.ppermute(value, axis, [(i, i ^ bit) for i in range(n)])  68.8 us
    ppermute x8, starting transfers between devices, ring_gather(): behind = lax.ppermute(behind, axis, [(i, (i - 1) % n) for i in range(n)])  38 us
    ppermute x12, starting transfers between devices, ring_gather(): ahead = lax.ppermute(ahead, axis, [(i, (i + 1) % n) for i in range(n)])  27.9 us
    ppermute x12, waiting for transfers between devices, ring_gather(): ahead = lax.ppermute(ahead, axis, [(i, (i + 1) % n) for i in range(n)])  24.4 us
    pallas_call x2, Pallas kernels, collect(): pl.pallas_call(collect_kernel, grid_spec=grid_spec, out_shape=jax.ShapeDt...  17.8 us
    unnamed x33, local copies, waits for them, and re-layouts  16.6 us
    ppermute x2, starting transfers between devices, gather_team(): other = lax.ppermute(rows, 'y_hi', perm=[(0, 1), (1, 0)])  15.1 us
  transfers between devices with their start and end apart: 41, of which 23 were waited for; matrix products, arithmetic and copies ran while one was open for 8% of the time, Pallas kernels for 0%

profile of v11, /device:TPU:1, one launch (start us, length us, event | category | flops | bytes accessed | tf_op | source)
XLA Modules:
  0.0 309.7 jit_solution(2629292925896139284)
XLA Ops:
  0.7 8.4 %collective-permute-start = (bf16[128,256]{1,0:T(8,128)(2,1)}, bf16[128,256]{1,0:T(8,128)(2,1)S(1)}, u32[]{:S(2)}, u32[]{:S(2)}) collective-permute-start(bf16[128,256]{1,0:T(8,128)(2,1)} %param.8), channel_id=1, source_target_pairs={{0,32},{32,0},{1,33},{33,1},{2,34},{34,2},{3,35},{35,3},{4,36},{36... | collective-permute-start | bytes 196616 | tf_op jit(solution)/shard_map/ppermute | solution.py:68
  34.8 8.6 %collective-permute-start.5 = (bf16[8,128,256]{2,1,0:T(8,128)(2,1)S(1)}, bf16[8,128,256]{2,1,0:T(8,128)(2,1)S(1)}, u32[]{:S(2)}, u32[]{:S(2)}) collective-permute-start(bf16[8,128,256]{2,1,0:T(8,128)(2,1)S(1)} %get-tuple-element.49), channel_id=1, source_target_pairs={{0,7},{1,0},{2,1},{3,2},{4,3},{5,4},{6,5},{7,6},{8,15},{9,8},{10,9... | collective-permute-start | bytes 1572872 | tf_op jit(solution)/shard_map/ppermute | solution.py:58
  43.4 5.4 %collective-permute-done.4 = bf16[8,128,256]{2,1,0:T(8,128)(2,1)S(1)} collective-permute-done((bf16[8,128,256]{2,1,0:T(8,128)(2,1)S(1)}, bf16[8,128,256]{2,1,0:T(8,128)(2,1)S(1)}, u32[]{:S(2)}, u32[]{:S(2)}) %collective-permute-start.4) | collective-permute-done | bytes 524320 | tf_op jit(solution)/shard_map/ppermute | solution.py:56
  55.3 4.6 %collective-permute-done.6 = bf16[8,128,256]{2,1,0:T(8,128)(2,1)S(1)} collective-permute-done((bf16[8,128,256]{2,1,0:T(8,128)(2,1)S(1)}, bf16[8,128,256]{2,1,0:T(8,128)(2,1)S(1)}, u32[]{:S(2)}, u32[]{:S(2)}) %collective-permute-start.6) | collective-permute-done | bytes 524320 | tf_op jit(solution)/shard_map/ppermute | solution.py:56
  79.2 5.0 %collective-permute-done.10 = bf16[8,128,256]{2,1,0:T(8,128)(2,1)S(1)} collective-permute-done((bf16[8,128,256]{2,1,0:T(8,128)(2,1)S(1)}, bf16[8,128,256]{2,1,0:T(8,128)(2,1)S(1)}, u32[]{:S(2)}, u32[]{:S(2)}) %collective-permute-start.10) | collective-permute-done | bytes 524320 | tf_op jit(solution)/shard_map/ppermute | solution.py:56
  85.0 8.9 %shard_map.111 = f32[1024,256]{1,0:T(8,128)} custom-call(s32[96]{0:T(128)} %fusion.27.slots_ref, bf16[1,8,1,12,128,128]{5,4,3,2,1,0:T(8,128)(2,1)} %vals_ref.3, bf16[64,128,256]{2,1,0:T(8,128)(2,1)} %constant_dynamic-update-slice_fusion.5.panels_ref), custom_call_target="tpu_custom_call" | custom-call | flops 805306368 | bytes 8388608 | tf_op jit(solution)/shard_map/pallas_call | solution.py:187
  95.9 10.7 %collective-permute-start.11 = (f32[4,128,256]{2,1,0:T(8,128)S(1)}, f32[4,128,256]{2,1,0:T(8,128)S(1)}, u32[]{:S(2)}, u32[]{:S(2)}) collective-permute-start(f32[4,128,256]{2,1,0:T(8,128)S(1)} %select_bitcast_fusion.1), channel_id=1, source_target_pairs={{0,64},{64,0},{1,65},{65,1},{2,66},{66,2},{3,67},{67,3},{4,68},{68... | collective-permute-start | bytes 1572872 | tf_op jit(solution)/shard_map/ppermute | solution.py:96
  111.1 6.5 %collective-permute-done.12 = f32[2,128,256]{2,1,0:T(8,128)S(1)} collective-permute-done((f32[2,128,256]{2,1,0:T(8,128)S(1)}, f32[2,128,256]{2,1,0:T(8,128)S(1)}, u32[]{:S(2)}, u32[]{:S(2)}) %collective-permute-start.12) | collective-permute-done | bytes 262176 | tf_op jit(solution)/shard_map/ppermute | solution.py:96
  117.8 6.8 %collective-permute-start.13 = (f32[1,128,256]{2,1,0:T(8,128)S(1)}, f32[1,128,256]{2,1,0:T(8,128)S(1)}, u32[]{:S(2)}, u32[]{:S(2)}) collective-permute-start(f32[1,128,256]{2,1,0:T(8,128)S(1)} %select_bitcast_fusion.5), channel_id=1, source_target_pairs={{0,256},{128,384},{256,0},{384,128},{1,257},{129,385},{257,1},{385... | collective-permute-start | bytes 393224 | tf_op jit(solution)/shard_map/ppermute | solution.py:96
  124.6 6.7 %collective-permute-done.13 = f32[1,128,256]{2,1,0:T(8,128)S(1)} collective-permute-done((f32[1,128,256]{2,1,0:T(8,128)S(1)}, f32[1,128,256]{2,1,0:T(8,128)S(1)}, u32[]{:S(2)}, u32[]{:S(2)}) %collective-permute-start.13) | collective-permute-done | bytes 131104 | tf_op jit(solution)/shard_map/ppermute | solution.py:96
  133.5 6.7 %collective-permute-start.14 = (bf16[128,256]{1,0:T(8,128)(2,1)S(1)}, bf16[128,256]{1,0:T(8,128)(2,1)S(1)}, u32[]{:S(2)}, u32[]{:S(2)}) collective-permute-start(bf16[128,256]{1,0:T(8,128)(2,1)S(1)} %get-tuple-element.41), channel_id=1, source_target_pairs={{0,32},{32,0},{1,33},{33,1},{2,34},{34,2},{3,35},{35,3},{4,36},{36... | collective-permute-start | bytes 196616 | tf_op jit(solution)/shard_map/ppermute | solution.py:68
  147.8 5.0 %collective-permute-start.18 = (bf16[2,128,256]{2,1,0:T(8,128)(2,1)S(1)}, bf16[2,128,256]{2,1,0:T(8,128)(2,1)S(1)}, u32[]{:S(2)}, u32[]{:S(2)}) collective-permute-start(bf16[2,128,256]{2,1,0:T(8,128)(2,1)S(1)} %fusion.3), channel_id=1, source_target_pairs={{0,256},{128,384},{256,0},{384,128},{1,257},{129,385},{257,1},{385... | collective-permute-start | bytes 393224 | tf_op jit(solution)/shard_map/ppermute | solution.py:96
  155.2 5.4 %collective-permute-start.20 = (bf16[4,128,256]{2,1,0:T(8,128)(2,1)S(1)}, bf16[4,128,256]{2,1,0:T(8,128)(2,1)S(1)}, u32[]{:S(2)}, u32[]{:S(2)}) collective-permute-start(bf16[4,128,256]{2,1,0:T(8,128)(2,1)S(1)} %maximum_select_fusion.2), channel_id=1, source_target_pairs={{0,64},{64,0},{1,65},{65,1},{2,66},{66,2},{3,67},{67,3},{4,68},{68... | collective-permute-start | bytes 786440 | tf_op jit(solution)/shard_map/ppermute | solution.py:96
  170.2 4.8 %collective-permute-start.23 = (bf16[8,128,256]{2,1,0:T(8,128)(2,1)S(1)}, bf16[8,128,256]{2,1,0:T(8,128)(2,1)S(1)}, u32[]{:S(2)}, u32[]{:S(2)}) collective-permute-start(bf16[8,128,256]{2,1,0:T(8,128)(2,1)S(1)} %get-tuple-element.43), channel_id=1, source_target_pairs={{0,7},{1,0},{2,1},{3,2},{4,3},{5,4},{6,5},{7,6},{8,15},{9,8},{10,9... | collective-permute-start | bytes 1572872 | tf_op jit(solution)/shard_map/ppermute | solution.py:58
  198.9 9.8 %collective-permute-done.28 = f32[132,256]{1,0:T(8,128)S(1)} collective-permute-done((f32[132,256]{1,0:T(8,128)S(1)}, f32[132,256]{1,0:T(8,128)S(1)}, u32[]{:S(2)}, u32[]{:S(2)}) %collective-permute-start.28) | collective-permute-done | bytes 135200 | tf_op jit(solution)/shard_map/ppermute | solution.py:96
  210.6 5.2 %collective-permute-done.29 = f32[132,256]{1,0:T(8,128)S(1)} collective-permute-done((f32[132,256]{1,0:T(8,128)S(1)}, f32[132,256]{1,0:T(8,128)S(1)}, u32[]{:S(2)}, u32[]{:S(2)}) %collective-permute-start.29) | collective-permute-done | bytes 135200 | tf_op jit(solution)/shard_map/ppermute | solution.py:96
  217.8 4.6 %collective-permute-start.31 = (bf16[8,128,256]{2,1,0:T(8,128)(2,1)S(1)}, bf16[8,128,256]{2,1,0:T(8,128)(2,1)S(1)}, u32[]{:S(2)}, u32[]{:S(2)}) collective-permute-start(bf16[8,128,256]{2,1,0:T(8,128)(2,1)S(1)} %collective-permute-done.27), channel_id=1, source_target_pairs={{0,7},{1,0},{2,1},{3,2},{4,3},{5,4},{6,5},{7,6},{8,15},{9,8},{10,9... | collective-permute-start | bytes 1572872 | tf_op jit(solution)/shard_map/ppermute | solution.py:58
  239.2 5.8 %collective-permute-start.35 = (f32[132,256]{1,0:T(8,128)S(1)}, f32[132,256]{1,0:T(8,128)S(1)}, u32[]{:S(2)}, u32[]{:S(2)}) collective-permute-start(f32[132,256]{1,0:T(8,128)S(1)} %add.188), channel_id=1, source_target_pairs={{0,4},{1,5},{2,6},{3,7},{4,0},{5,1},{6,2},{7,3},{8,12},{9,13},{10,... | collective-permute-start | bytes 405512 | tf_op jit(solution)/shard_map/ppermute | solution.py:96
  246.7 7.5 %collective-permute-done.35 = f32[132,256]{1,0:T(8,128)S(1)} collective-permute-done((f32[132,256]{1,0:T(8,128)S(1)}, f32[132,256]{1,0:T(8,128)S(1)}, u32[]{:S(2)}, u32[]{:S(2)}) %collective-permute-start.35) | collective-permute-done | bytes 135200 | tf_op jit(solution)/shard_map/ppermute | solution.py:96
  254.3 6.8 %collective-permute-start.36 = (f32[132,256]{1,0:T(8,128)S(1)}, f32[132,256]{1,0:T(8,128)S(1)}, u32[]{:S(2)}, u32[]{:S(2)}) collective-permute-start(f32[132,256]{1,0:T(8,128)S(1)} %add.189), channel_id=1, source_target_pairs={{0,32},{32,0},{1,33},{33,1},{2,34},{34,2},{3,35},{35,3},{4,36},{36... | collective-permute-start | bytes 405512 | tf_op jit(solution)/shard_map/ppermute | solution.py:96
  264.9 8.9 %shard_map.112 = f32[1024,256]{1,0:T(8,128)} custom-call(s32[96]{0:T(128)} %fusion.27.slots_ref, bf16[1,8,1,12,128,128]{5,4,3,2,1,0:T(8,128)(2,1)} %vals_ref.3, bf16[64,128,256]{2,1,0:T(8,128)(2,1)} %constant_dynamic-update-slice_fusion.22.panels_ref), custom_call_target="tpu_custom_call" | custom-call | flops 805306368 | bytes 8388608 | tf_op jit(solution)/shard_map/pallas_call | solution.py:187
  275.0 10.5 %collective-permute-start.37 = (f32[4,128,256]{2,1,0:T(8,128)S(1)}, f32[4,128,256]{2,1,0:T(8,128)S(1)}, u32[]{:S(2)}, u32[]{:S(2)}) collective-permute-start(f32[4,128,256]{2,1,0:T(8,128)S(1)} %select_bitcast_fusion), channel_id=1, source_target_pairs={{0,64},{64,0},{1,65},{65,1},{2,66},{66,2},{3,67},{67,3},{4,68},{68... | collective-permute-start | bytes 1572872 | tf_op jit(solution)/shard_map/ppermute | solution.py:96
  292.7 5.2 %collective-permute-done.38 = f32[2,128,256]{2,1,0:T(8,128)S(1)} collective-permute-done((f32[2,128,256]{2,1,0:T(8,128)S(1)}, f32[2,128,256]{2,1,0:T(8,128)S(1)}, u32[]{:S(2)}, u32[]{:S(2)}) %collective-permute-start.38) | collective-permute-done | bytes 262176 | tf_op jit(solution)/shard_map/ppermute | solution.py:96
  302.5 6.4 %collective-permute-done.39 = f32[1,128,256]{2,1,0:T(8,128)S(1)} collective-permute-done((f32[1,128,256]{2,1,0:T(8,128)S(1)}, f32[1,128,256]{2,1,0:T(8,128)S(1)}, u32[]{:S(2)}, u32[]{:S(2)}) %collective-permute-start.39) | collective-permute-done | bytes 131104 | tf_op jit(solution)/shard_map/ppermute | solution.py:96
  (143 shorter events, 143.9 us)
Async XLA Ops:
  11.9 13.9 %collective-permute-start.2 = (bf16[2,128,256]{2,1,0:T(8,128)(2,1)S(1)}, bf16[2,128,256]{2,1,0:T(8,128)(2,1)S(1)}, u32[]{:S(2)}, u32[]{:S(2)}) collective-permute-start(bf16[2,128,256]{2,1,0:T(8,128)(2,1)S(1)} %pad_maximum_fusion.3), channel_id=1, source_target_pairs={{0,24},{8,0},{16,8},{24,16},{1,25},{9,1},{17,9},{25,17},{2,26},{10... | collective-permute-start | bytes 393224 | tf_op jit(solution)/shard_map/ppermute | solution.py:58
  30.8 18.0 %collective-permute-start.4 = (bf16[8,128,256]{2,1,0:T(8,128)(2,1)S(1)}, bf16[8,128,256]{2,1,0:T(8,128)(2,1)S(1)}, u32[]{:S(2)}, u32[]{:S(2)}) collective-permute-start(bf16[8,128,256]{2,1,0:T(8,128)(2,1)S(1)} %get-tuple-element.49), channel_id=1, source_target_pairs={{0,1},{1,2},{2,3},{3,4},{4,5},{5,6},{6,7},{7,0},{8,9},{9,10},{10,1... | collective-permute-start | bytes 1572872 | tf_op jit(solution)/shard_map/ppermute | solution.py:56
  34.8 15.9 %collective-permute-start.5 = (bf16[8,128,256]{2,1,0:T(8,128)(2,1)S(1)}, bf16[8,128,256]{2,1,0:T(8,128)(2,1)S(1)}, u32[]{:S(2)}, u32[]{:S(2)}) collective-permute-start(bf16[8,128,256]{2,1,0:T(8,128)(2,1)S(1)} %get-tuple-element.49), channel_id=1, source_target_pairs={{0,7},{1,0},{2,1},{3,2},{4,3},{5,4},{6,5},{7,6},{8,15},{9,8},{10,9... | collective-permute-start | bytes 1572872 | tf_op jit(solution)/shard_map/ppermute | solution.py:58
  48.8 11.1 %collective-permute-start.6 = (bf16[8,128,256]{2,1,0:T(8,128)(2,1)S(1)}, bf16[8,128,256]{2,1,0:T(8,128)(2,1)S(1)}, u32[]{:S(2)}, u32[]{:S(2)}) collective-permute-start(bf16[8,128,256]{2,1,0:T(8,128)(2,1)S(1)} %collective-permute-done.4), channel_id=1, source_target_pairs={{0,1},{1,2},{2,3},{3,4},{4,5},{5,6},{6,7},{7,0},{8,9},{9,10},{10,1... | collective-permute-start | bytes 1572872 | tf_op jit(solution)/shard_map/ppermute | solution.py:56
  50.7 17.0 %collective-permute-start.7 = (bf16[8,128,256]{2,1,0:T(8,128)(2,1)S(1)}, bf16[8,128,256]{2,1,0:T(8,128)(2,1)S(1)}, u32[]{:S(2)}, u32[]{:S(2)}) collective-permute-start(bf16[8,128,256]{2,1,0:T(8,128)(2,1)S(1)} %collective-permute-done.5), channel_id=1, source_target_pairs={{0,7},{1,0},{2,1},{3,2},{4,3},{5,4},{6,5},{7,6},{8,15},{9,8},{10,9... | collective-permute-start | bytes 1572872 | tf_op jit(solution)/shard_map/ppermute | solution.py:58
  59.9 13.2 %collective-permute-start.8 = (bf16[8,128,256]{2,1,0:T(8,128)(2,1)S(1)}, bf16[8,128,256]{2,1,0:T(8,128)(2,1)S(1)}, u32[]{:S(2)}, u32[]{:S(2)}) collective-permute-start(bf16[8,128,256]{2,1,0:T(8,128)(2,1)S(1)} %collective-permute-done.6), channel_id=1, source_target_pairs={{0,1},{1,2},{2,3},{3,4},{4,5},{5,6},{6,7},{7,0},{8,9},{9,10},{10,1... | collective-permute-start | bytes 1572872 | tf_op jit(solution)/shard_map/ppermute | solution.py:56
  67.7 10.7 %collective-permute-start.9 = (bf16[8,128,256]{2,1,0:T(8,128)(2,1)S(1)}, bf16[8,128,256]{2,1,0:T(8,128)(2,1)S(1)}, u32[]{:S(2)}, u32[]{:S(2)}) collective-permute-start(bf16[8,128,256]{2,1,0:T(8,128)(2,1)S(1)} %collective-permute-done.7), channel_id=1, source_target_pairs={{0,7},{1,0},{2,1},{3,2},{4,3},{5,4},{6,5},{7,6},{8,15},{9,8},{10,9... | collective-permute-start | bytes 1572872 | tf_op jit(solution)/shard_map/ppermute | solution.py:58
  73.1 11.1 %collective-permute-start.10 = (bf16[8,128,256]{2,1,0:T(8,128)(2,1)S(1)}, bf16[8,128,256]{2,1,0:T(8,128)(2,1)S(1)}, u32[]{:S(2)}, u32[]{:S(2)}) collective-permute-start(bf16[8,128,256]{2,1,0:T(8,128)(2,1)S(1)} %collective-permute-done.8), channel_id=1, source_target_pairs={{0,1},{1,2},{2,3},{3,4},{4,5},{5,6},{6,7},{7,0},{8,9},{9,10},{10,1... | collective-permute-start | bytes 1572872 | tf_op jit(solution)/shard_map/ppermute | solution.py:56
  95.9 12.2 %collective-permute-start.11 = (f32[4,128,256]{2,1,0:T(8,128)S(1)}, f32[4,128,256]{2,1,0:T(8,128)S(1)}, u32[]{:S(2)}, u32[]{:S(2)}) collective-permute-start(f32[4,128,256]{2,1,0:T(8,128)S(1)} %select_bitcast_fusion.1), channel_id=1, source_target_pairs={{0,64},{64,0},{1,65},{65,1},{2,66},{66,2},{3,67},{67,3},{4,68},{68... | collective-permute-start | bytes 1572872 | tf_op jit(solution)/shard_map/ppermute | solution.py:96
  117.8 13.6 %collective-permute-start.13 = (f32[1,128,256]{2,1,0:T(8,128)S(1)}, f32[1,128,256]{2,1,0:T(8,128)S(1)}, u32[]{:S(2)}, u32[]{:S(2)}) collective-permute-start(f32[1,128,256]{2,1,0:T(8,128)S(1)} %select_bitcast_fusion.5), channel_id=1, source_target_pairs={{0,256},{128,384},{256,0},{384,128},{1,257},{129,385},{257,1},{385... | collective-permute-start | bytes 393224 | tf_op jit(solution)/shard_map/ppermute | solution.py:96
  142.5 12.7 %collective-permute-start.17 = (bf16[2,128,256]{2,1,0:T(8,128)(2,1)S(1)}, bf16[2,128,256]{2,1,0:T(8,128)(2,1)S(1)}, u32[]{:S(2)}, u32[]{:S(2)}) collective-permute-start(bf16[2,128,256]{2,1,0:T(8,128)(2,1)S(1)} %pad_maximum_fusion), channel_id=1, source_target_pairs={{0,24},{8,0},{16,8},{24,16},{1,25},{9,1},{17,9},{25,17},{2,26},{10... | collective-permute-start | bytes 393224 | tf_op jit(solution)/shard_map/ppermute | solution.py:58
  144.4 10.8 %collective-permute-start.16 = (bf16[2,128,256]{2,1,0:T(8,128)(2,1)S(1)}, bf16[2,128,256]{2,1,0:T(8,128)(2,1)S(1)}, u32[]{:S(2)}, u32[]{:S(2)}) collective-permute-start(bf16[2,128,256]{2,1,0:T(8,128)(2,1)S(1)} %pad_maximum_fusion), channel_id=1, source_target_pairs={{0,8},{8,16},{16,24},{24,0},{1,9},{9,17},{17,25},{25,1},{2,10},{10... | collective-permute-start | bytes 393224 | tf_op jit(solution)/shard_map/ppermute | solution.py:56
  170.2 19.0 %collective-permute-start.23 = (bf16[8,128,256]{2,1,0:T(8,128)(2,1)S(1)}, bf16[8,128,256]{2,1,0:T(8,128)(2,1)S(1)}, u32[]{:S(2)}, u32[]{:S(2)}) collective-permute-start(bf16[8,128,256]{2,1,0:T(8,128)(2,1)S(1)} %get-tuple-element.43), channel_id=1, source_target_pairs={{0,7},{1,0},{2,1},{3,2},{4,3},{5,4},{6,5},{7,6},{8,15},{9,8},{10,9... | collective-permute-start | bytes 1572872 | tf_op jit(solution)/shard_map/ppermute | solution.py:58
  175.0 15.4 %collective-permute-start.22 = (bf16[8,128,256]{2,1,0:T(8,128)(2,1)S(1)}, bf16[8,128,256]{2,1,0:T(8,128)(2,1)S(1)}, u32[]{:S(2)}, u32[]{:S(2)}) collective-permute-start(bf16[8,128,256]{2,1,0:T(8,128)(2,1)S(1)} %get-tuple-element.43), channel_id=1, source_target_pairs={{0,1},{1,2},{2,3},{3,4},{4,5},{5,6},{6,7},{7,0},{8,9},{9,10},{10,1... | collective-permute-start | bytes 1572872 | tf_op jit(solution)/shard_map/ppermute | solution.py:56
  190.5 25.4 %collective-permute-start.26 = (bf16[8,128,256]{2,1,0:T(8,128)(2,1)S(1)}, bf16[8,128,256]{2,1,0:T(8,128)(2,1)S(1)}, u32[]{:S(2)}, u32[]{:S(2)}) collective-permute-start(bf16[8,128,256]{2,1,0:T(8,128)(2,1)S(1)} %collective-permute-done.22), channel_id=1, source_target_pairs={{0,1},{1,2},{2,3},{3,4},{4,5},{5,6},{6,7},{7,0},{8,9},{9,10},{10,1... | collective-permute-start | bytes 1572872 | tf_op jit(solution)/shard_map/ppermute | solution.py:56
  192.4 23.5 %collective-permute-start.27 = (bf16[8,128,256]{2,1,0:T(8,128)(2,1)S(1)}, bf16[8,128,256]{2,1,0:T(8,128)(2,1)S(1)}, u32[]{:S(2)}, u32[]{:S(2)}) collective-permute-start(bf16[8,128,256]{2,1,0:T(8,128)(2,1)S(1)} %collective-permute-done.23), channel_id=1, source_target_pairs={{0,7},{1,0},{2,1},{3,2},{4,3},{5,4},{6,5},{7,6},{8,15},{9,8},{10,9... | collective-permute-start | bytes 1572872 | tf_op jit(solution)/shard_map/ppermute | solution.py:58
  197.0 11.7 %collective-permute-start.28 = (f32[132,256]{1,0:T(8,128)S(1)}, f32[132,256]{1,0:T(8,128)S(1)}, u32[]{:S(2)}, u32[]{:S(2)}) collective-permute-start(f32[132,256]{1,0:T(8,128)S(1)} %add.184), channel_id=1, source_target_pairs={{0,1},{1,0},{2,3},{3,2},{4,5},{5,4},{6,7},{7,6},{8,9},{9,8},{10,11... | collective-permute-start | bytes 405512 | tf_op jit(solution)/shard_map/ppermute | solution.py:96
  215.9 20.6 %collective-permute-start.30 = (bf16[8,128,256]{2,1,0:T(8,128)(2,1)S(1)}, bf16[8,128,256]{2,1,0:T(8,128)(2,1)S(1)}, u32[]{:S(2)}, u32[]{:S(2)}) collective-permute-start(bf16[8,128,256]{2,1,0:T(8,128)(2,1)S(1)} %collective-permute-done.26), channel_id=1, source_target_pairs={{0,1},{1,2},{2,3},{3,4},{4,5},{5,6},{6,7},{7,0},{8,9},{9,10},{10,1... | collective-permute-start | bytes 1572872 | tf_op jit(solution)/shard_map/ppermute | solution.py:56
  217.8 18.6 %collective-permute-start.31 = (bf16[8,128,256]{2,1,0:T(8,128)(2,1)S(1)}, bf16[8,128,256]{2,1,0:T(8,128)(2,1)S(1)}, u32[]{:S(2)}, u32[]{:S(2)}) collective-permute-start(bf16[8,128,256]{2,1,0:T(8,128)(2,1)S(1)} %collective-permute-done.27), channel_id=1, source_target_pairs={{0,7},{1,0},{2,1},{3,2},{4,3},{5,4},{6,5},{7,6},{8,15},{9,8},{10,9... | collective-permute-start | bytes 1572872 | tf_op jit(solution)/shard_map/ppermute | solution.py:58
  236.5 27.6 %collective-permute-start.34 = (bf16[8,128,256]{2,1,0:T(8,128)(2,1)S(1)}, bf16[8,128,256]{2,1,0:T(8,128)(2,1)S(1)}, u32[]{:S(2)}, u32[]{:S(2)}) collective-permute-start(bf16[8,128,256]{2,1,0:T(8,128)(2,1)S(1)} %collective-permute-done.30), channel_id=1, source_target_pairs={{0,1},{1,2},{2,3},{3,4},{4,5},{5,6},{6,7},{7,0},{8,9},{9,10},{10,1... | collective-permute-start | bytes 1572872 | tf_op jit(solution)/shard_map/ppermute | solution.py:56
  239.2 15.0 %collective-permute-start.35 = (f32[132,256]{1,0:T(8,128)S(1)}, f32[132,256]{1,0:T(8,128)S(1)}, u32[]{:S(2)}, u32[]{:S(2)}) collective-permute-start(f32[132,256]{1,0:T(8,128)S(1)} %add.188), channel_id=1, source_target_pairs={{0,4},{1,5},{2,6},{3,7},{4,0},{5,1},{6,2},{7,3},{8,12},{9,13},{10,... | collective-permute-start | bytes 405512 | tf_op jit(solution)/shard_map/ppermute | solution.py:96
  275.0 12.1 %collective-permute-start.37 = (f32[4,128,256]{2,1,0:T(8,128)S(1)}, f32[4,128,256]{2,1,0:T(8,128)S(1)}, u32[]{:S(2)}, u32[]{:S(2)}) collective-permute-start(f32[4,128,256]{2,1,0:T(8,128)S(1)} %select_bitcast_fusion), channel_id=1, source_target_pairs={{0,64},{64,0},{1,65},{65,1},{2,66},{66,2},{3,67},{67,3},{4,68},{68... | collective-permute-start | bytes 1572872 | tf_op jit(solution)/shard_map/ppermute | solution.py:96
  290.4 10.8 %collective-permute-start.40 = (f32[132,256]{1,0:T(8,128)S(1)}, f32[132,256]{1,0:T(8,128)S(1)}, u32[]{:S(2)}, u32[]{:S(2)}) collective-permute-start(f32[132,256]{1,0:T(8,128)S(1)} %add.190), channel_id=1, source_target_pairs={{0,64},{64,0},{1,65},{65,1},{2,66},{66,2},{3,67},{67,3},{4,68},{68... | collective-permute-start | bytes 405512 | tf_op jit(solution)/shard_map/ppermute | solution.py:96
  297.9 11.0 %collective-permute-start.39 = (f32[1,128,256]{2,1,0:T(8,128)S(1)}, f32[1,128,256]{2,1,0:T(8,128)S(1)}, u32[]{:S(2)}, u32[]{:S(2)}) collective-permute-start(f32[1,128,256]{2,1,0:T(8,128)S(1)} %select_bitcast_fusion.4), channel_id=1, source_target_pairs={{0,256},{128,384},{256,0},{384,128},{1,257},{129,385},{257,1},{385... | collective-permute-start | bytes 393224 | tf_op jit(solution)/shard_map/ppermute | solution.py:96
  (23 other events, 487.8 us)

commit v12 on v11

--- a/solution.py
+++ b/solution.py
@@ -1,3 +1,5 @@
+import functools
+
 import jax
 import jax.numpy as jnp
 from jax import lax
@@ -47,7 +49,7 @@
         return self.value
 
 
-def ring_gather(blocks, axis, chain=None, per_round=1):
+def ring_gather(blocks, axis, chain=None, per_round=1, join=True):
     n = SIZES[axis]
     ahead = blocks
     behind = blocks
@@ -61,7 +63,7 @@
         parts.append(ahead)
         if step < n - step:
             parts.append(behind)
-    return jnp.concatenate(parts, axis=0)
+    return jnp.concatenate(parts, axis=0) if join else parts
 
 
 def gather_team(rows, chain=None):
@@ -69,8 +71,7 @@
     if chain is not None:
         other = chain.tick(other)
     pair = jnp.stack([rows, other], axis=0)
-    full = ring_gather(ring_gather(pair, "x", chain), "z", chain, 2)
-    return full.reshape(-1, rows.shape[1])
+    return ring_gather(ring_gather(pair, "x", chain), "z", chain, 2, join=False)
 
 
 def ring_slot(delta, axis):
@@ -160,40 +161,59 @@
     return steps
 
 
-def collect_kernel(slots_ref, vals_ref, panels_ref, out_ref):
+def collect_kernel(count, slots_ref, vals_ref, *refs):
+    parts = refs[:count]
+    out_ref, held, sems = refs[count:]
     row = pl.program_id(0)
     nnz = vals_ref.shape[0]
+    size = held.shape[0] // count
+
+    @pl.when(row == 0)
+    def _():
+        copies = [
+            pltpu.make_async_copy(parts[i], held.at[pl.ds(i * size, size)], sems.at[i])
+            for i in range(count)
+        ]
+        for copy in copies:
+            copy.start()
+        for copy in copies:
+            copy.wait()
+
     total = jnp.zeros(out_ref.shape, jnp.float32)
     for k in range(nnz):
         slot = slots_ref[row * nnz + k]
-        total = total + jnp.dot(vals_ref[k], panels_ref[slot], preferred_element_type=jnp.float32)
+        total = total + jnp.dot(vals_ref[k], held[slot], preferred_element_type=jnp.float32)
     out_ref[...] = total
 
 
-def collect(panels, slots, adj_vals):
+def collect(parts, slots, adj_vals):
     block = adj_vals.shape[-1]
-    width = panels.shape[1]
+    width = parts[0].shape[-1]
     rows, nnz = slots.shape
-    stacked = panels.reshape(panels.shape[0] // block, block, width)
+    count = len(parts)
+    panels = count * parts[0].shape[0]
     grid_spec = pltpu.PrefetchScalarGridSpec(
         num_scalar_prefetch=1,
         grid=(rows,),
-        in_specs=[
-            pl.BlockSpec((None, None, None, nnz, block, block), lambda r, s: (0, r, 0, 0, 0, 0)),
-            pl.BlockSpec(stacked.shape, lambda r, s: (0, 0, 0)),
+        in_specs=[pl.BlockSpec((None, None, None, nnz, block, block), lambda r, s: (0, r, 0, 0, 0, 0))]
+        + [pl.BlockSpec(memory_space=pl.ANY)] * count,
+        out_specs=pl.BlockSpec((block, width), lambda r, s: (r, 0)),
+        scratch_shapes=[
+            pltpu.VMEM((panels, block, width), parts[0].dtype),
+            pltpu.SemaphoreType.DMA((count,)),
         ],
-        out_specs=pl.BlockSpec((block, width), lambda r, s: (r, 0)),
     )
     return pl.pallas_call(
-        collect_kernel,
+        functools.partial(collect_kernel, count),
         grid_spec=grid_spec,
         out_shape=jax.ShapeDtypeStruct((rows * block, width), jnp.float32),
+        compiler_params=pltpu.CompilerParams(dimension_semantics=("arbitrary",)),
         cost_estimate=pl.CostEstimate(
             flops=2 * rows * nnz * block * block * width,
             transcendentals=0,
-            bytes_accessed=stacked.size * 2 + rows * nnz * block * block * 2 + rows * block * width * 4,
+            bytes_accessed=panels * block * width * 2 + rows * nnz * block * block * 2 + rows * block * width * 4,
         ),
-    )(slots.reshape(-1), adj_vals, stacked)
+    )(slots.reshape(-1), adj_vals, *parts)
 
 
 def activation(value):

time: 312 us -> 309 us (level)
  local copies, waits for them, and re-layouts: 23.7 us -> 5.63 us
  waiting for transfers between devices: 95.9 us -> 108 us
    unnamed x33 -> x47, local copies, waits for them, and re-layouts: 16.6 us -> 1.53 us
    ppermute x12, waiting for transfers between devices: 24.4 us -> 35.9 us  [ring_gather(): ahead = lax.ppermute(ahead, axis, [(i, (i + 1) % n) for i in range(n)])]
  transfers between devices with their start and end apart: 41 -> 41, of which waited for: 23 -> 27; matrix products, arithmetic and copies ran while one was open for 8% -> 3% of each run, Pallas kernels for 0% -> 0%
where the time goes in v12:
time: 309 us; the launch traced here: 306 us
  starting transfers between devices  160 us (52%)
  waiting for transfers between devices  108 us (35%)
  Pallas kernels  19.7 us (6%)
  other arithmetic  7.72 us (2%)
  local copies, waits for them, and re-layouts  5.63 us (2%)
  matrix products  3.67 us (1%)
    ppermute x19, starting transfers between devices, swap(): return lax.ppermute(value, axis, [(i, i ^ bit) for i in range(n)])  79.8 us
    ppermute x19, waiting for transfers between devices, swap(): return lax.ppermute(value, axis, [(i, i ^ bit) for i in range(n)])  68.6 us
    ppermute x8, starting transfers between devices, ring_gather(): behind = lax.ppermute(behind, axis, [(i, (i - 1) % n) for i in range(n)])  36.7 us
    ppermute x12, waiting for transfers between devices, ring_gather(): ahead = lax.ppermute(ahead, axis, [(i, (i + 1) % n) for i in range(n)])  35.9 us
    ppermute x12, starting transfers between devices, ring_gather(): ahead = lax.ppermute(ahead, axis, [(i, (i + 1) % n) for i in range(n)])  26.9 us
    pallas_call x2, Pallas kernels, collect(): pl.pallas_call(functools.partial(collect_kernel, count), grid_spec=grid_s...  19.7 us
    ppermute x2, starting transfers between devices, gather_team(): other = lax.ppermute(rows, 'y_hi', perm=[(0, 1), (1, 0)])  16.3 us
  transfers between devices with their start and end apart: 41, of which 27 were waited for; matrix products, arithmetic and copies ran while one was open for 3% of the time, Pallas kernels for 0%

profile of v12, /device:TPU:1, one launch (start us, length us, event | category | flops | bytes accessed | tf_op | source)
XLA Modules:
  0.0 305.6 jit_solution(4314795900325680352)
XLA Ops:
  0.7 8.4 %collective-permute-start = (bf16[128,256]{1,0:T(8,128)(2,1)}, bf16[128,256]{1,0:T(8,128)(2,1)S(1)}, u32[]{:S(2)}, u32[]{:S(2)}) collective-permute-start(bf16[128,256]{1,0:T(8,128)(2,1)} %param.8), channel_id=1, source_target_pairs={{0,32},{32,0},{1,33},{33,1},{2,34},{34,2},{3,35},{35,3},{4,36},{36... | collective-permute-start | bytes 196616 | tf_op jit(solution)/shard_map/ppermute | solution.py:70
  18.2 5.0 %collective-permute-done.1 = bf16[2,128,256]{2,1,0:T(8,128)(2,1)S(1)} collective-permute-done((bf16[2,128,256]{2,1,0:T(8,128)(2,1)S(1)}, bf16[2,128,256]{2,1,0:T(8,128)(2,1)S(1)}, u32[]{:S(2)}, u32[]{:S(2)}) %collective-permute-start.1) | collective-permute-done | bytes 131104 | tf_op jit(solution)/shard_map/ppermute | solution.py:58
  25.2 4.9 %collective-permute-done.3 = bf16[2,128,256]{2,1,0:T(8,128)(2,1)S(1)} collective-permute-done((bf16[2,128,256]{2,1,0:T(8,128)(2,1)S(1)}, bf16[2,128,256]{2,1,0:T(8,128)(2,1)S(1)}, u32[]{:S(2)}, u32[]{:S(2)}) %collective-permute-start.3) | collective-permute-done | bytes 131104 | tf_op jit(solution)/shard_map/ppermute | solution.py:58
  34.1 8.6 %collective-permute-start.5 = (bf16[8,128,256]{2,1,0:T(8,128)(2,1)S(1)}, bf16[8,128,256]{2,1,0:T(8,128)(2,1)S(1)}, u32[]{:S(2)}, u32[]{:S(2)}) collective-permute-start(bf16[8,128,256]{2,1,0:T(8,128)(2,1)S(1)} %constant_dynamic-update-slice_fusion.refs_0_), channel_id=1, source_target_pairs={{0,7},{1,0},{2,1},{3,2},{4,3},{5,4},{6,5},{7,6},{8,15},{9,8},{10,9... | collective-permute-start | bytes 1572872 | tf_op jit(solution)/shard_map/ppermute | solution.py:60
  42.7 5.4 %collective-permute-done.4.refs_1_ = bf16[8,128,256]{2,1,0:T(8,128)(2,1)S(1)} collective-permute-done((bf16[8,128,256]{2,1,0:T(8,128)(2,1)S(1)}, bf16[8,128,256]{2,1,0:T(8,128)(2,1)S(1)}, u32[]{:S(2)}, u32[]{:S(2)}) %collective-permute-start.4) | collective-permute-done | bytes 524320 | tf_op jit(solution)/shard_map/ppermute | solution.py:58
  54.7 4.6 %collective-permute-done.6.refs_3_ = bf16[8,128,256]{2,1,0:T(8,128)(2,1)S(1)} collective-permute-done((bf16[8,128,256]{2,1,0:T(8,128)(2,1)S(1)}, bf16[8,128,256]{2,1,0:T(8,128)(2,1)S(1)}, u32[]{:S(2)}, u32[]{:S(2)}) %collective-permute-start.6) | collective-permute-done | bytes 524320 | tf_op jit(solution)/shard_map/ppermute | solution.py:58
  63.2 4.6 %collective-permute-start.9 = (bf16[8,128,256]{2,1,0:T(8,128)(2,1)S(1)}, bf16[8,128,256]{2,1,0:T(8,128)(2,1)}, u32[]{:S(2)}, u32[]{:S(2)}) collective-permute-start(bf16[8,128,256]{2,1,0:T(8,128)(2,1)S(1)} %collective-permute-done.7.refs_4_), channel_id=1, source_target_pairs={{0,7},{1,0},{2,1},{3,2},{4,3},{5,4},{6,5},{7,6},{8,15},{9,8},{10,9... | collective-permute-start | bytes 1572872 | tf_op jit(solution)/shard_map/ppermute | solution.py:60
  76.8 6.9 %collective-permute-done.10.refs_7_ = bf16[8,128,256]{2,1,0:T(8,128)(2,1)} collective-permute-done((bf16[8,128,256]{2,1,0:T(8,128)(2,1)S(1)}, bf16[8,128,256]{2,1,0:T(8,128)(2,1)}, u32[]{:S(2)}, u32[]{:S(2)}) %collective-permute-start.10) | collective-permute-done | bytes 524320 | tf_op jit(solution)/shard_map/ppermute | solution.py:58
  83.7 9.8 %shard_map.111 = f32[1024,256]{1,0:T(8,128)} custom-call(s32[96]{0:T(128)} %fusion.27.slots_ref, bf16[1,8,1,12,128,128]{5,4,3,2,1,0:T(8,128)(2,1)} %vals_ref.3, bf16[8,128,256]{2,1,0:T(8,128)(2,1)} %copy-done.4, bf16[8,128,256]{2,1,0:T(8,128)(2,1)} %copy-done.8, bf16[8,128,256]{2,1,0:T(8,128)(2,1)} %copy-done.9, bf16[8,128,256]{2,1,0:T(8,128)(2,1)} %copy-done.11, ...), custom_call_target="tpu_custom_call" | custom-call | flops 805306368 | bytes 8388608 | tf_op jit(solution)/shard_map/pallas_call | solution.py:206
  95.4 10.7 %collective-permute-start.11 = (f32[4,128,256]{2,1,0:T(8,128)S(1)}, f32[4,128,256]{2,1,0:T(8,128)S(1)}, u32[]{:S(2)}, u32[]{:S(2)}) collective-permute-start(f32[4,128,256]{2,1,0:T(8,128)S(1)} %select_bitcast_fusion.1), channel_id=1, source_target_pairs={{0,64},{64,0},{1,65},{65,1},{2,66},{66,2},{3,67},{67,3},{4,68},{68... | collective-permute-start | bytes 1572872 | tf_op jit(solution)/shard_map/ppermute | solution.py:97
  110.1 7.3 %collective-permute-done.12 = f32[2,128,256]{2,1,0:T(8,128)S(1)} collective-permute-done((f32[2,128,256]{2,1,0:T(8,128)S(1)}, f32[2,128,256]{2,1,0:T(8,128)S(1)}, u32[]{:S(2)}, u32[]{:S(2)}) %collective-permute-start.12) | collective-permute-done | bytes 262176 | tf_op jit(solution)/shard_map/ppermute | solution.py:97
  117.5 5.6 %collective-permute-start.13 = (f32[1,128,256]{2,1,0:T(8,128)S(1)}, f32[1,128,256]{2,1,0:T(8,128)S(1)}, u32[]{:S(2)}, u32[]{:S(2)}) collective-permute-start(f32[1,128,256]{2,1,0:T(8,128)S(1)} %select_bitcast_fusion.5), channel_id=1, source_target_pairs={{0,256},{128,384},{256,0},{384,128},{1,257},{129,385},{257,1},{385... | collective-permute-start | bytes 393224 | tf_op jit(solution)/shard_map/ppermute | solution.py:97
  123.1 6.7 %collective-permute-done.13 = f32[1,128,256]{2,1,0:T(8,128)S(1)} collective-permute-done((f32[1,128,256]{2,1,0:T(8,128)S(1)}, f32[1,128,256]{2,1,0:T(8,128)S(1)}, u32[]{:S(2)}, u32[]{:S(2)}) %collective-permute-start.13) | collective-permute-done | bytes 131104 | tf_op jit(solution)/shard_map/ppermute | solution.py:97
  131.9 7.9 %collective-permute-start.14 = (bf16[128,256]{1,0:T(8,128)(2,1)S(1)}, bf16[128,256]{1,0:T(8,128)(2,1)S(1)}, u32[]{:S(2)}, u32[]{:S(2)}) collective-permute-start(bf16[128,256]{1,0:T(8,128)(2,1)S(1)} %get-tuple-element.41), channel_id=1, source_target_pairs={{0,32},{32,0},{1,33},{33,1},{2,34},{34,2},{3,35},{35,3},{4,36},{36... | collective-permute-start | bytes 196616 | tf_op jit(solution)/shard_map/ppermute | solution.py:70
  155.0 5.0 %collective-permute-start.20 = (bf16[4,128,256]{2,1,0:T(8,128)(2,1)S(1)}, bf16[4,128,256]{2,1,0:T(8,128)(2,1)S(1)}, u32[]{:S(2)}, u32[]{:S(2)}) collective-permute-start(bf16[4,128,256]{2,1,0:T(8,128)(2,1)S(1)} %maximum_select_fusion.2), channel_id=1, source_target_pairs={{0,64},{64,0},{1,65},{65,1},{2,66},{66,2},{3,67},{67,3},{4,68},{68... | collective-permute-start | bytes 786440 | tf_op jit(solution)/shard_map/ppermute | solution.py:97
  194.4 8.8 %collective-permute-done.28 = f32[132,256]{1,0:T(8,128)S(1)} collective-permute-done((f32[132,256]{1,0:T(8,128)S(1)}, f32[132,256]{1,0:T(8,128)S(1)}, u32[]{:S(2)}, u32[]{:S(2)}) %collective-permute-start.28) | collective-permute-done | bytes 135200 | tf_op jit(solution)/shard_map/ppermute | solution.py:97
  216.5 5.2 %collective-permute-start.32 = (f32[132,256]{1,0:T(8,128)S(1)}, f32[132,256]{1,0:T(8,128)S(1)}, u32[]{:S(2)}, u32[]{:S(2)}) collective-permute-start(f32[132,256]{1,0:T(8,128)S(1)} %add.186), channel_id=1, source_target_pairs={{0,16},{8,24},{16,0},{24,8},{1,17},{9,25},{17,1},{25,9},{2,18},{10... | collective-permute-start | bytes 405512 | tf_op jit(solution)/shard_map/ppermute | solution.py:97
  227.5 6.1 %collective-permute-done.33 = f32[132,256]{1,0:T(8,128)S(1)} collective-permute-done((f32[132,256]{1,0:T(8,128)S(1)}, f32[132,256]{1,0:T(8,128)S(1)}, u32[]{:S(2)}, u32[]{:S(2)}) %collective-permute-start.33) | collective-permute-done | bytes 135200 | tf_op jit(solution)/shard_map/ppermute | solution.py:97
  235.6 4.9 %collective-permute-start.35 = (f32[132,256]{1,0:T(8,128)S(1)}, f32[132,256]{1,0:T(8,128)S(1)}, u32[]{:S(2)}, u32[]{:S(2)}) collective-permute-start(f32[132,256]{1,0:T(8,128)S(1)} %add.188), channel_id=1, source_target_pairs={{0,4},{1,5},{2,6},{3,7},{4,0},{5,1},{6,2},{7,3},{8,12},{9,13},{10,... | collective-permute-start | bytes 405512 | tf_op jit(solution)/shard_map/ppermute | solution.py:97
  240.5 9.4 %collective-permute-done.35 = f32[132,256]{1,0:T(8,128)S(1)} collective-permute-done((f32[132,256]{1,0:T(8,128)S(1)}, f32[132,256]{1,0:T(8,128)S(1)}, u32[]{:S(2)}, u32[]{:S(2)}) %collective-permute-start.35) | collective-permute-done | bytes 135200 | tf_op jit(solution)/shard_map/ppermute | solution.py:97
  249.9 7.6 %collective-permute-start.36 = (f32[132,256]{1,0:T(8,128)S(1)}, f32[132,256]{1,0:T(8,128)S(1)}, u32[]{:S(2)}, u32[]{:S(2)}) collective-permute-start(f32[132,256]{1,0:T(8,128)S(1)} %add.189), channel_id=1, source_target_pairs={{0,32},{32,0},{1,33},{33,1},{2,34},{34,2},{3,35},{35,3},{4,36},{36... | collective-permute-start | bytes 405512 | tf_op jit(solution)/shard_map/ppermute | solution.py:97
  260.1 9.8 %shard_map.112 = f32[1024,256]{1,0:T(8,128)} custom-call(s32[96]{0:T(128)} %fusion.27.slots_ref, bf16[1,8,1,12,128,128]{5,4,3,2,1,0:T(8,128)(2,1)} %vals_ref.3, bf16[8,128,256]{2,1,0:T(8,128)(2,1)} %copy-done.5, bf16[8,128,256]{2,1,0:T(8,128)(2,1)} %copy-done.7, bf16[8,128,256]{2,1,0:T(8,128)(2,1)} %copy-done.6, bf16[8,128,256]{2,1,0:T(8,128)(2,1)} %copy-done.10, ...), custom_call_target="tpu_custom_call" | custom-call | flops 805306368 | bytes 8388608 | tf_op jit(solution)/shard_map/pallas_call | solution.py:206
  271.2 10.7 %collective-permute-start.37 = (f32[4,128,256]{2,1,0:T(8,128)S(1)}, f32[4,128,256]{2,1,0:T(8,128)S(1)}, u32[]{:S(2)}, u32[]{:S(2)}) collective-permute-start(f32[4,128,256]{2,1,0:T(8,128)S(1)} %select_bitcast_fusion), channel_id=1, source_target_pairs={{0,64},{64,0},{1,65},{65,1},{2,66},{66,2},{3,67},{67,3},{4,68},{68... | collective-permute-start | bytes 1572872 | tf_op jit(solution)/shard_map/ppermute | solution.py:97
  289.2 5.0 %collective-permute-done.38 = f32[2,128,256]{2,1,0:T(8,128)S(1)} collective-permute-done((f32[2,128,256]{2,1,0:T(8,128)S(1)}, f32[2,128,256]{2,1,0:T(8,128)S(1)}, u32[]{:S(2)}, u32[]{:S(2)}) %collective-permute-start.38) | collective-permute-done | bytes 262176 | tf_op jit(solution)/shard_map/ppermute | solution.py:97
  (154 shorter events, 134.8 us)
Async XLA Ops:
  0.7 10.3 %collective-permute-start = (bf16[128,256]{1,0:T(8,128)(2,1)}, bf16[128,256]{1,0:T(8,128)(2,1)S(1)}, u32[]{:S(2)}, u32[]{:S(2)}) collective-permute-start(bf16[128,256]{1,0:T(8,128)(2,1)} %param.8), channel_id=1, source_target_pairs={{0,32},{32,0},{1,33},{33,1},{2,34},{34,2},{3,35},{35,3},{4,36},{36... | collective-permute-start | bytes 196616 | tf_op jit(solution)/shard_map/ppermute | solution.py:70
  11.9 13.3 %collective-permute-start.2 = (bf16[2,128,256]{2,1,0:T(8,128)(2,1)S(1)}, bf16[2,128,256]{2,1,0:T(8,128)(2,1)S(1)}, u32[]{:S(2)}, u32[]{:S(2)}) collective-permute-start(bf16[2,128,256]{2,1,0:T(8,128)(2,1)S(1)} %pad_maximum_fusion.3), channel_id=1, source_target_pairs={{0,24},{8,0},{16,8},{24,16},{1,25},{9,1},{17,9},{25,17},{2,26},{10... | collective-permute-start | bytes 393224 | tf_op jit(solution)/shard_map/ppermute | solution.py:60
  30.1 18.0 %collective-permute-start.4 = (bf16[8,128,256]{2,1,0:T(8,128)(2,1)S(1)}, bf16[8,128,256]{2,1,0:T(8,128)(2,1)S(1)}, u32[]{:S(2)}, u32[]{:S(2)}) collective-permute-start(bf16[8,128,256]{2,1,0:T(8,128)(2,1)S(1)} %constant_dynamic-update-slice_fusion.refs_0_), channel_id=1, source_target_pairs={{0,1},{1,2},{2,3},{3,4},{4,5},{5,6},{6,7},{7,0},{8,9},{9,10},{10,1... | collective-permute-start | bytes 1572872 | tf_op jit(solution)/shard_map/ppermute | solution.py:58
  34.1 15.9 %collective-permute-start.5 = (bf16[8,128,256]{2,1,0:T(8,128)(2,1)S(1)}, bf16[8,128,256]{2,1,0:T(8,128)(2,1)S(1)}, u32[]{:S(2)}, u32[]{:S(2)}) collective-permute-start(bf16[8,128,256]{2,1,0:T(8,128)(2,1)S(1)} %constant_dynamic-update-slice_fusion.refs_0_), channel_id=1, source_target_pairs={{0,7},{1,0},{2,1},{3,2},{4,3},{5,4},{6,5},{7,6},{8,15},{9,8},{10,9... | collective-permute-start | bytes 1572872 | tf_op jit(solution)/shard_map/ppermute | solution.py:60
  48.1 11.1 %collective-permute-start.6 = (bf16[8,128,256]{2,1,0:T(8,128)(2,1)S(1)}, bf16[8,128,256]{2,1,0:T(8,128)(2,1)S(1)}, u32[]{:S(2)}, u32[]{:S(2)}) collective-permute-start(bf16[8,128,256]{2,1,0:T(8,128)(2,1)S(1)} %collective-permute-done.4.refs_1_), channel_id=1, source_target_pairs={{0,1},{1,2},{2,3},{3,4},{4,5},{5,6},{6,7},{7,0},{8,9},{9,10},{10,1... | collective-permute-start | bytes 1572872 | tf_op jit(solution)/shard_map/ppermute | solution.py:58
  50.1 13.1 %collective-permute-start.7 = (bf16[8,128,256]{2,1,0:T(8,128)(2,1)S(1)}, bf16[8,128,256]{2,1,0:T(8,128)(2,1)S(1)}, u32[]{:S(2)}, u32[]{:S(2)}) collective-permute-start(bf16[8,128,256]{2,1,0:T(8,128)(2,1)S(1)} %collective-permute-done.5.refs_2_), channel_id=1, source_target_pairs={{0,7},{1,0},{2,1},{3,2},{4,3},{5,4},{6,5},{7,6},{8,15},{9,8},{10,9... | collective-permute-start | bytes 1572872 | tf_op jit(solution)/shard_map/ppermute | solution.py:60
  59.3 11.6 %collective-permute-start.8 = (bf16[8,128,256]{2,1,0:T(8,128)(2,1)S(1)}, bf16[8,128,256]{2,1,0:T(8,128)(2,1)S(1)}, u32[]{:S(2)}, u32[]{:S(2)}) collective-permute-start(bf16[8,128,256]{2,1,0:T(8,128)(2,1)S(1)} %collective-permute-done.6.refs_3_), channel_id=1, source_target_pairs={{0,1},{1,2},{2,3},{3,4},{4,5},{5,6},{6,7},{7,0},{8,9},{9,10},{10,1... | collective-permute-start | bytes 1572872 | tf_op jit(solution)/shard_map/ppermute | solution.py:58
  63.2 13.6 %collective-permute-start.9 = (bf16[8,128,256]{2,1,0:T(8,128)(2,1)S(1)}, bf16[8,128,256]{2,1,0:T(8,128)(2,1)}, u32[]{:S(2)}, u32[]{:S(2)}) collective-permute-start(bf16[8,128,256]{2,1,0:T(8,128)(2,1)S(1)} %collective-permute-done.7.refs_4_), channel_id=1, source_target_pairs={{0,7},{1,0},{2,1},{3,2},{4,3},{5,4},{6,5},{7,6},{8,15},{9,8},{10,9... | collective-permute-start | bytes 1572872 | tf_op jit(solution)/shard_map/ppermute | solution.py:60
  70.9 12.8 %collective-permute-start.10 = (bf16[8,128,256]{2,1,0:T(8,128)(2,1)S(1)}, bf16[8,128,256]{2,1,0:T(8,128)(2,1)}, u32[]{:S(2)}, u32[]{:S(2)}) collective-permute-start(bf16[8,128,256]{2,1,0:T(8,128)(2,1)S(1)} %collective-permute-done.8.refs_5_), channel_id=1, source_target_pairs={{0,1},{1,2},{2,3},{3,4},{4,5},{5,6},{6,7},{7,0},{8,9},{9,10},{10,1... | collective-permute-start | bytes 1572872 | tf_op jit(solution)/shard_map/ppermute | solution.py:58
  95.4 12.3 %collective-permute-start.11 = (f32[4,128,256]{2,1,0:T(8,128)S(1)}, f32[4,128,256]{2,1,0:T(8,128)S(1)}, u32[]{:S(2)}, u32[]{:S(2)}) collective-permute-start(f32[4,128,256]{2,1,0:T(8,128)S(1)} %select_bitcast_fusion.1), channel_id=1, source_target_pairs={{0,64},{64,0},{1,65},{65,1},{2,66},{66,2},{3,67},{67,3},{4,68},{68... | collective-permute-start | bytes 1572872 | tf_op jit(solution)/shard_map/ppermute | solution.py:97
  117.5 12.3 %collective-permute-start.13 = (f32[1,128,256]{2,1,0:T(8,128)S(1)}, f32[1,128,256]{2,1,0:T(8,128)S(1)}, u32[]{:S(2)}, u32[]{:S(2)}) collective-permute-start(f32[1,128,256]{2,1,0:T(8,128)S(1)} %select_bitcast_fusion.5), channel_id=1, source_target_pairs={{0,256},{128,384},{256,0},{384,128},{1,257},{129,385},{257,1},{385... | collective-permute-start | bytes 393224 | tf_op jit(solution)/shard_map/ppermute | solution.py:97
  168.3 17.5 %collective-permute-start.23 = (bf16[8,128,256]{2,1,0:T(8,128)(2,1)S(1)}, bf16[8,128,256]{2,1,0:T(8,128)(2,1)S(1)}, u32[]{:S(2)}, u32[]{:S(2)}) collective-permute-start(bf16[8,128,256]{2,1,0:T(8,128)(2,1)S(1)} %constant_dynamic-update-slice_fusion.5.refs_0_), channel_id=1, source_target_pairs={{0,7},{1,0},{2,1},{3,2},{4,3},{5,4},{6,5},{7,6},{8,15},{9,8},{10,9... | collective-permute-start | bytes 1572872 | tf_op jit(solution)/shard_map/ppermute | solution.py:60
  170.2 15.8 %collective-permute-start.22 = (bf16[8,128,256]{2,1,0:T(8,128)(2,1)S(1)}, bf16[8,128,256]{2,1,0:T(8,128)(2,1)S(1)}, u32[]{:S(2)}, u32[]{:S(2)}) collective-permute-start(bf16[8,128,256]{2,1,0:T(8,128)(2,1)S(1)} %constant_dynamic-update-slice_fusion.5.refs_0_), channel_id=1, source_target_pairs={{0,1},{1,2},{2,3},{3,4},{4,5},{5,6},{6,7},{7,0},{8,9},{9,10},{10,1... | collective-permute-start | bytes 1572872 | tf_op jit(solution)/shard_map/ppermute | solution.py:58
  186.0 24.0 %collective-permute-start.26 = (bf16[8,128,256]{2,1,0:T(8,128)(2,1)S(1)}, bf16[8,128,256]{2,1,0:T(8,128)(2,1)S(1)}, u32[]{:S(2)}, u32[]{:S(2)}) collective-permute-start(bf16[8,128,256]{2,1,0:T(8,128)(2,1)S(1)} %collective-permute-done.22.refs_1_), channel_id=1, source_target_pairs={{0,1},{1,2},{2,3},{3,4},{4,5},{5,6},{6,7},{7,0},{8,9},{9,10},{10,1... | collective-permute-start | bytes 1572872 | tf_op jit(solution)/shard_map/ppermute | solution.py:58
  187.9 22.1 %collective-permute-start.27 = (bf16[8,128,256]{2,1,0:T(8,128)(2,1)S(1)}, bf16[8,128,256]{2,1,0:T(8,128)(2,1)S(1)}, u32[]{:S(2)}, u32[]{:S(2)}) collective-permute-start(bf16[8,128,256]{2,1,0:T(8,128)(2,1)S(1)} %collective-permute-done.23.refs_2_), channel_id=1, source_target_pairs={{0,7},{1,0},{2,1},{3,2},{4,3},{5,4},{6,5},{7,6},{8,15},{9,8},{10,9... | collective-permute-start | bytes 1572872 | tf_op jit(solution)/shard_map/ppermute | solution.py:60
  192.5 10.8 %collective-permute-start.28 = (f32[132,256]{1,0:T(8,128)S(1)}, f32[132,256]{1,0:T(8,128)S(1)}, u32[]{:S(2)}, u32[]{:S(2)}) collective-permute-start(f32[132,256]{1,0:T(8,128)S(1)} %add.184), channel_id=1, source_target_pairs={{0,1},{1,0},{2,3},{3,2},{4,5},{5,4},{6,7},{7,6},{8,9},{9,8},{10,11... | collective-permute-start | bytes 405512 | tf_op jit(solution)/shard_map/ppermute | solution.py:97
  210.0 23.6 %collective-permute-start.30 = (bf16[8,128,256]{2,1,0:T(8,128)(2,1)S(1)}, bf16[8,128,256]{2,1,0:T(8,128)(2,1)S(1)}, u32[]{:S(2)}, u32[]{:S(2)}) collective-permute-start(bf16[8,128,256]{2,1,0:T(8,128)(2,1)S(1)} %collective-permute-done.26.refs_3_), channel_id=1, source_target_pairs={{0,1},{1,2},{2,3},{3,4},{4,5},{5,6},{6,7},{7,0},{8,9},{9,10},{10,1... | collective-permute-start | bytes 1572872 | tf_op jit(solution)/shard_map/ppermute | solution.py:58
  212.0 21.7 %collective-permute-start.31 = (bf16[8,128,256]{2,1,0:T(8,128)(2,1)S(1)}, bf16[8,128,256]{2,1,0:T(8,128)(2,1)S(1)}, u32[]{:S(2)}, u32[]{:S(2)}) collective-permute-start(bf16[8,128,256]{2,1,0:T(8,128)(2,1)S(1)} %collective-permute-done.27.refs_4_), channel_id=1, source_target_pairs={{0,7},{1,0},{2,1},{3,2},{4,3},{5,4},{6,5},{7,6},{8,15},{9,8},{10,9... | collective-permute-start | bytes 1572872 | tf_op jit(solution)/shard_map/ppermute | solution.py:60
  233.6 26.4 %collective-permute-start.34 = (bf16[8,128,256]{2,1,0:T(8,128)(2,1)S(1)}, bf16[8,128,256]{2,1,0:T(8,128)(2,1)}, u32[]{:S(2)}, u32[]{:S(2)}) collective-permute-start(bf16[8,128,256]{2,1,0:T(8,128)(2,1)S(1)} %collective-permute-done.30.refs_5_), channel_id=1, source_target_pairs={{0,1},{1,2},{2,3},{3,4},{4,5},{5,6},{6,7},{7,0},{8,9},{9,10},{10,1... | collective-permute-start | bytes 1572872 | tf_op jit(solution)/shard_map/ppermute | solution.py:58
  235.6 14.3 %collective-permute-start.35 = (f32[132,256]{1,0:T(8,128)S(1)}, f32[132,256]{1,0:T(8,128)S(1)}, u32[]{:S(2)}, u32[]{:S(2)}) collective-permute-start(f32[132,256]{1,0:T(8,128)S(1)} %add.188), channel_id=1, source_target_pairs={{0,4},{1,5},{2,6},{3,7},{4,0},{5,1},{6,2},{7,3},{8,12},{9,13},{10,... | collective-permute-start | bytes 405512 | tf_op jit(solution)/shard_map/ppermute | solution.py:97
  249.9 10.1 %collective-permute-start.36 = (f32[132,256]{1,0:T(8,128)S(1)}, f32[132,256]{1,0:T(8,128)S(1)}, u32[]{:S(2)}, u32[]{:S(2)}) collective-permute-start(f32[132,256]{1,0:T(8,128)S(1)} %add.189), channel_id=1, source_target_pairs={{0,32},{32,0},{1,33},{33,1},{2,34},{34,2},{3,35},{35,3},{4,36},{36... | collective-permute-start | bytes 405512 | tf_op jit(solution)/shard_map/ppermute | solution.py:97
  271.2 12.3 %collective-permute-start.37 = (f32[4,128,256]{2,1,0:T(8,128)S(1)}, f32[4,128,256]{2,1,0:T(8,128)S(1)}, u32[]{:S(2)}, u32[]{:S(2)}) collective-permute-start(f32[4,128,256]{2,1,0:T(8,128)S(1)} %select_bitcast_fusion), channel_id=1, source_target_pairs={{0,64},{64,0},{1,65},{65,1},{2,66},{66,2},{3,67},{67,3},{4,68},{68... | collective-permute-start | bytes 1572872 | tf_op jit(solution)/shard_map/ppermute | solution.py:97
  286.7 12.2 %collective-permute-start.40 = (f32[132,256]{1,0:T(8,128)S(1)}, f32[132,256]{1,0:T(8,128)S(1)}, u32[]{:S(2)}, u32[]{:S(2)}) collective-permute-start(f32[132,256]{1,0:T(8,128)S(1)} %add.190), channel_id=1, source_target_pairs={{0,64},{64,0},{1,65},{65,1},{2,66},{66,2},{3,67},{67,3},{4,68},{68... | collective-permute-start | bytes 405512 | tf_op jit(solution)/shard_map/ppermute | solution.py:97
  294.3 10.4 %collective-permute-start.39 = (f32[1,128,256]{2,1,0:T(8,128)S(1)}, f32[1,128,256]{2,1,0:T(8,128)S(1)}, u32[]{:S(2)}, u32[]{:S(2)}) collective-permute-start(f32[1,128,256]{2,1,0:T(8,128)S(1)} %select_bitcast_fusion.4), channel_id=1, source_target_pairs={{0,256},{128,384},{256,0},{384,128},{1,257},{129,385},{257,1},{385... | collective-permute-start | bytes 393224 | tf_op jit(solution)/shard_map/ppermute | solution.py:97
  (36 other events, 1020.7 us)

commit v13 on v12

--- a/solution.py
+++ b/solution.py
@@ -161,9 +161,12 @@
     return steps
 
 
-def collect_kernel(count, slots_ref, vals_ref, *refs):
+def collect_kernel(count, with_weight, slots_ref, vals_ref, *refs):
     parts = refs[:count]
-    out_ref, held, sems = refs[count:]
+    if with_weight:
+        weight_ref, out_ref, mixed_ref, held, sems = refs[count:]
+    else:
+        out_ref, held, sems = refs[count:]
     row = pl.program_id(0)
     nnz = vals_ref.shape[0]
     size = held.shape[0] // count
@@ -184,36 +187,49 @@
         slot = slots_ref[row * nnz + k]
         total = total + jnp.dot(vals_ref[k], held[slot], preferred_element_type=jnp.float32)
     out_ref[...] = total
-
-
-def collect(parts, slots, adj_vals):
+    if with_weight:
+        mixed_ref[...] = jnp.dot(
+            total,
+            weight_ref[...].astype(jnp.float32),
+            precision=lax.Precision.HIGHEST,
+            preferred_element_type=jnp.float32,
+        )
+
+
+def collect(parts, slots, adj_vals, weight=None):
     block = adj_vals.shape[-1]
     width = parts[0].shape[-1]
     rows, nnz = slots.shape
     count = len(parts)
     panels = count * parts[0].shape[0]
+    with_weight = weight is not None
+    row_spec = pl.BlockSpec((block, width), lambda r, s: (r, 0))
+    out = jax.ShapeDtypeStruct((rows * block, width), jnp.float32)
+    extra = [pl.BlockSpec(weight.shape, lambda r, s: (0, 0))] if with_weight else []
     grid_spec = pltpu.PrefetchScalarGridSpec(
         num_scalar_prefetch=1,
         grid=(rows,),
         in_specs=[pl.BlockSpec((None, None, None, nnz, block, block), lambda r, s: (0, r, 0, 0, 0, 0))]
-        + [pl.BlockSpec(memory_space=pl.ANY)] * count,
-        out_specs=pl.BlockSpec((block, width), lambda r, s: (r, 0)),
+        + [pl.BlockSpec(memory_space=pl.ANY)] * count
+        + extra,
+        out_specs=[row_spec, row_spec] if with_weight else row_spec,
         scratch_shapes=[
             pltpu.VMEM((panels, block, width), parts[0].dtype),
             pltpu.SemaphoreType.DMA((count,)),
         ],
     )
+    operands = [slots.reshape(-1), adj_vals, *parts] + ([weight] if with_weight else [])
     return pl.pallas_call(
-        functools.partial(collect_kernel, count),
+        functools.partial(collect_kernel, count, with_weight),
         grid_spec=grid_spec,
-        out_shape=jax.ShapeDtypeStruct((rows * block, width), jnp.float32),
+        out_shape=(out, out) if with_weight else out,
         compiler_params=pltpu.CompilerParams(dimension_semantics=("arbitrary",)),
         cost_estimate=pl.CostEstimate(
-            flops=2 * rows * nnz * block * block * width,
+            flops=2 * rows * nnz * block * block * width + (6 * rows * block * width * width if with_weight else 0),
             transcendentals=0,
             bytes_accessed=panels * block * width * 2 + rows * nnz * block * block * 2 + rows * block * width * 4,
         ),
-    )(slots.reshape(-1), adj_vals, *parts)
+    )(*operands)
 
 
 def activation(value):
@@ -224,13 +240,7 @@
     slots = member_slots(adj_cols[0, :, 0, :])
     width = features.shape[1]
     gathered = gather_team(features)
-    partial_ax = collect(gathered, slots, adj_vals)
-    partial_rows = jnp.dot(
-        partial_ax,
-        weight.astype(jnp.float32),
-        precision=lax.Precision.HIGHEST,
-        preferred_element_type=jnp.float32,
-    )
+    partial_ax, partial_rows = collect(gathered, slots, adj_vals, weight)
     summed = blk_reduce_scatter(partial_rows)
     pre = summed + bias[None, :]
     activated, pullback = jax.vjp(activation, pre)

time: 309 us -> 310 us (level)
  starting transfers between devices: 160 us -> 155 us
  waiting for transfers between devices: 108 us -> 113 us
    ppermute x19, waiting for transfers between devices: 68.6 us -> 77.2 us  [swap(): return lax.ppermute(value, axis, [(i, i ^ bit) for i in range(n)])]
    ppermute x12, waiting for transfers between devices: 35.9 us -> 29.3 us  [ring_gather(): ahead = lax.ppermute(ahead, axis, [(i, (i + 1) % n) for i in range(n)])]
    ppermute x2, starting transfers between devices: 16.3 us -> 13.1 us  [gather_team(): other = lax.ppermute(rows, 'y_hi', perm=[(0, 1), (1, 0)])]
  transfers between devices with their start and end apart: 41 -> 41, of which waited for: 27 -> 26; matrix products, arithmetic and copies ran while one was open for 3% -> 3% of each run, Pallas kernels for 0% -> 0%
where the time goes in v13:
time: 310 us; the launch traced here: 308 us
  starting transfers between devices  155 us (50%)
  waiting for transfers between devices  113 us (36%)
  Pallas kernels  21.4 us (7%)
  other arithmetic  10.2 us (3%)
  local copies, waits for them, and re-layouts  5.63 us (2%)
    ppermute x19, waiting for transfers between devices, swap(): return lax.ppermute(value, axis, [(i, i ^ bit) for i in range(n)])  77.2 us
    ppermute x19, starting transfers between devices, swap(): return lax.ppermute(value, axis, [(i, i ^ bit) for i in range(n)])  77.1 us
    ppermute x8, starting transfers between devices, ring_gather(): behind = lax.ppermute(behind, axis, [(i, (i - 1) % n) for i in range(n)])  39.4 us
    ppermute x12, waiting for transfers between devices, ring_gather(): ahead = lax.ppermute(ahead, axis, [(i, (i + 1) % n) for i in range(n)])  29.3 us
    ppermute x12, starting transfers between devices, ring_gather(): ahead = lax.ppermute(ahead, axis, [(i, (i + 1) % n) for i in range(n)])  25 us
    pallas_call x2, Pallas kernels, collect(): pl.pallas_call(functools.partial(collect_kernel, count, with_weight), gri...  21.4 us
    ppermute x2, starting transfers between devices, gather_team(): other = lax.ppermute(rows, 'y_hi', perm=[(0, 1), (1, 0)])  13.1 us
  transfers between devices with their start and end apart: 41, of which 26 were waited for; matrix products, arithmetic and copies ran while one was open for 3% of the time, Pallas kernels for 0%

profile of v13, /device:TPU:1, one launch (start us, length us, event | category | flops | bytes accessed | tf_op | source)
XLA Modules:
  0.0 308.5 jit_solution(16085163556509516369)
XLA Ops:
  0.7 8.3 %collective-permute-start = (bf16[128,256]{1,0:T(8,128)(2,1)}, bf16[128,256]{1,0:T(8,128)(2,1)S(1)}, u32[]{:S(2)}, u32[]{:S(2)}) collective-permute-start(bf16[128,256]{1,0:T(8,128)(2,1)} %param.8), channel_id=1, source_target_pairs={{0,32},{32,0},{1,33},{33,1},{2,34},{34,2},{3,35},{35,3},{4,36},{36... | collective-permute-start | bytes 196616 | tf_op jit(solution)/shard_map/ppermute | solution.py:70
  20.6 6.2 %collective-permute-done.3 = bf16[2,128,256]{2,1,0:T(8,128)(2,1)S(1)} collective-permute-done((bf16[2,128,256]{2,1,0:T(8,128)(2,1)S(1)}, bf16[2,128,256]{2,1,0:T(8,128)(2,1)S(1)}, u32[]{:S(2)}, u32[]{:S(2)}) %collective-permute-start.3) | collective-permute-done | bytes 131104 | tf_op jit(solution)/shard_map/ppermute | solution.py:58
  29.6 8.6 %collective-permute-start.5 = (bf16[8,128,256]{2,1,0:T(8,128)(2,1)S(1)}, bf16[8,128,256]{2,1,0:T(8,128)(2,1)S(1)}, u32[]{:S(2)}, u32[]{:S(2)}) collective-permute-start(bf16[8,128,256]{2,1,0:T(8,128)(2,1)S(1)} %constant_dynamic-update-slice_fusion.refs_0_), channel_id=1, source_target_pairs={{0,7},{1,0},{2,1},{3,2},{4,3},{5,4},{6,5},{7,6},{8,15},{9,8},{10,9... | collective-permute-start | bytes 1572872 | tf_op jit(solution)/shard_map/ppermute | solution.py:60
  38.2 5.7 %collective-permute-done.4.refs_1_ = bf16[8,128,256]{2,1,0:T(8,128)(2,1)S(1)} collective-permute-done((bf16[8,128,256]{2,1,0:T(8,128)(2,1)S(1)}, bf16[8,128,256]{2,1,0:T(8,128)(2,1)S(1)}, u32[]{:S(2)}, u32[]{:S(2)}) %collective-permute-start.4) | collective-permute-done | bytes 524320 | tf_op jit(solution)/shard_map/ppermute | solution.py:58
  61.5 4.8 %collective-permute-done.8.refs_5_ = bf16[8,128,256]{2,1,0:T(8,128)(2,1)S(1)} collective-permute-done((bf16[8,128,256]{2,1,0:T(8,128)(2,1)S(1)}, bf16[8,128,256]{2,1,0:T(8,128)(2,1)S(1)}, u32[]{:S(2)}, u32[]{:S(2)}) %collective-permute-start.8) | collective-permute-done | bytes 524320 | tf_op jit(solution)/shard_map/ppermute | solution.py:58
  74.2 4.7 %collective-permute-done.10.refs_7_ = bf16[8,128,256]{2,1,0:T(8,128)(2,1)} collective-permute-done((bf16[8,128,256]{2,1,0:T(8,128)(2,1)S(1)}, bf16[8,128,256]{2,1,0:T(8,128)(2,1)}, u32[]{:S(2)}, u32[]{:S(2)}) %collective-permute-start.10) | collective-permute-done | bytes 524320 | tf_op jit(solution)/shard_map/ppermute | solution.py:58
  78.8 11.6 %shard_map.111 = (f32[1024,256]{1,0:T(8,128)}, f32[1024,256]{1,0:T(8,128)}) custom-call(s32[96]{0:T(128)} %fusion.27.slots_ref, bf16[1,8,1,12,128,128]{5,4,3,2,1,0:T(8,128)(2,1)} %vals_ref.3, bf16[8,128,256]{2,1,0:T(8,128)(2,1)} %copy-done.3, bf16[8,128,256]{2,1,0:T(8,128)(2,1)} %copy-done.8, bf16[8,128,256]{2,1,0:T(8,128)(2,1)} %copy-done.9, ...), custom_call_target="tpu_custom_call" | custom-call | flops 1207959552 | bytes 8388608 | tf_op jit(solution)/shard_map/pallas_call | solution.py:222
  91.7 10.5 %collective-permute-start.11 = (f32[4,128,256]{2,1,0:T(8,128)S(1)}, f32[4,128,256]{2,1,0:T(8,128)S(1)}, u32[]{:S(2)}, u32[]{:S(2)}) collective-permute-start(f32[4,128,256]{2,1,0:T(8,128)S(1)} %select_bitcast_fusion.1), channel_id=1, source_target_pairs={{0,64},{64,0},{1,65},{65,1},{2,66},{66,2},{3,67},{67,3},{4,68},{68... | collective-permute-start | bytes 1572872 | tf_op jit(solution)/shard_map/ppermute | solution.py:97
  107.9 6.7 %collective-permute-done.12 = f32[2,128,256]{2,1,0:T(8,128)S(1)} collective-permute-done((f32[2,128,256]{2,1,0:T(8,128)S(1)}, f32[2,128,256]{2,1,0:T(8,128)S(1)}, u32[]{:S(2)}, u32[]{:S(2)}) %collective-permute-start.12) | collective-permute-done | bytes 262176 | tf_op jit(solution)/shard_map/ppermute | solution.py:97
  114.7 7.7 %collective-permute-start.13 = (f32[1,128,256]{2,1,0:T(8,128)S(1)}, f32[1,128,256]{2,1,0:T(8,128)S(1)}, u32[]{:S(2)}, u32[]{:S(2)}) collective-permute-start(f32[1,128,256]{2,1,0:T(8,128)S(1)} %select_bitcast_fusion.5), channel_id=1, source_target_pairs={{0,256},{128,384},{256,0},{384,128},{1,257},{129,385},{257,1},{385... | collective-permute-start | bytes 393224 | tf_op jit(solution)/shard_map/ppermute | solution.py:97
  122.4 6.7 %collective-permute-done.13 = f32[1,128,256]{2,1,0:T(8,128)S(1)} collective-permute-done((f32[1,128,256]{2,1,0:T(8,128)S(1)}, f32[1,128,256]{2,1,0:T(8,128)S(1)}, u32[]{:S(2)}, u32[]{:S(2)}) %collective-permute-start.13) | collective-permute-done | bytes 131104 | tf_op jit(solution)/shard_map/ppermute | solution.py:97
  131.2 4.8 %collective-permute-start.14 = (bf16[128,256]{1,0:T(8,128)(2,1)S(1)}, bf16[128,256]{1,0:T(8,128)(2,1)S(1)}, u32[]{:S(2)}, u32[]{:S(2)}) collective-permute-start(bf16[128,256]{1,0:T(8,128)(2,1)S(1)} %get-tuple-element.45), channel_id=1, source_target_pairs={{0,32},{32,0},{1,33},{33,1},{2,34},{34,2},{3,35},{35,3},{4,36},{36... | collective-permute-start | bytes 196616 | tf_op jit(solution)/shard_map/ppermute | solution.py:70
  140.2 5.0 %collective-permute-start.18 = (bf16[2,128,256]{2,1,0:T(8,128)(2,1)S(1)}, bf16[2,128,256]{2,1,0:T(8,128)(2,1)S(1)}, u32[]{:S(2)}, u32[]{:S(2)}) collective-permute-start(bf16[2,128,256]{2,1,0:T(8,128)(2,1)S(1)} %fusion.3), channel_id=1, source_target_pairs={{0,256},{128,384},{256,0},{384,128},{1,257},{129,385},{257,1},{385... | collective-permute-start | bytes 393224 | tf_op jit(solution)/shard_map/ppermute | solution.py:97
  153.7 4.7 %collective-permute-start.20 = (bf16[4,128,256]{2,1,0:T(8,128)(2,1)S(1)}, bf16[4,128,256]{2,1,0:T(8,128)(2,1)S(1)}, u32[]{:S(2)}, u32[]{:S(2)}) collective-permute-start(bf16[4,128,256]{2,1,0:T(8,128)(2,1)S(1)} %maximum_select_fusion.2), channel_id=1, source_target_pairs={{0,64},{64,0},{1,65},{65,1},{2,66},{66,2},{3,67},{67,3},{4,68},{68... | collective-permute-start | bytes 786440 | tf_op jit(solution)/shard_map/ppermute | solution.py:97
  194.6 8.6 %collective-permute-done.28 = f32[132,256]{1,0:T(8,128)S(1)} collective-permute-done((f32[132,256]{1,0:T(8,128)S(1)}, f32[132,256]{1,0:T(8,128)S(1)}, u32[]{:S(2)}, u32[]{:S(2)}) %collective-permute-start.28) | collective-permute-done | bytes 135200 | tf_op jit(solution)/shard_map/ppermute | solution.py:97
  205.6 5.8 %collective-permute-done.29 = f32[132,256]{1,0:T(8,128)S(1)} collective-permute-done((f32[132,256]{1,0:T(8,128)S(1)}, f32[132,256]{1,0:T(8,128)S(1)}, u32[]{:S(2)}, u32[]{:S(2)}) %collective-permute-start.29) | collective-permute-done | bytes 135200 | tf_op jit(solution)/shard_map/ppermute | solution.py:97
  227.8 5.9 %collective-permute-done.33 = f32[132,256]{1,0:T(8,128)S(1)} collective-permute-done((f32[132,256]{1,0:T(8,128)S(1)}, f32[132,256]{1,0:T(8,128)S(1)}, u32[]{:S(2)}, u32[]{:S(2)}) %collective-permute-start.33) | collective-permute-done | bytes 135200 | tf_op jit(solution)/shard_map/ppermute | solution.py:97
  235.7 5.3 %collective-permute-start.35 = (f32[132,256]{1,0:T(8,128)S(1)}, f32[132,256]{1,0:T(8,128)S(1)}, u32[]{:S(2)}, u32[]{:S(2)}) collective-permute-start(f32[132,256]{1,0:T(8,128)S(1)} %add.188), channel_id=1, source_target_pairs={{0,4},{1,5},{2,6},{3,7},{4,0},{5,1},{6,2},{7,3},{8,12},{9,13},{10,... | collective-permute-start | bytes 405512 | tf_op jit(solution)/shard_map/ppermute | solution.py:97
  241.0 9.9 %collective-permute-done.35 = f32[132,256]{1,0:T(8,128)S(1)} collective-permute-done((f32[132,256]{1,0:T(8,128)S(1)}, f32[132,256]{1,0:T(8,128)S(1)}, u32[]{:S(2)}, u32[]{:S(2)}) %collective-permute-start.35) | collective-permute-done | bytes 135200 | tf_op jit(solution)/shard_map/ppermute | solution.py:97
  255.4 6.3 %collective-permute-done.36 = f32[132,256]{1,0:T(8,128)S(1)} collective-permute-done((f32[132,256]{1,0:T(8,128)S(1)}, f32[132,256]{1,0:T(8,128)S(1)}, u32[]{:S(2)}, u32[]{:S(2)}) %collective-permute-start.36) | collective-permute-done | bytes 135200 | tf_op jit(solution)/shard_map/ppermute | solution.py:97
  261.8 9.8 %shard_map.112 = f32[1024,256]{1,0:T(8,128)} custom-call(s32[96]{0:T(128)} %fusion.27.slots_ref, bf16[1,8,1,12,128,128]{5,4,3,2,1,0:T(8,128)(2,1)} %vals_ref.3, bf16[8,128,256]{2,1,0:T(8,128)(2,1)} %copy-done.4, bf16[8,128,256]{2,1,0:T(8,128)(2,1)} %copy-done.6, bf16[8,128,256]{2,1,0:T(8,128)(2,1)} %copy-done.7, bf16[8,128,256]{2,1,0:T(8,128)(2,1)} %copy-done.11, ...), custom_call_target="tpu_custom_call" | custom-call | flops 805306368 | bytes 8388608 | tf_op jit(solution)/shard_map/pallas_call | solution.py:222
  273.0 11.3 %collective-permute-start.37 = (f32[4,128,256]{2,1,0:T(8,128)S(1)}, f32[4,128,256]{2,1,0:T(8,128)S(1)}, u32[]{:S(2)}, u32[]{:S(2)}) collective-permute-start(f32[4,128,256]{2,1,0:T(8,128)S(1)} %select_bitcast_fusion), channel_id=1, source_target_pairs={{0,64},{64,0},{1,65},{65,1},{2,66},{66,2},{3,67},{67,3},{4,68},{68... | collective-permute-start | bytes 1572872 | tf_op jit(solution)/shard_map/ppermute | solution.py:97
  291.4 5.2 %collective-permute-done.38 = f32[2,128,256]{2,1,0:T(8,128)S(1)} collective-permute-done((f32[2,128,256]{2,1,0:T(8,128)S(1)}, f32[2,128,256]{2,1,0:T(8,128)S(1)}, u32[]{:S(2)}, u32[]{:S(2)}) %collective-permute-start.38) | collective-permute-done | bytes 262176 | tf_op jit(solution)/shard_map/ppermute | solution.py:97
  300.6 7.0 %collective-permute-done.39 = f32[1,128,256]{2,1,0:T(8,128)S(1)} collective-permute-done((f32[1,128,256]{2,1,0:T(8,128)S(1)}, f32[1,128,256]{2,1,0:T(8,128)S(1)}, u32[]{:S(2)}, u32[]{:S(2)}) %collective-permute-start.39) | collective-permute-done | bytes 131104 | tf_op jit(solution)/shard_map/ppermute | solution.py:97
  (153 shorter events, 135.6 us)
Async XLA Ops:
  0.7 10.2 %collective-permute-start = (bf16[128,256]{1,0:T(8,128)(2,1)}, bf16[128,256]{1,0:T(8,128)(2,1)S(1)}, u32[]{:S(2)}, u32[]{:S(2)}) collective-permute-start(bf16[128,256]{1,0:T(8,128)(2,1)} %param.8), channel_id=1, source_target_pairs={{0,32},{32,0},{1,33},{33,1},{2,34},{34,2},{3,35},{35,3},{4,36},{36... | collective-permute-start | bytes 196616 | tf_op jit(solution)/shard_map/ppermute | solution.py:70
  26.9 17.0 %collective-permute-start.4 = (bf16[8,128,256]{2,1,0:T(8,128)(2,1)S(1)}, bf16[8,128,256]{2,1,0:T(8,128)(2,1)S(1)}, u32[]{:S(2)}, u32[]{:S(2)}) collective-permute-start(bf16[8,128,256]{2,1,0:T(8,128)(2,1)S(1)} %constant_dynamic-update-slice_fusion.refs_0_), channel_id=1, source_target_pairs={{0,1},{1,2},{2,3},{3,4},{4,5},{5,6},{6,7},{7,0},{8,9},{9,10},{10,1... | collective-permute-start | bytes 1572872 | tf_op jit(solution)/shard_map/ppermute | solution.py:58
  29.6 16.2 %collective-permute-start.5 = (bf16[8,128,256]{2,1,0:T(8,128)(2,1)S(1)}, bf16[8,128,256]{2,1,0:T(8,128)(2,1)S(1)}, u32[]{:S(2)}, u32[]{:S(2)}) collective-permute-start(bf16[8,128,256]{2,1,0:T(8,128)(2,1)S(1)} %constant_dynamic-update-slice_fusion.refs_0_), channel_id=1, source_target_pairs={{0,7},{1,0},{2,1},{3,2},{4,3},{5,4},{6,5},{7,6},{8,15},{9,8},{10,9... | collective-permute-start | bytes 1572872 | tf_op jit(solution)/shard_map/ppermute | solution.py:60
  43.9 11.1 %collective-permute-start.6 = (bf16[8,128,256]{2,1,0:T(8,128)(2,1)S(1)}, bf16[8,128,256]{2,1,0:T(8,128)(2,1)S(1)}, u32[]{:S(2)}, u32[]{:S(2)}) collective-permute-start(bf16[8,128,256]{2,1,0:T(8,128)(2,1)S(1)} %collective-permute-done.4.refs_1_), channel_id=1, source_target_pairs={{0,1},{1,2},{2,3},{3,4},{4,5},{5,6},{6,7},{7,0},{8,9},{9,10},{10,1... | collective-permute-start | bytes 1572872 | tf_op jit(solution)/shard_map/ppermute | solution.py:58
  45.8 11.1 %collective-permute-start.7 = (bf16[8,128,256]{2,1,0:T(8,128)(2,1)S(1)}, bf16[8,128,256]{2,1,0:T(8,128)(2,1)S(1)}, u32[]{:S(2)}, u32[]{:S(2)}) collective-permute-start(bf16[8,128,256]{2,1,0:T(8,128)(2,1)S(1)} %collective-permute-done.5.refs_2_), channel_id=1, source_target_pairs={{0,7},{1,0},{2,1},{3,2},{4,3},{5,4},{6,5},{7,6},{8,15},{9,8},{10,9... | collective-permute-start | bytes 1572872 | tf_op jit(solution)/shard_map/ppermute | solution.py:60
  55.0 11.3 %collective-permute-start.8 = (bf16[8,128,256]{2,1,0:T(8,128)(2,1)S(1)}, bf16[8,128,256]{2,1,0:T(8,128)(2,1)S(1)}, u32[]{:S(2)}, u32[]{:S(2)}) collective-permute-start(bf16[8,128,256]{2,1,0:T(8,128)(2,1)S(1)} %collective-permute-done.6.refs_3_), channel_id=1, source_target_pairs={{0,1},{1,2},{2,3},{3,4},{4,5},{5,6},{6,7},{7,0},{8,9},{9,10},{10,1... | collective-permute-start | bytes 1572872 | tf_op jit(solution)/shard_map/ppermute | solution.py:58
  57.0 17.2 %collective-permute-start.9 = (bf16[8,128,256]{2,1,0:T(8,128)(2,1)S(1)}, bf16[8,128,256]{2,1,0:T(8,128)(2,1)}, u32[]{:S(2)}, u32[]{:S(2)}) collective-permute-start(bf16[8,128,256]{2,1,0:T(8,128)(2,1)S(1)} %collective-permute-done.7.refs_4_), channel_id=1, source_target_pairs={{0,7},{1,0},{2,1},{3,2},{4,3},{5,4},{6,5},{7,6},{8,15},{9,8},{10,9... | collective-permute-start | bytes 1572872 | tf_op jit(solution)/shard_map/ppermute | solution.py:60
  66.3 12.5 %collective-permute-start.10 = (bf16[8,128,256]{2,1,0:T(8,128)(2,1)S(1)}, bf16[8,128,256]{2,1,0:T(8,128)(2,1)}, u32[]{:S(2)}, u32[]{:S(2)}) collective-permute-start(bf16[8,128,256]{2,1,0:T(8,128)(2,1)S(1)} %collective-permute-done.8.refs_5_), channel_id=1, source_target_pairs={{0,1},{1,2},{2,3},{3,4},{4,5},{5,6},{6,7},{7,0},{8,9},{9,10},{10,1... | collective-permute-start | bytes 1572872 | tf_op jit(solution)/shard_map/ppermute | solution.py:58
  91.7 12.0 %collective-permute-start.11 = (f32[4,128,256]{2,1,0:T(8,128)S(1)}, f32[4,128,256]{2,1,0:T(8,128)S(1)}, u32[]{:S(2)}, u32[]{:S(2)}) collective-permute-start(f32[4,128,256]{2,1,0:T(8,128)S(1)} %select_bitcast_fusion.1), channel_id=1, source_target_pairs={{0,64},{64,0},{1,65},{65,1},{2,66},{66,2},{3,67},{67,3},{4,68},{68... | collective-permute-start | bytes 1572872 | tf_op jit(solution)/shard_map/ppermute | solution.py:97
  114.7 14.4 %collective-permute-start.13 = (f32[1,128,256]{2,1,0:T(8,128)S(1)}, f32[1,128,256]{2,1,0:T(8,128)S(1)}, u32[]{:S(2)}, u32[]{:S(2)}) collective-permute-start(f32[1,128,256]{2,1,0:T(8,128)S(1)} %select_bitcast_fusion.5), channel_id=1, source_target_pairs={{0,256},{128,384},{256,0},{384,128},{1,257},{129,385},{257,1},{385... | collective-permute-start | bytes 393224 | tf_op jit(solution)/shard_map/ppermute | solution.py:97
  140.2 11.6 %collective-permute-start.18 = (bf16[2,128,256]{2,1,0:T(8,128)(2,1)S(1)}, bf16[2,128,256]{2,1,0:T(8,128)(2,1)S(1)}, u32[]{:S(2)}, u32[]{:S(2)}) collective-permute-start(bf16[2,128,256]{2,1,0:T(8,128)(2,1)S(1)} %fusion.3), channel_id=1, source_target_pairs={{0,256},{128,384},{256,0},{384,128},{1,257},{129,385},{257,1},{385... | collective-permute-start | bytes 393224 | tf_op jit(solution)/shard_map/ppermute | solution.py:97
  167.6 18.5 %collective-permute-start.22 = (bf16[8,128,256]{2,1,0:T(8,128)(2,1)S(1)}, bf16[8,128,256]{2,1,0:T(8,128)(2,1)S(1)}, u32[]{:S(2)}, u32[]{:S(2)}) collective-permute-start(bf16[8,128,256]{2,1,0:T(8,128)(2,1)S(1)} %constant_dynamic-update-slice_fusion.5.refs_0_), channel_id=1, source_target_pairs={{0,1},{1,2},{2,3},{3,4},{4,5},{5,6},{6,7},{7,0},{8,9},{9,10},{10,1... | collective-permute-start | bytes 1572872 | tf_op jit(solution)/shard_map/ppermute | solution.py:58
  169.6 16.5 %collective-permute-start.23 = (bf16[8,128,256]{2,1,0:T(8,128)(2,1)S(1)}, bf16[8,128,256]{2,1,0:T(8,128)(2,1)S(1)}, u32[]{:S(2)}, u32[]{:S(2)}) collective-permute-start(bf16[8,128,256]{2,1,0:T(8,128)(2,1)S(1)} %constant_dynamic-update-slice_fusion.5.refs_0_), channel_id=1, source_target_pairs={{0,7},{1,0},{2,1},{3,2},{4,3},{5,4},{6,5},{7,6},{8,15},{9,8},{10,9... | collective-permute-start | bytes 1572872 | tf_op jit(solution)/shard_map/ppermute | solution.py:60
  186.1 25.3 %collective-permute-start.26 = (bf16[8,128,256]{2,1,0:T(8,128)(2,1)S(1)}, bf16[8,128,256]{2,1,0:T(8,128)(2,1)S(1)}, u32[]{:S(2)}, u32[]{:S(2)}) collective-permute-start(bf16[8,128,256]{2,1,0:T(8,128)(2,1)S(1)} %collective-permute-done.22.refs_1_), channel_id=1, source_target_pairs={{0,1},{1,2},{2,3},{3,4},{4,5},{5,6},{6,7},{7,0},{8,9},{9,10},{10,1... | collective-permute-start | bytes 1572872 | tf_op jit(solution)/shard_map/ppermute | solution.py:58
  188.1 23.4 %collective-permute-start.27 = (bf16[8,128,256]{2,1,0:T(8,128)(2,1)S(1)}, bf16[8,128,256]{2,1,0:T(8,128)(2,1)S(1)}, u32[]{:S(2)}, u32[]{:S(2)}) collective-permute-start(bf16[8,128,256]{2,1,0:T(8,128)(2,1)S(1)} %collective-permute-done.23.refs_2_), channel_id=1, source_target_pairs={{0,7},{1,0},{2,1},{3,2},{4,3},{5,4},{6,5},{7,6},{8,15},{9,8},{10,9... | collective-permute-start | bytes 1572872 | tf_op jit(solution)/shard_map/ppermute | solution.py:60
  192.6 10.6 %collective-permute-start.28 = (f32[132,256]{1,0:T(8,128)S(1)}, f32[132,256]{1,0:T(8,128)S(1)}, u32[]{:S(2)}, u32[]{:S(2)}) collective-permute-start(f32[132,256]{1,0:T(8,128)S(1)} %add.184), channel_id=1, source_target_pairs={{0,1},{1,0},{2,3},{3,2},{4,5},{5,4},{6,7},{7,6},{8,9},{9,8},{10,11... | collective-permute-start | bytes 405512 | tf_op jit(solution)/shard_map/ppermute | solution.py:97
  211.5 22.2 %collective-permute-start.30 = (bf16[8,128,256]{2,1,0:T(8,128)(2,1)S(1)}, bf16[8,128,256]{2,1,0:T(8,128)(2,1)S(1)}, u32[]{:S(2)}, u32[]{:S(2)}) collective-permute-start(bf16[8,128,256]{2,1,0:T(8,128)(2,1)S(1)} %collective-permute-done.26.refs_3_), channel_id=1, source_target_pairs={{0,1},{1,2},{2,3},{3,4},{4,5},{5,6},{6,7},{7,0},{8,9},{9,10},{10,1... | collective-permute-start | bytes 1572872 | tf_op jit(solution)/shard_map/ppermute | solution.py:58
  213.4 20.3 %collective-permute-start.31 = (bf16[8,128,256]{2,1,0:T(8,128)(2,1)S(1)}, bf16[8,128,256]{2,1,0:T(8,128)(2,1)S(1)}, u32[]{:S(2)}, u32[]{:S(2)}) collective-permute-start(bf16[8,128,256]{2,1,0:T(8,128)(2,1)S(1)} %collective-permute-done.27.refs_4_), channel_id=1, source_target_pairs={{0,7},{1,0},{2,1},{3,2},{4,3},{5,4},{6,5},{7,6},{8,15},{9,8},{10,9... | collective-permute-start | bytes 1572872 | tf_op jit(solution)/shard_map/ppermute | solution.py:60
  233.7 28.0 %collective-permute-start.34 = (bf16[8,128,256]{2,1,0:T(8,128)(2,1)S(1)}, bf16[8,128,256]{2,1,0:T(8,128)(2,1)}, u32[]{:S(2)}, u32[]{:S(2)}) collective-permute-start(bf16[8,128,256]{2,1,0:T(8,128)(2,1)S(1)} %collective-permute-done.30.refs_5_), channel_id=1, source_target_pairs={{0,1},{1,2},{2,3},{3,4},{4,5},{5,6},{6,7},{7,0},{8,9},{9,10},{10,1... | collective-permute-start | bytes 1572872 | tf_op jit(solution)/shard_map/ppermute | solution.py:58
  235.7 15.2 %collective-permute-start.35 = (f32[132,256]{1,0:T(8,128)S(1)}, f32[132,256]{1,0:T(8,128)S(1)}, u32[]{:S(2)}, u32[]{:S(2)}) collective-permute-start(f32[132,256]{1,0:T(8,128)S(1)} %add.188), channel_id=1, source_target_pairs={{0,4},{1,5},{2,6},{3,7},{4,0},{5,1},{6,2},{7,3},{8,12},{9,13},{10,... | collective-permute-start | bytes 405512 | tf_op jit(solution)/shard_map/ppermute | solution.py:97
  250.9 10.8 %collective-permute-start.36 = (f32[132,256]{1,0:T(8,128)S(1)}, f32[132,256]{1,0:T(8,128)S(1)}, u32[]{:S(2)}, u32[]{:S(2)}) collective-permute-start(f32[132,256]{1,0:T(8,128)S(1)} %add.189), channel_id=1, source_target_pairs={{0,32},{32,0},{1,33},{33,1},{2,34},{34,2},{3,35},{35,3},{4,36},{36... | collective-permute-start | bytes 405512 | tf_op jit(solution)/shard_map/ppermute | solution.py:97
  273.0 12.9 %collective-permute-start.37 = (f32[4,128,256]{2,1,0:T(8,128)S(1)}, f32[4,128,256]{2,1,0:T(8,128)S(1)}, u32[]{:S(2)}, u32[]{:S(2)}) collective-permute-start(f32[4,128,256]{2,1,0:T(8,128)S(1)} %select_bitcast_fusion), channel_id=1, source_target_pairs={{0,64},{64,0},{1,65},{65,1},{2,66},{66,2},{3,67},{67,3},{4,68},{68... | collective-permute-start | bytes 1572872 | tf_op jit(solution)/shard_map/ppermute | solution.py:97
  289.1 10.2 %collective-permute-start.40 = (f32[132,256]{1,0:T(8,128)S(1)}, f32[132,256]{1,0:T(8,128)S(1)}, u32[]{:S(2)}, u32[]{:S(2)}) collective-permute-start(f32[132,256]{1,0:T(8,128)S(1)} %add.190), channel_id=1, source_target_pairs={{0,64},{64,0},{1,65},{65,1},{2,66},{66,2},{3,67},{67,3},{4,68},{68... | collective-permute-start | bytes 405512 | tf_op jit(solution)/shard_map/ppermute | solution.py:97
  296.7 11.0 %collective-permute-start.39 = (f32[1,128,256]{2,1,0:T(8,128)S(1)}, f32[1,128,256]{2,1,0:T(8,128)S(1)}, u32[]{:S(2)}, u32[]{:S(2)}) collective-permute-start(f32[1,128,256]{2,1,0:T(8,128)S(1)} %select_bitcast_fusion.4), channel_id=1, source_target_pairs={{0,256},{128,384},{256,0},{384,128},{1,257},{129,385},{257,1},{385... | collective-permute-start | bytes 393224 | tf_op jit(solution)/shard_map/ppermute | solution.py:97
  (36 other events, 982.7 us)

commit v14 on v12

--- a/solution.py
+++ b/solution.py
@@ -71,7 +71,7 @@
     if chain is not None:
         other = chain.tick(other)
     pair = jnp.stack([rows, other], axis=0)
-    return ring_gather(ring_gather(pair, "x", chain), "z", chain, 2, join=False)
+    return ring_gather(ring_gather(pair, "x", chain, 2), "z", chain, 2, join=False)
 
 
 def ring_slot(delta, axis):

time: 309 us -> 320 us (1.036)
  waiting for transfers between devices: 108 us -> 116 us
  starting transfers between devices: 160 us -> 164 us
    ppermute x19, waiting for transfers between devices: 68.6 us -> 78.4 us  [swap(): return lax.ppermute(value, axis, [(i, i ^ bit) for i in range(n)])]
    ppermute x19, starting transfers between devices: 79.8 us -> 83.7 us  [swap(): return lax.ppermute(value, axis, [(i, i ^ bit) for i in range(n)])]
where the time goes in v14:
time: 320 us; the launch traced here: 318 us
  starting transfers between devices  164 us (51%)
  waiting for transfers between devices  116 us (36%)
  Pallas kernels  19.7 us (6%)
  other arithmetic  8.41 us (3%)
  local copies, waits for them, and re-layouts  5.64 us (2%)
  matrix products  3.67 us (1%)
    ppermute x19, starting transfers between devices, swap(): return lax.ppermute(value, axis, [(i, i ^ bit) for i in range(n)])  83.7 us
    ppermute x19, waiting for transfers between devices, swap(): return lax.ppermute(value, axis, [(i, i ^ bit) for i in range(n)])  78.4 us
    ppermute x8, starting transfers between devices, ring_gather(): behind = lax.ppermute(behind, axis, [(i, (i - 1) % n) for i in range(n)])  34.4 us
    ppermute x12, waiting for transfers between devices, ring_gather(): ahead = lax.ppermute(ahead, axis, [(i, (i + 1) % n) for i in range(n)])  33.1 us
    ppermute x12, starting transfers between devices, ring_gather(): ahead = lax.ppermute(ahead, axis, [(i, (i + 1) % n) for i in range(n)])  29.4 us
    pallas_call x2, Pallas kernels, collect(): pl.pallas_call(functools.partial(collect_kernel, count), grid_spec=grid_s...  19.7 us
    ppermute x2, starting transfers between devices, gather_team(): other = lax.ppermute(rows, 'y_hi', perm=[(0, 1), (1, 0)])  16.3 us
  transfers between devices with their start and end apart: 41, of which 27 were waited for; matrix products, arithmetic and copies ran while one was open for 3% of the time, Pallas kernels for 0%

profile of v14, /device:TPU:1, one launch (start us, length us, event | category | flops | bytes accessed | tf_op | source)
XLA Modules:
  0.0 318.4 jit_solution(420126583812877641)
XLA Ops:
  0.7 8.4 %collective-permute-start = (bf16[128,256]{1,0:T(8,128)(2,1)}, bf16[128,256]{1,0:T(8,128)(2,1)S(1)}, u32[]{:S(2)}, u32[]{:S(2)}) collective-permute-start(bf16[128,256]{1,0:T(8,128)(2,1)} %param.8), channel_id=1, source_target_pairs={{0,32},{32,0},{1,33},{33,1},{2,34},{34,2},{3,35},{35,3},{4,36},{36... | collective-permute-start | bytes 196616 | tf_op jit(solution)/shard_map/ppermute | solution.py:70
  18.2 5.0 %collective-permute-done.1 = bf16[2,128,256]{2,1,0:T(8,128)(2,1)S(1)} collective-permute-done((bf16[2,128,256]{2,1,0:T(8,128)(2,1)S(1)}, bf16[2,128,256]{2,1,0:T(8,128)(2,1)S(1)}, u32[]{:S(2)}, u32[]{:S(2)}) %collective-permute-start.1) | collective-permute-done | bytes 131104 | tf_op jit(solution)/shard_map/ppermute | solution.py:58
  25.2 4.9 %collective-permute-done.3 = bf16[2,128,256]{2,1,0:T(8,128)(2,1)S(1)} collective-permute-done((bf16[2,128,256]{2,1,0:T(8,128)(2,1)S(1)}, bf16[2,128,256]{2,1,0:T(8,128)(2,1)S(1)}, u32[]{:S(2)}, u32[]{:S(2)}) %collective-permute-start.3) | collective-permute-done | bytes 131104 | tf_op jit(solution)/shard_map/ppermute | solution.py:58
  34.1 8.6 %collective-permute-start.5 = (bf16[8,128,256]{2,1,0:T(8,128)(2,1)S(1)}, bf16[8,128,256]{2,1,0:T(8,128)(2,1)S(1)}, u32[]{:S(2)}, u32[]{:S(2)}) collective-permute-start(bf16[8,128,256]{2,1,0:T(8,128)(2,1)S(1)} %constant_dynamic-update-slice_fusion.refs_0_), channel_id=1, source_target_pairs={{0,7},{1,0},{2,1},{3,2},{4,3},{5,4},{6,5},{7,6},{8,15},{9,8},{10,9... | collective-permute-start | bytes 1572872 | tf_op jit(solution)/shard_map/ppermute | solution.py:60
  42.7 5.4 %collective-permute-done.4.refs_1_ = bf16[8,128,256]{2,1,0:T(8,128)(2,1)S(1)} collective-permute-done((bf16[8,128,256]{2,1,0:T(8,128)(2,1)S(1)}, bf16[8,128,256]{2,1,0:T(8,128)(2,1)S(1)}, u32[]{:S(2)}, u32[]{:S(2)}) %collective-permute-start.4) | collective-permute-done | bytes 524320 | tf_op jit(solution)/shard_map/ppermute | solution.py:58
  76.8 6.9 %collective-permute-done.10.refs_7_ = bf16[8,128,256]{2,1,0:T(8,128)(2,1)} collective-permute-done((bf16[8,128,256]{2,1,0:T(8,128)(2,1)S(1)}, bf16[8,128,256]{2,1,0:T(8,128)(2,1)}, u32[]{:S(2)}, u32[]{:S(2)}) %collective-permute-start.10) | collective-permute-done | bytes 524320 | tf_op jit(solution)/shard_map/ppermute | solution.py:58
  83.7 9.8 %shard_map.111 = f32[1024,256]{1,0:T(8,128)} custom-call(s32[96]{0:T(128)} %fusion.27.slots_ref, bf16[1,8,1,12,128,128]{5,4,3,2,1,0:T(8,128)(2,1)} %vals_ref.3, bf16[8,128,256]{2,1,0:T(8,128)(2,1)} %copy-done.5, bf16[8,128,256]{2,1,0:T(8,128)(2,1)} %copy-done.8, bf16[8,128,256]{2,1,0:T(8,128)(2,1)} %copy-done.9, bf16[8,128,256]{2,1,0:T(8,128)(2,1)} %copy-done.10, ...), custom_call_target="tpu_custom_call" | custom-call | flops 805306368 | bytes 8388608 | tf_op jit(solution)/shard_map/pallas_call | solution.py:206
  95.5 10.7 %collective-permute-start.11 = (f32[4,128,256]{2,1,0:T(8,128)S(1)}, f32[4,128,256]{2,1,0:T(8,128)S(1)}, u32[]{:S(2)}, u32[]{:S(2)}) collective-permute-start(f32[4,128,256]{2,1,0:T(8,128)S(1)} %select_bitcast_fusion.1), channel_id=1, source_target_pairs={{0,64},{64,0},{1,65},{65,1},{2,66},{66,2},{3,67},{67,3},{4,68},{68... | collective-permute-start | bytes 1572872 | tf_op jit(solution)/shard_map/ppermute | solution.py:97
  110.1 7.3 %collective-permute-done.12 = f32[2,128,256]{2,1,0:T(8,128)S(1)} collective-permute-done((f32[2,128,256]{2,1,0:T(8,128)S(1)}, f32[2,128,256]{2,1,0:T(8,128)S(1)}, u32[]{:S(2)}, u32[]{:S(2)}) %collective-permute-start.12) | collective-permute-done | bytes 262176 | tf_op jit(solution)/shard_map/ppermute | solution.py:97
  117.5 5.6 %collective-permute-start.13 = (f32[1,128,256]{2,1,0:T(8,128)S(1)}, f32[1,128,256]{2,1,0:T(8,128)S(1)}, u32[]{:S(2)}, u32[]{:S(2)}) collective-permute-start(f32[1,128,256]{2,1,0:T(8,128)S(1)} %select_bitcast_fusion.5), channel_id=1, source_target_pairs={{0,256},{128,384},{256,0},{384,128},{1,257},{129,385},{257,1},{385... | collective-permute-start | bytes 393224 | tf_op jit(solution)/shard_map/ppermute | solution.py:97
  123.1 6.7 %collective-permute-done.13 = f32[1,128,256]{2,1,0:T(8,128)S(1)} collective-permute-done((f32[1,128,256]{2,1,0:T(8,128)S(1)}, f32[1,128,256]{2,1,0:T(8,128)S(1)}, u32[]{:S(2)}, u32[]{:S(2)}) %collective-permute-start.13) | collective-permute-done | bytes 131104 | tf_op jit(solution)/shard_map/ppermute | solution.py:97
  132.5 7.9 %collective-permute-start.14 = (bf16[128,256]{1,0:T(8,128)(2,1)S(1)}, bf16[128,256]{1,0:T(8,128)(2,1)S(1)}, u32[]{:S(2)}, u32[]{:S(2)}) collective-permute-start(bf16[128,256]{1,0:T(8,128)(2,1)S(1)} %get-tuple-element.41), channel_id=1, source_target_pairs={{0,32},{32,0},{1,33},{33,1},{2,34},{34,2},{3,35},{35,3},{4,36},{36... | collective-permute-start | bytes 196616 | tf_op jit(solution)/shard_map/ppermute | solution.py:70
  148.7 7.5 %collective-permute-start.19 = (bf16[4,128,256]{2,1,0:T(8,128)(2,1)S(1)}, bf16[4,128,256]{2,1,0:T(8,128)(2,1)S(1)}, u32[]{:S(2)}, u32[]{:S(2)}) collective-permute-start(bf16[4,128,256]{2,1,0:T(8,128)(2,1)S(1)} %maximum_select_fusion.2), channel_id=1, source_target_pairs={{0,64},{64,0},{1,65},{65,1},{2,66},{66,2},{3,67},{67,3},{4,68},{68... | collective-permute-start | bytes 786440 | tf_op jit(solution)/shard_map/ppermute | solution.py:97
  190.2 9.0 %collective-permute-done.26 = f32[132,256]{1,0:T(8,128)S(1)} collective-permute-done((f32[132,256]{1,0:T(8,128)S(1)}, f32[132,256]{1,0:T(8,128)S(1)}, u32[]{:S(2)}, u32[]{:S(2)}) %collective-permute-start.26) | collective-permute-done | bytes 135200 | tf_op jit(solution)/shard_map/ppermute | solution.py:97
  201.4 6.0 %collective-permute-done.27 = f32[132,256]{1,0:T(8,128)S(1)} collective-permute-done((f32[132,256]{1,0:T(8,128)S(1)}, f32[132,256]{1,0:T(8,128)S(1)}, u32[]{:S(2)}, u32[]{:S(2)}) %collective-permute-start.27) | collective-permute-done | bytes 135200 | tf_op jit(solution)/shard_map/ppermute | solution.py:97
  216.5 4.8 %collective-permute-done.30 = f32[132,256]{1,0:T(8,128)S(1)} collective-permute-done((f32[132,256]{1,0:T(8,128)S(1)}, f32[132,256]{1,0:T(8,128)S(1)}, u32[]{:S(2)}, u32[]{:S(2)}) %collective-permute-start.30) | collective-permute-done | bytes 135200 | tf_op jit(solution)/shard_map/ppermute | solution.py:97
  223.9 6.1 %collective-permute-done.31 = f32[132,256]{1,0:T(8,128)S(1)} collective-permute-done((f32[132,256]{1,0:T(8,128)S(1)}, f32[132,256]{1,0:T(8,128)S(1)}, u32[]{:S(2)}, u32[]{:S(2)}) %collective-permute-start.31) | collective-permute-done | bytes 135200 | tf_op jit(solution)/shard_map/ppermute | solution.py:97
  241.4 7.0 %collective-permute-done.34 = f32[132,256]{1,0:T(8,128)S(1)} collective-permute-done((f32[132,256]{1,0:T(8,128)S(1)}, f32[132,256]{1,0:T(8,128)S(1)}, u32[]{:S(2)}, u32[]{:S(2)}) %collective-permute-start.34) | collective-permute-done | bytes 135200 | tf_op jit(solution)/shard_map/ppermute | solution.py:97
  248.3 7.4 %collective-permute-start.35 = (f32[132,256]{1,0:T(8,128)S(1)}, f32[132,256]{1,0:T(8,128)S(1)}, u32[]{:S(2)}, u32[]{:S(2)}) collective-permute-start(f32[132,256]{1,0:T(8,128)S(1)} %add.189), channel_id=1, source_target_pairs={{0,32},{32,0},{1,33},{33,1},{2,34},{34,2},{3,35},{35,3},{4,36},{36... | collective-permute-start | bytes 405512 | tf_op jit(solution)/shard_map/ppermute | solution.py:97
  260.8 11.8 %collective-permute-start.37 = (f32[132,256]{1,0:T(8,128)S(1)}, f32[132,256]{1,0:T(8,128)S(1)}, u32[]{:S(2)}, u32[]{:S(2)}) collective-permute-start(f32[132,256]{1,0:T(8,128)S(1)} %add.190), channel_id=1, source_target_pairs={{0,64},{64,0},{1,65},{65,1},{2,66},{66,2},{3,67},{67,3},{4,68},{68... | collective-permute-start | bytes 405512 | tf_op jit(solution)/shard_map/ppermute | solution.py:97
  273.7 9.8 %shard_map.112 = f32[1024,256]{1,0:T(8,128)} custom-call(s32[96]{0:T(128)} %fusion.27.slots_ref, bf16[1,8,1,12,128,128]{5,4,3,2,1,0:T(8,128)(2,1)} %vals_ref.3, bf16[8,128,256]{2,1,0:T(8,128)(2,1)} %copy-done.4, bf16[8,128,256]{2,1,0:T(8,128)(2,1)} %copy-done.7, bf16[8,128,256]{2,1,0:T(8,128)(2,1)} %copy-done.6, bf16[8,128,256]{2,1,0:T(8,128)(2,1)} %copy-done.12, ...), custom_call_target="tpu_custom_call" | custom-call | flops 805306368 | bytes 8388608 | tf_op jit(solution)/shard_map/pallas_call | solution.py:206
  284.8 9.4 %collective-permute-start.38 = (f32[4,128,256]{2,1,0:T(8,128)S(1)}, f32[4,128,256]{2,1,0:T(8,128)S(1)}, u32[]{:S(2)}, u32[]{:S(2)}) collective-permute-start(f32[4,128,256]{2,1,0:T(8,128)S(1)} %select_bitcast_fusion), channel_id=1, source_target_pairs={{0,64},{64,0},{1,65},{65,1},{2,66},{66,2},{3,67},{67,3},{4,68},{68... | collective-permute-start | bytes 1572872 | tf_op jit(solution)/shard_map/ppermute | solution.py:97
  299.0 7.5 %collective-permute-done.39 = f32[2,128,256]{2,1,0:T(8,128)S(1)} collective-permute-done((f32[2,128,256]{2,1,0:T(8,128)S(1)}, f32[2,128,256]{2,1,0:T(8,128)S(1)}, u32[]{:S(2)}, u32[]{:S(2)}) %collective-permute-start.39) | collective-permute-done | bytes 262176 | tf_op jit(solution)/shard_map/ppermute | solution.py:97
  310.5 7.1 %collective-permute-done.40 = f32[1,128,256]{2,1,0:T(8,128)S(1)} collective-permute-done((f32[1,128,256]{2,1,0:T(8,128)S(1)}, f32[1,128,256]{2,1,0:T(8,128)S(1)}, u32[]{:S(2)}, u32[]{:S(2)}) %collective-permute-start.40) | collective-permute-done | bytes 131104 | tf_op jit(solution)/shard_map/ppermute | solution.py:97
  (157 shorter events, 136.2 us)
Async XLA Ops:
  0.7 10.3 %collective-permute-start = (bf16[128,256]{1,0:T(8,128)(2,1)}, bf16[128,256]{1,0:T(8,128)(2,1)S(1)}, u32[]{:S(2)}, u32[]{:S(2)}) collective-permute-start(bf16[128,256]{1,0:T(8,128)(2,1)} %param.8), channel_id=1, source_target_pairs={{0,32},{32,0},{1,33},{33,1},{2,34},{34,2},{3,35},{35,3},{4,36},{36... | collective-permute-start | bytes 196616 | tf_op jit(solution)/shard_map/ppermute | solution.py:70
  11.9 13.3 %collective-permute-start.2 = (bf16[2,128,256]{2,1,0:T(8,128)(2,1)S(1)}, bf16[2,128,256]{2,1,0:T(8,128)(2,1)S(1)}, u32[]{:S(2)}, u32[]{:S(2)}) collective-permute-start(bf16[2,128,256]{2,1,0:T(8,128)(2,1)S(1)} %pad_maximum_fusion.3), channel_id=1, source_target_pairs={{0,24},{8,0},{16,8},{24,16},{1,25},{9,1},{17,9},{25,17},{2,26},{10... | collective-permute-start | bytes 393224 | tf_op jit(solution)/shard_map/ppermute | solution.py:60
  30.1 18.0 %collective-permute-start.4 = (bf16[8,128,256]{2,1,0:T(8,128)(2,1)S(1)}, bf16[8,128,256]{2,1,0:T(8,128)(2,1)S(1)}, u32[]{:S(2)}, u32[]{:S(2)}) collective-permute-start(bf16[8,128,256]{2,1,0:T(8,128)(2,1)S(1)} %constant_dynamic-update-slice_fusion.refs_0_), channel_id=1, source_target_pairs={{0,1},{1,2},{2,3},{3,4},{4,5},{5,6},{6,7},{7,0},{8,9},{9,10},{10,1... | collective-permute-start | bytes 1572872 | tf_op jit(solution)/shard_map/ppermute | solution.py:58
  34.1 15.9 %collective-permute-start.5 = (bf16[8,128,256]{2,1,0:T(8,128)(2,1)S(1)}, bf16[8,128,256]{2,1,0:T(8,128)(2,1)S(1)}, u32[]{:S(2)}, u32[]{:S(2)}) collective-permute-start(bf16[8,128,256]{2,1,0:T(8,128)(2,1)S(1)} %constant_dynamic-update-slice_fusion.refs_0_), channel_id=1, source_target_pairs={{0,7},{1,0},{2,1},{3,2},{4,3},{5,4},{6,5},{7,6},{8,15},{9,8},{10,9... | collective-permute-start | bytes 1572872 | tf_op jit(solution)/shard_map/ppermute | solution.py:60
  48.1 11.1 %collective-permute-start.6 = (bf16[8,128,256]{2,1,0:T(8,128)(2,1)S(1)}, bf16[8,128,256]{2,1,0:T(8,128)(2,1)S(1)}, u32[]{:S(2)}, u32[]{:S(2)}) collective-permute-start(bf16[8,128,256]{2,1,0:T(8,128)(2,1)S(1)} %collective-permute-done.4.refs_1_), channel_id=1, source_target_pairs={{0,1},{1,2},{2,3},{3,4},{4,5},{5,6},{6,7},{7,0},{8,9},{9,10},{10,1... | collective-permute-start | bytes 1572872 | tf_op jit(solution)/shard_map/ppermute | solution.py:58
  50.1 13.1 %collective-permute-start.7 = (bf16[8,128,256]{2,1,0:T(8,128)(2,1)S(1)}, bf16[8,128,256]{2,1,0:T(8,128)(2,1)S(1)}, u32[]{:S(2)}, u32[]{:S(2)}) collective-permute-start(bf16[8,128,256]{2,1,0:T(8,128)(2,1)S(1)} %collective-permute-done.5.refs_2_), channel_id=1, source_target_pairs={{0,7},{1,0},{2,1},{3,2},{4,3},{5,4},{6,5},{7,6},{8,15},{9,8},{10,9... | collective-permute-start | bytes 1572872 | tf_op jit(solution)/shard_map/ppermute | solution.py:60
  59.3 11.6 %collective-permute-start.8 = (bf16[8,128,256]{2,1,0:T(8,128)(2,1)S(1)}, bf16[8,128,256]{2,1,0:T(8,128)(2,1)S(1)}, u32[]{:S(2)}, u32[]{:S(2)}) collective-permute-start(bf16[8,128,256]{2,1,0:T(8,128)(2,1)S(1)} %collective-permute-done.6.refs_3_), channel_id=1, source_target_pairs={{0,1},{1,2},{2,3},{3,4},{4,5},{5,6},{6,7},{7,0},{8,9},{9,10},{10,1... | collective-permute-start | bytes 1572872 | tf_op jit(solution)/shard_map/ppermute | solution.py:58
  63.2 13.6 %collective-permute-start.9 = (bf16[8,128,256]{2,1,0:T(8,128)(2,1)S(1)}, bf16[8,128,256]{2,1,0:T(8,128)(2,1)}, u32[]{:S(2)}, u32[]{:S(2)}) collective-permute-start(bf16[8,128,256]{2,1,0:T(8,128)(2,1)S(1)} %collective-permute-done.7.refs_4_), channel_id=1, source_target_pairs={{0,7},{1,0},{2,1},{3,2},{4,3},{5,4},{6,5},{7,6},{8,15},{9,8},{10,9... | collective-permute-start | bytes 1572872 | tf_op jit(solution)/shard_map/ppermute | solution.py:60
  70.9 12.8 %collective-permute-start.10 = (bf16[8,128,256]{2,1,0:T(8,128)(2,1)S(1)}, bf16[8,128,256]{2,1,0:T(8,128)(2,1)}, u32[]{:S(2)}, u32[]{:S(2)}) collective-permute-start(bf16[8,128,256]{2,1,0:T(8,128)(2,1)S(1)} %collective-permute-done.8.refs_5_), channel_id=1, source_target_pairs={{0,1},{1,2},{2,3},{3,4},{4,5},{5,6},{6,7},{7,0},{8,9},{9,10},{10,1... | collective-permute-start | bytes 1572872 | tf_op jit(solution)/shard_map/ppermute | solution.py:58
  95.5 12.3 %collective-permute-start.11 = (f32[4,128,256]{2,1,0:T(8,128)S(1)}, f32[4,128,256]{2,1,0:T(8,128)S(1)}, u32[]{:S(2)}, u32[]{:S(2)}) collective-permute-start(f32[4,128,256]{2,1,0:T(8,128)S(1)} %select_bitcast_fusion.1), channel_id=1, source_target_pairs={{0,64},{64,0},{1,65},{65,1},{2,66},{66,2},{3,67},{67,3},{4,68},{68... | collective-permute-start | bytes 1572872 | tf_op jit(solution)/shard_map/ppermute | solution.py:97
  117.5 12.3 %collective-permute-start.13 = (f32[1,128,256]{2,1,0:T(8,128)S(1)}, f32[1,128,256]{2,1,0:T(8,128)S(1)}, u32[]{:S(2)}, u32[]{:S(2)}) collective-permute-start(f32[1,128,256]{2,1,0:T(8,128)S(1)} %select_bitcast_fusion.5), channel_id=1, source_target_pairs={{0,256},{128,384},{256,0},{384,128},{1,257},{129,385},{257,1},{385... | collective-permute-start | bytes 393224 | tf_op jit(solution)/shard_map/ppermute | solution.py:97
  172.9 10.0 %collective-permute-start.21 = (bf16[2,128,256]{2,1,0:T(8,128)(2,1)S(1)}, bf16[2,128,256]{2,1,0:T(8,128)(2,1)S(1)}, u32[]{:S(2)}, u32[]{:S(2)}) collective-permute-start(bf16[2,128,256]{2,1,0:T(8,128)(2,1)S(1)} %collective-permute-done.16), channel_id=1, source_target_pairs={{0,8},{8,16},{16,24},{24,0},{1,9},{9,17},{17,25},{25,1},{2,10},{10... | collective-permute-start | bytes 393224 | tf_op jit(solution)/shard_map/ppermute | solution.py:58
  183.0 24.5 %collective-permute-start.25 = (bf16[8,128,256]{2,1,0:T(8,128)(2,1)S(1)}, bf16[8,128,256]{2,1,0:T(8,128)(2,1)S(1)}, u32[]{:S(2)}, u32[]{:S(2)}) collective-permute-start(bf16[8,128,256]{2,1,0:T(8,128)(2,1)S(1)} %constant_dynamic-update-slice_fusion.5.refs_0_), channel_id=1, source_target_pairs={{0,7},{1,0},{2,1},{3,2},{4,3},{5,4},{6,5},{7,6},{8,15},{9,8},{10,9... | collective-permute-start | bytes 1572872 | tf_op jit(solution)/shard_map/ppermute | solution.py:60
  186.3 21.1 %collective-permute-start.24 = (bf16[8,128,256]{2,1,0:T(8,128)(2,1)S(1)}, bf16[8,128,256]{2,1,0:T(8,128)(2,1)S(1)}, u32[]{:S(2)}, u32[]{:S(2)}) collective-permute-start(bf16[8,128,256]{2,1,0:T(8,128)(2,1)S(1)} %constant_dynamic-update-slice_fusion.5.refs_0_), channel_id=1, source_target_pairs={{0,1},{1,2},{2,3},{3,4},{4,5},{5,6},{6,7},{7,0},{8,9},{9,10},{10,1... | collective-permute-start | bytes 1572872 | tf_op jit(solution)/shard_map/ppermute | solution.py:58
  188.3 10.9 %collective-permute-start.26 = (f32[132,256]{1,0:T(8,128)S(1)}, f32[132,256]{1,0:T(8,128)S(1)}, u32[]{:S(2)}, u32[]{:S(2)}) collective-permute-start(f32[132,256]{1,0:T(8,128)S(1)} %add.184), channel_id=1, source_target_pairs={{0,1},{1,0},{2,3},{3,2},{4,5},{5,4},{6,7},{7,6},{8,9},{9,8},{10,11... | collective-permute-start | bytes 405512 | tf_op jit(solution)/shard_map/ppermute | solution.py:97
  207.5 22.6 %collective-permute-start.28 = (bf16[8,128,256]{2,1,0:T(8,128)(2,1)S(1)}, bf16[8,128,256]{2,1,0:T(8,128)(2,1)S(1)}, u32[]{:S(2)}, u32[]{:S(2)}) collective-permute-start(bf16[8,128,256]{2,1,0:T(8,128)(2,1)S(1)} %collective-permute-done.24.refs_1_), channel_id=1, source_target_pairs={{0,1},{1,2},{2,3},{3,4},{4,5},{5,6},{6,7},{7,0},{8,9},{9,10},{10,1... | collective-permute-start | bytes 1572872 | tf_op jit(solution)/shard_map/ppermute | solution.py:58
  211.6 18.5 %collective-permute-start.29 = (bf16[8,128,256]{2,1,0:T(8,128)(2,1)S(1)}, bf16[8,128,256]{2,1,0:T(8,128)(2,1)S(1)}, u32[]{:S(2)}, u32[]{:S(2)}) collective-permute-start(bf16[8,128,256]{2,1,0:T(8,128)(2,1)S(1)} %collective-permute-done.25.refs_2_), channel_id=1, source_target_pairs={{0,7},{1,0},{2,1},{3,2},{4,3},{5,4},{6,5},{7,6},{8,15},{9,8},{10,9... | collective-permute-start | bytes 1572872 | tf_op jit(solution)/shard_map/ppermute | solution.py:60
  230.1 28.1 %collective-permute-start.32 = (bf16[8,128,256]{2,1,0:T(8,128)(2,1)S(1)}, bf16[8,128,256]{2,1,0:T(8,128)(2,1)S(1)}, u32[]{:S(2)}, u32[]{:S(2)}) collective-permute-start(bf16[8,128,256]{2,1,0:T(8,128)(2,1)S(1)} %collective-permute-done.28.refs_3_), channel_id=1, source_target_pairs={{0,1},{1,2},{2,3},{3,4},{4,5},{5,6},{6,7},{7,0},{8,9},{9,10},{10,1... | collective-permute-start | bytes 1572872 | tf_op jit(solution)/shard_map/ppermute | solution.py:58
  232.0 26.2 %collective-permute-start.33 = (bf16[8,128,256]{2,1,0:T(8,128)(2,1)S(1)}, bf16[8,128,256]{2,1,0:T(8,128)(2,1)S(1)}, u32[]{:S(2)}, u32[]{:S(2)}) collective-permute-start(bf16[8,128,256]{2,1,0:T(8,128)(2,1)S(1)} %collective-permute-done.29.refs_4_), channel_id=1, source_target_pairs={{0,7},{1,0},{2,1},{3,2},{4,3},{5,4},{6,5},{7,6},{8,15},{9,8},{10,9... | collective-permute-start | bytes 1572872 | tf_op jit(solution)/shard_map/ppermute | solution.py:60
  236.6 11.7 %collective-permute-start.34 = (f32[132,256]{1,0:T(8,128)S(1)}, f32[132,256]{1,0:T(8,128)S(1)}, u32[]{:S(2)}, u32[]{:S(2)}) collective-permute-start(f32[132,256]{1,0:T(8,128)S(1)} %add.188), channel_id=1, source_target_pairs={{0,4},{1,5},{2,6},{3,7},{4,0},{5,1},{6,2},{7,3},{8,12},{9,13},{10,... | collective-permute-start | bytes 405512 | tf_op jit(solution)/shard_map/ppermute | solution.py:97
  258.2 15.4 %collective-permute-start.36 = (bf16[8,128,256]{2,1,0:T(8,128)(2,1)S(1)}, bf16[8,128,256]{2,1,0:T(8,128)(2,1)}, u32[]{:S(2)}, u32[]{:S(2)}) collective-permute-start(bf16[8,128,256]{2,1,0:T(8,128)(2,1)S(1)} %collective-permute-done.32.refs_5_), channel_id=1, source_target_pairs={{0,1},{1,2},{2,3},{3,4},{4,5},{5,6},{6,7},{7,0},{8,9},{9,10},{10,1... | collective-permute-start | bytes 1572872 | tf_op jit(solution)/shard_map/ppermute | solution.py:58
  260.8 12.8 %collective-permute-start.37 = (f32[132,256]{1,0:T(8,128)S(1)}, f32[132,256]{1,0:T(8,128)S(1)}, u32[]{:S(2)}, u32[]{:S(2)}) collective-permute-start(f32[132,256]{1,0:T(8,128)S(1)} %add.190), channel_id=1, source_target_pairs={{0,64},{64,0},{1,65},{65,1},{2,66},{66,2},{3,67},{67,3},{4,68},{68... | collective-permute-start | bytes 405512 | tf_op jit(solution)/shard_map/ppermute | solution.py:97
  284.8 10.9 %collective-permute-start.38 = (f32[4,128,256]{2,1,0:T(8,128)S(1)}, f32[4,128,256]{2,1,0:T(8,128)S(1)}, u32[]{:S(2)}, u32[]{:S(2)}) collective-permute-start(f32[4,128,256]{2,1,0:T(8,128)S(1)} %select_bitcast_fusion), channel_id=1, source_target_pairs={{0,64},{64,0},{1,65},{65,1},{2,66},{66,2},{3,67},{67,3},{4,68},{68... | collective-permute-start | bytes 1572872 | tf_op jit(solution)/shard_map/ppermute | solution.py:97
  306.6 11.0 %collective-permute-start.40 = (f32[1,128,256]{2,1,0:T(8,128)S(1)}, f32[1,128,256]{2,1,0:T(8,128)S(1)}, u32[]{:S(2)}, u32[]{:S(2)}) collective-permute-start(f32[1,128,256]{2,1,0:T(8,128)S(1)} %select_bitcast_fusion.4), channel_id=1, source_target_pairs={{0,256},{128,384},{256,0},{384,128},{1,257},{129,385},{257,1},{385... | collective-permute-start | bytes 393224 | tf_op jit(solution)/shard_map/ppermute | solution.py:97
  (37 other events, 995.4 us)
